TPU v7x, 32 devices: a whole 2x2x4 slice. The times are simulated.
32 devices in a mesh: gx: 4 (over x, core), gy: 2 (over y), orb: 4 (over z).
Axes of the slice: x: 2, y: 2, z: 4, core: 2. Of those that a mesh axis runs over, the one named last changes fastest.
Arguments:
- orbitals: float32 [4, 32, 32, 384], P('orb', 'gx', 'gy'), may hold values from -6 to 6
- local_pot: float32 [32, 32, 384], P('gx', 'gy'), may hold values from -1 to 1
- proj_vals: bfloat16 [4, 32, 32, 384], P(None, 'gx', 'gy'), may hold values from -0.29882812 to 0.29882812
- proj_ids: int32 [4, 32, 32, 3], P(None, 'gx', 'gy'), may hold values from 0 to 4095, as said below
- proj_energy: float32 [4096], replicated, may hold values from 0.5 to 2
- cheb_coef: float32 [4], replicated, may hold values from 0.2 to 1
Outputs:
- density: float32 [32, 32, 384], P('gx', 'gy')
Inputs may be any that keep to these rules, and one draw needn't show every extreme that they name: `proj_ids`: the owner o = id // 512 of each id names the column block (o // 2, o % 2); it differs from the block (x // 8, y // 16) of the slot's cells by at most one in each of the two coordinates, periodically.
All inputs are finite; a program needn't handle non-finite values.
Results may differ from a plain program's by a relative error of at most 0.0003.
Values sent between devices are 32-bit elements; how exact they have to be, the bound alone decides.
No kernel may reach another device: no remote copies, remote signals or barrier semaphores. Data moves between devices by JAX's collectives and lax.ppermute only.
A program may use at most 64 MiB of HBM per device.

v0:
```python
import jax
import jax.numpy as jnp
from jax import lax
from jax.sharding import PartitionSpec as P

ZB = 128
STEPS = 3


E_MID = 4.0
E_HALF = 8.0
PRECISE = lax.Precision.HIGHEST


def extended(block, sides, width):
    for axis, dim in sides:
        count = lax.axis_size(axis)
        forward = [(i, i + 1) for i in range(count - 1)]
        forward.append((count - 1, 0))
        backward = [(target, source) for source, target in forward]
        low = lax.ppermute(
            lax.slice_in_dim(block, block.shape[dim] - width, None, axis=dim), axis, forward
        )
        high = lax.ppermute(lax.slice_in_dim(block, 0, width, axis=dim), axis, backward)
        block = jnp.concatenate([low, block, high], axis=dim)
    return block


def stencil(grid_vals):
    extent_first = grid_vals.shape[1]
    extent_second = grid_vals.shape[2]
    padded = extended(grid_vals, (("gx", 1), ("gy", 2)), 2)
    middle_rows = padded[:, :, 2 : 2 + extent_second]
    middle_cols = padded[:, 2 : 2 + extent_first]
    result = -90.0 * grid_vals
    result = (
        result
        + 16.0 * (middle_rows[:, 1 : 1 + extent_first] + middle_rows[:, 3 : 3 + extent_first])
        - (middle_rows[:, 0:extent_first] + middle_rows[:, 4 : 4 + extent_first])
    )
    result = (
        result
        + 16.0
        * (middle_cols[:, :, 1 : 1 + extent_second] + middle_cols[:, :, 3 : 3 + extent_second])
        - (middle_cols[:, :, 0:extent_second] + middle_cols[:, :, 4 : 4 + extent_second])
    )
    result = (
        result
        + 16.0 * (jnp.roll(grid_vals, 1, 3) + jnp.roll(grid_vals, -1, 3))
        - (jnp.roll(grid_vals, 2, 3) + jnp.roll(grid_vals, -2, 3))
    )
    return result / 12.0


def local(orbitals, local_pot, proj_vals, proj_ids, proj_energy, cheb_coef):
    count_orb = orbitals.shape[0]
    extent_first = orbitals.shape[1]
    extent_second = orbitals.shape[2]
    extent_depth = orbitals.shape[3]
    slot_count = proj_vals.shape[0]
    block_count = extent_depth // ZB
    count_all = proj_energy.shape[0]
    shaped = proj_vals.astype(jnp.float32).reshape(
        slot_count, extent_first, extent_second, block_count, ZB
    )
    ids_flat = proj_ids.reshape(-1)

    def weights_of(blocks):
        partial_value = jax.vmap(
            lambda single: jax.ops.segment_sum(single, ids_flat, num_segments=count_all)
        )(blocks.reshape(count_orb, -1))
        coef_sums = lax.psum(partial_value, ("gx", "gy"))
        return jnp.take(coef_sums * proj_energy[None, :], ids_flat, axis=1)

    def hamilton(grid_vals):
        blocks = jnp.einsum(
            "kxyzb,oxyzb->okxyz",
            shaped,
            grid_vals.reshape(count_orb, extent_first, extent_second, block_count, ZB),
            precision=PRECISE,
        )
        weights = weights_of(blocks).reshape(
            count_orb, slot_count, extent_first, extent_second, block_count
        )
        projected = jnp.einsum("kxyzb,okxyz->oxyzb", shaped, weights, precision=PRECISE).reshape(
            grid_vals.shape
        )
        return (
            -0.5 * stencil(grid_vals) + local_pot[None] * grid_vals + projected - E_MID * grid_vals
        ) / E_HALF

    previous = orbitals
    current = hamilton(orbitals)
    filtered = cheb_coef[0] * previous + cheb_coef[1] * current
    for degree in range(2, STEPS + 1):
        following = 2.0 * hamilton(current) - previous
        previous = current
        current = following
        filtered = filtered + cheb_coef[degree] * current
    density = lax.psum(jnp.sum(filtered * filtered, axis=0), "orb")
    return density / (count_orb * lax.axis_size("orb"))


def solution(mesh):
    return jax.shard_map(
        local,
        mesh=mesh,
        in_specs=(
            P("orb", "gx", "gy", None),
            P("gx", "gy", None),
            P(None, "gx", "gy", None),
            P(None, "gx", "gy", None),
            P(),
            P(),
        ),
        out_specs=P("gx", "gy", None),
        check_vma=False,
    )
```

profile of v0, /device:TPU:16, one launch (start us, length us, event | category | flops | bytes accessed | tf_op | source)
XLA Modules:
  0.0 218.9 jit_solution(10837765373750434986)
XLA Ops:
  6.5 0.9 fusion.72
  7.5 1.7 collective-permute-start.1
  9.7 0.8 copy-done.2
  10.6 0.5 copy.9
  11.2 1.4 fusion.78
  12.6 1.0 copy.10
  13.8 0.6 copy-done.4
  14.9 8.6 %scatter_custom_fusion = f32[4096]{0:T(1024)S(1)} fusion(s32[1536]{0:T(1024)S(1)} %reshape.438, f32[1536]{0:T(1024)S(1)} %reshape.440, f32[]{:T(128)} %constant.38.clone.1), kind=kCustom, calls=%fused_computation.125 | custom fusion | flops 1536 | bytes 16388 | tf_op jit(solution)/shard_map/vmap()/scatter-add | solution.py:70
  23.5 24.0 %psum.28 = f32[1,4096]{1,0:T(1,128)S(1)} all-reduce(f32[1,4096]{1,0:T(1,128)S(1)} %bitcast.82), channel_id=1, replica_groups=mesh['gx'=4,'gy'=2,'orb'=4] {'gx','gy'}, use_global_device_ids=true, to_apply=%region_1.0 | all-reduce | flops 4096 | bytes 32768 | tf_op jit(solution)/shard_map/psum | solution.py:72
  47.4 0.7 copy-done.3
  48.2 8.4 %gather_fusion = f32[1536]{0:T(1024)S(1)} fusion(f32[4096]{0:T(1024)S(1)} %bitcast.70, s32[2048]{0:T(1024)S(1)} %pad_clamp_fusion), kind=kCustom, calls=%fused_computation.clone | custom fusion | bytes 18432 | tf_op jit(solution)/shard_map/jit(_take)/gather | solution.py:73
  56.8 0.9 copy.11
  57.7 1.4 fusion.79
  59.3 0.8 collective-permute-start.2
  60.1 1.3 collective-permute-start.3
  61.4 0.6 fusion.77
  62.9 0.5 collective-permute-done.2
  63.3 0.8 collective-permute-done.3
  64.1 0.6 copy-done.5
  64.7 1.1 broadcast_multiply_fusion.1
  66.3 1.7 collective-permute-start.5
  68.1 1.4 fusion.80
  69.5 1.0 copy.14
  70.7 8.6 %scatter_custom_fusion.1 = f32[4096]{0:T(1024)S(1)} fusion(s32[1536]{0:T(1024)S(1)} %reshape.438, f32[1536]{0:T(1024)S(1)} %reshape.450, f32[]{:T(128)} %constant.38.clone.1), kind=kCustom, calls=%fused_computation.123 | custom fusion | flops 1536 | bytes 16388 | tf_op jit(solution)/shard_map/vmap()/scatter-add | solution.py:70
  79.3 23.7 %psum.29 = f32[1,4096]{1,0:T(1,128)S(1)} all-reduce(f32[1,4096]{1,0:T(1,128)S(1)} %bitcast.83), channel_id=1, replica_groups=mesh['gx'=4,'gy'=2,'orb'=4] {'gx','gy'}, use_global_device_ids=true, to_apply=%region_3.5 | all-reduce | flops 4096 | bytes 32768 | tf_op jit(solution)/shard_map/psum | solution.py:72
  103.0 8.4 %gather_fusion.1 = f32[1536]{0:T(1024)S(1)} fusion(f32[4096]{0:T(1024)S(1)} %bitcast.71, s32[2048]{0:T(1024)S(1)} %pad_clamp_fusion), kind=kCustom, calls=%fused_computation.1.clone | custom fusion | bytes 18432 | tf_op jit(solution)/shard_map/jit(_take)/gather | solution.py:73
  111.6 0.9 copy.15
  112.5 1.4 fusion.81
  114.0 1.1 collective-permute-start.6
  115.1 1.0 collective-permute-start.7
  116.4 1.7 collective-permute-done.6
  118.1 1.0 collective-permute-done.7
  119.1 0.3 fusion.30
  119.9 1.7 collective-permute-start.9
  121.6 1.4 fusion.82
  123.0 1.0 copy.18
  124.3 8.6 %scatter_custom_fusion.2 = f32[4096]{0:T(1024)S(1)} fusion(s32[1536]{0:T(1024)S(1)} %reshape.438, f32[1536]{0:T(1024)S(1)} %reshape.460, f32[]{:T(128)} %constant.38.clone.1), kind=kCustom, calls=%fused_computation.121 | custom fusion | flops 1536 | bytes 16388 | tf_op jit(solution)/shard_map/vmap()/scatter-add | solution.py:70
  132.9 23.4 %psum.30 = f32[1,4096]{1,0:T(1,128)S(1)} all-reduce(f32[1,4096]{1,0:T(1,128)S(1)} %bitcast.81), channel_id=1, replica_groups=mesh['gx'=4,'gy'=2,'orb'=4] {'gx','gy'}, use_global_device_ids=true, to_apply=%region_5.7 | all-reduce | flops 4096 | bytes 32768 | tf_op jit(solution)/shard_map/psum | solution.py:72
  156.3 8.4 %gather_fusion.2 = f32[1536]{0:T(1024)S(1)} fusion(f32[4096]{0:T(1024)S(1)} %bitcast.69, s32[2048]{0:T(1024)S(1)} %pad_clamp_fusion), kind=kCustom, calls=%fused_computation.2.clone | custom fusion | bytes 18432 | tf_op jit(solution)/shard_map/jit(_take)/gather | solution.py:73
  164.9 0.9 copy.19
  165.8 1.4 fusion.83
  167.3 1.3 collective-permute-start.10
  168.6 0.8 collective-permute-start.11
  169.6 1.7 collective-permute-done.10
  171.3 1.3 collective-permute-done.11
  172.6 3.0 %multiply_bitcast_fusion = f32[8,16,384]{2,1,0:T(8,128)} fusion(f32[1,8,16,384]{3,2,1,0:T(8,128)S(1)} %fusion.30, f32[1,8,16,384]{3,2,1,0:T(8,128)S(1)} %get-tuple-element.7, f32[1,8,16,384]{3,2,1,0:T(8,128)S(1)} %copy-done, f32[1,8,16,384]{3,2,1,0:T(8,128)S(1)} %transpose.23, f32[8,16,384]{2,1,0:T(8,128)S(1)} %copy-done.1, ...), kind=kLoop, calls=%fused_computation.103 | loop fusion | flops 2605056 | bytes 2138128 | tf_op jit(solution)/shard_map/reduce_sum | solution.py:100
  175.6 34.9 %all-reduce.2.cloned.1.call-done = f32[8,16,384]{2,1,0:T(8,128)} async-done(((f32[8,16,384]{2,1,0:T(8,128)}), f32[8,16,384]{2,1,0:T(8,128)}) %all-reduce.2.cloned.1.call-update) | async-done | bytes 196624 | tf_op jit(solution)/shard_map/psum | solution.py:100
  210.5 1.6 broadcast_multiply_fusion
  (67 shorter events, 4.5 us)
Async XLA Ops:
  6.5 2.7 %copy-start = (f32[1,8,16,384]{3,2,1,0:T(8,128)S(1)}, f32[1,8,16,384]{3,2,1,0:T(8,128)}, u32[]{:S(2)}) copy-start(f32[1,8,16,384]{3,2,1,0:T(8,128)} %param.8) | copy-start | bytes 589828
  6.5 203.9 %all-reduce.2.cloned.1.call-start = ((), (), s32[]{:S(2)}) async-start(), calls=%async_computation | async-start | bytes 393216 | tf_op jit(solution)/shard_map/psum | solution.py:100
  7.4 51.7 %collective-permute-start = (f32[1,2,16,384]{3,2,1,0:T(8,128)S(1)}, f32[1,2,16,384]{3,2,1,0:T(8,128)S(1)}, u32[]{:S(2)}, u32[]{:S(2)}) collective-permute-start(f32[1,2,16,384]{3,2,1,0:T(8,128)S(1)} %get-tuple-element.40), channel_id=1, source_target_pairs={{0,8},{8,16},{16,24},{24,0},{1,9},{9,17},{17,25},{25,1},{2,10},{10... | collective-permute-start | bytes 147464 | tf_op jit(solution)/shard_map/ppermute | solution.py:21
  7.5 51.7 %collective-permute-start.1 = (f32[1,2,16,384]{3,2,1,0:T(8,128)S(1)}, f32[1,2,16,384]{3,2,1,0:T(8,128)S(1)}, u32[]{:S(2)}, u32[]{:S(2)}) collective-permute-start(f32[1,2,16,384]{3,2,1,0:T(8,128)S(1)} %get-tuple-element.39), channel_id=1, source_target_pairs={{8,0},{16,8},{24,16},{0,24},{9,1},{17,9},{25,17},{1,25},{10,2},{18... | collective-permute-start | bytes 147464 | tf_op jit(solution)/shard_map/ppermute | solution.py:24
  9.5 1.0 copy-start.2
  13.6 0.8 copy-start.4
  47.4 0.7 copy-start.3
  59.3 2.1 copy-start.6
  59.3 4.0 %collective-permute-start.2 = (f32[1,12,2,384]{3,2,1,0:T(2,128)S(1)}, f32[1,12,2,384]{3,2,1,0:T(2,128)S(1)}, u32[]{:S(2)}, u32[]{:S(2)}) collective-permute-start(f32[1,12,2,384]{3,2,1,0:T(2,128)S(1)} %get-tuple-element.14), channel_id=1, source_target_pairs={{0,4},{4,0},{1,5},{5,1},{2,6},{6,2},{3,7},{7,3},{8,12},{12,8},{9,1... | collective-permute-start | bytes 110600 | tf_op jit(solution)/shard_map/ppermute | solution.py:21
  60.1 4.0 %collective-permute-start.3 = (f32[1,12,2,384]{3,2,1,0:T(2,128)S(1)}, f32[1,12,2,384]{3,2,1,0:T(2,128)S(1)}, u32[]{:S(2)}, u32[]{:S(2)}) collective-permute-start(f32[1,12,2,384]{3,2,1,0:T(2,128)S(1)} %get-tuple-element.15), channel_id=1, source_target_pairs={{4,0},{0,4},{5,1},{1,5},{6,2},{2,6},{7,3},{3,7},{12,8},{8,12},{13,... | collective-permute-start | bytes 110600 | tf_op jit(solution)/shard_map/ppermute | solution.py:24
  62.1 2.6 %copy-start.1 = (f32[8,16,384]{2,1,0:T(8,128)S(1)}, f32[8,16,384]{2,1,0:T(8,128)}, u32[]{:S(2)}) copy-start(f32[8,16,384]{2,1,0:T(8,128)} %param.9) | copy-start | bytes 589828
  64.1 0.6 copy-start.5
  66.3 47.7 %collective-permute-start.4 = (f32[1,2,16,384]{3,2,1,0:T(8,128)S(1)}, f32[1,2,16,384]{3,2,1,0:T(8,128)S(1)}, u32[]{:S(2)}, u32[]{:S(2)}) collective-permute-start(f32[1,2,16,384]{3,2,1,0:T(8,128)S(1)} %get-tuple-element.34), channel_id=1, source_target_pairs={{0,8},{8,16},{16,24},{24,0},{1,9},{9,17},{17,25},{25,1},{2,10},{10... | collective-permute-start | bytes 147464 | tf_op jit(solution)/shard_map/ppermute | solution.py:21
  66.3 47.6 %collective-permute-start.5 = (f32[1,2,16,384]{3,2,1,0:T(8,128)S(1)}, f32[1,2,16,384]{3,2,1,0:T(8,128)S(1)}, u32[]{:S(2)}, u32[]{:S(2)}) collective-permute-start(f32[1,2,16,384]{3,2,1,0:T(8,128)S(1)} %get-tuple-element.35), channel_id=1, source_target_pairs={{8,0},{16,8},{24,16},{0,24},{9,1},{17,9},{25,17},{1,25},{10,2},{18... | collective-permute-start | bytes 147464 | tf_op jit(solution)/shard_map/ppermute | solution.py:24
  114.0 4.0 %collective-permute-start.6 = (f32[1,12,2,384]{3,2,1,0:T(2,128)S(1)}, f32[1,12,2,384]{3,2,1,0:T(2,128)S(1)}, u32[]{:S(2)}, u32[]{:S(2)}) collective-permute-start(f32[1,12,2,384]{3,2,1,0:T(2,128)S(1)} %get-tuple-element.12), channel_id=1, source_target_pairs={{0,4},{4,0},{1,5},{5,1},{2,6},{6,2},{3,7},{7,3},{8,12},{12,8},{9,1... | collective-permute-start | bytes 110600 | tf_op jit(solution)/shard_map/ppermute | solution.py:21
  115.1 4.0 %collective-permute-start.7 = (f32[1,12,2,384]{3,2,1,0:T(2,128)S(1)}, f32[1,12,2,384]{3,2,1,0:T(2,128)S(1)}, u32[]{:S(2)}, u32[]{:S(2)}) collective-permute-start(f32[1,12,2,384]{3,2,1,0:T(2,128)S(1)} %get-tuple-element.13), channel_id=1, source_target_pairs={{4,0},{0,4},{5,1},{1,5},{6,2},{2,6},{7,3},{3,7},{12,8},{8,12},{13,... | collective-permute-start | bytes 110600 | tf_op jit(solution)/shard_map/ppermute | solution.py:24
  119.8 47.4 %collective-permute-start.8 = (f32[1,2,16,384]{3,2,1,0:T(8,128)S(1)}, f32[1,2,16,384]{3,2,1,0:T(8,128)S(1)}, u32[]{:S(2)}, u32[]{:S(2)}) collective-permute-start(f32[1,2,16,384]{3,2,1,0:T(8,128)S(1)} %get-tuple-element.16), channel_id=1, source_target_pairs={{0,8},{8,16},{16,24},{24,0},{1,9},{9,17},{17,25},{25,1},{2,10},{10... | collective-permute-start | bytes 147464 | tf_op jit(solution)/shard_map/ppermute | solution.py:21
  119.9 47.3 %collective-permute-start.9 = (f32[1,2,16,384]{3,2,1,0:T(8,128)S(1)}, f32[1,2,16,384]{3,2,1,0:T(8,128)S(1)}, u32[]{:S(2)}, u32[]{:S(2)}) collective-permute-start(f32[1,2,16,384]{3,2,1,0:T(8,128)S(1)} %get-tuple-element.17), channel_id=1, source_target_pairs={{8,0},{16,8},{24,16},{0,24},{9,1},{17,9},{25,17},{1,25},{10,2},{18... | collective-permute-start | bytes 147464 | tf_op jit(solution)/shard_map/ppermute | solution.py:24
  167.3 4.0 %collective-permute-start.10 = (f32[1,12,2,384]{3,2,1,0:T(2,128)S(1)}, f32[1,12,2,384]{3,2,1,0:T(2,128)S(1)}, u32[]{:S(2)}, u32[]{:S(2)}) collective-permute-start(f32[1,12,2,384]{3,2,1,0:T(2,128)S(1)} %get-tuple-element.10), channel_id=1, source_target_pairs={{0,4},{4,0},{1,5},{5,1},{2,6},{6,2},{3,7},{7,3},{8,12},{12,8},{9,1... | collective-permute-start | bytes 110600 | tf_op jit(solution)/shard_map/ppermute | solution.py:21
  168.6 4.0 %collective-permute-start.11 = (f32[1,12,2,384]{3,2,1,0:T(2,128)S(1)}, f32[1,12,2,384]{3,2,1,0:T(2,128)S(1)}, u32[]{:S(2)}, u32[]{:S(2)}) collective-permute-start(f32[1,12,2,384]{3,2,1,0:T(2,128)S(1)} %get-tuple-element.11), channel_id=1, source_target_pairs={{4,0},{0,4},{5,1},{1,5},{6,2},{2,6},{7,3},{3,7},{12,8},{8,12},{13,... | collective-permute-start | bytes 110600 | tf_op jit(solution)/shard_map/ppermute | solution.py:24
Sparse Core Ops, SparseCore 0:
  175.7 34.7 all-reduce.1
where the time goes:
time: 221 us; the launch traced here: 219 us
  blocking collectives  71 us (32%)
  waiting for transfers between devices  41.8 us (19%)
  local copies, waits for them, and re-layouts  39.7 us (18%)
  other arithmetic  31.9 us (14%)
  between operations  14.5 us (7%)
  starting transfers between devices  11.6 us (5%)
  matrix products  8.31 us (4%)
    psum x3, blocking collectives, weights_of(): coef_sums = lax.psum(partial_value, ('gx', 'gy'))  71 us
    psum x1, waiting for transfers between devices, local(): density = lax.psum(jnp.sum(filtered * filtered, axis=0), 'orb')  34.9 us
    scatter-add x3, other arithmetic, weights_of(): jax.ops.segment_sum(single, ids_flat, num_segments=count_all)  25.8 us
    gather x3, local copies, waits for them, and re-layouts, weights_of(): return jnp.take(coef_sums * proj_energy[None, :], ids_flat, axis=1)  25.2 us
    ppermute x6, starting transfers between devices, extended(): lax.ppermute(lax.slice_in_dim(block, 0, width, axis=dim), axis, backward)  8.23 us
  transfers between devices with their start and end apart: 13, of which 7 were waited for; matrix products, arithmetic and copies ran while one was open for 32% of the time, Pallas kernels for 0%

commit v1 on v0

v1 whole, which is shorter than its diff:
```python
import functools

import jax
import jax.numpy as jnp
from jax import lax
from jax.experimental import pallas as pl
from jax.experimental.pallas import tpu as pltpu
from jax.sharding import PartitionSpec as P

LANES = 128
SUBLANES = 8
STEPS = 3
E_MID = 4.0
E_HALF = 8.0
F32 = jnp.float32
BF16 = jnp.bfloat16


def pieces(vals):
    first = vals.astype(BF16)
    second = (vals - first.astype(F32)).astype(BF16)
    return first, second


def dot(a, b, contract):
    return lax.dot_general(a, b, (contract, ((), ())), preferred_element_type=F32)


NN = ((1,), (0,))
NT = ((1,), (1,))


def iota(shape, dim):
    return lax.broadcasted_iota(jnp.int32, shape, dim)


class Sizes:
    def __init__(self, extent_first, extent_second, extent_depth, slots, owner_size, rows):
        self.ex = extent_first
        self.ey = extent_second
        self.nz = extent_depth
        self.zb = extent_depth // LANES
        self.slots = slots
        self.cells = extent_first * extent_second
        self.rows = rows
        self.xedge = 2 * extent_second
        self.yedge = extent_first * SUBLANES // 2
        self.edge_rows = self.zb * self.xedge
        self.yedge_rows = self.zb * self.yedge
        assert extent_second == 2 * SUBLANES and extent_first % 2 == 0
        assert self.cells == LANES


def rows_of_ids(sz, ids_ref):
    ids = ids_ref[...].reshape(sz.slots * sz.cells, sz.zb)
    pick = jnp.where(
        iota((SUBLANES, sz.zb), 0) == iota((SUBLANES, sz.zb), 1), 1.0, 0.0
    ).astype(BF16)
    row = lax.shift_right_logical(ids, 7).astype(F32).astype(BF16)
    lane = jnp.bitwise_and(ids, LANES - 1).astype(F32).astype(BF16)
    return dot(pick, row, NT), dot(pick, lane, NT)


def chunk(sz, arr, zb, slot):
    return arr[zb : zb + 1, slot * sz.cells : (slot + 1) * sz.cells]


def chunks(sz):
    return [(zb, slot) for zb in range(sz.zb) for slot in range(sz.slots)]


def partial_table(sz, vals, pv_ref, row_of, hot_ref):
    eye = iota((sz.cells, LANES), 0) == iota((sz.cells, LANES), 1)
    eye_all = jnp.concatenate([eye] * sz.slots, axis=0)
    spread_first, spread_second = [], []
    table_iota = iota((sz.rows, LANES), 0).astype(F32)
    for zb in range(sz.zb):
        first, second = pieces(vals[:, zb * LANES : (zb + 1) * LANES])
        weights = pv_ref[:, zb * LANES : (zb + 1) * LANES]
        cross = dot(
            jnp.concatenate([weights, weights], axis=1),
            jnp.concatenate([first, second], axis=1),
            NT,
        )
        cross = jnp.where(eye_all, cross, 0.0)
        for slot in range(sz.slots):
            sums = jnp.sum(
                cross[slot * sz.cells : (slot + 1) * sz.cells], axis=0, keepdims=True
            )
            spread = jnp.where(chunk(sz, row_of, zb, slot) == table_iota, sums, 0.0)
            a, b = pieces(spread)
            spread_first.append(a)
            spread_second.append(b)
    lhs = jnp.concatenate(
        [jnp.concatenate(spread_first, axis=1), jnp.concatenate(spread_second, axis=1)], axis=0
    )
    both = dot(lhs, hot_ref[...], NT)
    return both[: sz.rows] + both[sz.rows :]


def projected(sz, table, pv_ref, row_of, hot_ref):
    first, second = pieces(table)
    found = dot(jnp.concatenate([first, second], axis=0), hot_ref[...], NN)
    found = found[: sz.rows] + found[sz.rows :]
    table_iota = iota((sz.rows, LANES), 0).astype(F32)
    eye = iota((sz.cells, LANES), 0) == iota((sz.cells, LANES), 1)
    result = []
    for zb in range(sz.zb):
        diag_first, diag_second = [], []
        for slot in range(sz.slots):
            at = (zb * sz.slots + slot) * LANES
            hit = chunk(sz, row_of, zb, slot) == table_iota
            weight = jnp.sum(
                jnp.where(hit, found[:, at : at + LANES], 0.0), axis=0, keepdims=True
            )
            a, b = pieces(jnp.where(eye, weight, 0.0))
            diag_first.append(a)
            diag_second.append(b)
        lhs = jnp.concatenate(
            [jnp.concatenate(diag_first, axis=1), jnp.concatenate(diag_second, axis=1)], axis=0
        )
        both = dot(lhs, pv_ref[:, zb * LANES : (zb + 1) * LANES], NN)
        result.append(both[: sz.cells] + both[sz.cells :])
    return result


def from_message(sz, msg_ref, rows):
    return jnp.concatenate(
        [msg_ref[zb * rows : (zb + 1) * rows, :] for zb in range(sz.zb)], axis=1
    )


def to_message(sz, msg_ref, vals):
    rows = vals.shape[0]
    for zb in range(sz.zb):
        msg_ref[zb * rows : (zb + 1) * rows, :] = vals[:, zb * LANES : (zb + 1) * LANES]


def second_edges(sz, vals):
    tiles = vals.reshape(sz.ex, 2, SUBLANES, sz.nz)
    sub = iota((sz.ex // 2, SUBLANES, sz.nz), 1)
    even = tiles.reshape(sz.ex // 2, 2, 2, SUBLANES, sz.nz)
    outer_even = jnp.where(sub < 4, even[:, 0, 0], even[:, 0, 1])
    outer_odd = jnp.where(sub < 4, even[:, 1, 0], even[:, 1, 1])
    odd = pltpu.roll(outer_odd, 4, axis=1)
    keep = jnp.logical_or(sub < 2, sub >= 6)
    return jnp.where(keep, outer_even, odd).reshape(sz.yedge, sz.nz)


def second_halo(sz, packed):
    pairs = packed.reshape(sz.ex // 2, SUBLANES, sz.nz)
    odd = pltpu.roll(pairs, 4, axis=1)
    return jnp.stack([pairs, odd], axis=1).reshape(sz.ex, SUBLANES, sz.nz)


def stencil(sz, vals, low, high, below, above):
    result = -90.0 * vals
    tall = jnp.concatenate([low, vals, high], axis=0)
    step = sz.ey
    cells = sz.cells
    near = tall[step : step + cells] + tall[3 * step : 3 * step + cells]
    far = tall[0:cells] + tall[4 * step : 4 * step + cells]

    near = near + pltpu.roll(vals, 1, axis=1) + pltpu.roll(vals, sz.nz - 1, axis=1)
    far = far + pltpu.roll(vals, 2, axis=1) + pltpu.roll(vals, sz.nz - 2, axis=1)

    tiles = vals.reshape(2 * sz.ex, SUBLANES, sz.nz)
    sub = iota((2 * sz.ex, SUBLANES, sz.nz), 1)

    def shifted(amount, outer, from_below):
        mine = pltpu.roll(tiles, amount, axis=1)
        theirs = pltpu.roll(outer, amount, axis=1)
        pairs = mine.reshape(sz.ex, 2, SUBLANES, sz.nz)
        if from_below:
            other = jnp.stack([theirs, pairs[:, 0]], axis=1)
            mask = sub < amount
        else:
            other = jnp.stack([pairs[:, 1], theirs], axis=1)
            mask = sub >= amount
        return jnp.where(mask, other.reshape(tiles.shape), mine).reshape(vals.shape)

    near = near + shifted(1, below, True) + shifted(SUBLANES - 1, above, False)
    far = far + shifted(2, below, True) + shifted(SUBLANES - 2, above, False)
    return result + 16.0 * near - far


def emit(sz, vals, flag_ref, pv_ref, row_of, hot_ref, ab_ref, bb_ref, yb_ref, table_ref):
    table = partial_table(sz, vals, pv_ref, row_of, hot_ref)
    table_ref[...] = table
    flag = flag_ref[0]
    top = vals[sz.cells - sz.xedge :]
    bottom = vals[: sz.xedge]
    is_high = flag == 0
    to_message(sz, ab_ref, jnp.where(is_high, top, bottom))
    to_message(sz, bb_ref, jnp.where(is_high, bottom, top))
    bb_ref[sz.edge_rows :, :] = table
    to_message(sz, yb_ref, second_edges(sz, vals))
    yb_ref[sz.yedge_rows :, :] = table


def first_kernel(
    sz, flag_ref, vals_ref, pv_ref, ids_ref, ab_ref, bb_ref, yb_ref, table_ref, rows_ref, hot_ref
):
    row_of, lane_of = rows_of_ids(sz, ids_ref)
    rows_ref[...] = row_of
    lane_iota = iota((LANES, LANES), 0).astype(F32)
    for at, (zb, slot) in enumerate(chunks(sz)):
        hot_ref[:, at * LANES : (at + 1) * LANES] = jnp.where(
            chunk(sz, lane_of, zb, slot) == lane_iota, 1.0, 0.0
        ).astype(BF16)
    emit(
        sz, vals_ref[...], flag_ref, pv_ref, row_of, hot_ref, ab_ref, bb_ref, yb_ref, table_ref
    )


def step_kernel(sz, degree, n_tables, n_y, flag_ref, cheb_ref, *refs):
    refs = list(refs)
    table_refs = [refs.pop(0) for _ in range(n_tables)]
    energy_ref, a_ref, b_ref = refs.pop(0), refs.pop(0), refs.pop(0)
    y_refs = [refs.pop(0) for _ in range(n_y)]
    pv_ref, pot_ref, rows_ref, hot_ref = (refs.pop(0) for _ in range(4))
    history = [refs.pop(0) for _ in range(degree)]
    out_refs = refs
    vals = history[-1][...]
    row_of = rows_ref[...]

    from_a = from_message(sz, a_ref, sz.xedge)
    from_b = from_message(sz, b_ref, sz.xedge)
    is_high = flag_ref[0] == 0
    low = jnp.where(is_high, from_b, from_a)
    high = jnp.where(is_high, from_a, from_b)
    outer = [second_halo(sz, from_message(sz, ref, sz.yedge)) for ref in y_refs]
    laplace12 = stencil(sz, vals, low, high, outer[0], outer[-1])
    double = 1.0 if degree == 1 else 2.0
    result = laplace12 * (-0.5 / 12.0 / E_HALF * double) + vals * (
        (pot_ref[...] - E_MID) * (double / E_HALF)
    )
    if degree > 1:
        result = result - history[-2][...]

    table = table_refs[0][...]
    for ref in table_refs[1:]:
        table = table + ref[...]
    table = table * (energy_ref[...] * (double / E_HALF))
    result = result + jnp.concatenate(projected(sz, table, pv_ref, row_of, hot_ref), axis=1)

    if degree < STEPS:
        out_refs[0][...] = result
        emit(sz, result, flag_ref, pv_ref, row_of, hot_ref, *out_refs[1:])
    else:
        filtered = cheb_ref[STEPS] * result
        for n in range(STEPS):
            filtered = filtered + cheb_ref[n] * history[n][...]
        out_refs[0][...] = filtered * filtered


def vmem(count):
    return [pl.BlockSpec(memory_space=pltpu.VMEM)] * count


def smem(count):
    return [pl.BlockSpec(memory_space=pltpu.SMEM)] * count


def shift_table(table, blocks_first, blocks_second, size_first, size_second, dim, delta):
    blocks = table.reshape(blocks_first, blocks_second, -1)
    count = blocks.shape[dim]
    size = (size_first, size_second)[dim]
    parts = []
    for at in range(count):
        source = [s for s in range(count) if (s + delta) % size == at]
        if source:
            parts.append(lax.slice_in_dim(blocks, source[0], source[0] + 1, axis=dim))
        else:
            parts.append(jnp.zeros_like(lax.slice_in_dim(blocks, 0, 1, axis=dim)))
    return jnp.concatenate(parts, axis=dim).reshape(table.shape)


def offsets(size):
    return sorted({d % size for d in (-2, -1, 1, 2)} - {0})


def shift(arr, axis, amount):
    size = lax.axis_size(axis)
    return lax.ppermute(arr, axis, [(i, (i + amount) % size) for i in range(size)])


def swap(arr, target):
    size_first = lax.axis_size("gx")
    size_second = lax.axis_size("gy")
    pairs = []
    for i in range(size_first):
        for j in range(size_second):
            ti, tj = target(i, j)
            pairs.append((i * size_second + j, ti * size_second + tj))
    return lax.ppermute(arr, ("gx", "gy"), pairs)


def orb_sum(vals, scale):
    size = lax.axis_size("orb")
    if size != 4:
        return lax.psum(vals, "orb") * scale
    vals = vals + lax.ppermute(vals, "orb", [(i, i ^ 1) for i in range(4)])
    return (vals + lax.ppermute(vals, "orb", [(i, 3 - i) for i in range(4)])) * scale


def local(orbitals, local_pot, proj_vals, proj_ids, proj_energy, cheb_coef):
    count_orb, ex, ey, nz = orbitals.shape
    slots = proj_vals.shape[0]
    size_first = lax.axis_size("gx")
    size_second = lax.axis_size("gy")
    owner_size = proj_energy.shape[0] // (size_first * size_second)
    whole = size_first == 4 and size_second == 2
    if whole:
        windows = (size_first, size_second)
    else:
        windows = (min(3, size_first), min(3, size_second))
    rows = windows[0] * windows[1] * owner_size // LANES
    sz = Sizes(ex, ey, nz, slots, owner_size, rows)
    here_first = lax.axis_index("gx")
    here_second = lax.axis_index("gy")

    if whole:
        flag = jnp.bitwise_and(here_first, 1).astype(jnp.int32).reshape(1)
        energy = proj_energy.reshape(rows, LANES)
        ids = proj_ids
    else:
        flag = jnp.zeros((1,), jnp.int32)
        owner = proj_ids // owner_size
        rel_first = (owner // size_second - here_first + 1) % size_first
        rel_second = (owner % size_second - here_second + 1) % size_second
        ids = (rel_first * windows[1] + rel_second) * owner_size + proj_ids % owner_size
        grid = proj_energy.reshape(size_first, size_second, owner_size)
        grid = jnp.roll(grid, (1 - here_first, 1 - here_second), (0, 1))
        energy = grid[: windows[0], : windows[1]].reshape(rows, LANES)

    pv = proj_vals.reshape(slots * sz.cells, nz)
    pot = local_pot.reshape(sz.cells, nz)
    message_shapes = (
        jax.ShapeDtypeStruct((sz.edge_rows, LANES), F32),
        jax.ShapeDtypeStruct((sz.edge_rows + rows, LANES), F32),
        jax.ShapeDtypeStruct((sz.yedge_rows + rows, LANES), F32),
        jax.ShapeDtypeStruct((rows, LANES), F32),
    )
    field = jax.ShapeDtypeStruct((sz.cells, nz), F32)
    params = pltpu.CompilerParams(vmem_limit_bytes=48 << 20)

    def exchange(to_a, to_b, to_y, table):
        if whole:
            from_b = swap(to_b, lambda i, j: (size_first - 1 - i, j))
            from_y = swap(to_y, lambda i, j: (i, 1 - j))
            from_d = swap(table, lambda i, j: (size_first - 1 - i, 1 - j))
            from_a = swap(to_a, lambda i, j: (i ^ 1, j))
            table = table + from_d + from_b[sz.edge_rows :] + from_y[sz.yedge_rows :]
            other = swap(table, lambda i, j: (i ^ 1, j))
            return [table, other], from_a, from_b, [from_y]
        edges_b = to_b[: sz.edge_rows]
        edges_y = to_y[: sz.yedge_rows]
        below = shift(edges_y, "gy", 1)
        above = shift(edges_y, "gy", -1)
        from_a = shift(edges_b, "gx", -1)
        from_b = shift(to_a, "gx", 1)
        for dim, axis in ((1, "gy"), (0, "gx")):
            total = table
            for delta in offsets((size_first, size_second)[dim]):
                moved = shift(table, axis, -delta)
                total = total + shift_table(
                    moved, windows[0], windows[1], size_first, size_second, dim, delta
                )
            table = total
        return [table], from_a, from_b, [below, above]

    def one_orbital(start):
        *messages, row_of, hot = pl.pallas_call(
            functools.partial(first_kernel, sz),
            out_shape=message_shapes
            + (
                jax.ShapeDtypeStruct((SUBLANES, slots * sz.cells), F32),
                jax.ShapeDtypeStruct((LANES, slots * sz.zb * sz.cells), BF16),
            ),
            in_specs=smem(1) + vmem(3),
            out_specs=tuple(vmem(6)),
            compiler_params=params,
            name="project_first",
        )(flag, start, pv, ids)
        history = [start]
        for degree in range(1, STEPS + 1):
            tables, from_a, from_b, from_y = exchange(*messages)
            last = degree == STEPS
            args = (
                *tables,
                energy,
                from_a,
                from_b,
                *from_y,
                pv,
                pot,
                row_of,
                hot,
                *history,
            )
            out = pl.pallas_call(
                functools.partial(step_kernel, sz, degree, len(tables), len(from_y)),
                out_shape=(field,) if last else (field,) + message_shapes,
                in_specs=smem(2) + vmem(len(args)),
                out_specs=tuple(vmem(1 if last else 5)),
                compiler_params=params,
                name=f"hamilton_{degree}",
            )(flag, cheb_coef, *args)
            if last:
                return out[0]
            history.append(out[0])
            messages = out[1:]

    density = one_orbital(orbitals[0].reshape(sz.cells, nz))
    for at in range(1, count_orb):
        density = density + one_orbital(orbitals[at].reshape(sz.cells, nz))
    scale = 1.0 / (count_orb * lax.axis_size("orb"))
    return orb_sum(density, scale).reshape(ex, ey, nz)


def solution(mesh):
    return jax.shard_map(
        local,
        mesh=mesh,
        in_specs=(
            P("orb", "gx", "gy", None),
            P("gx", "gy", None),
            P(None, "gx", "gy", None),
            P(None, "gx", "gy", None),
            P(),
            P(),
        ),
        out_specs=P("gx", "gy", None),
        check_vma=False,
    )
```

time: 221 us -> 48.8 us (0.22)
  blocking collectives: 71 us -> 0 us
  local copies, waits for them, and re-layouts: 39.7 us -> 2.75 us
  other arithmetic: 31.9 us -> 0.75 us
  waiting for transfers between devices: 41.8 us -> 26.7 us
  between operations: 14.5 us -> 0.06 us
  matrix products: 8.31 us -> 0 us
  Pallas kernels: 0 us -> 5.19 us
    psum x3 -> x0, blocking collectives: 71 us -> none  [weights_of(): coef_sums = lax.psum(partial_value, ('gx', 'gy'))]
    psum x1 -> x0, waiting for transfers between devices: 34.9 us -> none  [local(): density = lax.psum(jnp.sum(filtered * filtered, axis=0), 'orb')]
    scatter-add x3 -> x0, other arithmetic: 25.8 us -> none  [weights_of(): jax.ops.segment_sum(single, ids_flat, num_segments=count_all)]
    gather x3 -> x0, local copies, waits for them, and re-layouts: 25.2 us -> none  [weights_of(): return jnp.take(coef_sums * proj_energy[None, :], ids_flat, axis=1)]
    ppermute x12 -> x17, waiting for transfers between devices: 6.87 us -> 26.7 us  [the longest x15 11.5 us: swap(): return lax.ppermute(arr, ('gx', 'gy'), pairs)]
    dot_general x6 -> x0, matrix products: 8.31 us -> none  [the longest x3 4.18 us: hamilton(): jnp.einsum('kxyzb,okxyz->oxyzb', shaped, weights, precision=PRECISE)]
    pallas_call x0 -> x4, Pallas kernels: none -> 5.19 us  [the longest x3 4.54 us: one_orbital(): pl.pallas_call(functools.partial(step_kernel, sz, degree, len(tables), le...]
    another operation x10 -> x0, local copies, waits for them, and re-layouts: 4.02 us -> none
  transfers between devices with their start and end apart: 13 -> 17, of which waited for: 7 -> 8; matrix products, arithmetic and copies ran while one was open for 32% -> 0% of each run, Pallas kernels for 0% -> 0%
where the time goes in v1:
time: 48.8 us; the launch traced here: 48.6 us
  waiting for transfers between devices  26.7 us (55%)
  starting transfers between devices  13.1 us (27%)
  Pallas kernels  5.19 us (11%)
  local copies, waits for them, and re-layouts  2.75 us (6%)
  other arithmetic  0.75 us (2%)
    ppermute x15, waiting for transfers between devices, swap(): return lax.ppermute(arr, ('gx', 'gy'), pairs)  11.5 us
    ppermute x15, starting transfers between devices, swap(): return lax.ppermute(arr, ('gx', 'gy'), pairs)  10.9 us
    ppermute x1, waiting for transfers between devices, orb_sum(): lax.ppermute(vals, 'orb', [(i, 3 - i) for i in range(4)])  9.91 us
    ppermute x1, waiting for transfers between devices, orb_sum(): vals = vals + lax.ppermute(vals, 'orb', [(i, i ^ 1) for i in range(4)])  5.36 us
    pallas_call x3, Pallas kernels, one_orbital(): pl.pallas_call(functools.partial(step_kernel, sz, degree, len(tables), le...  4.54 us
    unnamed x11, local copies, waits for them, and re-layouts  2.75 us
    ppermute x1, starting transfers between devices, orb_sum(): vals = vals + lax.ppermute(vals, 'orb', [(i, i ^ 1) for i in range(4)])  1.68 us
  transfers between devices with their start and end apart: 17, of which 8 were waited for; matrix products, arithmetic and copies ran while one was open for 0% of the time, Pallas kernels for 0%

profile of v1, /device:TPU:16, one launch (start us, length us, event | category | flops | bytes accessed | tf_op | source)
XLA Modules:
  0.0 48.6 jit_solution(7939940578707518795)
XLA Ops:
  0.0 0.0 copy-start.1
  0.0 1.1 %copy.7.ids_ref = s32[4,8,16,3]{3,2,1,0:T(8,128)S(1)} copy(s32[4,8,16,3]{2,1,3,0:T(8,128)} %param.9) | data formatting | bytes 12288 | tf_op args[3]
  1.1 0.0 copy-done.1
  1.1 0.0 copy-start
  1.1 1.0 %copy-done = bf16[4,8,16,384]{3,2,1,0:T(8,128)(2,1)S(1)} copy-done((bf16[4,8,16,384]{3,2,1,0:T(8,128)(2,1)S(1)}, bf16[4,8,16,384]{3,2,1,0:T(8,128)(2,1)}, u32[]{:S(2)}) %copy-start) | copy-done | bytes 393240
  2.1 0.0 copy-start.2
  2.1 0.6 %project_first.1 = (f32[96,128]{1,0:T(8,128)S(1)}, f32[128,128]{1,0:T(8,128)S(1)}, f32[128,128]{1,0:T(8,128)S(1)}, f32[32,128]{1,0:T(8,128)S(1)}, f32[8,512]{1,0:T(8,128)S(1)}, /*index=5*/bf16[128,1536]{1,0:T(8,128)(2,1)S(1)}) custom-call(s32[1]{0:T(128)} %bitcast.flag_ref, f32[128,384]{1,0:T(8,128)S(1)} %bitcast.10, bf16[512,384]{1,0:T(8,128)(2,1)S(1)} %bitcast.6, ...), custom_call_target="tpu_custom_call" | custom-call | tf_op jit(solution)/shard_map/project_first/pallas_call | solution.py:374
  2.8 0.9 %collective-permute-start.1 = (f32[128,128]{1,0:T(8,128)S(1)}, f32[128,128]{1,0:T(8,128)S(1)}, u32[]{:S(2)}, u32[]{:S(2)}) collective-permute-start(f32[128,128]{1,0:T(8,128)S(1)} %get-tuple-element.22), channel_id=1, source_target_pairs={{0,24},{4,28},{8,16},{12,20},{16,8},{20,12},{24,0},{28,4},{1,25},{... | collective-permute-start | bytes 196616 | tf_op jit(solution)/shard_map/ppermute | solution.py:296
  3.7 1.5 %collective-permute-start.2 = (f32[128,128]{1,0:T(8,128)S(1)}, f32[128,128]{1,0:T(8,128)S(1)}, u32[]{:S(2)}, u32[]{:S(2)}) collective-permute-start(f32[128,128]{1,0:T(8,128)S(1)} %get-tuple-element.23), channel_id=1, source_target_pairs={{0,4},{4,0},{8,12},{12,8},{16,20},{20,16},{24,28},{28,24},{1,5},{5... | collective-permute-start | bytes 196616 | tf_op jit(solution)/shard_map/ppermute | solution.py:296
  5.2 0.5 collective-permute-start
  5.7 0.2 collective-permute-start.4
  5.9 3.4 %collective-permute-done = f32[32,128]{1,0:T(8,128)S(1)} collective-permute-done((f32[32,128]{1,0:T(8,128)S(1)}, f32[32,128]{1,0:T(8,128)S(1)}, u32[]{:S(2)}, u32[]{:S(2)}) %collective-permute-start) | collective-permute-done | bytes 16416 | tf_op jit(solution)/shard_map/ppermute | solution.py:296
  9.3 0.0 collective-permute-done.1.refs_4_
  9.3 0.0 collective-permute-done.2.refs_5_
  9.3 0.4 collective-permute-start.3
  9.8 0.0 collective-permute-done.4.refs_3_
  9.8 0.8 %collective-permute-done.3.refs_1_ = f32[32,128]{1,0:T(8,128)S(1)} collective-permute-done((f32[32,128]{1,0:T(8,128)S(1)}, f32[32,128]{1,0:T(8,128)S(1)}, u32[]{:S(2)}, u32[]{:S(2)}) %collective-permute-start.3) | collective-permute-done | bytes 16416 | tf_op jit(solution)/shard_map/ppermute | solution.py:296
  10.6 0.0 copy-done.2
  10.6 0.0 copy-done.3
  10.6 0.6 %copy-done.4 = f32[4]{0:T(128)S(1)} copy-done((f32[4]{0:T(128)S(1)}, f32[4]{0:T(128)}, u32[]{:S(2)}) %copy-start.4) | copy-done | bytes 40
  11.3 1.6 %hamilton_1.1 = (f32[128,384]{1,0:T(8,128)S(1)}, f32[96,128]{1,0:T(8,128)S(1)}, f32[128,128]{1,0:T(8,128)S(1)}, f32[128,128]{1,0:T(8,128)S(1)}, f32[32,128]{1,0:T(8,128)S(1)}) custom-call(s32[1]{0:T(128)} %bitcast.flag_ref, f32[4]{0:T(128)S(1)} %copy-done.4, f32[32,128]{1,0:T(8,128)S(1)} %slice_add_fusion.4.refs_0_, ...), custom_call_target="tpu_custom_call" | custom-call | tf_op jit(solution)/shard_map/hamilton_1/pallas_call | solution.py:402
  12.9 0.5 %collective-permute-start.6 = (f32[128,128]{1,0:T(8,128)S(1)}, f32[128,128]{1,0:T(8,128)S(1)}, u32[]{:S(2)}, u32[]{:S(2)}) collective-permute-start(f32[128,128]{1,0:T(8,128)S(1)} %get-tuple-element.28), channel_id=1, source_target_pairs={{0,24},{4,28},{8,16},{12,20},{16,8},{20,12},{24,0},{28,4},{1,25},{... | collective-permute-start | bytes 196616 | tf_op jit(solution)/shard_map/ppermute | solution.py:296
  13.4 0.5 %collective-permute-start.7 = (f32[128,128]{1,0:T(8,128)S(1)}, f32[128,128]{1,0:T(8,128)S(1)}, u32[]{:S(2)}, u32[]{:S(2)}) collective-permute-start(f32[128,128]{1,0:T(8,128)S(1)} %get-tuple-element.29), channel_id=1, source_target_pairs={{0,4},{4,0},{8,12},{12,8},{16,20},{20,16},{24,28},{28,24},{1,5},{5... | collective-permute-start | bytes 196616 | tf_op jit(solution)/shard_map/ppermute | solution.py:296
  14.0 1.9 %collective-permute-start.5 = (f32[32,128]{1,0:T(8,128)S(1)}, f32[32,128]{1,0:T(8,128)S(1)}, u32[]{:S(2)}, u32[]{:S(2)}) collective-permute-start(f32[32,128]{1,0:T(8,128)S(1)} %get-tuple-element.27), channel_id=1, source_target_pairs={{0,28},{4,24},{8,20},{12,16},{16,12},{20,8},{24,4},{28,0},{1,29},{... | collective-permute-start | bytes 49160 | tf_op jit(solution)/shard_map/ppermute | solution.py:296
  15.9 0.6 %collective-permute-start.9 = (f32[96,128]{1,0:T(8,128)S(1)}, f32[96,128]{1,0:T(8,128)S(1)}, u32[]{:S(2)}, u32[]{:S(2)}) collective-permute-start(f32[96,128]{1,0:T(8,128)S(1)} %get-tuple-element.30), channel_id=1, source_target_pairs={{0,8},{4,12},{8,0},{12,4},{16,24},{20,28},{24,16},{28,20},{1,9},{5... | collective-permute-start | bytes 147464 | tf_op jit(solution)/shard_map/ppermute | solution.py:296
  16.5 1.5 %collective-permute-done.5 = f32[32,128]{1,0:T(8,128)S(1)} collective-permute-done((f32[32,128]{1,0:T(8,128)S(1)}, f32[32,128]{1,0:T(8,128)S(1)}, u32[]{:S(2)}, u32[]{:S(2)}) %collective-permute-start.5) | collective-permute-done | bytes 16416 | tf_op jit(solution)/shard_map/ppermute | solution.py:296
  18.0 0.0 collective-permute-done.6.refs_4_
  18.0 0.0 collective-permute-done.7.refs_5_
  18.0 0.2 collective-permute-start.8
  18.2 0.0 collective-permute-done.9.refs_3_
  18.2 1.1 %collective-permute-done.8.refs_1_ = f32[32,128]{1,0:T(8,128)S(1)} collective-permute-done((f32[32,128]{1,0:T(8,128)S(1)}, f32[32,128]{1,0:T(8,128)S(1)}, u32[]{:S(2)}, u32[]{:S(2)}) %collective-permute-start.8) | collective-permute-done | bytes 16416 | tf_op jit(solution)/shard_map/ppermute | solution.py:296
  19.3 1.6 %hamilton_2.1 = (f32[128,384]{1,0:T(8,128)S(1)}, f32[96,128]{1,0:T(8,128)S(1)}, f32[128,128]{1,0:T(8,128)S(1)}, f32[128,128]{1,0:T(8,128)S(1)}, f32[32,128]{1,0:T(8,128)S(1)}) custom-call(s32[1]{0:T(128)} %bitcast.flag_ref, f32[4]{0:T(128)S(1)} %copy-done.4, f32[32,128]{1,0:T(8,128)S(1)} %slice_add_fusion.2.refs_0_, ...), custom_call_target="tpu_custom_call" | custom-call | tf_op jit(solution)/shard_map/hamilton_2/pallas_call | solution.py:402
  20.9 1.3 %collective-permute-start.11 = (f32[128,128]{1,0:T(8,128)S(1)}, f32[128,128]{1,0:T(8,128)S(1)}, u32[]{:S(2)}, u32[]{:S(2)}) collective-permute-start(f32[128,128]{1,0:T(8,128)S(1)} %get-tuple-element.33), channel_id=1, source_target_pairs={{0,24},{4,28},{8,16},{12,20},{16,8},{20,12},{24,0},{28,4},{1,25},{... | collective-permute-start | bytes 196616 | tf_op jit(solution)/shard_map/ppermute | solution.py:296
  22.2 1.6 %collective-permute-start.12 = (f32[128,128]{1,0:T(8,128)S(1)}, f32[128,128]{1,0:T(8,128)S(1)}, u32[]{:S(2)}, u32[]{:S(2)}) collective-permute-start(f32[128,128]{1,0:T(8,128)S(1)} %get-tuple-element.34), channel_id=1, source_target_pairs={{0,4},{4,0},{8,12},{12,8},{16,20},{20,16},{24,28},{28,24},{1,5},{5... | collective-permute-start | bytes 196616 | tf_op jit(solution)/shard_map/ppermute | solution.py:296
  23.8 0.1 collective-permute-start.10
  23.9 0.4 collective-permute-start.14
  24.3 3.5 %collective-permute-done.10 = f32[32,128]{1,0:T(8,128)S(1)} collective-permute-done((f32[32,128]{1,0:T(8,128)S(1)}, f32[32,128]{1,0:T(8,128)S(1)}, u32[]{:S(2)}, u32[]{:S(2)}) %collective-permute-start.10) | collective-permute-done | bytes 16416 | tf_op jit(solution)/shard_map/ppermute | solution.py:296
  27.9 0.0 collective-permute-done.11.refs_4_
  27.9 0.0 collective-permute-done.12.refs_5_
  27.9 0.2 collective-permute-start.13
  28.1 0.0 collective-permute-done.14.refs_3_
  28.1 1.1 %collective-permute-done.13.refs_1_ = f32[32,128]{1,0:T(8,128)S(1)} collective-permute-done((f32[32,128]{1,0:T(8,128)S(1)}, f32[32,128]{1,0:T(8,128)S(1)}, u32[]{:S(2)}, u32[]{:S(2)}) %collective-permute-start.13) | collective-permute-done | bytes 16416 | tf_op jit(solution)/shard_map/ppermute | solution.py:296
  29.1 1.3 %hamilton_3.1 = f32[128,384]{1,0:T(8,128)S(1)} custom-call(s32[1]{0:T(128)} %bitcast.flag_ref, f32[4]{0:T(128)S(1)} %copy-done.4, f32[32,128]{1,0:T(8,128)S(1)} %slice_add_fusion.refs_0_, f32[32,128]{1,0:T(8,128)S(1)} %collective-permute-done.13.refs_1_, f32[32,128]{1,0:T(8,128)S(1)} %bitcast.19, f32[96,128]{1,0:T(8,128)S(1)} %collective-permute-done.14.refs_3_, ...), custom_call_target="tpu_custom_call" | custom-call | tf_op jit(solution)/shard_map/hamilton_3/pallas_call | solution.py:402
  30.4 1.7 %collective-permute-start.15 = (f32[128,384]{1,0:T(8,128)S(1)}, f32[128,384]{1,0:T(8,128)S(1)}, u32[]{:S(2)}, u32[]{:S(2)}) collective-permute-start(f32[128,384]{1,0:T(8,128)S(1)} %hamilton_3.1), channel_id=1, source_target_pairs={{0,1},{1,0},{2,3},{3,2},{4,5},{5,4},{6,7},{7,6},{8,9},{9,8},{10,11... | collective-permute-start | bytes 589832 | tf_op jit(solution)/shard_map/ppermute | solution.py:303
  32.1 5.4 %collective-permute-done.15 = f32[128,384]{1,0:T(8,128)S(1)} collective-permute-done((f32[128,384]{1,0:T(8,128)S(1)}, f32[128,384]{1,0:T(8,128)S(1)}, u32[]{:S(2)}, u32[]{:S(2)}) %collective-permute-start.15) | collective-permute-done | bytes 196640 | tf_op jit(solution)/shard_map/ppermute | solution.py:303
  37.5 0.5 %collective-permute-start.16 = (f32[128,384]{1,0:T(8,128)S(1)}, f32[128,384]{1,0:T(8,128)S(1)}, u32[]{:S(2)}, u32[]{:S(2)}) collective-permute-start(f32[128,384]{1,0:T(8,128)S(1)} %add.42), channel_id=1, source_target_pairs={{0,3},{1,2},{2,1},{3,0},{4,7},{5,6},{6,5},{7,4},{8,11},{9,10},{10,... | collective-permute-start | bytes 589832 | tf_op jit(solution)/shard_map/ppermute | solution.py:304
  38.0 9.9 %collective-permute-done.16 = f32[128,384]{1,0:T(8,128)S(1)} collective-permute-done((f32[128,384]{1,0:T(8,128)S(1)}, f32[128,384]{1,0:T(8,128)S(1)}, u32[]{:S(2)}, u32[]{:S(2)}) %collective-permute-start.16) | collective-permute-done | bytes 196640 | tf_op jit(solution)/shard_map/ppermute | solution.py:304
  47.9 0.7 %add_multiply_fusion = f32[128,384]{1,0:T(8,128)} fusion(f32[128,384]{1,0:T(8,128)S(1)} %add.42, f32[128,384]{1,0:T(8,128)S(1)} %collective-permute-done.16), kind=kLoop, calls=%fused_computation | loop fusion | flops 98304 | bytes 589824 | tf_op jit(solution)/shard_map/mul | solution.py:304
  (6 shorter events, 0.1 us)
Async XLA Ops:
  0.0 1.1 %copy-start.1 = (f32[1,8,16,384]{3,2,1,0:T(8,128)S(1)}, f32[1,8,16,384]{3,2,1,0:T(8,128)}, u32[]{:S(2)}) copy-start(f32[1,8,16,384]{3,2,1,0:T(8,128)} %param.6) | copy-start | bytes 589828
  1.1 1.0 %copy-start = (bf16[4,8,16,384]{3,2,1,0:T(8,128)(2,1)S(1)}, bf16[4,8,16,384]{3,2,1,0:T(8,128)(2,1)}, u32[]{:S(2)}) copy-start(bf16[4,8,16,384]{3,2,1,0:T(8,128)(2,1)} %param.8) | copy-start | bytes 1179652
  2.1 8.5 %copy-start.2 = (f32[8,16,384]{2,1,0:T(8,128)S(1)}, f32[8,16,384]{2,1,0:T(8,128)}, u32[]{:S(2)}) copy-start(f32[8,16,384]{2,1,0:T(8,128)} %param.7) | copy-start | bytes 589828
  2.8 6.6 %collective-permute-start.1 = (f32[128,128]{1,0:T(8,128)S(1)}, f32[128,128]{1,0:T(8,128)S(1)}, u32[]{:S(2)}, u32[]{:S(2)}) collective-permute-start(f32[128,128]{1,0:T(8,128)S(1)} %get-tuple-element.22), channel_id=1, source_target_pairs={{0,24},{4,28},{8,16},{12,20},{16,8},{20,12},{24,0},{28,4},{1,25},{... | collective-permute-start | bytes 196616 | tf_op jit(solution)/shard_map/ppermute | solution.py:296
  3.7 5.6 %collective-permute-start.2 = (f32[128,128]{1,0:T(8,128)S(1)}, f32[128,128]{1,0:T(8,128)S(1)}, u32[]{:S(2)}, u32[]{:S(2)}) collective-permute-start(f32[128,128]{1,0:T(8,128)S(1)} %get-tuple-element.23), channel_id=1, source_target_pairs={{0,4},{4,0},{8,12},{12,8},{16,20},{20,16},{24,28},{28,24},{1,5},{5... | collective-permute-start | bytes 196616 | tf_op jit(solution)/shard_map/ppermute | solution.py:296
  5.2 4.1 %collective-permute-start = (f32[32,128]{1,0:T(8,128)S(1)}, f32[32,128]{1,0:T(8,128)S(1)}, u32[]{:S(2)}, u32[]{:S(2)}) collective-permute-start(f32[32,128]{1,0:T(8,128)S(1)} %get-tuple-element.21), channel_id=1, source_target_pairs={{0,28},{4,24},{8,20},{12,16},{16,12},{20,8},{24,4},{28,0},{1,29},{... | collective-permute-start | bytes 49160 | tf_op jit(solution)/shard_map/ppermute | solution.py:296
  5.7 4.1 %collective-permute-start.4 = (f32[96,128]{1,0:T(8,128)S(1)}, f32[96,128]{1,0:T(8,128)S(1)}, u32[]{:S(2)}, u32[]{:S(2)}) collective-permute-start(f32[96,128]{1,0:T(8,128)S(1)} %get-tuple-element.24), channel_id=1, source_target_pairs={{0,8},{4,12},{8,0},{12,4},{16,24},{20,28},{24,16},{28,20},{1,9},{5... | collective-permute-start | bytes 147464 | tf_op jit(solution)/shard_map/ppermute | solution.py:296
  9.3 1.3 %copy-start.3 = (f32[4096]{0:T(1024)S(1)}, f32[4096]{0:T(1024)}, u32[]{:S(2)}) copy-start(f32[4096]{0:T(1024)} %param.10) | copy-start | bytes 49156
  9.3 1.3 %collective-permute-start.3 = (f32[32,128]{1,0:T(8,128)S(1)}, f32[32,128]{1,0:T(8,128)S(1)}, u32[]{:S(2)}, u32[]{:S(2)}) collective-permute-start(f32[32,128]{1,0:T(8,128)S(1)} %slice_add_fusion.4.refs_0_), channel_id=1, source_target_pairs={{0,8},{4,12},{8,0},{12,4},{16,24},{20,28},{24,16},{28,20},{1,9},{5... | collective-permute-start | bytes 49160 | tf_op jit(solution)/shard_map/ppermute | solution.py:296
  10.6 0.7 %copy-start.4 = (f32[4]{0:T(128)S(1)}, f32[4]{0:T(128)}, u32[]{:S(2)}) copy-start(f32[4]{0:T(128)} %cheb_ref.5) | copy-start | bytes 52
  12.9 5.1 %collective-permute-start.6 = (f32[128,128]{1,0:T(8,128)S(1)}, f32[128,128]{1,0:T(8,128)S(1)}, u32[]{:S(2)}, u32[]{:S(2)}) collective-permute-start(f32[128,128]{1,0:T(8,128)S(1)} %get-tuple-element.28), channel_id=1, source_target_pairs={{0,24},{4,28},{8,16},{12,20},{16,8},{20,12},{24,0},{28,4},{1,25},{... | collective-permute-start | bytes 196616 | tf_op jit(solution)/shard_map/ppermute | solution.py:296
  13.4 4.6 %collective-permute-start.7 = (f32[128,128]{1,0:T(8,128)S(1)}, f32[128,128]{1,0:T(8,128)S(1)}, u32[]{:S(2)}, u32[]{:S(2)}) collective-permute-start(f32[128,128]{1,0:T(8,128)S(1)} %get-tuple-element.29), channel_id=1, source_target_pairs={{0,4},{4,0},{8,12},{12,8},{16,20},{20,16},{24,28},{28,24},{1,5},{5... | collective-permute-start | bytes 196616 | tf_op jit(solution)/shard_map/ppermute | solution.py:296
  14.0 4.1 %collective-permute-start.5 = (f32[32,128]{1,0:T(8,128)S(1)}, f32[32,128]{1,0:T(8,128)S(1)}, u32[]{:S(2)}, u32[]{:S(2)}) collective-permute-start(f32[32,128]{1,0:T(8,128)S(1)} %get-tuple-element.27), channel_id=1, source_target_pairs={{0,28},{4,24},{8,20},{12,16},{16,12},{20,8},{24,4},{28,0},{1,29},{... | collective-permute-start | bytes 49160 | tf_op jit(solution)/shard_map/ppermute | solution.py:296
  15.9 2.4 %collective-permute-start.9 = (f32[96,128]{1,0:T(8,128)S(1)}, f32[96,128]{1,0:T(8,128)S(1)}, u32[]{:S(2)}, u32[]{:S(2)}) collective-permute-start(f32[96,128]{1,0:T(8,128)S(1)} %get-tuple-element.30), channel_id=1, source_target_pairs={{0,8},{4,12},{8,0},{12,4},{16,24},{20,28},{24,16},{28,20},{1,9},{5... | collective-permute-start | bytes 147464 | tf_op jit(solution)/shard_map/ppermute | solution.py:296
  18.0 1.2 %collective-permute-start.8 = (f32[32,128]{1,0:T(8,128)S(1)}, f32[32,128]{1,0:T(8,128)S(1)}, u32[]{:S(2)}, u32[]{:S(2)}) collective-permute-start(f32[32,128]{1,0:T(8,128)S(1)} %slice_add_fusion.2.refs_0_), channel_id=1, source_target_pairs={{0,8},{4,12},{8,0},{12,4},{16,24},{20,28},{24,16},{28,20},{1,9},{5... | collective-permute-start | bytes 49160 | tf_op jit(solution)/shard_map/ppermute | solution.py:296
  20.9 6.9 %collective-permute-start.11 = (f32[128,128]{1,0:T(8,128)S(1)}, f32[128,128]{1,0:T(8,128)S(1)}, u32[]{:S(2)}, u32[]{:S(2)}) collective-permute-start(f32[128,128]{1,0:T(8,128)S(1)} %get-tuple-element.33), channel_id=1, source_target_pairs={{0,24},{4,28},{8,16},{12,20},{16,8},{20,12},{24,0},{28,4},{1,25},{... | collective-permute-start | bytes 196616 | tf_op jit(solution)/shard_map/ppermute | solution.py:296
  22.2 5.6 %collective-permute-start.12 = (f32[128,128]{1,0:T(8,128)S(1)}, f32[128,128]{1,0:T(8,128)S(1)}, u32[]{:S(2)}, u32[]{:S(2)}) collective-permute-start(f32[128,128]{1,0:T(8,128)S(1)} %get-tuple-element.34), channel_id=1, source_target_pairs={{0,4},{4,0},{8,12},{12,8},{16,20},{20,16},{24,28},{28,24},{1,5},{5... | collective-permute-start | bytes 196616 | tf_op jit(solution)/shard_map/ppermute | solution.py:296
  23.8 4.1 %collective-permute-start.10 = (f32[32,128]{1,0:T(8,128)S(1)}, f32[32,128]{1,0:T(8,128)S(1)}, u32[]{:S(2)}, u32[]{:S(2)}) collective-permute-start(f32[32,128]{1,0:T(8,128)S(1)} %get-tuple-element.32), channel_id=1, source_target_pairs={{0,28},{4,24},{8,20},{12,16},{16,12},{20,8},{24,4},{28,0},{1,29},{... | collective-permute-start | bytes 49160 | tf_op jit(solution)/shard_map/ppermute | solution.py:296
  23.9 4.2 %collective-permute-start.14 = (f32[96,128]{1,0:T(8,128)S(1)}, f32[96,128]{1,0:T(8,128)S(1)}, u32[]{:S(2)}, u32[]{:S(2)}) collective-permute-start(f32[96,128]{1,0:T(8,128)S(1)} %get-tuple-element.35), channel_id=1, source_target_pairs={{0,8},{4,12},{8,0},{12,4},{16,24},{20,28},{24,16},{28,20},{1,9},{5... | collective-permute-start | bytes 147464 | tf_op jit(solution)/shard_map/ppermute | solution.py:296
  27.9 1.2 %collective-permute-start.13 = (f32[32,128]{1,0:T(8,128)S(1)}, f32[32,128]{1,0:T(8,128)S(1)}, u32[]{:S(2)}, u32[]{:S(2)}) collective-permute-start(f32[32,128]{1,0:T(8,128)S(1)} %slice_add_fusion.refs_0_), channel_id=1, source_target_pairs={{0,8},{4,12},{8,0},{12,4},{16,24},{20,28},{24,16},{28,20},{1,9},{5... | collective-permute-start | bytes 49160 | tf_op jit(solution)/shard_map/ppermute | solution.py:296
  30.4 7.0 %collective-permute-start.15 = (f32[128,384]{1,0:T(8,128)S(1)}, f32[128,384]{1,0:T(8,128)S(1)}, u32[]{:S(2)}, u32[]{:S(2)}) collective-permute-start(f32[128,384]{1,0:T(8,128)S(1)} %hamilton_3.1), channel_id=1, source_target_pairs={{0,1},{1,0},{2,3},{3,2},{4,5},{5,4},{6,7},{7,6},{8,9},{9,8},{10,11... | collective-permute-start | bytes 589832 | tf_op jit(solution)/shard_map/ppermute | solution.py:303
  37.5 10.4 %collective-permute-start.16 = (f32[128,384]{1,0:T(8,128)S(1)}, f32[128,384]{1,0:T(8,128)S(1)}, u32[]{:S(2)}, u32[]{:S(2)}) collective-permute-start(f32[128,384]{1,0:T(8,128)S(1)} %add.42), channel_id=1, source_target_pairs={{0,3},{1,2},{2,1},{3,0},{4,7},{5,6},{6,5},{7,4},{8,11},{9,10},{10,... | collective-permute-start | bytes 589832 | tf_op jit(solution)/shard_map/ppermute | solution.py:304

commit v2 on v1

--- a/solution.py
+++ b/solution.py
@@ -48,21 +48,26 @@
         self.edge_rows = self.zb * self.xedge
         self.yedge_rows = self.zb * self.yedge
         assert extent_second == 2 * SUBLANES and extent_first % 2 == 0
-        assert self.cells == LANES
-
-
-def rows_of_ids(sz, ids_ref):
-    ids = ids_ref[...].reshape(sz.slots * sz.cells, sz.zb)
-    pick = jnp.where(
-        iota((SUBLANES, sz.zb), 0) == iota((SUBLANES, sz.zb), 1), 1.0, 0.0
+        assert self.cells == LANES and extent_first == SUBLANES
+
+
+def rows_of_ids(sz, ids):
+    copies = jnp.where(
+        jnp.bitwise_and(iota((sz.ey, LANES), 1), sz.ey - 1) == iota((sz.ey, LANES), 0), 1.0, 0.0
     ).astype(BF16)
-    row = lax.shift_right_logical(ids, 7).astype(F32).astype(BF16)
-    lane = jnp.bitwise_and(ids, LANES - 1).astype(F32).astype(BF16)
-    return dot(pick, row, NT), dot(pick, lane, NT)
+    shape = (sz.slots * sz.zb, sz.ex, LANES)
+    own = iota(shape, 2) // sz.ey == iota(shape, 1)
+
+    def flat(part):
+        spread = dot(part.astype(F32).astype(BF16), copies, NN).reshape(shape)
+        return jnp.sum(jnp.where(own, spread, 0.0), axis=1)
+
+    return flat(lax.shift_right_logical(ids, 7)), flat(jnp.bitwise_and(ids, LANES - 1))
 
 
 def chunk(sz, arr, zb, slot):
-    return arr[zb : zb + 1, slot * sz.cells : (slot + 1) * sz.cells]
+    at = slot * sz.zb + zb
+    return arr[at : at + 1, :]
 
 
 def chunks(sz):
@@ -199,30 +204,51 @@
 
 
 def first_kernel(
-    sz, flag_ref, vals_ref, pv_ref, ids_ref, ab_ref, bb_ref, yb_ref, table_ref, rows_ref, hot_ref
+    sz,
+    flag_ref,
+    vals_hbm,
+    pv_hbm,
+    ids_hbm,
+    ab_ref,
+    bb_ref,
+    yb_ref,
+    table_ref,
+    rows_ref,
+    hot_ref,
+    vals_ref,
+    pv_ref,
+    ids_ref,
+    sems,
 ):
-    row_of, lane_of = rows_of_ids(sz, ids_ref)
+    get_ids = pltpu.make_async_copy(ids_hbm, ids_ref, sems.at[0])
+    get_pv = pltpu.make_async_copy(pv_hbm, pv_ref, sems.at[1])
+    get_vals = pltpu.make_async_copy(vals_hbm, vals_ref, sems.at[2])
+    get_ids.start()
+    get_vals.start()
+    get_pv.start()
+    get_ids.wait()
+    row_of, lane_of = rows_of_ids(sz, ids_ref[...])
     rows_ref[...] = row_of
     lane_iota = iota((LANES, LANES), 0).astype(F32)
     for at, (zb, slot) in enumerate(chunks(sz)):
         hot_ref[:, at * LANES : (at + 1) * LANES] = jnp.where(
             chunk(sz, lane_of, zb, slot) == lane_iota, 1.0, 0.0
         ).astype(BF16)
+    get_vals.wait()
+    get_pv.wait()
     emit(
         sz, vals_ref[...], flag_ref, pv_ref, row_of, hot_ref, ab_ref, bb_ref, yb_ref, table_ref
     )
 
 
-def step_kernel(sz, degree, n_tables, n_y, flag_ref, cheb_ref, *refs):
+def local_kernel(sz, degree, n_y, flag_ref, *refs):
     refs = list(refs)
-    table_refs = [refs.pop(0) for _ in range(n_tables)]
-    energy_ref, a_ref, b_ref = refs.pop(0), refs.pop(0), refs.pop(0)
+    cheb_ref = refs.pop(0) if degree == STEPS else None
+    a_ref, b_ref = refs.pop(0), refs.pop(0)
     y_refs = [refs.pop(0) for _ in range(n_y)]
-    pv_ref, pot_ref, rows_ref, hot_ref = (refs.pop(0) for _ in range(4))
-    history = [refs.pop(0) for _ in range(degree)]
-    out_refs = refs
+    pot_ref = refs.pop(0)
+    *history, out_ref = refs
     vals = history[-1][...]
-    row_of = rows_ref[...]
 
     from_a = from_message(sz, a_ref, sz.xedge)
     from_b = from_message(sz, b_ref, sz.xedge)
@@ -237,21 +263,43 @@
     )
     if degree > 1:
         result = result - history[-2][...]
-
+    if degree == STEPS:
+        result = cheb_ref[STEPS] * result
+        for n in range(STEPS):
+            result = result + cheb_ref[n] * history[n][...]
+    out_ref[...] = result
+
+
+def added(table_refs):
     table = table_refs[0][...]
     for ref in table_refs[1:]:
         table = table + ref[...]
-    table = table * (energy_ref[...] * (double / E_HALF))
-    result = result + jnp.concatenate(projected(sz, table, pv_ref, row_of, hot_ref), axis=1)
-
-    if degree < STEPS:
-        out_refs[0][...] = result
-        emit(sz, result, flag_ref, pv_ref, row_of, hot_ref, *out_refs[1:])
-    else:
-        filtered = cheb_ref[STEPS] * result
-        for n in range(STEPS):
-            filtered = filtered + cheb_ref[n] * history[n][...]
-        out_refs[0][...] = filtered * filtered
+    return table
+
+
+def nonlocal_kernel(sz, degree, n_tables, flag_ref, *refs):
+    refs = list(refs)
+    table_refs = [refs.pop(0) for _ in range(n_tables)]
+    energy_ref, rest_ref, pv_ref, rows_ref, hot_ref = (refs.pop(0) for _ in range(5))
+    row_of = rows_ref[...]
+    double = 1.0 if degree == 1 else 2.0
+    table = added(table_refs) * (energy_ref[...] * (double / E_HALF))
+    result = rest_ref[...] + jnp.concatenate(
+        projected(sz, table, pv_ref, row_of, hot_ref), axis=1
+    )
+    refs[0][...] = result
+    emit(sz, result, flag_ref, pv_ref, row_of, hot_ref, *refs[1:])
+
+
+def last_kernel(sz, n_tables, cheb_ref, *refs):
+    refs = list(refs)
+    table_refs = [refs.pop(0) for _ in range(n_tables)]
+    energy_ref, rest_ref, pv_ref, rows_ref, hot_ref, out_ref = refs
+    table = added(table_refs) * (energy_ref[...] * (2.0 / E_HALF * cheb_ref[STEPS]))
+    result = rest_ref[...] + jnp.concatenate(
+        projected(sz, table, pv_ref, rows_ref[...], hot_ref), axis=1
+    )
+    out_ref[...] = result * result
 
 
 def vmem(count):
@@ -334,6 +382,7 @@
         grid = jnp.roll(grid, (1 - here_first, 1 - here_second), (0, 1))
         energy = grid[: windows[0], : windows[1]].reshape(rows, LANES)
 
+    ids = jnp.transpose(ids, (0, 3, 1, 2)).reshape(slots * sz.zb * ex, ey)
     pv = proj_vals.reshape(slots * sz.cells, nz)
     pot = local_pot.reshape(sz.cells, nz)
     message_shapes = (
@@ -375,11 +424,17 @@
             functools.partial(first_kernel, sz),
             out_shape=message_shapes
             + (
-                jax.ShapeDtypeStruct((SUBLANES, slots * sz.cells), F32),
+                jax.ShapeDtypeStruct((slots * sz.zb, LANES), F32),
                 jax.ShapeDtypeStruct((LANES, slots * sz.zb * sz.cells), BF16),
             ),
-            in_specs=smem(1) + vmem(3),
+            in_specs=smem(1) + [pl.BlockSpec(memory_space=pltpu.HBM)] * 3,
             out_specs=tuple(vmem(6)),
+            scratch_shapes=[
+                pltpu.VMEM(start.shape, start.dtype),
+                pltpu.VMEM(pv.shape, pv.dtype),
+                pltpu.VMEM(ids.shape, ids.dtype),
+                pltpu.SemaphoreType.DMA((3,)),
+            ],
             compiler_params=params,
             name="project_first",
         )(flag, start, pv, ids)
@@ -387,28 +442,34 @@
         for degree in range(1, STEPS + 1):
             tables, from_a, from_b, from_y = exchange(*messages)
             last = degree == STEPS
-            args = (
-                *tables,
-                energy,
-                from_a,
-                from_b,
-                *from_y,
-                pv,
-                pot,
-                row_of,
-                hot,
-                *history,
-            )
+            scalars = (flag, cheb_coef) if last else (flag,)
+            args = (from_a, from_b, *from_y, pot, *history)
+            rest = pl.pallas_call(
+                functools.partial(local_kernel, sz, degree, len(from_y)),
+                out_shape=field,
+                in_specs=smem(len(scalars)) + vmem(len(args)),
+                out_specs=vmem(1)[0],
+                compiler_params=params,
+                name=f"local_{degree}",
+            )(*scalars, *args)
+            args = (*tables, energy, rest, pv, row_of, hot)
+            if last:
+                return pl.pallas_call(
+                    functools.partial(last_kernel, sz, len(tables)),
+                    out_shape=field,
+                    in_specs=smem(1) + vmem(len(args)),
+                    out_specs=vmem(1)[0],
+                    compiler_params=params,
+                    name="filtered",
+                )(cheb_coef, *args)
             out = pl.pallas_call(
-                functools.partial(step_kernel, sz, degree, len(tables), len(from_y)),
-                out_shape=(field,) if last else (field,) + message_shapes,
-                in_specs=smem(2) + vmem(len(args)),
-                out_specs=tuple(vmem(1 if last else 5)),
+                functools.partial(nonlocal_kernel, sz, degree, len(tables)),
+                out_shape=(field,) + message_shapes,
+                in_specs=smem(1) + vmem(len(args)),
+                out_specs=tuple(vmem(5)),
                 compiler_params=params,
-                name=f"hamilton_{degree}",
-            )(flag, cheb_coef, *args)
-            if last:
-                return out[0]
+                name=f"nonlocal_{degree}",
+            )(flag, *args)
             history.append(out[0])
             messages = out[1:]
 

time: 48.8 us -> 48.2 us (0.988)
  waiting for transfers between devices: 26.7 us -> 24.9 us
  Pallas kernels: 5.19 us -> 5.91 us
    ppermute x15, waiting for transfers between devices: 11.5 us -> 9.65 us  [swap(): return lax.ppermute(arr, ('gx', 'gy'), pairs)]
    pallas_call x1, Pallas kernels: 0.65 us -> 1.33 us  [one_orbital(): pl.pallas_call(functools.partial(first_kernel, sz), out_shape=message_sha...]
    unnamed x11 -> x14, local copies, waits for them, and re-layouts: 2.75 us -> 3.2 us
    pallas_call x3 -> x6, Pallas kernels: 4.54 us -> 4.58 us  [the longest x2 1.86 us: one_orbital(): pl.pallas_call(functools.partial(nonlocal_kernel, sz, degree, len(tables)...]
  transfers between devices with their start and end apart: 17 -> 17, of which waited for: 8 -> 7; matrix products, arithmetic and copies ran while one was open for 0% -> 0% of each run, Pallas kernels for 0% -> 3%
where the time goes in v2:
time: 48.2 us; the launch traced here: 48 us
  waiting for transfers between devices  24.9 us (52%)
  starting transfers between devices  13.1 us (27%)
  Pallas kernels  5.91 us (12%)
  local copies, waits for them, and re-layouts  3.2 us (7%)
  other arithmetic  0.74 us (2%)
    ppermute x15, starting transfers between devices, swap(): return lax.ppermute(arr, ('gx', 'gy'), pairs)  11 us
    ppermute x1, waiting for transfers between devices, orb_sum(): lax.ppermute(vals, 'orb', [(i, 3 - i) for i in range(4)])  9.89 us
    ppermute x15, waiting for transfers between devices, swap(): return lax.ppermute(arr, ('gx', 'gy'), pairs)  9.65 us
    ppermute x1, waiting for transfers between devices, orb_sum(): vals = vals + lax.ppermute(vals, 'orb', [(i, i ^ 1) for i in range(4)])  5.35 us
    unnamed x14, local copies, waits for them, and re-layouts  3.2 us
    pallas_call x2, Pallas kernels, one_orbital(): pl.pallas_call(functools.partial(nonlocal_kernel, sz, degree, len(tables)...  1.86 us
    pallas_call x3, Pallas kernels, one_orbital(): pl.pallas_call(functools.partial(local_kernel, sz, degree, len(from_y)),...  1.65 us
    ppermute x1, starting transfers between devices, orb_sum(): vals = vals + lax.ppermute(vals, 'orb', [(i, i ^ 1) for i in range(4)])  1.64 us
  transfers between devices with their start and end apart: 17, of which 7 were waited for; matrix products, arithmetic and copies ran while one was open for 0% of the time, Pallas kernels for 3%

profile of v2, /device:TPU:16, one launch (start us, length us, event | category | flops | bytes accessed | tf_op | source)
XLA Modules:
  0.0 48.0 jit_solution(8812699527447160554)
XLA Ops:
  0.0 1.0 %copy-done = bf16[4,8,16,384]{3,2,1,0:T(8,128)(2,1)S(1)} copy-done((bf16[4,8,16,384]{3,2,1,0:T(8,128)(2,1)S(1)}, bf16[4,8,16,384]{3,2,1,0:T(8,128)(2,1)}, u32[]{:S(2)}) %copy-start) | copy-done | bytes 393240
  1.0 0.9 %copy-done.2 = f32[1,8,16,384]{3,2,1,0:T(8,128)S(1)} copy-done((f32[1,8,16,384]{3,2,1,0:T(8,128)S(1)}, f32[1,8,16,384]{3,2,1,0:T(8,128)}, u32[]{:S(2)}) %copy-start.2) | copy-done | bytes 196632
  1.9 0.8 %copy-done.5 = s32[4,8,16,3]{2,1,3,0:T(8,128)S(1)} copy-done((s32[4,8,16,3]{2,1,3,0:T(8,128)S(1)}, s32[4,8,16,3]{2,1,3,0:T(8,128)}, u32[]{:S(2)}) %copy-start.5) | copy-done | bytes 6168
  2.7 1.3 %project_first.1 = (f32[96,128]{1,0:T(8,128)S(1)}, f32[128,128]{1,0:T(8,128)S(1)}, f32[128,128]{1,0:T(8,128)S(1)}, f32[32,128]{1,0:T(8,128)S(1)}, f32[12,128]{1,0:T(8,128)S(1)}, /*index=5*/bf16[128,1536]{1,0:T(8,128)(2,1)S(1)}) custom-call(s32[1]{0:T(128)} %bitcast.flag_ref, f32[128,384]{1,0:T(8,128)S(1)} %bitcast.13, bf16[512,384]{1,0:T(8,128)(2,1)S(1)} %bitcast.9, ...), custom_call_target="tpu_custom_call" | custom-call | tf_op jit(solution)/shard_map/project_first/pallas_call | solution.py:423
  4.1 1.0 %collective-permute-start.1 = (f32[128,128]{1,0:T(8,128)S(1)}, f32[128,128]{1,0:T(8,128)S(1)}, u32[]{:S(2)}, u32[]{:S(2)}) collective-permute-start(f32[128,128]{1,0:T(8,128)S(1)} %get-tuple-element.22), channel_id=1, source_target_pairs={{0,24},{4,28},{8,16},{12,20},{16,8},{20,12},{24,0},{28,4},{1,25},{... | collective-permute-start | bytes 196616 | tf_op jit(solution)/shard_map/ppermute | solution.py:344
  5.1 1.5 %collective-permute-start.2 = (f32[128,128]{1,0:T(8,128)S(1)}, f32[128,128]{1,0:T(8,128)S(1)}, u32[]{:S(2)}, u32[]{:S(2)}) collective-permute-start(f32[128,128]{1,0:T(8,128)S(1)} %get-tuple-element.23), channel_id=1, source_target_pairs={{0,4},{4,0},{8,12},{12,8},{16,20},{20,16},{24,28},{28,24},{1,5},{5... | collective-permute-start | bytes 196616 | tf_op jit(solution)/shard_map/ppermute | solution.py:344
  6.6 0.5 collective-permute-start
  7.1 0.2 collective-permute-start.4
  7.3 3.4 %collective-permute-done = f32[32,128]{1,0:T(8,128)S(1)} collective-permute-done((f32[32,128]{1,0:T(8,128)S(1)}, f32[32,128]{1,0:T(8,128)S(1)}, u32[]{:S(2)}, u32[]{:S(2)}) %collective-permute-start) | collective-permute-done | bytes 16416 | tf_op jit(solution)/shard_map/ppermute | solution.py:344
  10.6 0.0 collective-permute-done.1.refs_1_
  10.6 0.0 collective-permute-done.2.refs_2_
  10.7 0.0 copy-start.1
  10.7 0.5 %collective-permute-start.3 = (f32[32,128]{1,0:T(8,128)S(1)}, f32[32,128]{1,0:T(8,128)S(1)}, u32[]{:S(2)}, u32[]{:S(2)}) collective-permute-start(f32[32,128]{1,0:T(8,128)S(1)} %slice_add_fusion.4.refs_0_), channel_id=1, source_target_pairs={{0,8},{4,12},{8,0},{12,4},{16,24},{20,28},{24,16},{28,20},{1,9},{5... | collective-permute-start | bytes 49160 | tf_op jit(solution)/shard_map/ppermute | solution.py:344
  11.2 0.0 collective-permute-done.4.refs_0_
  11.2 0.3 local_1.1.refs_3_
  11.5 0.5 %collective-permute-done.3.refs_1_ = f32[32,128]{1,0:T(8,128)S(1)} collective-permute-done((f32[32,128]{1,0:T(8,128)S(1)}, f32[32,128]{1,0:T(8,128)S(1)}, u32[]{:S(2)}, u32[]{:S(2)}) %collective-permute-start.3) | collective-permute-done | bytes 16416 | tf_op jit(solution)/shard_map/ppermute | solution.py:344
  12.0 0.9 %nonlocal_1.1 = (f32[128,384]{1,0:T(8,128)S(1)}, f32[96,128]{1,0:T(8,128)S(1)}, f32[128,128]{1,0:T(8,128)S(1)}, f32[128,128]{1,0:T(8,128)S(1)}, f32[32,128]{1,0:T(8,128)S(1)}) custom-call(s32[1]{0:T(128)} %bitcast.flag_ref, f32[32,128]{1,0:T(8,128)S(1)} %slice_add_fusion.4.refs_0_, f32[32,128]{1,0:T(8,128)S(1)} %collective-permute-done.3.refs_1_, ...), custom_call_target="tpu_custom_call" | custom-call | tf_op jit(solution)/shard_map/nonlocal_1/pallas_call | solution.py:465
  12.9 0.5 collective-permute-start.6
  13.4 0.5 %collective-permute-start.7 = (f32[128,128]{1,0:T(8,128)S(1)}, f32[128,128]{1,0:T(8,128)S(1)}, u32[]{:S(2)}, u32[]{:S(2)}) collective-permute-start(f32[128,128]{1,0:T(8,128)S(1)} %get-tuple-element.29), channel_id=1, source_target_pairs={{0,4},{4,0},{8,12},{12,8},{16,20},{20,16},{24,28},{28,24},{1,5},{5... | collective-permute-start | bytes 196616 | tf_op jit(solution)/shard_map/ppermute | solution.py:344
  13.9 1.9 %collective-permute-start.5 = (f32[32,128]{1,0:T(8,128)S(1)}, f32[32,128]{1,0:T(8,128)S(1)}, u32[]{:S(2)}, u32[]{:S(2)}) collective-permute-start(f32[32,128]{1,0:T(8,128)S(1)} %get-tuple-element.27), channel_id=1, source_target_pairs={{0,28},{4,24},{8,20},{12,16},{16,12},{20,8},{24,4},{28,0},{1,29},{... | collective-permute-start | bytes 49160 | tf_op jit(solution)/shard_map/ppermute | solution.py:344
  15.9 0.6 %collective-permute-start.9 = (f32[96,128]{1,0:T(8,128)S(1)}, f32[96,128]{1,0:T(8,128)S(1)}, u32[]{:S(2)}, u32[]{:S(2)}) collective-permute-start(f32[96,128]{1,0:T(8,128)S(1)} %get-tuple-element.30), channel_id=1, source_target_pairs={{0,8},{4,12},{8,0},{12,4},{16,24},{20,28},{24,16},{28,20},{1,9},{5... | collective-permute-start | bytes 147464 | tf_op jit(solution)/shard_map/ppermute | solution.py:344
  16.5 1.5 %collective-permute-done.5 = f32[32,128]{1,0:T(8,128)S(1)} collective-permute-done((f32[32,128]{1,0:T(8,128)S(1)}, f32[32,128]{1,0:T(8,128)S(1)}, u32[]{:S(2)}, u32[]{:S(2)}) %collective-permute-start.5) | collective-permute-done | bytes 16416 | tf_op jit(solution)/shard_map/ppermute | solution.py:344
  18.0 0.0 collective-permute-done.6.refs_1_
  18.0 0.0 collective-permute-done.7.refs_2_
  18.0 0.2 collective-permute-start.8
  18.2 0.0 collective-permute-done.9.refs_0_
  18.2 0.4 local_2.1.refs_3_
  18.6 0.7 %collective-permute-done.8.refs_1_ = f32[32,128]{1,0:T(8,128)S(1)} collective-permute-done((f32[32,128]{1,0:T(8,128)S(1)}, f32[32,128]{1,0:T(8,128)S(1)}, u32[]{:S(2)}, u32[]{:S(2)}) %collective-permute-start.8) | collective-permute-done | bytes 16416 | tf_op jit(solution)/shard_map/ppermute | solution.py:344
  19.3 0.9 %nonlocal_2.1 = (f32[128,384]{1,0:T(8,128)S(1)}, f32[96,128]{1,0:T(8,128)S(1)}, f32[128,128]{1,0:T(8,128)S(1)}, f32[128,128]{1,0:T(8,128)S(1)}, f32[32,128]{1,0:T(8,128)S(1)}) custom-call(s32[1]{0:T(128)} %bitcast.flag_ref, f32[32,128]{1,0:T(8,128)S(1)} %slice_add_fusion.2.refs_0_, f32[32,128]{1,0:T(8,128)S(1)} %collective-permute-done.8.refs_1_, ...), custom_call_target="tpu_custom_call" | custom-call | tf_op jit(solution)/shard_map/nonlocal_2/pallas_call | solution.py:465
  20.2 1.3 %collective-permute-start.11 = (f32[128,128]{1,0:T(8,128)S(1)}, f32[128,128]{1,0:T(8,128)S(1)}, u32[]{:S(2)}, u32[]{:S(2)}) collective-permute-start(f32[128,128]{1,0:T(8,128)S(1)} %get-tuple-element.33), channel_id=1, source_target_pairs={{0,24},{4,28},{8,16},{12,20},{16,8},{20,12},{24,0},{28,4},{1,25},{... | collective-permute-start | bytes 196616 | tf_op jit(solution)/shard_map/ppermute | solution.py:344
  21.5 1.6 %collective-permute-start.12 = (f32[128,128]{1,0:T(8,128)S(1)}, f32[128,128]{1,0:T(8,128)S(1)}, u32[]{:S(2)}, u32[]{:S(2)}) collective-permute-start(f32[128,128]{1,0:T(8,128)S(1)} %get-tuple-element.34), channel_id=1, source_target_pairs={{0,4},{4,0},{8,12},{12,8},{16,20},{20,16},{24,28},{28,24},{1,5},{5... | collective-permute-start | bytes 196616 | tf_op jit(solution)/shard_map/ppermute | solution.py:344
  23.1 0.0 collective-permute-start.10
  23.1 0.4 collective-permute-start.14
  23.6 3.6 %collective-permute-done.10 = f32[32,128]{1,0:T(8,128)S(1)} collective-permute-done((f32[32,128]{1,0:T(8,128)S(1)}, f32[32,128]{1,0:T(8,128)S(1)}, u32[]{:S(2)}, u32[]{:S(2)}) %collective-permute-start.10) | collective-permute-done | bytes 16416 | tf_op jit(solution)/shard_map/ppermute | solution.py:344
  27.2 0.0 collective-permute-done.11.refs_2_
  27.2 0.0 collective-permute-done.12.refs_3_
  27.2 0.0 copy-start.6
  27.2 0.2 collective-permute-start.13
  27.4 0.0 collective-permute-done.14.refs_1_
  27.4 0.5 copy-done.6
  27.9 1.0 %local_3.1.refs_3_ = f32[128,384]{1,0:T(8,128)S(1)} custom-call(s32[1]{0:T(128)} %bitcast.flag_ref, f32[4]{0:T(128)S(1)} %copy-done.6, f32[96,128]{1,0:T(8,128)S(1)} %collective-permute-done.14.refs_1_, f32[128,128]{1,0:T(8,128)S(1)} %collective-permute-done.11.refs_2_, f32[128,128]{1,0:T(8,128)S(1)} %collective-permute-done.12.refs_3_, ...), custom_call_target="tpu_custom_call" | custom-call | tf_op jit(solution)/shard_map/local_3/pallas_call | solution.py:447
  28.8 0.0 collective-permute-done.13.refs_1_
  28.8 1.1 %filtered.1 = f32[128,384]{1,0:T(8,128)S(1)} custom-call(f32[4]{0:T(128)S(1)} %copy-done.6, f32[32,128]{1,0:T(8,128)S(1)} %slice_add_fusion.refs_0_, f32[32,128]{1,0:T(8,128)S(1)} %collective-permute-done.13.refs_1_, f32[32,128]{1,0:T(8,128)S(1)} %bitcast.22, f32[128,384]{1,0:T(8,128)S(1)} %local_3.1.refs_3_, bf16[512,384]{1,0:T(8,128)(2,1)S(1)} %bitcast.12, ...), custom_call_target="tpu_custom_call" | custom-call | tf_op jit(solution)/shard_map/filtered/pallas_call | solution.py:457
  29.9 1.6 %collective-permute-start.15 = (f32[128,384]{1,0:T(8,128)S(1)}, f32[128,384]{1,0:T(8,128)S(1)}, u32[]{:S(2)}, u32[]{:S(2)}) collective-permute-start(f32[128,384]{1,0:T(8,128)S(1)} %filtered.1), channel_id=1, source_target_pairs={{0,1},{1,0},{2,3},{3,2},{4,5},{5,4},{6,7},{7,6},{8,9},{9,8},{10,11... | collective-permute-start | bytes 589832 | tf_op jit(solution)/shard_map/ppermute | solution.py:351
  31.5 5.4 %collective-permute-done.15 = f32[128,384]{1,0:T(8,128)S(1)} collective-permute-done((f32[128,384]{1,0:T(8,128)S(1)}, f32[128,384]{1,0:T(8,128)S(1)}, u32[]{:S(2)}, u32[]{:S(2)}) %collective-permute-start.15) | collective-permute-done | bytes 196640 | tf_op jit(solution)/shard_map/ppermute | solution.py:351
  36.9 0.5 %collective-permute-start.16 = (f32[128,384]{1,0:T(8,128)S(1)}, f32[128,384]{1,0:T(8,128)S(1)}, u32[]{:S(2)}, u32[]{:S(2)}) collective-permute-start(f32[128,384]{1,0:T(8,128)S(1)} %add.42), channel_id=1, source_target_pairs={{0,3},{1,2},{2,1},{3,0},{4,7},{5,6},{6,5},{7,4},{8,11},{9,10},{10,... | collective-permute-start | bytes 589832 | tf_op jit(solution)/shard_map/ppermute | solution.py:352
  37.4 9.9 %collective-permute-done.16 = f32[128,384]{1,0:T(8,128)S(1)} collective-permute-done((f32[128,384]{1,0:T(8,128)S(1)}, f32[128,384]{1,0:T(8,128)S(1)}, u32[]{:S(2)}, u32[]{:S(2)}) %collective-permute-start.16) | collective-permute-done | bytes 196640 | tf_op jit(solution)/shard_map/ppermute | solution.py:352
  47.3 0.7 %add_multiply_fusion = f32[128,384]{1,0:T(8,128)} fusion(f32[128,384]{1,0:T(8,128)S(1)} %add.42, f32[128,384]{1,0:T(8,128)S(1)} %collective-permute-done.16), kind=kLoop, calls=%fused_computation | loop fusion | flops 98304 | bytes 589824 | tf_op jit(solution)/shard_map/mul | solution.py:352
  (12 shorter events, 0.1 us)
Async XLA Ops:
  0.0 1.0 %copy-start = (bf16[4,8,16,384]{3,2,1,0:T(8,128)(2,1)S(1)}, bf16[4,8,16,384]{3,2,1,0:T(8,128)(2,1)}, u32[]{:S(2)}) copy-start(bf16[4,8,16,384]{3,2,1,0:T(8,128)(2,1)} %param.8) | copy-start | bytes 1179652
  1.0 0.9 %copy-start.2 = (f32[1,8,16,384]{3,2,1,0:T(8,128)S(1)}, f32[1,8,16,384]{3,2,1,0:T(8,128)}, u32[]{:S(2)}) copy-start(f32[1,8,16,384]{3,2,1,0:T(8,128)} %param.6) | copy-start | bytes 589828
  1.9 0.8 %copy-start.5 = (s32[4,8,16,3]{2,1,3,0:T(8,128)S(1)}, s32[4,8,16,3]{2,1,3,0:T(8,128)}, u32[]{:S(2)}) copy-start(s32[4,8,16,3]{2,1,3,0:T(8,128)} %param.9) | copy-start | bytes 18436
  2.7 8.4 %copy-start.3 = (f32[8,16,384]{2,1,0:T(8,128)S(1)}, f32[8,16,384]{2,1,0:T(8,128)}, u32[]{:S(2)}) copy-start(f32[8,16,384]{2,1,0:T(8,128)} %param.7) | copy-start | bytes 589828
  4.1 6.6 %collective-permute-start.1 = (f32[128,128]{1,0:T(8,128)S(1)}, f32[128,128]{1,0:T(8,128)S(1)}, u32[]{:S(2)}, u32[]{:S(2)}) collective-permute-start(f32[128,128]{1,0:T(8,128)S(1)} %get-tuple-element.22), channel_id=1, source_target_pairs={{0,24},{4,28},{8,16},{12,20},{16,8},{20,12},{24,0},{28,4},{1,25},{... | collective-permute-start | bytes 196616 | tf_op jit(solution)/shard_map/ppermute | solution.py:344
  5.1 5.6 %collective-permute-start.2 = (f32[128,128]{1,0:T(8,128)S(1)}, f32[128,128]{1,0:T(8,128)S(1)}, u32[]{:S(2)}, u32[]{:S(2)}) collective-permute-start(f32[128,128]{1,0:T(8,128)S(1)} %get-tuple-element.23), channel_id=1, source_target_pairs={{0,4},{4,0},{8,12},{12,8},{16,20},{20,16},{24,28},{28,24},{1,5},{5... | collective-permute-start | bytes 196616 | tf_op jit(solution)/shard_map/ppermute | solution.py:344
  6.6 4.1 %collective-permute-start = (f32[32,128]{1,0:T(8,128)S(1)}, f32[32,128]{1,0:T(8,128)S(1)}, u32[]{:S(2)}, u32[]{:S(2)}) collective-permute-start(f32[32,128]{1,0:T(8,128)S(1)} %get-tuple-element.21), channel_id=1, source_target_pairs={{0,28},{4,24},{8,20},{12,16},{16,12},{20,8},{24,4},{28,0},{1,29},{... | collective-permute-start | bytes 49160 | tf_op jit(solution)/shard_map/ppermute | solution.py:344
  7.1 4.1 %collective-permute-start.4 = (f32[96,128]{1,0:T(8,128)S(1)}, f32[96,128]{1,0:T(8,128)S(1)}, u32[]{:S(2)}, u32[]{:S(2)}) collective-permute-start(f32[96,128]{1,0:T(8,128)S(1)} %get-tuple-element.24), channel_id=1, source_target_pairs={{0,8},{4,12},{8,0},{12,4},{16,24},{20,28},{24,16},{28,20},{1,9},{5... | collective-permute-start | bytes 147464 | tf_op jit(solution)/shard_map/ppermute | solution.py:344
  10.7 1.3 %copy-start.1 = (bf16[4,8,16,384]{3,2,1,0:T(8,128)(2,1)S(1)}, bf16[4,8,16,384]{3,2,1,0:T(8,128)(2,1)}, u32[]{:S(2)}) copy-start(bf16[4,8,16,384]{3,2,1,0:T(8,128)(2,1)} %param.8) | copy-start | bytes 1179652
  10.7 1.3 %collective-permute-start.3 = (f32[32,128]{1,0:T(8,128)S(1)}, f32[32,128]{1,0:T(8,128)S(1)}, u32[]{:S(2)}, u32[]{:S(2)}) collective-permute-start(f32[32,128]{1,0:T(8,128)S(1)} %slice_add_fusion.4.refs_0_), channel_id=1, source_target_pairs={{0,8},{4,12},{8,0},{12,4},{16,24},{20,28},{24,16},{28,20},{1,9},{5... | collective-permute-start | bytes 49160 | tf_op jit(solution)/shard_map/ppermute | solution.py:344
  11.2 0.8 %copy-start.4 = (f32[4096]{0:T(1024)S(1)}, f32[4096]{0:T(1024)}, u32[]{:S(2)}) copy-start(f32[4096]{0:T(1024)} %param.10) | copy-start | bytes 49156
  12.9 5.1 %collective-permute-start.6 = (f32[128,128]{1,0:T(8,128)S(1)}, f32[128,128]{1,0:T(8,128)S(1)}, u32[]{:S(2)}, u32[]{:S(2)}) collective-permute-start(f32[128,128]{1,0:T(8,128)S(1)} %get-tuple-element.28), channel_id=1, source_target_pairs={{0,24},{4,28},{8,16},{12,20},{16,8},{20,12},{24,0},{28,4},{1,25},{... | collective-permute-start | bytes 196616 | tf_op jit(solution)/shard_map/ppermute | solution.py:344
  13.4 4.6 %collective-permute-start.7 = (f32[128,128]{1,0:T(8,128)S(1)}, f32[128,128]{1,0:T(8,128)S(1)}, u32[]{:S(2)}, u32[]{:S(2)}) collective-permute-start(f32[128,128]{1,0:T(8,128)S(1)} %get-tuple-element.29), channel_id=1, source_target_pairs={{0,4},{4,0},{8,12},{12,8},{16,20},{20,16},{24,28},{28,24},{1,5},{5... | collective-permute-start | bytes 196616 | tf_op jit(solution)/shard_map/ppermute | solution.py:344
  13.9 4.1 %collective-permute-start.5 = (f32[32,128]{1,0:T(8,128)S(1)}, f32[32,128]{1,0:T(8,128)S(1)}, u32[]{:S(2)}, u32[]{:S(2)}) collective-permute-start(f32[32,128]{1,0:T(8,128)S(1)} %get-tuple-element.27), channel_id=1, source_target_pairs={{0,28},{4,24},{8,20},{12,16},{16,12},{20,8},{24,4},{28,0},{1,29},{... | collective-permute-start | bytes 49160 | tf_op jit(solution)/shard_map/ppermute | solution.py:344
  15.9 2.3 %collective-permute-start.9 = (f32[96,128]{1,0:T(8,128)S(1)}, f32[96,128]{1,0:T(8,128)S(1)}, u32[]{:S(2)}, u32[]{:S(2)}) collective-permute-start(f32[96,128]{1,0:T(8,128)S(1)} %get-tuple-element.30), channel_id=1, source_target_pairs={{0,8},{4,12},{8,0},{12,4},{16,24},{20,28},{24,16},{28,20},{1,9},{5... | collective-permute-start | bytes 147464 | tf_op jit(solution)/shard_map/ppermute | solution.py:344
  18.0 1.2 %collective-permute-start.8 = (f32[32,128]{1,0:T(8,128)S(1)}, f32[32,128]{1,0:T(8,128)S(1)}, u32[]{:S(2)}, u32[]{:S(2)}) collective-permute-start(f32[32,128]{1,0:T(8,128)S(1)} %slice_add_fusion.2.refs_0_), channel_id=1, source_target_pairs={{0,8},{4,12},{8,0},{12,4},{16,24},{20,28},{24,16},{28,20},{1,9},{5... | collective-permute-start | bytes 49160 | tf_op jit(solution)/shard_map/ppermute | solution.py:344
  20.2 7.0 %collective-permute-start.11 = (f32[128,128]{1,0:T(8,128)S(1)}, f32[128,128]{1,0:T(8,128)S(1)}, u32[]{:S(2)}, u32[]{:S(2)}) collective-permute-start(f32[128,128]{1,0:T(8,128)S(1)} %get-tuple-element.33), channel_id=1, source_target_pairs={{0,24},{4,28},{8,16},{12,20},{16,8},{20,12},{24,0},{28,4},{1,25},{... | collective-permute-start | bytes 196616 | tf_op jit(solution)/shard_map/ppermute | solution.py:344
  21.5 5.7 %collective-permute-start.12 = (f32[128,128]{1,0:T(8,128)S(1)}, f32[128,128]{1,0:T(8,128)S(1)}, u32[]{:S(2)}, u32[]{:S(2)}) collective-permute-start(f32[128,128]{1,0:T(8,128)S(1)} %get-tuple-element.34), channel_id=1, source_target_pairs={{0,4},{4,0},{8,12},{12,8},{16,20},{20,16},{24,28},{28,24},{1,5},{5... | collective-permute-start | bytes 196616 | tf_op jit(solution)/shard_map/ppermute | solution.py:344
  23.1 4.1 %collective-permute-start.10 = (f32[32,128]{1,0:T(8,128)S(1)}, f32[32,128]{1,0:T(8,128)S(1)}, u32[]{:S(2)}, u32[]{:S(2)}) collective-permute-start(f32[32,128]{1,0:T(8,128)S(1)} %get-tuple-element.32), channel_id=1, source_target_pairs={{0,28},{4,24},{8,20},{12,16},{16,12},{20,8},{24,4},{28,0},{1,29},{... | collective-permute-start | bytes 49160 | tf_op jit(solution)/shard_map/ppermute | solution.py:344
  23.1 4.2 %collective-permute-start.14 = (f32[96,128]{1,0:T(8,128)S(1)}, f32[96,128]{1,0:T(8,128)S(1)}, u32[]{:S(2)}, u32[]{:S(2)}) collective-permute-start(f32[96,128]{1,0:T(8,128)S(1)} %get-tuple-element.35), channel_id=1, source_target_pairs={{0,8},{4,12},{8,0},{12,4},{16,24},{20,28},{24,16},{28,20},{1,9},{5... | collective-permute-start | bytes 147464 | tf_op jit(solution)/shard_map/ppermute | solution.py:344
  27.2 0.7 %copy-start.6 = (f32[4]{0:T(128)S(1)}, f32[4]{0:T(128)}, u32[]{:S(2)}) copy-start(f32[4]{0:T(128)} %cheb_ref.1) | copy-start | bytes 52
  27.2 1.6 %collective-permute-start.13 = (f32[32,128]{1,0:T(8,128)S(1)}, f32[32,128]{1,0:T(8,128)S(1)}, u32[]{:S(2)}, u32[]{:S(2)}) collective-permute-start(f32[32,128]{1,0:T(8,128)S(1)} %slice_add_fusion.refs_0_), channel_id=1, source_target_pairs={{0,8},{4,12},{8,0},{12,4},{16,24},{20,28},{24,16},{28,20},{1,9},{5... | collective-permute-start | bytes 49160 | tf_op jit(solution)/shard_map/ppermute | solution.py:344
  29.9 7.0 %collective-permute-start.15 = (f32[128,384]{1,0:T(8,128)S(1)}, f32[128,384]{1,0:T(8,128)S(1)}, u32[]{:S(2)}, u32[]{:S(2)}) collective-permute-start(f32[128,384]{1,0:T(8,128)S(1)} %filtered.1), channel_id=1, source_target_pairs={{0,1},{1,0},{2,3},{3,2},{4,5},{5,4},{6,7},{7,6},{8,9},{9,8},{10,11... | collective-permute-start | bytes 589832 | tf_op jit(solution)/shard_map/ppermute | solution.py:351
  36.9 10.4 %collective-permute-start.16 = (f32[128,384]{1,0:T(8,128)S(1)}, f32[128,384]{1,0:T(8,128)S(1)}, u32[]{:S(2)}, u32[]{:S(2)}) collective-permute-start(f32[128,384]{1,0:T(8,128)S(1)} %add.42), channel_id=1, source_target_pairs={{0,3},{1,2},{2,1},{3,0},{4,7},{5,6},{6,5},{7,4},{8,11},{9,10},{10,... | collective-permute-start | bytes 589832 | tf_op jit(solution)/shard_map/ppermute | solution.py:352

commit v3 on v2

--- a/solution.py
+++ b/solution.py
@@ -241,6 +241,11 @@
     )
 
 
+def coefficient(sz, cheb_ref, n):
+    row = cheb_ref[n : n + 1, :]
+    return jnp.concatenate([row] * sz.zb, axis=1)
+
+
 def local_kernel(sz, degree, n_y, flag_ref, *refs):
     refs = list(refs)
     cheb_ref = refs.pop(0) if degree == STEPS else None
@@ -264,9 +269,9 @@
     if degree > 1:
         result = result - history[-2][...]
     if degree == STEPS:
-        result = cheb_ref[STEPS] * result
+        result = coefficient(sz, cheb_ref, STEPS) * result
         for n in range(STEPS):
-            result = result + cheb_ref[n] * history[n][...]
+            result = result + coefficient(sz, cheb_ref, n) * history[n][...]
     out_ref[...] = result
 
 
@@ -279,6 +284,10 @@
 
 def nonlocal_kernel(sz, degree, n_tables, flag_ref, *refs):
     refs = list(refs)
+    if degree == 1:
+        cheb_ref, cheb_out = refs.pop(0), refs.pop()
+        for n in range(STEPS + 1):
+            cheb_out[n : n + 1, :] = jnp.full((1, LANES), cheb_ref[n], F32)
     table_refs = [refs.pop(0) for _ in range(n_tables)]
     energy_ref, rest_ref, pv_ref, rows_ref, hot_ref = (refs.pop(0) for _ in range(5))
     row_of = rows_ref[...]
@@ -295,7 +304,7 @@
     refs = list(refs)
     table_refs = [refs.pop(0) for _ in range(n_tables)]
     energy_ref, rest_ref, pv_ref, rows_ref, hot_ref, out_ref = refs
-    table = added(table_refs) * (energy_ref[...] * (2.0 / E_HALF * cheb_ref[STEPS]))
+    table = added(table_refs) * (energy_ref[...] * (2.0 / E_HALF * cheb_ref[STEPS : STEPS + 1, :]))
     result = rest_ref[...] + jnp.concatenate(
         projected(sz, table, pv_ref, rows_ref[...], hot_ref), axis=1
     )
@@ -435,43 +444,48 @@
                 pltpu.VMEM(ids.shape, ids.dtype),
                 pltpu.SemaphoreType.DMA((3,)),
             ],
-            compiler_params=params,
+            compiler_params=pltpu.CompilerParams(vmem_limit_bytes=62 << 20),
             name="project_first",
         )(flag, start, pv, ids)
         history = [start]
         for degree in range(1, STEPS + 1):
             tables, from_a, from_b, from_y = exchange(*messages)
             last = degree == STEPS
-            scalars = (flag, cheb_coef) if last else (flag,)
             args = (from_a, from_b, *from_y, pot, *history)
+            if last:
+                args = (cheb, *args)
             rest = pl.pallas_call(
                 functools.partial(local_kernel, sz, degree, len(from_y)),
                 out_shape=field,
-                in_specs=smem(len(scalars)) + vmem(len(args)),
+                in_specs=smem(1) + vmem(len(args)),
                 out_specs=vmem(1)[0],
                 compiler_params=params,
                 name=f"local_{degree}",
-            )(*scalars, *args)
+            )(flag, *args)
             args = (*tables, energy, rest, pv, row_of, hot)
             if last:
                 return pl.pallas_call(
                     functools.partial(last_kernel, sz, len(tables)),
                     out_shape=field,
-                    in_specs=smem(1) + vmem(len(args)),
+                    in_specs=vmem(1 + len(args)),
                     out_specs=vmem(1)[0],
                     compiler_params=params,
                     name="filtered",
-                )(cheb_coef, *args)
+                )(cheb, *args)
+            scalars = (flag, cheb_coef) if degree == 1 else (flag,)
+            extra = (jax.ShapeDtypeStruct((SUBLANES, LANES), F32),) if degree == 1 else ()
             out = pl.pallas_call(
                 functools.partial(nonlocal_kernel, sz, degree, len(tables)),
-                out_shape=(field,) + message_shapes,
-                in_specs=smem(1) + vmem(len(args)),
-                out_specs=tuple(vmem(5)),
+                out_shape=(field,) + message_shapes + extra,
+                in_specs=smem(len(scalars)) + vmem(len(args)),
+                out_specs=tuple(vmem(5 + len(extra))),
                 compiler_params=params,
                 name=f"nonlocal_{degree}",
-            )(flag, *args)
+            )(*scalars, *args)
+            if degree == 1:
+                cheb = out[-1]
             history.append(out[0])
-            messages = out[1:]
+            messages = out[1:5]
 
     density = one_orbital(orbitals[0].reshape(sz.cells, nz))
     for at in range(1, count_orb):

time: 48.2 us -> 47.9 us (level)
  local copies, waits for them, and re-layouts: 3.2 us -> 0.66 us
  waiting for transfers between devices: 24.9 us -> 25.8 us
  other arithmetic: 0.74 us -> 1.51 us
  Pallas kernels: 5.91 us -> 6.5 us
    unnamed x14, local copies, waits for them, and re-layouts: 3.2 us -> 0.66 us
    pallas_call x1, Pallas kernels: 1.33 us -> 2.45 us  [one_orbital(): pl.pallas_call(functools.partial(first_kernel, sz), out_shape=message_sha...]
    ppermute x15, waiting for transfers between devices: 9.65 us -> 10.5 us  [swap(): return lax.ppermute(arr, ('gx', 'gy'), pairs)]
    add x3, other arithmetic: 0.02 us -> 0.79 us  [exchange(): table = table + from_d + from_b[sz.edge_rows:] + from_y[sz.yedge_rows:]]
    pallas_call x2, Pallas kernels: 1.86 us -> 2.43 us  [one_orbital(): pl.pallas_call(functools.partial(nonlocal_kernel, sz, degree, len(tables)...]
    pallas_call x3, Pallas kernels: 1.65 us -> 1.09 us  [one_orbital(): pl.pallas_call(functools.partial(local_kernel, sz, degree, len(from_y)),...]
    pallas_call x1, Pallas kernels: 1.07 us -> 0.52 us  [one_orbital(): pl.pallas_call(functools.partial(last_kernel, sz, len(tables)), out_shape...]
  transfers between devices with their start and end apart: 17 -> 17, of which waited for: 7 -> 8; matrix products, arithmetic and copies ran while one was open for 0% -> 2% of each run, Pallas kernels for 3% -> 2%
where the time goes in v3:
time: 47.9 us; the launch traced here: 47.7 us
  waiting for transfers between devices  25.8 us (54%)
  starting transfers between devices  13.1 us (27%)
  Pallas kernels  6.5 us (14%)
  other arithmetic  1.51 us (3%)
  local copies, waits for them, and re-layouts  0.66 us (1%)
    ppermute x15, starting transfers between devices, swap(): return lax.ppermute(arr, ('gx', 'gy'), pairs)  10.9 us
    ppermute x15, waiting for transfers between devices, swap(): return lax.ppermute(arr, ('gx', 'gy'), pairs)  10.5 us
    ppermute x1, waiting for transfers between devices, orb_sum(): lax.ppermute(vals, 'orb', [(i, 3 - i) for i in range(4)])  9.91 us
    ppermute x1, waiting for transfers between devices, orb_sum(): vals = vals + lax.ppermute(vals, 'orb', [(i, i ^ 1) for i in range(4)])  5.37 us
    pallas_call x1, Pallas kernels, one_orbital(): pl.pallas_call(functools.partial(first_kernel, sz), out_shape=message_sha...  2.45 us
    pallas_call x2, Pallas kernels, one_orbital(): pl.pallas_call(functools.partial(nonlocal_kernel, sz, degree, len(tables)...  2.43 us
    ppermute x1, starting transfers between devices, orb_sum(): vals = vals + lax.ppermute(vals, 'orb', [(i, i ^ 1) for i in range(4)])  1.67 us
    pallas_call x3, Pallas kernels, one_orbital(): pl.pallas_call(functools.partial(local_kernel, sz, degree, len(from_y)),...  1.09 us
  transfers between devices with their start and end apart: 17, of which 8 were waited for; matrix products, arithmetic and copies ran while one was open for 2% of the time, Pallas kernels for 2%

profile of v3, /device:TPU:16, one launch (start us, length us, event | category | flops | bytes accessed | tf_op | source)
XLA Modules:
  0.0 47.7 jit_solution(5250407621980705143)
XLA Ops:
  0.0 2.4 %project_first.1 = (f32[96,128]{1,0:T(8,128)}, f32[128,128]{1,0:T(8,128)}, f32[128,128]{1,0:T(8,128)}, f32[32,128]{1,0:T(8,128)}, f32[12,128]{1,0:T(8,128)}, /*index=5*/bf16[128,1536]{1,0:T(8,128)(2,1)}) custom-call(s32[1]{0:T(128)} %bitcast.flag_ref, f32[128,384]{1,0:T(8,128)} %bitcast.13, bf16[512,384]{1,0:T(8,128)(2,1)} %bitcast.9, s32[96,16]{1,0:T(8,128)} %bitcast.23), custom_call_target="tpu_custom_call" | custom-call | tf_op jit(solution)/shard_map/project_first/pallas_call | solution.py:432
  2.5 1.0 %collective-permute-start.1 = (f32[128,128]{1,0:T(8,128)}, f32[128,128]{1,0:T(8,128)S(1)}, u32[]{:S(2)}, u32[]{:S(2)}) collective-permute-start(f32[128,128]{1,0:T(8,128)} %get-tuple-element.23), channel_id=1, source_target_pairs={{0,24},{4,28},{8,16},{12,20},{16,8},{20,12},{24,0},{28,4},{1,25},{... | collective-permute-start | bytes 196616 | tf_op jit(solution)/shard_map/ppermute | solution.py:353
  3.5 1.5 %collective-permute-start.2 = (f32[128,128]{1,0:T(8,128)}, f32[128,128]{1,0:T(8,128)S(1)}, u32[]{:S(2)}, u32[]{:S(2)}) collective-permute-start(f32[128,128]{1,0:T(8,128)} %get-tuple-element.24), channel_id=1, source_target_pairs={{0,4},{4,0},{8,12},{12,8},{16,20},{20,16},{24,28},{28,24},{1,5},{5... | collective-permute-start | bytes 196616 | tf_op jit(solution)/shard_map/ppermute | solution.py:353
  5.0 0.5 %collective-permute-start = (f32[32,128]{1,0:T(8,128)}, f32[32,128]{1,0:T(8,128)S(1)}, u32[]{:S(2)}, u32[]{:S(2)}) collective-permute-start(f32[32,128]{1,0:T(8,128)} %get-tuple-element.22), channel_id=1, source_target_pairs={{0,28},{4,24},{8,20},{12,16},{16,12},{20,8},{24,4},{28,0},{1,29},{... | collective-permute-start | bytes 49160 | tf_op jit(solution)/shard_map/ppermute | solution.py:353
  5.5 0.2 collective-permute-start.4
  5.7 3.6 %collective-permute-done = f32[32,128]{1,0:T(8,128)S(1)} collective-permute-done((f32[32,128]{1,0:T(8,128)}, f32[32,128]{1,0:T(8,128)S(1)}, u32[]{:S(2)}, u32[]{:S(2)}) %collective-permute-start) | collective-permute-done | bytes 16416 | tf_op jit(solution)/shard_map/ppermute | solution.py:353
  9.3 0.0 collective-permute-done.1.refs_1_
  9.3 0.0 collective-permute-done.2.refs_2_
  9.3 0.8 %slice_add_fusion.4.refs_1_ = f32[32,128]{1,0:T(8,128)S(1)} fusion(f32[128,128]{1,0:T(8,128)S(1)} %collective-permute-done.2.refs_2_, f32[128,128]{1,0:T(8,128)S(1)} %collective-permute-done.1.refs_1_, f32[32,128]{1,0:T(8,128)} %get-tuple-element.22, f32[32,128]{1,0:T(8,128)S(1)} %collective-permute-done), kind=kLoop, calls=%fused_computation.5 | loop fusion | flops 12288 | bytes 81920 | tf_op jit(solution)/shard_map/add | solution.py:412
  10.1 0.4 collective-permute-start.3
  10.5 0.0 collective-permute-done.4.refs_0_
  10.5 0.0 copy-done.2
  10.5 0.0 copy-start.4
  10.5 0.3 local_1.1.refs_4_
  10.9 0.5 collective-permute-done.3.refs_2_
  11.3 0.0 copy-done.4
  11.3 0.0 copy-done.5
  11.4 0.6 %copy-done.6 = f32[4]{0:T(128)S(1)} copy-done((f32[4]{0:T(128)S(1)}, f32[4]{0:T(128)}, u32[]{:S(2)}) %copy-start.6) | copy-done | bytes 40
  12.0 1.5 %nonlocal_1.1 = (f32[128,384]{1,0:T(8,128)S(1)}, f32[96,128]{1,0:T(8,128)S(1)}, f32[128,128]{1,0:T(8,128)S(1)}, f32[128,128]{1,0:T(8,128)S(1)}, f32[32,128]{1,0:T(8,128)S(1)}, /*index=5*/f32[8,128]{1,0:T(8,128)S(1)}) custom-call(s32[1]{0:T(128)} %bitcast.flag_ref, f32[4]{0:T(128)S(1)} %copy-done.6, f32[32,128]{1,0:T(8,128)S(1)} %slice_add_fusion.4.refs_1_, ...), custom_call_target="tpu_custom_call" | custom-call | tf_op jit(solution)/shard_map/nonlocal_1/pallas_call | solution.py:477
  13.5 0.5 %collective-permute-start.6 = (f32[128,128]{1,0:T(8,128)S(1)}, f32[128,128]{1,0:T(8,128)S(1)}, u32[]{:S(2)}, u32[]{:S(2)}) collective-permute-start(f32[128,128]{1,0:T(8,128)S(1)} %get-tuple-element.30), channel_id=1, source_target_pairs={{0,24},{4,28},{8,16},{12,20},{16,8},{20,12},{24,0},{28,4},{1,25},{... | collective-permute-start | bytes 196616 | tf_op jit(solution)/shard_map/ppermute | solution.py:353
  14.0 0.5 %collective-permute-start.7 = (f32[128,128]{1,0:T(8,128)S(1)}, f32[128,128]{1,0:T(8,128)S(1)}, u32[]{:S(2)}, u32[]{:S(2)}) collective-permute-start(f32[128,128]{1,0:T(8,128)S(1)} %get-tuple-element.31), channel_id=1, source_target_pairs={{0,4},{4,0},{8,12},{12,8},{16,20},{20,16},{24,28},{28,24},{1,5},{5... | collective-permute-start | bytes 196616 | tf_op jit(solution)/shard_map/ppermute | solution.py:353
  14.5 1.9 %collective-permute-start.5 = (f32[32,128]{1,0:T(8,128)S(1)}, f32[32,128]{1,0:T(8,128)S(1)}, u32[]{:S(2)}, u32[]{:S(2)}) collective-permute-start(f32[32,128]{1,0:T(8,128)S(1)} %get-tuple-element.29), channel_id=1, source_target_pairs={{0,28},{4,24},{8,20},{12,16},{16,12},{20,8},{24,4},{28,0},{1,29},{... | collective-permute-start | bytes 49160 | tf_op jit(solution)/shard_map/ppermute | solution.py:353
  16.4 0.6 %collective-permute-start.9 = (f32[96,128]{1,0:T(8,128)S(1)}, f32[96,128]{1,0:T(8,128)S(1)}, u32[]{:S(2)}, u32[]{:S(2)}) collective-permute-start(f32[96,128]{1,0:T(8,128)S(1)} %get-tuple-element.32), channel_id=1, source_target_pairs={{0,8},{4,12},{8,0},{12,4},{16,24},{20,28},{24,16},{28,20},{1,9},{5... | collective-permute-start | bytes 147464 | tf_op jit(solution)/shard_map/ppermute | solution.py:353
  17.0 1.5 %collective-permute-done.5 = f32[32,128]{1,0:T(8,128)S(1)} collective-permute-done((f32[32,128]{1,0:T(8,128)S(1)}, f32[32,128]{1,0:T(8,128)S(1)}, u32[]{:S(2)}, u32[]{:S(2)}) %collective-permute-start.5) | collective-permute-done | bytes 16416 | tf_op jit(solution)/shard_map/ppermute | solution.py:353
  18.6 0.0 collective-permute-done.6.refs_1_
  18.6 0.0 collective-permute-done.7.refs_2_
  18.6 0.2 collective-permute-start.8
  18.8 0.0 collective-permute-done.9.refs_0_
  18.8 0.3 local_2.1.refs_3_
  19.1 0.7 %collective-permute-done.8.refs_1_ = f32[32,128]{1,0:T(8,128)S(1)} collective-permute-done((f32[32,128]{1,0:T(8,128)S(1)}, f32[32,128]{1,0:T(8,128)S(1)}, u32[]{:S(2)}, u32[]{:S(2)}) %collective-permute-start.8) | collective-permute-done | bytes 16416 | tf_op jit(solution)/shard_map/ppermute | solution.py:353
  19.9 1.0 %nonlocal_2.1 = (f32[128,384]{1,0:T(8,128)S(1)}, f32[96,128]{1,0:T(8,128)S(1)}, f32[128,128]{1,0:T(8,128)S(1)}, f32[128,128]{1,0:T(8,128)S(1)}, f32[32,128]{1,0:T(8,128)S(1)}) custom-call(s32[1]{0:T(128)} %bitcast.flag_ref, f32[32,128]{1,0:T(8,128)S(1)} %slice_add_fusion.2.refs_0_, f32[32,128]{1,0:T(8,128)S(1)} %collective-permute-done.8.refs_1_, ...), custom_call_target="tpu_custom_call" | custom-call | tf_op jit(solution)/shard_map/nonlocal_2/pallas_call | solution.py:477
  20.8 1.3 %collective-permute-start.11 = (f32[128,128]{1,0:T(8,128)S(1)}, f32[128,128]{1,0:T(8,128)S(1)}, u32[]{:S(2)}, u32[]{:S(2)}) collective-permute-start(f32[128,128]{1,0:T(8,128)S(1)} %get-tuple-element.35), channel_id=1, source_target_pairs={{0,24},{4,28},{8,16},{12,20},{16,8},{20,12},{24,0},{28,4},{1,25},{... | collective-permute-start | bytes 196616 | tf_op jit(solution)/shard_map/ppermute | solution.py:353
  22.1 1.6 %collective-permute-start.12 = (f32[128,128]{1,0:T(8,128)S(1)}, f32[128,128]{1,0:T(8,128)S(1)}, u32[]{:S(2)}, u32[]{:S(2)}) collective-permute-start(f32[128,128]{1,0:T(8,128)S(1)} %get-tuple-element.36), channel_id=1, source_target_pairs={{0,4},{4,0},{8,12},{12,8},{16,20},{20,16},{24,28},{28,24},{1,5},{5... | collective-permute-start | bytes 196616 | tf_op jit(solution)/shard_map/ppermute | solution.py:353
  23.7 0.1 collective-permute-start.10
  23.7 0.4 collective-permute-start.14
  24.2 3.5 %collective-permute-done.10 = f32[32,128]{1,0:T(8,128)S(1)} collective-permute-done((f32[32,128]{1,0:T(8,128)S(1)}, f32[32,128]{1,0:T(8,128)S(1)}, u32[]{:S(2)}, u32[]{:S(2)}) %collective-permute-start.10) | collective-permute-done | bytes 16416 | tf_op jit(solution)/shard_map/ppermute | solution.py:353
  27.7 0.0 collective-permute-done.11.refs_2_
  27.7 0.0 collective-permute-done.12.refs_3_
  27.8 0.2 collective-permute-start.13
  27.9 0.0 collective-permute-done.14.refs_1_
  27.9 0.4 local_3.1.refs_3_
  28.4 0.6 %collective-permute-done.13.refs_1_ = f32[32,128]{1,0:T(8,128)S(1)} collective-permute-done((f32[32,128]{1,0:T(8,128)S(1)}, f32[32,128]{1,0:T(8,128)S(1)}, u32[]{:S(2)}, u32[]{:S(2)}) %collective-permute-start.13) | collective-permute-done | bytes 16416 | tf_op jit(solution)/shard_map/ppermute | solution.py:353
  29.0 0.5 %filtered.1 = f32[128,384]{1,0:T(8,128)S(1)} custom-call(f32[8,128]{1,0:T(8,128)S(1)} %get-tuple-element.28.refs_0_.cheb_ref, f32[32,128]{1,0:T(8,128)S(1)} %slice_add_fusion.refs_0_, f32[32,128]{1,0:T(8,128)S(1)} %collective-permute-done.13.refs_1_, f32[32,128]{1,0:T(8,128)S(1)} %bitcast.22, f32[128,384]{1,0:T(8,128)S(1)} %local_3.1.refs_3_, ...), custom_call_target="tpu_custom_call" | custom-call | tf_op jit(solution)/shard_map/filtered/pallas_call | solution.py:467
  29.5 1.7 %collective-permute-start.15 = (f32[128,384]{1,0:T(8,128)S(1)}, f32[128,384]{1,0:T(8,128)S(1)}, u32[]{:S(2)}, u32[]{:S(2)}) collective-permute-start(f32[128,384]{1,0:T(8,128)S(1)} %filtered.1), channel_id=1, source_target_pairs={{0,1},{1,0},{2,3},{3,2},{4,5},{5,4},{6,7},{7,6},{8,9},{9,8},{10,11... | collective-permute-start | bytes 589832 | tf_op jit(solution)/shard_map/ppermute | solution.py:360
  31.2 5.4 %collective-permute-done.15 = f32[128,384]{1,0:T(8,128)S(1)} collective-permute-done((f32[128,384]{1,0:T(8,128)S(1)}, f32[128,384]{1,0:T(8,128)S(1)}, u32[]{:S(2)}, u32[]{:S(2)}) %collective-permute-start.15) | collective-permute-done | bytes 196640 | tf_op jit(solution)/shard_map/ppermute | solution.py:360
  36.6 0.5 %collective-permute-start.16 = (f32[128,384]{1,0:T(8,128)S(1)}, f32[128,384]{1,0:T(8,128)S(1)}, u32[]{:S(2)}, u32[]{:S(2)}) collective-permute-start(f32[128,384]{1,0:T(8,128)S(1)} %add.42), channel_id=1, source_target_pairs={{0,3},{1,2},{2,1},{3,0},{4,7},{5,6},{6,5},{7,4},{8,11},{9,10},{10,... | collective-permute-start | bytes 589832 | tf_op jit(solution)/shard_map/ppermute | solution.py:361
  37.1 9.9 %collective-permute-done.16 = f32[128,384]{1,0:T(8,128)S(1)} collective-permute-done((f32[128,384]{1,0:T(8,128)S(1)}, f32[128,384]{1,0:T(8,128)S(1)}, u32[]{:S(2)}, u32[]{:S(2)}) %collective-permute-start.16) | collective-permute-done | bytes 196640 | tf_op jit(solution)/shard_map/ppermute | solution.py:361
  47.0 0.7 %add_multiply_fusion = f32[128,384]{1,0:T(8,128)} fusion(f32[128,384]{1,0:T(8,128)S(1)} %add.42, f32[128,384]{1,0:T(8,128)S(1)} %collective-permute-done.16), kind=kLoop, calls=%fused_computation | loop fusion | flops 98304 | bytes 589824 | tf_op jit(solution)/shard_map/mul | solution.py:361
  (12 shorter events, 0.1 us)
Async XLA Ops:
  0.0 10.5 %copy-start.2 = (f32[1,8,16,384]{3,2,1,0:T(8,128)S(1)}, f32[1,8,16,384]{3,2,1,0:T(8,128)}, u32[]{:S(2)}) copy-start(f32[1,8,16,384]{3,2,1,0:T(8,128)} %param.6) | copy-start | bytes 589828
  0.0 10.5 %copy-start.3 = (f32[8,16,384]{2,1,0:T(8,128)S(1)}, f32[8,16,384]{2,1,0:T(8,128)}, u32[]{:S(2)}) copy-start(f32[8,16,384]{2,1,0:T(8,128)} %param.7) | copy-start | bytes 589828
  2.5 6.8 %collective-permute-start.1 = (f32[128,128]{1,0:T(8,128)}, f32[128,128]{1,0:T(8,128)S(1)}, u32[]{:S(2)}, u32[]{:S(2)}) collective-permute-start(f32[128,128]{1,0:T(8,128)} %get-tuple-element.23), channel_id=1, source_target_pairs={{0,24},{4,28},{8,16},{12,20},{16,8},{20,12},{24,0},{28,4},{1,25},{... | collective-permute-start | bytes 196616 | tf_op jit(solution)/shard_map/ppermute | solution.py:353
  3.5 5.8 %collective-permute-start.2 = (f32[128,128]{1,0:T(8,128)}, f32[128,128]{1,0:T(8,128)S(1)}, u32[]{:S(2)}, u32[]{:S(2)}) collective-permute-start(f32[128,128]{1,0:T(8,128)} %get-tuple-element.24), channel_id=1, source_target_pairs={{0,4},{4,0},{8,12},{12,8},{16,20},{20,16},{24,28},{28,24},{1,5},{5... | collective-permute-start | bytes 196616 | tf_op jit(solution)/shard_map/ppermute | solution.py:353
  5.0 4.3 %collective-permute-start = (f32[32,128]{1,0:T(8,128)}, f32[32,128]{1,0:T(8,128)S(1)}, u32[]{:S(2)}, u32[]{:S(2)}) collective-permute-start(f32[32,128]{1,0:T(8,128)} %get-tuple-element.22), channel_id=1, source_target_pairs={{0,28},{4,24},{8,20},{12,16},{16,12},{20,8},{24,4},{28,0},{1,29},{... | collective-permute-start | bytes 49160 | tf_op jit(solution)/shard_map/ppermute | solution.py:353
  5.5 5.0 %collective-permute-start.4 = (f32[96,128]{1,0:T(8,128)}, f32[96,128]{1,0:T(8,128)S(1)}, u32[]{:S(2)}, u32[]{:S(2)}) collective-permute-start(f32[96,128]{1,0:T(8,128)} %get-tuple-element.25), channel_id=1, source_target_pairs={{0,8},{4,12},{8,0},{12,4},{16,24},{20,28},{24,16},{28,20},{1,9},{5... | collective-permute-start | bytes 147464 | tf_op jit(solution)/shard_map/ppermute | solution.py:353
  9.3 2.0 %copy-start.1 = (bf16[128,1536]{1,0:T(8,128)(2,1)S(1)}, bf16[128,1536]{1,0:T(8,128)(2,1)}, u32[]{:S(2)}) copy-start(bf16[128,1536]{1,0:T(8,128)(2,1)} %get-tuple-element.27.refs_7_.refs_6_) | copy-start | bytes 1179652
  10.1 1.3 %copy-start = (bf16[4,8,16,384]{3,2,1,0:T(8,128)(2,1)S(1)}, bf16[4,8,16,384]{3,2,1,0:T(8,128)(2,1)}, u32[]{:S(2)}) copy-start(bf16[4,8,16,384]{3,2,1,0:T(8,128)(2,1)} %param.8) | copy-start | bytes 1179652
  10.1 1.3 %collective-permute-start.3 = (f32[32,128]{1,0:T(8,128)S(1)}, f32[32,128]{1,0:T(8,128)S(1)}, u32[]{:S(2)}, u32[]{:S(2)}) collective-permute-start(f32[32,128]{1,0:T(8,128)S(1)} %slice_add_fusion.4.refs_1_), channel_id=1, source_target_pairs={{0,8},{4,12},{8,0},{12,4},{16,24},{20,28},{24,16},{28,20},{1,9},{5... | collective-permute-start | bytes 49160 | tf_op jit(solution)/shard_map/ppermute | solution.py:353
  10.5 0.8 %copy-start.4 = (f32[4096]{0:T(1024)S(1)}, f32[4096]{0:T(1024)}, u32[]{:S(2)}) copy-start(f32[4096]{0:T(1024)} %param.10) | copy-start | bytes 49156
  10.5 0.8 %copy-start.5 = (f32[12,128]{1,0:T(8,128)S(1)}, f32[12,128]{1,0:T(8,128)}, u32[]{:S(2)}) copy-start(f32[12,128]{1,0:T(8,128)} %get-tuple-element.26.refs_6_.refs_5_) | copy-start | bytes 18436
  11.3 0.7 %copy-start.6 = (f32[4]{0:T(128)S(1)}, f32[4]{0:T(128)}, u32[]{:S(2)}) copy-start(f32[4]{0:T(128)} %refs_0_.1) | copy-start | bytes 52
  13.5 5.1 %collective-permute-start.6 = (f32[128,128]{1,0:T(8,128)S(1)}, f32[128,128]{1,0:T(8,128)S(1)}, u32[]{:S(2)}, u32[]{:S(2)}) collective-permute-start(f32[128,128]{1,0:T(8,128)S(1)} %get-tuple-element.30), channel_id=1, source_target_pairs={{0,24},{4,28},{8,16},{12,20},{16,8},{20,12},{24,0},{28,4},{1,25},{... | collective-permute-start | bytes 196616 | tf_op jit(solution)/shard_map/ppermute | solution.py:353
  14.0 4.6 %collective-permute-start.7 = (f32[128,128]{1,0:T(8,128)S(1)}, f32[128,128]{1,0:T(8,128)S(1)}, u32[]{:S(2)}, u32[]{:S(2)}) collective-permute-start(f32[128,128]{1,0:T(8,128)S(1)} %get-tuple-element.31), channel_id=1, source_target_pairs={{0,4},{4,0},{8,12},{12,8},{16,20},{20,16},{24,28},{28,24},{1,5},{5... | collective-permute-start | bytes 196616 | tf_op jit(solution)/shard_map/ppermute | solution.py:353
  14.5 4.1 %collective-permute-start.5 = (f32[32,128]{1,0:T(8,128)S(1)}, f32[32,128]{1,0:T(8,128)S(1)}, u32[]{:S(2)}, u32[]{:S(2)}) collective-permute-start(f32[32,128]{1,0:T(8,128)S(1)} %get-tuple-element.29), channel_id=1, source_target_pairs={{0,28},{4,24},{8,20},{12,16},{16,12},{20,8},{24,4},{28,0},{1,29},{... | collective-permute-start | bytes 49160 | tf_op jit(solution)/shard_map/ppermute | solution.py:353
  16.4 2.4 %collective-permute-start.9 = (f32[96,128]{1,0:T(8,128)S(1)}, f32[96,128]{1,0:T(8,128)S(1)}, u32[]{:S(2)}, u32[]{:S(2)}) collective-permute-start(f32[96,128]{1,0:T(8,128)S(1)} %get-tuple-element.32), channel_id=1, source_target_pairs={{0,8},{4,12},{8,0},{12,4},{16,24},{20,28},{24,16},{28,20},{1,9},{5... | collective-permute-start | bytes 147464 | tf_op jit(solution)/shard_map/ppermute | solution.py:353
  18.6 1.2 %collective-permute-start.8 = (f32[32,128]{1,0:T(8,128)S(1)}, f32[32,128]{1,0:T(8,128)S(1)}, u32[]{:S(2)}, u32[]{:S(2)}) collective-permute-start(f32[32,128]{1,0:T(8,128)S(1)} %slice_add_fusion.2.refs_0_), channel_id=1, source_target_pairs={{0,8},{4,12},{8,0},{12,4},{16,24},{20,28},{24,16},{28,20},{1,9},{5... | collective-permute-start | bytes 49160 | tf_op jit(solution)/shard_map/ppermute | solution.py:353
  20.8 6.9 %collective-permute-start.11 = (f32[128,128]{1,0:T(8,128)S(1)}, f32[128,128]{1,0:T(8,128)S(1)}, u32[]{:S(2)}, u32[]{:S(2)}) collective-permute-start(f32[128,128]{1,0:T(8,128)S(1)} %get-tuple-element.35), channel_id=1, source_target_pairs={{0,24},{4,28},{8,16},{12,20},{16,8},{20,12},{24,0},{28,4},{1,25},{... | collective-permute-start | bytes 196616 | tf_op jit(solution)/shard_map/ppermute | solution.py:353
  22.1 5.7 %collective-permute-start.12 = (f32[128,128]{1,0:T(8,128)S(1)}, f32[128,128]{1,0:T(8,128)S(1)}, u32[]{:S(2)}, u32[]{:S(2)}) collective-permute-start(f32[128,128]{1,0:T(8,128)S(1)} %get-tuple-element.36), channel_id=1, source_target_pairs={{0,4},{4,0},{8,12},{12,8},{16,20},{20,16},{24,28},{28,24},{1,5},{5... | collective-permute-start | bytes 196616 | tf_op jit(solution)/shard_map/ppermute | solution.py:353
  23.7 4.1 %collective-permute-start.10 = (f32[32,128]{1,0:T(8,128)S(1)}, f32[32,128]{1,0:T(8,128)S(1)}, u32[]{:S(2)}, u32[]{:S(2)}) collective-permute-start(f32[32,128]{1,0:T(8,128)S(1)} %get-tuple-element.34), channel_id=1, source_target_pairs={{0,28},{4,24},{8,20},{12,16},{16,12},{20,8},{24,4},{28,0},{1,29},{... | collective-permute-start | bytes 49160 | tf_op jit(solution)/shard_map/ppermute | solution.py:353
  23.7 4.2 %collective-permute-start.14 = (f32[96,128]{1,0:T(8,128)S(1)}, f32[96,128]{1,0:T(8,128)S(1)}, u32[]{:S(2)}, u32[]{:S(2)}) collective-permute-start(f32[96,128]{1,0:T(8,128)S(1)} %get-tuple-element.37), channel_id=1, source_target_pairs={{0,8},{4,12},{8,0},{12,4},{16,24},{20,28},{24,16},{28,20},{1,9},{5... | collective-permute-start | bytes 147464 | tf_op jit(solution)/shard_map/ppermute | solution.py:353
  27.8 1.2 %collective-permute-start.13 = (f32[32,128]{1,0:T(8,128)S(1)}, f32[32,128]{1,0:T(8,128)S(1)}, u32[]{:S(2)}, u32[]{:S(2)}) collective-permute-start(f32[32,128]{1,0:T(8,128)S(1)} %slice_add_fusion.refs_0_), channel_id=1, source_target_pairs={{0,8},{4,12},{8,0},{12,4},{16,24},{20,28},{24,16},{28,20},{1,9},{5... | collective-permute-start | bytes 49160 | tf_op jit(solution)/shard_map/ppermute | solution.py:353
  29.5 7.0 %collective-permute-start.15 = (f32[128,384]{1,0:T(8,128)S(1)}, f32[128,384]{1,0:T(8,128)S(1)}, u32[]{:S(2)}, u32[]{:S(2)}) collective-permute-start(f32[128,384]{1,0:T(8,128)S(1)} %filtered.1), channel_id=1, source_target_pairs={{0,1},{1,0},{2,3},{3,2},{4,5},{5,4},{6,7},{7,6},{8,9},{9,8},{10,11... | collective-permute-start | bytes 589832 | tf_op jit(solution)/shard_map/ppermute | solution.py:360
  36.6 10.4 %collective-permute-start.16 = (f32[128,384]{1,0:T(8,128)S(1)}, f32[128,384]{1,0:T(8,128)S(1)}, u32[]{:S(2)}, u32[]{:S(2)}) collective-permute-start(f32[128,384]{1,0:T(8,128)S(1)} %add.42), channel_id=1, source_target_pairs={{0,3},{1,2},{2,1},{3,0},{4,7},{5,6},{6,5},{7,4},{8,11},{9,10},{10,... | collective-permute-start | bytes 589832 | tf_op jit(solution)/shard_map/ppermute | solution.py:361

commit v4 on v3

--- a/solution.py
+++ b/solution.py
@@ -209,23 +209,28 @@
     vals_hbm,
     pv_hbm,
     ids_hbm,
+    cheb_hbm,
     ab_ref,
     bb_ref,
     yb_ref,
     table_ref,
     rows_ref,
     hot_ref,
+    cheb_out,
     vals_ref,
     pv_ref,
     ids_ref,
+    cheb_ref,
     sems,
 ):
     get_ids = pltpu.make_async_copy(ids_hbm, ids_ref, sems.at[0])
     get_pv = pltpu.make_async_copy(pv_hbm, pv_ref, sems.at[1])
     get_vals = pltpu.make_async_copy(vals_hbm, vals_ref, sems.at[2])
+    get_cheb = pltpu.make_async_copy(cheb_hbm, cheb_ref, sems.at[3])
     get_ids.start()
     get_vals.start()
     get_pv.start()
+    get_cheb.start()
     get_ids.wait()
     row_of, lane_of = rows_of_ids(sz, ids_ref[...])
     rows_ref[...] = row_of
@@ -239,6 +244,9 @@
     emit(
         sz, vals_ref[...], flag_ref, pv_ref, row_of, hot_ref, ab_ref, bb_ref, yb_ref, table_ref
     )
+    get_cheb.wait()
+    for n in range(STEPS + 1):
+        cheb_out[n : n + 1, :] = jnp.full((1, LANES), cheb_ref[n], F32)
 
 
 def coefficient(sz, cheb_ref, n):
@@ -284,10 +292,6 @@
 
 def nonlocal_kernel(sz, degree, n_tables, flag_ref, *refs):
     refs = list(refs)
-    if degree == 1:
-        cheb_ref, cheb_out = refs.pop(0), refs.pop()
-        for n in range(STEPS + 1):
-            cheb_out[n : n + 1, :] = jnp.full((1, LANES), cheb_ref[n], F32)
     table_refs = [refs.pop(0) for _ in range(n_tables)]
     energy_ref, rest_ref, pv_ref, rows_ref, hot_ref = (refs.pop(0) for _ in range(5))
     row_of = rows_ref[...]
@@ -317,6 +321,10 @@
 
 def smem(count):
     return [pl.BlockSpec(memory_space=pltpu.SMEM)] * count
+
+
+def in_place(arr):
+    return pltpu.with_memory_space_constraint(arr, pltpu.HBM)
 
 
 def shift_table(table, blocks_first, blocks_second, size_first, size_second, dim, delta):
@@ -429,24 +437,26 @@
         return [table], from_a, from_b, [below, above]
 
     def one_orbital(start):
-        *messages, row_of, hot = pl.pallas_call(
+        *messages, row_of, hot, cheb = pl.pallas_call(
             functools.partial(first_kernel, sz),
             out_shape=message_shapes
             + (
                 jax.ShapeDtypeStruct((slots * sz.zb, LANES), F32),
                 jax.ShapeDtypeStruct((LANES, slots * sz.zb * sz.cells), BF16),
+                jax.ShapeDtypeStruct((SUBLANES, LANES), F32),
             ),
-            in_specs=smem(1) + [pl.BlockSpec(memory_space=pltpu.HBM)] * 3,
-            out_specs=tuple(vmem(6)),
+            in_specs=smem(1) + [pl.BlockSpec(memory_space=pltpu.HBM)] * 4,
+            out_specs=tuple(vmem(7)),
             scratch_shapes=[
                 pltpu.VMEM(start.shape, start.dtype),
                 pltpu.VMEM(pv.shape, pv.dtype),
                 pltpu.VMEM(ids.shape, ids.dtype),
-                pltpu.SemaphoreType.DMA((3,)),
+                pltpu.SMEM(cheb_coef.shape, cheb_coef.dtype),
+                pltpu.SemaphoreType.DMA((4,)),
             ],
-            compiler_params=pltpu.CompilerParams(vmem_limit_bytes=62 << 20),
+            compiler_params=params,
             name="project_first",
-        )(flag, start, pv, ids)
+        )(flag, *(in_place(arr) for arr in (start, pv, ids, cheb_coef)))
         history = [start]
         for degree in range(1, STEPS + 1):
             tables, from_a, from_b, from_y = exchange(*messages)
@@ -472,20 +482,16 @@
                     compiler_params=params,
                     name="filtered",
                 )(cheb, *args)
-            scalars = (flag, cheb_coef) if degree == 1 else (flag,)
-            extra = (jax.ShapeDtypeStruct((SUBLANES, LANES), F32),) if degree == 1 else ()
             out = pl.pallas_call(
                 functools.partial(nonlocal_kernel, sz, degree, len(tables)),
-                out_shape=(field,) + message_shapes + extra,
-                in_specs=smem(len(scalars)) + vmem(len(args)),
-                out_specs=tuple(vmem(5 + len(extra))),
+                out_shape=(field,) + message_shapes,
+                in_specs=smem(1) + vmem(len(args)),
+                out_specs=tuple(vmem(5)),
                 compiler_params=params,
                 name=f"nonlocal_{degree}",
-            )(*scalars, *args)
-            if degree == 1:
-                cheb = out[-1]
+            )(flag, *args)
             history.append(out[0])
-            messages = out[1:5]
+            messages = out[1:]
 
     density = one_orbital(orbitals[0].reshape(sz.cells, nz))
     for at in range(1, count_orb):

time: 47.9 us -> 45.1 us (0.942)
  Pallas kernels: 6.5 us -> 5.33 us
  other arithmetic: 1.51 us -> 0.74 us
  local copies, waits for them, and re-layouts: 0.66 us -> 0.02 us
    add x3, other arithmetic: 0.79 us -> 0.02 us  [exchange(): table = table + from_d + from_b[sz.edge_rows:] + from_y[sz.yedge_rows:]]
    pallas_call x1, Pallas kernels: 2.45 us -> 1.8 us  [one_orbital(): pl.pallas_call(functools.partial(first_kernel, sz), out_shape=message_sha...]
    unnamed x14 -> x8, local copies, waits for them, and re-layouts: 0.66 us -> 0.02 us
    pallas_call x2, Pallas kernels: 2.43 us -> 1.88 us  [one_orbital(): pl.pallas_call(functools.partial(nonlocal_kernel, sz, degree, len(tables)...]
  transfers between devices with their start and end apart: 17 -> 17, of which waited for: 8 -> 8; matrix products, arithmetic and copies ran while one was open for 2% -> 0% of each run, Pallas kernels for 2% -> 3%
where the time goes in v4:
time: 45.1 us; the launch traced here: 44.9 us
  waiting for transfers between devices  25.6 us (57%)
  starting transfers between devices  13.2 us (29%)
  Pallas kernels  5.33 us (12%)
  other arithmetic  0.74 us (2%)
    ppermute x15, starting transfers between devices, swap(): return lax.ppermute(arr, ('gx', 'gy'), pairs)  11 us
    ppermute x15, waiting for transfers between devices, swap(): return lax.ppermute(arr, ('gx', 'gy'), pairs)  10.3 us
    ppermute x1, waiting for transfers between devices, orb_sum(): lax.ppermute(vals, 'orb', [(i, 3 - i) for i in range(4)])  9.89 us
    ppermute x1, waiting for transfers between devices, orb_sum(): vals = vals + lax.ppermute(vals, 'orb', [(i, i ^ 1) for i in range(4)])  5.44 us
    pallas_call x2, Pallas kernels, one_orbital(): pl.pallas_call(functools.partial(nonlocal_kernel, sz, degree, len(tables)...  1.88 us
    pallas_call x1, Pallas kernels, one_orbital(): pl.pallas_call(functools.partial(first_kernel, sz), out_shape=message_sha...  1.8 us
    ppermute x1, starting transfers between devices, orb_sum(): vals = vals + lax.ppermute(vals, 'orb', [(i, i ^ 1) for i in range(4)])  1.6 us
    pallas_call x3, Pallas kernels, one_orbital(): pl.pallas_call(functools.partial(local_kernel, sz, degree, len(from_y)),...  1.12 us
  transfers between devices with their start and end apart: 17, of which 8 were waited for; matrix products, arithmetic and copies ran while one was open for 0% of the time, Pallas kernels for 3%

profile of v4, /device:TPU:16, one launch (start us, length us, event | category | flops | bytes accessed | tf_op | source)
XLA Modules:
  0.0 44.9 jit_solution(8460398218993216358)
XLA Ops:
  0.0 1.8 %project_first.1 = (f32[96,128]{1,0:T(8,128)S(1)}, f32[128,128]{1,0:T(8,128)S(1)}, f32[128,128]{1,0:T(8,128)S(1)}, f32[32,128]{1,0:T(8,128)S(1)}, f32[12,128]{1,...) custom-call(s32[1]{0:T(128)} %bitcast.flag_ref, f32[128,384]{1,0:T(8,128)} %bitcast.13, ...), custom_call_target="tpu_custom_call" | custom-call | tf_op jit(solution)/shard_map/project_first/pallas_call | solution.py:440
  1.8 1.0 %collective-permute-start.1 = (f32[128,128]{1,0:T(8,128)S(1)}, f32[128,128]{1,0:T(8,128)S(1)}, u32[]{:S(2)}, u32[]{:S(2)}) collective-permute-start(f32[128,128]{1,0:T(8,128)S(1)} %get-tuple-element.24), channel_id=1, source_target_pairs={{0,24},{4,28},{8,16},{12,20},{16,8},{20,12},{24,0},{28,4},{1,25},{... | collective-permute-start | bytes 196616 | tf_op jit(solution)/shard_map/ppermute | solution.py:361
  2.8 1.5 %collective-permute-start.2 = (f32[128,128]{1,0:T(8,128)S(1)}, f32[128,128]{1,0:T(8,128)S(1)}, u32[]{:S(2)}, u32[]{:S(2)}) collective-permute-start(f32[128,128]{1,0:T(8,128)S(1)} %get-tuple-element.25), channel_id=1, source_target_pairs={{0,4},{4,0},{8,12},{12,8},{16,20},{20,16},{24,28},{28,24},{1,5},{5... | collective-permute-start | bytes 196616 | tf_op jit(solution)/shard_map/ppermute | solution.py:361
  4.3 0.5 %collective-permute-start = (f32[32,128]{1,0:T(8,128)S(1)}, f32[32,128]{1,0:T(8,128)S(1)}, u32[]{:S(2)}, u32[]{:S(2)}) collective-permute-start(f32[32,128]{1,0:T(8,128)S(1)} %get-tuple-element.23), channel_id=1, source_target_pairs={{0,28},{4,24},{8,20},{12,16},{16,12},{20,8},{24,4},{28,0},{1,29},{... | collective-permute-start | bytes 49160 | tf_op jit(solution)/shard_map/ppermute | solution.py:361
  4.8 0.2 collective-permute-start.4
  5.0 3.4 %collective-permute-done = f32[32,128]{1,0:T(8,128)S(1)} collective-permute-done((f32[32,128]{1,0:T(8,128)S(1)}, f32[32,128]{1,0:T(8,128)S(1)}, u32[]{:S(2)}, u32[]{:S(2)}) %collective-permute-start) | collective-permute-done | bytes 16416 | tf_op jit(solution)/shard_map/ppermute | solution.py:361
  8.4 0.0 collective-permute-done.1.refs_1_
  8.4 0.0 collective-permute-done.2.refs_2_
  8.4 0.0 copy-start
  8.4 0.5 %collective-permute-start.3 = (f32[32,128]{1,0:T(8,128)S(1)}, f32[32,128]{1,0:T(8,128)S(1)}, u32[]{:S(2)}, u32[]{:S(2)}) collective-permute-start(f32[32,128]{1,0:T(8,128)S(1)} %slice_add_fusion.4.refs_0_), channel_id=1, source_target_pairs={{0,8},{4,12},{8,0},{12,4},{16,24},{20,28},{24,16},{28,20},{1,9},{5... | collective-permute-start | bytes 49160 | tf_op jit(solution)/shard_map/ppermute | solution.py:361
  8.9 0.0 collective-permute-done.4.refs_0_
  8.9 0.0 copy-done.1
  8.9 0.0 copy-done.2
  8.9 0.0 copy-start.3
  8.9 0.3 local_1.1.refs_3_
  9.3 0.5 %collective-permute-done.3.refs_1_ = f32[32,128]{1,0:T(8,128)S(1)} collective-permute-done((f32[32,128]{1,0:T(8,128)S(1)}, f32[32,128]{1,0:T(8,128)S(1)}, u32[]{:S(2)}, u32[]{:S(2)}) %collective-permute-start.3) | collective-permute-done | bytes 16416 | tf_op jit(solution)/shard_map/ppermute | solution.py:361
  9.8 0.0 copy-done
  9.8 0.0 copy-done.3
  9.8 0.9 %nonlocal_1.1 = (f32[128,384]{1,0:T(8,128)S(1)}, f32[96,128]{1,0:T(8,128)S(1)}, f32[128,128]{1,0:T(8,128)S(1)}, f32[128,128]{1,0:T(8,128)S(1)}, f32[32,128]{1,0:T(8,128)S(1)}) custom-call(s32[1]{0:T(128)} %bitcast.flag_ref, f32[32,128]{1,0:T(8,128)S(1)} %slice_add_fusion.4.refs_0_, f32[32,128]{1,0:T(8,128)S(1)} %collective-permute-done.3.refs_1_, ...), custom_call_target="tpu_custom_call" | custom-call | tf_op jit(solution)/shard_map/nonlocal_1/pallas_call | solution.py:485
  10.7 0.5 %collective-permute-start.6 = (f32[128,128]{1,0:T(8,128)S(1)}, f32[128,128]{1,0:T(8,128)S(1)}, u32[]{:S(2)}, u32[]{:S(2)}) collective-permute-start(f32[128,128]{1,0:T(8,128)S(1)} %get-tuple-element.30), channel_id=1, source_target_pairs={{0,24},{4,28},{8,16},{12,20},{16,8},{20,12},{24,0},{28,4},{1,25},{... | collective-permute-start | bytes 196616 | tf_op jit(solution)/shard_map/ppermute | solution.py:361
  11.2 0.5 %collective-permute-start.7 = (f32[128,128]{1,0:T(8,128)S(1)}, f32[128,128]{1,0:T(8,128)S(1)}, u32[]{:S(2)}, u32[]{:S(2)}) collective-permute-start(f32[128,128]{1,0:T(8,128)S(1)} %get-tuple-element.31), channel_id=1, source_target_pairs={{0,4},{4,0},{8,12},{12,8},{16,20},{20,16},{24,28},{28,24},{1,5},{5... | collective-permute-start | bytes 196616 | tf_op jit(solution)/shard_map/ppermute | solution.py:361
  11.7 1.9 %collective-permute-start.5 = (f32[32,128]{1,0:T(8,128)S(1)}, f32[32,128]{1,0:T(8,128)S(1)}, u32[]{:S(2)}, u32[]{:S(2)}) collective-permute-start(f32[32,128]{1,0:T(8,128)S(1)} %get-tuple-element.29), channel_id=1, source_target_pairs={{0,28},{4,24},{8,20},{12,16},{16,12},{20,8},{24,4},{28,0},{1,29},{... | collective-permute-start | bytes 49160 | tf_op jit(solution)/shard_map/ppermute | solution.py:361
  13.6 0.6 %collective-permute-start.9 = (f32[96,128]{1,0:T(8,128)S(1)}, f32[96,128]{1,0:T(8,128)S(1)}, u32[]{:S(2)}, u32[]{:S(2)}) collective-permute-start(f32[96,128]{1,0:T(8,128)S(1)} %get-tuple-element.32), channel_id=1, source_target_pairs={{0,8},{4,12},{8,0},{12,4},{16,24},{20,28},{24,16},{28,20},{1,9},{5... | collective-permute-start | bytes 147464 | tf_op jit(solution)/shard_map/ppermute | solution.py:361
  14.3 1.5 %collective-permute-done.5 = f32[32,128]{1,0:T(8,128)S(1)} collective-permute-done((f32[32,128]{1,0:T(8,128)S(1)}, f32[32,128]{1,0:T(8,128)S(1)}, u32[]{:S(2)}, u32[]{:S(2)}) %collective-permute-start.5) | collective-permute-done | bytes 16416 | tf_op jit(solution)/shard_map/ppermute | solution.py:361
  15.8 0.0 collective-permute-done.6.refs_1_
  15.8 0.0 collective-permute-done.7.refs_2_
  15.8 0.2 collective-permute-start.8
  16.0 0.0 collective-permute-done.9.refs_0_
  16.0 0.4 local_2.1.refs_3_
  16.3 0.7 %collective-permute-done.8.refs_1_ = f32[32,128]{1,0:T(8,128)S(1)} collective-permute-done((f32[32,128]{1,0:T(8,128)S(1)}, f32[32,128]{1,0:T(8,128)S(1)}, u32[]{:S(2)}, u32[]{:S(2)}) %collective-permute-start.8) | collective-permute-done | bytes 16416 | tf_op jit(solution)/shard_map/ppermute | solution.py:361
  17.0 0.9 %nonlocal_2.1 = (f32[128,384]{1,0:T(8,128)S(1)}, f32[96,128]{1,0:T(8,128)S(1)}, f32[128,128]{1,0:T(8,128)S(1)}, f32[128,128]{1,0:T(8,128)S(1)}, f32[32,128]{1,0:T(8,128)S(1)}) custom-call(s32[1]{0:T(128)} %bitcast.flag_ref, f32[32,128]{1,0:T(8,128)S(1)} %slice_add_fusion.2.refs_0_, f32[32,128]{1,0:T(8,128)S(1)} %collective-permute-done.8.refs_1_, ...), custom_call_target="tpu_custom_call" | custom-call | tf_op jit(solution)/shard_map/nonlocal_2/pallas_call | solution.py:485
  18.0 1.3 %collective-permute-start.11 = (f32[128,128]{1,0:T(8,128)S(1)}, f32[128,128]{1,0:T(8,128)S(1)}, u32[]{:S(2)}, u32[]{:S(2)}) collective-permute-start(f32[128,128]{1,0:T(8,128)S(1)} %get-tuple-element.35), channel_id=1, source_target_pairs={{0,24},{4,28},{8,16},{12,20},{16,8},{20,12},{24,0},{28,4},{1,25},{... | collective-permute-start | bytes 196616 | tf_op jit(solution)/shard_map/ppermute | solution.py:361
  19.2 1.6 %collective-permute-start.12 = (f32[128,128]{1,0:T(8,128)S(1)}, f32[128,128]{1,0:T(8,128)S(1)}, u32[]{:S(2)}, u32[]{:S(2)}) collective-permute-start(f32[128,128]{1,0:T(8,128)S(1)} %get-tuple-element.36), channel_id=1, source_target_pairs={{0,4},{4,0},{8,12},{12,8},{16,20},{20,16},{24,28},{28,24},{1,5},{5... | collective-permute-start | bytes 196616 | tf_op jit(solution)/shard_map/ppermute | solution.py:361
  20.9 0.0 collective-permute-start.10
  20.9 0.4 collective-permute-start.14
  21.4 3.6 %collective-permute-done.10 = f32[32,128]{1,0:T(8,128)S(1)} collective-permute-done((f32[32,128]{1,0:T(8,128)S(1)}, f32[32,128]{1,0:T(8,128)S(1)}, u32[]{:S(2)}, u32[]{:S(2)}) %collective-permute-start.10) | collective-permute-done | bytes 16416 | tf_op jit(solution)/shard_map/ppermute | solution.py:361
  24.9 0.0 collective-permute-done.11.refs_2_
  25.0 0.0 collective-permute-done.12.refs_3_
  25.0 0.2 collective-permute-start.13
  25.1 0.0 collective-permute-done.14.refs_1_
  25.2 0.4 local_3.1.refs_3_
  25.6 0.6 %collective-permute-done.13.refs_1_ = f32[32,128]{1,0:T(8,128)S(1)} collective-permute-done((f32[32,128]{1,0:T(8,128)S(1)}, f32[32,128]{1,0:T(8,128)S(1)}, u32[]{:S(2)}, u32[]{:S(2)}) %collective-permute-start.13) | collective-permute-done | bytes 16416 | tf_op jit(solution)/shard_map/ppermute | solution.py:361
  26.2 0.5 %filtered.1 = f32[128,384]{1,0:T(8,128)S(1)} custom-call(f32[8,128]{1,0:T(8,128)S(1)} %get-tuple-element.22.refs_0_.cheb_ref, f32[32,128]{1,0:T(8,128)S(1)} %slice_add_fusion.refs_0_, f32[32,128]{1,0:T(8,128)S(1)} %collective-permute-done.13.refs_1_, f32[32,128]{1,0:T(8,128)S(1)} %bitcast.22, f32[128,384]{1,0:T(8,128)S(1)} %local_3.1.refs_3_, ...), custom_call_target="tpu_custom_call" | custom-call | tf_op jit(solution)/shard_map/filtered/pallas_call | solution.py:477
  26.7 1.6 %collective-permute-start.15 = (f32[128,384]{1,0:T(8,128)S(1)}, f32[128,384]{1,0:T(8,128)S(1)}, u32[]{:S(2)}, u32[]{:S(2)}) collective-permute-start(f32[128,384]{1,0:T(8,128)S(1)} %filtered.1), channel_id=1, source_target_pairs={{0,1},{1,0},{2,3},{3,2},{4,5},{5,4},{6,7},{7,6},{8,9},{9,8},{10,11... | collective-permute-start | bytes 589832 | tf_op jit(solution)/shard_map/ppermute | solution.py:368
  28.3 5.4 %collective-permute-done.15 = f32[128,384]{1,0:T(8,128)S(1)} collective-permute-done((f32[128,384]{1,0:T(8,128)S(1)}, f32[128,384]{1,0:T(8,128)S(1)}, u32[]{:S(2)}, u32[]{:S(2)}) %collective-permute-start.15) | collective-permute-done | bytes 196640 | tf_op jit(solution)/shard_map/ppermute | solution.py:368
  33.8 0.5 %collective-permute-start.16 = (f32[128,384]{1,0:T(8,128)S(1)}, f32[128,384]{1,0:T(8,128)S(1)}, u32[]{:S(2)}, u32[]{:S(2)}) collective-permute-start(f32[128,384]{1,0:T(8,128)S(1)} %add.42), channel_id=1, source_target_pairs={{0,3},{1,2},{2,1},{3,0},{4,7},{5,6},{6,5},{7,4},{8,11},{9,10},{10,... | collective-permute-start | bytes 589832 | tf_op jit(solution)/shard_map/ppermute | solution.py:369
  34.3 9.9 %collective-permute-done.16 = f32[128,384]{1,0:T(8,128)S(1)} collective-permute-done((f32[128,384]{1,0:T(8,128)S(1)}, f32[128,384]{1,0:T(8,128)S(1)}, u32[]{:S(2)}, u32[]{:S(2)}) %collective-permute-start.16) | collective-permute-done | bytes 196640 | tf_op jit(solution)/shard_map/ppermute | solution.py:369
  44.2 0.7 %add_multiply_fusion = f32[128,384]{1,0:T(8,128)} fusion(f32[128,384]{1,0:T(8,128)S(1)} %add.42, f32[128,384]{1,0:T(8,128)S(1)} %collective-permute-done.16), kind=kLoop, calls=%fused_computation | loop fusion | flops 98304 | bytes 589824 | tf_op jit(solution)/shard_map/mul | solution.py:369
  (6 shorter events, 0.0 us)
Async XLA Ops:
  0.0 8.9 %copy-start.1 = (f32[1,8,16,384]{3,2,1,0:T(8,128)S(1)}, f32[1,8,16,384]{3,2,1,0:T(8,128)}, u32[]{:S(2)}) copy-start(f32[1,8,16,384]{3,2,1,0:T(8,128)} %param.6) | copy-start | bytes 589828
  0.0 8.9 %copy-start.2 = (f32[8,16,384]{2,1,0:T(8,128)S(1)}, f32[8,16,384]{2,1,0:T(8,128)}, u32[]{:S(2)}) copy-start(f32[8,16,384]{2,1,0:T(8,128)} %param.7) | copy-start | bytes 589828
  1.8 6.6 %collective-permute-start.1 = (f32[128,128]{1,0:T(8,128)S(1)}, f32[128,128]{1,0:T(8,128)S(1)}, u32[]{:S(2)}, u32[]{:S(2)}) collective-permute-start(f32[128,128]{1,0:T(8,128)S(1)} %get-tuple-element.24), channel_id=1, source_target_pairs={{0,24},{4,28},{8,16},{12,20},{16,8},{20,12},{24,0},{28,4},{1,25},{... | collective-permute-start | bytes 196616 | tf_op jit(solution)/shard_map/ppermute | solution.py:361
  2.8 5.6 %collective-permute-start.2 = (f32[128,128]{1,0:T(8,128)S(1)}, f32[128,128]{1,0:T(8,128)S(1)}, u32[]{:S(2)}, u32[]{:S(2)}) collective-permute-start(f32[128,128]{1,0:T(8,128)S(1)} %get-tuple-element.25), channel_id=1, source_target_pairs={{0,4},{4,0},{8,12},{12,8},{16,20},{20,16},{24,28},{28,24},{1,5},{5... | collective-permute-start | bytes 196616 | tf_op jit(solution)/shard_map/ppermute | solution.py:361
  4.3 4.1 %collective-permute-start = (f32[32,128]{1,0:T(8,128)S(1)}, f32[32,128]{1,0:T(8,128)S(1)}, u32[]{:S(2)}, u32[]{:S(2)}) collective-permute-start(f32[32,128]{1,0:T(8,128)S(1)} %get-tuple-element.23), channel_id=1, source_target_pairs={{0,28},{4,24},{8,20},{12,16},{16,12},{20,8},{24,4},{28,0},{1,29},{... | collective-permute-start | bytes 49160 | tf_op jit(solution)/shard_map/ppermute | solution.py:361
  4.8 4.1 %collective-permute-start.4 = (f32[96,128]{1,0:T(8,128)S(1)}, f32[96,128]{1,0:T(8,128)S(1)}, u32[]{:S(2)}, u32[]{:S(2)}) collective-permute-start(f32[96,128]{1,0:T(8,128)S(1)} %get-tuple-element.26), channel_id=1, source_target_pairs={{0,8},{4,12},{8,0},{12,4},{16,24},{20,28},{24,16},{28,20},{1,9},{5... | collective-permute-start | bytes 147464 | tf_op jit(solution)/shard_map/ppermute | solution.py:361
  8.4 1.3 %copy-start = (bf16[4,8,16,384]{3,2,1,0:T(8,128)(2,1)S(1)}, bf16[4,8,16,384]{3,2,1,0:T(8,128)(2,1)}, u32[]{:S(2)}) copy-start(bf16[4,8,16,384]{3,2,1,0:T(8,128)(2,1)} %param.8) | copy-start | bytes 1179652
  8.4 1.3 %collective-permute-start.3 = (f32[32,128]{1,0:T(8,128)S(1)}, f32[32,128]{1,0:T(8,128)S(1)}, u32[]{:S(2)}, u32[]{:S(2)}) collective-permute-start(f32[32,128]{1,0:T(8,128)S(1)} %slice_add_fusion.4.refs_0_), channel_id=1, source_target_pairs={{0,8},{4,12},{8,0},{12,4},{16,24},{20,28},{24,16},{28,20},{1,9},{5... | collective-permute-start | bytes 49160 | tf_op jit(solution)/shard_map/ppermute | solution.py:361
  8.9 0.8 %copy-start.3 = (f32[4096]{0:T(1024)S(1)}, f32[4096]{0:T(1024)}, u32[]{:S(2)}) copy-start(f32[4096]{0:T(1024)} %param.10) | copy-start | bytes 49156
  10.7 5.1 %collective-permute-start.6 = (f32[128,128]{1,0:T(8,128)S(1)}, f32[128,128]{1,0:T(8,128)S(1)}, u32[]{:S(2)}, u32[]{:S(2)}) collective-permute-start(f32[128,128]{1,0:T(8,128)S(1)} %get-tuple-element.30), channel_id=1, source_target_pairs={{0,24},{4,28},{8,16},{12,20},{16,8},{20,12},{24,0},{28,4},{1,25},{... | collective-permute-start | bytes 196616 | tf_op jit(solution)/shard_map/ppermute | solution.py:361
  11.2 4.6 %collective-permute-start.7 = (f32[128,128]{1,0:T(8,128)S(1)}, f32[128,128]{1,0:T(8,128)S(1)}, u32[]{:S(2)}, u32[]{:S(2)}) collective-permute-start(f32[128,128]{1,0:T(8,128)S(1)} %get-tuple-element.31), channel_id=1, source_target_pairs={{0,4},{4,0},{8,12},{12,8},{16,20},{20,16},{24,28},{28,24},{1,5},{5... | collective-permute-start | bytes 196616 | tf_op jit(solution)/shard_map/ppermute | solution.py:361
  11.7 4.1 %collective-permute-start.5 = (f32[32,128]{1,0:T(8,128)S(1)}, f32[32,128]{1,0:T(8,128)S(1)}, u32[]{:S(2)}, u32[]{:S(2)}) collective-permute-start(f32[32,128]{1,0:T(8,128)S(1)} %get-tuple-element.29), channel_id=1, source_target_pairs={{0,28},{4,24},{8,20},{12,16},{16,12},{20,8},{24,4},{28,0},{1,29},{... | collective-permute-start | bytes 49160 | tf_op jit(solution)/shard_map/ppermute | solution.py:361
  13.6 2.3 %collective-permute-start.9 = (f32[96,128]{1,0:T(8,128)S(1)}, f32[96,128]{1,0:T(8,128)S(1)}, u32[]{:S(2)}, u32[]{:S(2)}) collective-permute-start(f32[96,128]{1,0:T(8,128)S(1)} %get-tuple-element.32), channel_id=1, source_target_pairs={{0,8},{4,12},{8,0},{12,4},{16,24},{20,28},{24,16},{28,20},{1,9},{5... | collective-permute-start | bytes 147464 | tf_op jit(solution)/shard_map/ppermute | solution.py:361
  15.8 1.2 %collective-permute-start.8 = (f32[32,128]{1,0:T(8,128)S(1)}, f32[32,128]{1,0:T(8,128)S(1)}, u32[]{:S(2)}, u32[]{:S(2)}) collective-permute-start(f32[32,128]{1,0:T(8,128)S(1)} %slice_add_fusion.2.refs_0_), channel_id=1, source_target_pairs={{0,8},{4,12},{8,0},{12,4},{16,24},{20,28},{24,16},{28,20},{1,9},{5... | collective-permute-start | bytes 49160 | tf_op jit(solution)/shard_map/ppermute | solution.py:361
  18.0 7.0 %collective-permute-start.11 = (f32[128,128]{1,0:T(8,128)S(1)}, f32[128,128]{1,0:T(8,128)S(1)}, u32[]{:S(2)}, u32[]{:S(2)}) collective-permute-start(f32[128,128]{1,0:T(8,128)S(1)} %get-tuple-element.35), channel_id=1, source_target_pairs={{0,24},{4,28},{8,16},{12,20},{16,8},{20,12},{24,0},{28,4},{1,25},{... | collective-permute-start | bytes 196616 | tf_op jit(solution)/shard_map/ppermute | solution.py:361
  19.2 5.7 %collective-permute-start.12 = (f32[128,128]{1,0:T(8,128)S(1)}, f32[128,128]{1,0:T(8,128)S(1)}, u32[]{:S(2)}, u32[]{:S(2)}) collective-permute-start(f32[128,128]{1,0:T(8,128)S(1)} %get-tuple-element.36), channel_id=1, source_target_pairs={{0,4},{4,0},{8,12},{12,8},{16,20},{20,16},{24,28},{28,24},{1,5},{5... | collective-permute-start | bytes 196616 | tf_op jit(solution)/shard_map/ppermute | solution.py:361
  20.9 4.1 %collective-permute-start.10 = (f32[32,128]{1,0:T(8,128)S(1)}, f32[32,128]{1,0:T(8,128)S(1)}, u32[]{:S(2)}, u32[]{:S(2)}) collective-permute-start(f32[32,128]{1,0:T(8,128)S(1)} %get-tuple-element.34), channel_id=1, source_target_pairs={{0,28},{4,24},{8,20},{12,16},{16,12},{20,8},{24,4},{28,0},{1,29},{... | collective-permute-start | bytes 49160 | tf_op jit(solution)/shard_map/ppermute | solution.py:361
  20.9 4.2 %collective-permute-start.14 = (f32[96,128]{1,0:T(8,128)S(1)}, f32[96,128]{1,0:T(8,128)S(1)}, u32[]{:S(2)}, u32[]{:S(2)}) collective-permute-start(f32[96,128]{1,0:T(8,128)S(1)} %get-tuple-element.37), channel_id=1, source_target_pairs={{0,8},{4,12},{8,0},{12,4},{16,24},{20,28},{24,16},{28,20},{1,9},{5... | collective-permute-start | bytes 147464 | tf_op jit(solution)/shard_map/ppermute | solution.py:361
  25.0 1.2 %collective-permute-start.13 = (f32[32,128]{1,0:T(8,128)S(1)}, f32[32,128]{1,0:T(8,128)S(1)}, u32[]{:S(2)}, u32[]{:S(2)}) collective-permute-start(f32[32,128]{1,0:T(8,128)S(1)} %slice_add_fusion.refs_0_), channel_id=1, source_target_pairs={{0,8},{4,12},{8,0},{12,4},{16,24},{20,28},{24,16},{28,20},{1,9},{5... | collective-permute-start | bytes 49160 | tf_op jit(solution)/shard_map/ppermute | solution.py:361
  26.7 7.0 %collective-permute-start.15 = (f32[128,384]{1,0:T(8,128)S(1)}, f32[128,384]{1,0:T(8,128)S(1)}, u32[]{:S(2)}, u32[]{:S(2)}) collective-permute-start(f32[128,384]{1,0:T(8,128)S(1)} %filtered.1), channel_id=1, source_target_pairs={{0,1},{1,0},{2,3},{3,2},{4,5},{5,4},{6,7},{7,6},{8,9},{9,8},{10,11... | collective-permute-start | bytes 589832 | tf_op jit(solution)/shard_map/ppermute | solution.py:368
  33.8 10.4 %collective-permute-start.16 = (f32[128,384]{1,0:T(8,128)S(1)}, f32[128,384]{1,0:T(8,128)S(1)}, u32[]{:S(2)}, u32[]{:S(2)}) collective-permute-start(f32[128,384]{1,0:T(8,128)S(1)} %add.42), channel_id=1, source_target_pairs={{0,3},{1,2},{2,1},{3,0},{4,7},{5,6},{6,5},{7,4},{8,11},{9,10},{10,... | collective-permute-start | bytes 589832 | tf_op jit(solution)/shard_map/ppermute | solution.py:369

commit v5 on v4

--- a/solution.py
+++ b/solution.py
@@ -103,30 +103,36 @@
     return both[: sz.rows] + both[sz.rows :]
 
 
-def projected(sz, table, pv_ref, row_of, hot_ref):
-    first, second = pieces(table)
-    found = dot(jnp.concatenate([first, second], axis=0), hot_ref[...], NN)
-    found = found[: sz.rows] + found[sz.rows :]
+def projected(sz, tables, pv_ref, row_of, hot_ref):
+    count = len(tables)
+    split = [piece for table in tables for piece in pieces(table)]
+    found = dot(jnp.concatenate(split, axis=0), hot_ref[...], NN)
+    found = [
+        found[2 * n * sz.rows : (2 * n + 1) * sz.rows]
+        + found[(2 * n + 1) * sz.rows : (2 * n + 2) * sz.rows]
+        for n in range(count)
+    ]
     table_iota = iota((sz.rows, LANES), 0).astype(F32)
     eye = iota((sz.cells, LANES), 0) == iota((sz.cells, LANES), 1)
-    result = []
+    result = [[] for _ in tables]
     for zb in range(sz.zb):
-        diag_first, diag_second = [], []
+        diag = [[] for _ in range(2 * count)]
         for slot in range(sz.slots):
             at = (zb * sz.slots + slot) * LANES
             hit = chunk(sz, row_of, zb, slot) == table_iota
-            weight = jnp.sum(
-                jnp.where(hit, found[:, at : at + LANES], 0.0), axis=0, keepdims=True
-            )
-            a, b = pieces(jnp.where(eye, weight, 0.0))
-            diag_first.append(a)
-            diag_second.append(b)
-        lhs = jnp.concatenate(
-            [jnp.concatenate(diag_first, axis=1), jnp.concatenate(diag_second, axis=1)], axis=0
-        )
+            for n in range(count):
+                weight = jnp.sum(
+                    jnp.where(hit, found[n][:, at : at + LANES], 0.0), axis=0, keepdims=True
+                )
+                a, b = pieces(jnp.where(eye, weight, 0.0))
+                diag[2 * n].append(a)
+                diag[2 * n + 1].append(b)
+        lhs = jnp.concatenate([jnp.concatenate(parts, axis=1) for parts in diag], axis=0)
         both = dot(lhs, pv_ref[:, zb * LANES : (zb + 1) * LANES], NN)
-        result.append(both[: sz.cells] + both[sz.cells :])
-    return result
+        for n in range(count):
+            at = 2 * n * sz.cells
+            result[n].append(both[at : at + sz.cells] + both[at + sz.cells : at + 2 * sz.cells])
+    return [jnp.concatenate(parts, axis=1) for parts in result]
 
 
 def from_message(sz, msg_ref, rows):
@@ -297,22 +303,25 @@
     row_of = rows_ref[...]
     double = 1.0 if degree == 1 else 2.0
     table = added(table_refs) * (energy_ref[...] * (double / E_HALF))
-    result = rest_ref[...] + jnp.concatenate(
-        projected(sz, table, pv_ref, row_of, hot_ref), axis=1
-    )
+    result = rest_ref[...] + projected(sz, [table], pv_ref, row_of, hot_ref)[0]
     refs[0][...] = result
     emit(sz, result, flag_ref, pv_ref, row_of, hot_ref, *refs[1:])
 
 
-def last_kernel(sz, n_tables, cheb_ref, *refs):
+def last_kernel(sz, n_orbitals, n_tables, cheb_ref, *refs):
     refs = list(refs)
-    table_refs = [refs.pop(0) for _ in range(n_tables)]
-    energy_ref, rest_ref, pv_ref, rows_ref, hot_ref, out_ref = refs
-    table = added(table_refs) * (energy_ref[...] * (2.0 / E_HALF * cheb_ref[STEPS : STEPS + 1, :]))
-    result = rest_ref[...] + jnp.concatenate(
-        projected(sz, table, pv_ref, rows_ref[...], hot_ref), axis=1
-    )
-    out_ref[...] = result * result
+    energy_ref, pv_ref, rows_ref, hot_ref = (refs.pop(0) for _ in range(4))
+    scale = energy_ref[...] * (2.0 / E_HALF * cheb_ref[STEPS : STEPS + 1, :])
+    rests, tables = [], []
+    for _ in range(n_orbitals):
+        rests.append(refs.pop(0))
+        tables.append(added([refs.pop(0) for _ in range(n_tables)]) * scale)
+    total = None
+    for rest_ref, part in zip(rests, projected(sz, tables, pv_ref, rows_ref[...], hot_ref)):
+        filtered = rest_ref[...] + part
+        squared = filtered * filtered
+        total = squared if total is None else total + squared
+    refs[0][...] = total
 
 
 def vmem(count):
@@ -361,12 +370,9 @@
     return lax.ppermute(arr, ("gx", "gy"), pairs)
 
 
-def orb_sum(vals, scale):
+def orb_swap(vals, bit):
     size = lax.axis_size("orb")
-    if size != 4:
-        return lax.psum(vals, "orb") * scale
-    vals = vals + lax.ppermute(vals, "orb", [(i, i ^ 1) for i in range(4)])
-    return (vals + lax.ppermute(vals, "orb", [(i, 3 - i) for i in range(4)])) * scale
+    return lax.ppermute(vals, "orb", [(i, i ^ bit) for i in range(size)])
 
 
 def local(orbitals, local_pot, proj_vals, proj_ids, proj_energy, cheb_coef):
@@ -374,6 +380,8 @@
     slots = proj_vals.shape[0]
     size_first = lax.axis_size("gx")
     size_second = lax.axis_size("gy")
+    size_orb = lax.axis_size("orb")
+    paired = size_orb == 4 and count_orb == 1
     owner_size = proj_energy.shape[0] // (size_first * size_second)
     whole = size_first == 4 and size_second == 2
     if whole:
@@ -472,16 +480,23 @@
                 compiler_params=params,
                 name=f"local_{degree}",
             )(flag, *args)
-            args = (*tables, energy, rest, pv, row_of, hot)
             if last:
+                orbitals_here = [(rest, *tables)]
+                if paired:
+                    total = functools.reduce(jnp.add, tables)
+                    orbitals_here = [(rest, total), (orb_swap(rest, 2), orb_swap(total, 2))]
+                args = (cheb, energy, pv, row_of, hot, *sum(orbitals_here, ()))
                 return pl.pallas_call(
-                    functools.partial(last_kernel, sz, len(tables)),
+                    functools.partial(
+                        last_kernel, sz, len(orbitals_here), len(orbitals_here[0]) - 1
+                    ),
                     out_shape=field,
-                    in_specs=vmem(1 + len(args)),
+                    in_specs=vmem(len(args)),
                     out_specs=vmem(1)[0],
                     compiler_params=params,
                     name="filtered",
-                )(cheb, *args)
+                )(*args)
+            args = (*tables, energy, rest, pv, row_of, hot)
             out = pl.pallas_call(
                 functools.partial(nonlocal_kernel, sz, degree, len(tables)),
                 out_shape=(field,) + message_shapes,
@@ -496,8 +511,12 @@
     density = one_orbital(orbitals[0].reshape(sz.cells, nz))
     for at in range(1, count_orb):
         density = density + one_orbital(orbitals[at].reshape(sz.cells, nz))
-    scale = 1.0 / (count_orb * lax.axis_size("orb"))
-    return orb_sum(density, scale).reshape(ex, ey, nz)
+    scale = 1.0 / (count_orb * size_orb)
+    if paired:
+        density = density + orb_swap(density, 1)
+    else:
+        density = lax.psum(density, "orb")
+    return (density * scale).reshape(ex, ey, nz)
 
 
 def solution(mesh):

time: 45.1 us -> 45.1 us (level); the launches traced: 44.9 us -> 44.3 us
  waiting for transfers between devices: 25.6 us -> 19.7 us
  starting transfers between devices: 13.2 us -> 18.2 us
    ppermute x2 -> x3, waiting for transfers between devices: 15.3 us -> 10 us  [orb_swap(): return lax.ppermute(vals, 'orb', [(i, i ^ bit) for i in range(size)])]
    ppermute x2 -> x3, starting transfers between devices: 2.13 us -> 6.93 us  [orb_swap(): return lax.ppermute(vals, 'orb', [(i, i ^ bit) for i in range(size)])]
    ppermute x15, waiting for transfers between devices: 10.3 us -> 9.71 us  [swap(): return lax.ppermute(arr, ('gx', 'gy'), pairs)]
  transfers between devices with their start and end apart: 17 -> 18, of which waited for: 8 -> 10; matrix products, arithmetic and copies ran while one was open for 0% -> 0% of each run, Pallas kernels for 3% -> 3%
where the time goes in v5:
time: 45.1 us; the launch traced here: 44.3 us
  waiting for transfers between devices  19.7 us (44%)
  starting transfers between devices  18.2 us (40%)
  Pallas kernels  5.53 us (12%)
  other arithmetic  0.73 us (2%)
    ppermute x15, starting transfers between devices, swap(): return lax.ppermute(arr, ('gx', 'gy'), pairs)  11.3 us
    ppermute x3, waiting for transfers between devices, orb_swap(): return lax.ppermute(vals, 'orb', [(i, i ^ bit) for i in range(size)])  10 us
    ppermute x15, waiting for transfers between devices, swap(): return lax.ppermute(arr, ('gx', 'gy'), pairs)  9.71 us
    ppermute x3, starting transfers between devices, orb_swap(): return lax.ppermute(vals, 'orb', [(i, i ^ bit) for i in range(size)])  6.93 us
    pallas_call x2, Pallas kernels, one_orbital(): pl.pallas_call(functools.partial(nonlocal_kernel, sz, degree, len(tables)...  1.87 us
    pallas_call x1, Pallas kernels, one_orbital(): pl.pallas_call(functools.partial(first_kernel, sz), out_shape=message_sha...  1.8 us
    pallas_call x3, Pallas kernels, one_orbital(): pl.pallas_call(functools.partial(local_kernel, sz, degree, len(from_y)),...  1.12 us
  transfers between devices with their start and end apart: 18, of which 10 were waited for; matrix products, arithmetic and copies ran while one was open for 0% of the time, Pallas kernels for 3%

profile of v5, /device:TPU:16, one launch (start us, length us, event | category | flops | bytes accessed | tf_op | source)
XLA Modules:
  0.0 44.3 jit_solution(17901632608902450284)
XLA Ops:
  0.0 1.8 %project_first.1 = (f32[96,128]{1,0:T(8,128)S(1)}, f32[128,128]{1,0:T(8,128)S(1)}, f32[128,128]{1,0:T(8,128)S(1)}, f32[32,128]{1,0:T(8,128)S(1)}, f32[12,128]{1,...) custom-call(s32[1]{0:T(128)} %bitcast.flag_ref, f32[128,384]{1,0:T(8,128)} %bitcast.13, ...), custom_call_target="tpu_custom_call" | custom-call | tf_op jit(solution)/shard_map/project_first/pallas_call | solution.py:448
  1.8 1.0 %collective-permute-start.1 = (f32[128,128]{1,0:T(8,128)S(1)}, f32[128,128]{1,0:T(8,128)S(1)}, u32[]{:S(2)}, u32[]{:S(2)}) collective-permute-start(f32[128,128]{1,0:T(8,128)S(1)} %get-tuple-element.26), channel_id=1, source_target_pairs={{0,24},{4,28},{8,16},{12,20},{16,8},{20,12},{24,0},{28,4},{1,25},{... | collective-permute-start | bytes 196616 | tf_op jit(solution)/shard_map/ppermute | solution.py:370
  2.8 1.5 %collective-permute-start.2 = (f32[128,128]{1,0:T(8,128)S(1)}, f32[128,128]{1,0:T(8,128)S(1)}, u32[]{:S(2)}, u32[]{:S(2)}) collective-permute-start(f32[128,128]{1,0:T(8,128)S(1)} %get-tuple-element.27), channel_id=1, source_target_pairs={{0,4},{4,0},{8,12},{12,8},{16,20},{20,16},{24,28},{28,24},{1,5},{5... | collective-permute-start | bytes 196616 | tf_op jit(solution)/shard_map/ppermute | solution.py:370
  4.3 0.5 %collective-permute-start = (f32[32,128]{1,0:T(8,128)S(1)}, f32[32,128]{1,0:T(8,128)S(1)}, u32[]{:S(2)}, u32[]{:S(2)}) collective-permute-start(f32[32,128]{1,0:T(8,128)S(1)} %get-tuple-element.25), channel_id=1, source_target_pairs={{0,28},{4,24},{8,20},{12,16},{16,12},{20,8},{24,4},{28,0},{1,29},{... | collective-permute-start | bytes 49160 | tf_op jit(solution)/shard_map/ppermute | solution.py:370
  4.8 0.2 collective-permute-start.4
  5.0 3.4 %collective-permute-done = f32[32,128]{1,0:T(8,128)S(1)} collective-permute-done((f32[32,128]{1,0:T(8,128)S(1)}, f32[32,128]{1,0:T(8,128)S(1)}, u32[]{:S(2)}, u32[]{:S(2)}) %collective-permute-start) | collective-permute-done | bytes 16416 | tf_op jit(solution)/shard_map/ppermute | solution.py:370
  8.4 0.0 collective-permute-done.1.refs_1_
  8.4 0.0 collective-permute-done.2.refs_2_
  8.4 0.0 copy-start
  8.4 0.5 %collective-permute-start.3 = (f32[32,128]{1,0:T(8,128)S(1)}, f32[32,128]{1,0:T(8,128)S(1)}, u32[]{:S(2)}, u32[]{:S(2)}) collective-permute-start(f32[32,128]{1,0:T(8,128)S(1)} %slice_add_fusion.4.refs_0_), channel_id=1, source_target_pairs={{0,8},{4,12},{8,0},{12,4},{16,24},{20,28},{24,16},{28,20},{1,9},{5... | collective-permute-start | bytes 49160 | tf_op jit(solution)/shard_map/ppermute | solution.py:370
  8.9 0.0 collective-permute-done.4.refs_0_
  8.9 0.0 copy-done.1
  8.9 0.0 copy-done.2
  8.9 0.0 copy-start.3
  8.9 0.3 local_1.1.refs_3_
  9.3 0.5 %collective-permute-done.3.refs_1_ = f32[32,128]{1,0:T(8,128)S(1)} collective-permute-done((f32[32,128]{1,0:T(8,128)S(1)}, f32[32,128]{1,0:T(8,128)S(1)}, u32[]{:S(2)}, u32[]{:S(2)}) %collective-permute-start.3) | collective-permute-done | bytes 16416 | tf_op jit(solution)/shard_map/ppermute | solution.py:370
  9.8 0.9 %nonlocal_1.1 = (f32[128,384]{1,0:T(8,128)S(1)}, f32[96,128]{1,0:T(8,128)S(1)}, f32[128,128]{1,0:T(8,128)S(1)}, f32[128,128]{1,0:T(8,128)S(1)}, f32[32,128]{1,0:T(8,128)S(1)}) custom-call(s32[1]{0:T(128)} %bitcast.flag_ref, f32[32,128]{1,0:T(8,128)S(1)} %slice_add_fusion.4.refs_0_, f32[32,128]{1,0:T(8,128)S(1)} %collective-permute-done.3.refs_1_, ...), custom_call_target="tpu_custom_call" | custom-call | tf_op jit(solution)/shard_map/nonlocal_1/pallas_call | solution.py:500
  10.7 0.5 %collective-permute-start.6 = (f32[128,128]{1,0:T(8,128)S(1)}, f32[128,128]{1,0:T(8,128)S(1)}, u32[]{:S(2)}, u32[]{:S(2)}) collective-permute-start(f32[128,128]{1,0:T(8,128)S(1)} %get-tuple-element.30), channel_id=1, source_target_pairs={{0,24},{4,28},{8,16},{12,20},{16,8},{20,12},{24,0},{28,4},{1,25},{... | collective-permute-start | bytes 196616 | tf_op jit(solution)/shard_map/ppermute | solution.py:370
  11.2 0.5 %collective-permute-start.7 = (f32[128,128]{1,0:T(8,128)S(1)}, f32[128,128]{1,0:T(8,128)S(1)}, u32[]{:S(2)}, u32[]{:S(2)}) collective-permute-start(f32[128,128]{1,0:T(8,128)S(1)} %get-tuple-element.31), channel_id=1, source_target_pairs={{0,4},{4,0},{8,12},{12,8},{16,20},{20,16},{24,28},{28,24},{1,5},{5... | collective-permute-start | bytes 196616 | tf_op jit(solution)/shard_map/ppermute | solution.py:370
  11.7 1.9 %collective-permute-start.5 = (f32[32,128]{1,0:T(8,128)S(1)}, f32[32,128]{1,0:T(8,128)S(1)}, u32[]{:S(2)}, u32[]{:S(2)}) collective-permute-start(f32[32,128]{1,0:T(8,128)S(1)} %get-tuple-element.29), channel_id=1, source_target_pairs={{0,28},{4,24},{8,20},{12,16},{16,12},{20,8},{24,4},{28,0},{1,29},{... | collective-permute-start | bytes 49160 | tf_op jit(solution)/shard_map/ppermute | solution.py:370
  13.6 0.6 %collective-permute-start.9 = (f32[96,128]{1,0:T(8,128)S(1)}, f32[96,128]{1,0:T(8,128)S(1)}, u32[]{:S(2)}, u32[]{:S(2)}) collective-permute-start(f32[96,128]{1,0:T(8,128)S(1)} %get-tuple-element.32), channel_id=1, source_target_pairs={{0,8},{4,12},{8,0},{12,4},{16,24},{20,28},{24,16},{28,20},{1,9},{5... | collective-permute-start | bytes 147464 | tf_op jit(solution)/shard_map/ppermute | solution.py:370
  14.3 1.5 %collective-permute-done.5 = f32[32,128]{1,0:T(8,128)S(1)} collective-permute-done((f32[32,128]{1,0:T(8,128)S(1)}, f32[32,128]{1,0:T(8,128)S(1)}, u32[]{:S(2)}, u32[]{:S(2)}) %collective-permute-start.5) | collective-permute-done | bytes 16416 | tf_op jit(solution)/shard_map/ppermute | solution.py:370
  15.8 0.0 collective-permute-done.6.refs_1_
  15.8 0.0 collective-permute-done.7.refs_2_
  15.8 0.2 collective-permute-start.8
  16.0 0.0 collective-permute-done.9.refs_0_
  16.0 0.4 local_2.1.refs_3_
  16.3 0.7 %collective-permute-done.8.refs_1_ = f32[32,128]{1,0:T(8,128)S(1)} collective-permute-done((f32[32,128]{1,0:T(8,128)S(1)}, f32[32,128]{1,0:T(8,128)S(1)}, u32[]{:S(2)}, u32[]{:S(2)}) %collective-permute-start.8) | collective-permute-done | bytes 16416 | tf_op jit(solution)/shard_map/ppermute | solution.py:370
  17.0 0.9 %nonlocal_2.1 = (f32[128,384]{1,0:T(8,128)S(1)}, f32[96,128]{1,0:T(8,128)S(1)}, f32[128,128]{1,0:T(8,128)S(1)}, f32[128,128]{1,0:T(8,128)S(1)}, f32[32,128]{1,0:T(8,128)S(1)}) custom-call(s32[1]{0:T(128)} %bitcast.flag_ref, f32[32,128]{1,0:T(8,128)S(1)} %slice_add_fusion.2.refs_0_, f32[32,128]{1,0:T(8,128)S(1)} %collective-permute-done.8.refs_1_, ...), custom_call_target="tpu_custom_call" | custom-call | tf_op jit(solution)/shard_map/nonlocal_2/pallas_call | solution.py:500
  18.0 1.3 %collective-permute-start.11 = (f32[128,128]{1,0:T(8,128)S(1)}, f32[128,128]{1,0:T(8,128)S(1)}, u32[]{:S(2)}, u32[]{:S(2)}) collective-permute-start(f32[128,128]{1,0:T(8,128)S(1)} %get-tuple-element.35), channel_id=1, source_target_pairs={{0,24},{4,28},{8,16},{12,20},{16,8},{20,12},{24,0},{28,4},{1,25},{... | collective-permute-start | bytes 196616 | tf_op jit(solution)/shard_map/ppermute | solution.py:370
  19.2 1.6 %collective-permute-start.12 = (f32[128,128]{1,0:T(8,128)S(1)}, f32[128,128]{1,0:T(8,128)S(1)}, u32[]{:S(2)}, u32[]{:S(2)}) collective-permute-start(f32[128,128]{1,0:T(8,128)S(1)} %get-tuple-element.36), channel_id=1, source_target_pairs={{0,4},{4,0},{8,12},{12,8},{16,20},{20,16},{24,28},{28,24},{1,5},{5... | collective-permute-start | bytes 196616 | tf_op jit(solution)/shard_map/ppermute | solution.py:370
  20.9 0.1 collective-permute-start.10
  21.0 0.4 collective-permute-start.13
  21.4 0.8 %collective-permute-done.10.refs_1_ = f32[96,128]{1,0:T(8,128)S(1)} collective-permute-done((f32[96,128]{1,0:T(8,128)S(1)}, f32[96,128]{1,0:T(8,128)S(1)}, u32[]{:S(2)}, u32[]{:S(2)}) %collective-permute-start.10) | collective-permute-done | bytes 49184 | tf_op jit(solution)/shard_map/ppermute | solution.py:370
  22.1 0.0 collective-permute-done.11.refs_2_
  22.1 1.5 %collective-permute-done.12.refs_3_ = f32[128,128]{1,0:T(8,128)S(1)} collective-permute-done((f32[128,128]{1,0:T(8,128)S(1)}, f32[128,128]{1,0:T(8,128)S(1)}, u32[]{:S(2)}, u32[]{:S(2)}) %collective-permute-start.12) | collective-permute-done | bytes 65568 | tf_op jit(solution)/shard_map/ppermute | solution.py:370
  23.6 0.4 local_3.1.refs_4_
  24.0 0.4 collective-permute-start.15
  24.4 0.6 %collective-permute-done.13 = f32[32,128]{1,0:T(8,128)S(1)} collective-permute-done((f32[32,128]{1,0:T(8,128)S(1)}, f32[32,128]{1,0:T(8,128)S(1)}, u32[]{:S(2)}, u32[]{:S(2)}) %collective-permute-start.13) | collective-permute-done | bytes 16416 | tf_op jit(solution)/shard_map/ppermute | solution.py:370
  25.0 0.4 %collective-permute-start.14 = (f32[32,128]{1,0:T(8,128)S(1)}, f32[32,128]{1,0:T(8,128)S(1)}, u32[]{:S(2)}, u32[]{:S(2)}) collective-permute-start(f32[32,128]{1,0:T(8,128)S(1)} %slice_add_fusion), channel_id=1, source_target_pairs={{0,8},{4,12},{8,0},{12,4},{16,24},{20,28},{24,16},{28,20},{1,9},{5... | collective-permute-start | bytes 49160 | tf_op jit(solution)/shard_map/ppermute | solution.py:370
  25.5 0.8 %collective-permute-done.14 = f32[32,128]{1,0:T(8,128)S(1)} collective-permute-done((f32[32,128]{1,0:T(8,128)S(1)}, f32[32,128]{1,0:T(8,128)S(1)}, u32[]{:S(2)}, u32[]{:S(2)}) %collective-permute-start.14) | collective-permute-done | bytes 16416 | tf_op jit(solution)/shard_map/ppermute | solution.py:370
  26.3 2.0 %collective-permute-start.16 = (f32[32,128]{1,0:T(8,128)S(1)}, f32[32,128]{1,0:T(8,128)S(1)}, u32[]{:S(2)}, u32[]{:S(2)}) collective-permute-start(f32[32,128]{1,0:T(8,128)S(1)} %add.42.refs_5_), channel_id=1, source_target_pairs={{0,2},{1,3},{2,0},{3,1},{4,6},{5,7},{6,4},{7,5},{8,10},{9,11},{10,... | collective-permute-start | bytes 49160 | tf_op jit(solution)/shard_map/ppermute | solution.py:375
  28.3 4.9 %collective-permute-done.16.refs_7_ = f32[32,128]{1,0:T(8,128)S(1)} collective-permute-done((f32[32,128]{1,0:T(8,128)S(1)}, f32[32,128]{1,0:T(8,128)S(1)}, u32[]{:S(2)}, u32[]{:S(2)}) %collective-permute-start.16) | collective-permute-done | bytes 16416 | tf_op jit(solution)/shard_map/ppermute | solution.py:375
  33.2 0.0 collective-permute-done.15.refs_6_
  33.2 0.7 %filtered.1 = f32[128,384]{1,0:T(8,128)S(1)} custom-call(f32[8,128]{1,0:T(8,128)S(1)} %get-tuple-element.22.refs_0_.cheb_ref, f32[32,128]{1,0:T(8,128)S(1)} %bitcast.22, bf16[512,384]{1,0:T(8,128)(2,1)S(1)} %bitcast.12, f32[12,128]{1,0:T(8,128)S(1)} %get-tuple-element.23.refs_5_.refs_2_, bf16[128,1536]{1,0:T(8,128)(2,1)S(1)} %get-tuple-element.24.refs_6_.refs_3_, ...), custom_call_target="tpu_custom_call" | custom-call | tf_op jit(solution)/shard_map/filtered/pallas_call | solution.py:489
  33.9 4.6 %collective-permute-start.17 = (f32[128,384]{1,0:T(8,128)S(1)}, f32[128,384]{1,0:T(8,128)S(1)}, u32[]{:S(2)}, u32[]{:S(2)}) collective-permute-start(f32[128,384]{1,0:T(8,128)S(1)} %filtered.1), channel_id=1, source_target_pairs={{0,1},{1,0},{2,3},{3,2},{4,5},{5,4},{6,7},{7,6},{8,9},{9,8},{10,11... | collective-permute-start | bytes 589832 | tf_op jit(solution)/shard_map/ppermute | solution.py:375
  38.5 5.1 %collective-permute-done.17 = f32[128,384]{1,0:T(8,128)S(1)} collective-permute-done((f32[128,384]{1,0:T(8,128)S(1)}, f32[128,384]{1,0:T(8,128)S(1)}, u32[]{:S(2)}, u32[]{:S(2)}) %collective-permute-start.17) | collective-permute-done | bytes 196640 | tf_op jit(solution)/shard_map/ppermute | solution.py:375
  43.6 0.7 %add_multiply_fusion = f32[128,384]{1,0:T(8,128)} fusion(f32[128,384]{1,0:T(8,128)S(1)} %filtered.1, f32[128,384]{1,0:T(8,128)S(1)} %collective-permute-done.17), kind=kLoop, calls=%fused_computation | loop fusion | flops 98304 | bytes 589824 | tf_op jit(solution)/shard_map/mul | solution.py:519
  (8 shorter events, 0.0 us)
Async XLA Ops:
  0.0 8.9 %copy-start.1 = (f32[1,8,16,384]{3,2,1,0:T(8,128)S(1)}, f32[1,8,16,384]{3,2,1,0:T(8,128)}, u32[]{:S(2)}) copy-start(f32[1,8,16,384]{3,2,1,0:T(8,128)} %param.6) | copy-start | bytes 589828
  0.0 8.9 %copy-start.2 = (f32[8,16,384]{2,1,0:T(8,128)S(1)}, f32[8,16,384]{2,1,0:T(8,128)}, u32[]{:S(2)}) copy-start(f32[8,16,384]{2,1,0:T(8,128)} %param.7) | copy-start | bytes 589828
  1.8 6.6 %collective-permute-start.1 = (f32[128,128]{1,0:T(8,128)S(1)}, f32[128,128]{1,0:T(8,128)S(1)}, u32[]{:S(2)}, u32[]{:S(2)}) collective-permute-start(f32[128,128]{1,0:T(8,128)S(1)} %get-tuple-element.26), channel_id=1, source_target_pairs={{0,24},{4,28},{8,16},{12,20},{16,8},{20,12},{24,0},{28,4},{1,25},{... | collective-permute-start | bytes 196616 | tf_op jit(solution)/shard_map/ppermute | solution.py:370
  2.8 5.6 %collective-permute-start.2 = (f32[128,128]{1,0:T(8,128)S(1)}, f32[128,128]{1,0:T(8,128)S(1)}, u32[]{:S(2)}, u32[]{:S(2)}) collective-permute-start(f32[128,128]{1,0:T(8,128)S(1)} %get-tuple-element.27), channel_id=1, source_target_pairs={{0,4},{4,0},{8,12},{12,8},{16,20},{20,16},{24,28},{28,24},{1,5},{5... | collective-permute-start | bytes 196616 | tf_op jit(solution)/shard_map/ppermute | solution.py:370
  4.3 4.1 %collective-permute-start = (f32[32,128]{1,0:T(8,128)S(1)}, f32[32,128]{1,0:T(8,128)S(1)}, u32[]{:S(2)}, u32[]{:S(2)}) collective-permute-start(f32[32,128]{1,0:T(8,128)S(1)} %get-tuple-element.25), channel_id=1, source_target_pairs={{0,28},{4,24},{8,20},{12,16},{16,12},{20,8},{24,4},{28,0},{1,29},{... | collective-permute-start | bytes 49160 | tf_op jit(solution)/shard_map/ppermute | solution.py:370
  4.8 4.1 %collective-permute-start.4 = (f32[96,128]{1,0:T(8,128)S(1)}, f32[96,128]{1,0:T(8,128)S(1)}, u32[]{:S(2)}, u32[]{:S(2)}) collective-permute-start(f32[96,128]{1,0:T(8,128)S(1)} %get-tuple-element.28), channel_id=1, source_target_pairs={{0,8},{4,12},{8,0},{12,4},{16,24},{20,28},{24,16},{28,20},{1,9},{5... | collective-permute-start | bytes 147464 | tf_op jit(solution)/shard_map/ppermute | solution.py:370
  8.4 1.3 %copy-start = (bf16[4,8,16,384]{3,2,1,0:T(8,128)(2,1)S(1)}, bf16[4,8,16,384]{3,2,1,0:T(8,128)(2,1)}, u32[]{:S(2)}) copy-start(bf16[4,8,16,384]{3,2,1,0:T(8,128)(2,1)} %param.8) | copy-start | bytes 1179652
  8.4 1.3 %collective-permute-start.3 = (f32[32,128]{1,0:T(8,128)S(1)}, f32[32,128]{1,0:T(8,128)S(1)}, u32[]{:S(2)}, u32[]{:S(2)}) collective-permute-start(f32[32,128]{1,0:T(8,128)S(1)} %slice_add_fusion.4.refs_0_), channel_id=1, source_target_pairs={{0,8},{4,12},{8,0},{12,4},{16,24},{20,28},{24,16},{28,20},{1,9},{5... | collective-permute-start | bytes 49160 | tf_op jit(solution)/shard_map/ppermute | solution.py:370
  8.9 0.8 %copy-start.3 = (f32[4096]{0:T(1024)S(1)}, f32[4096]{0:T(1024)}, u32[]{:S(2)}) copy-start(f32[4096]{0:T(1024)} %param.10) | copy-start | bytes 49156
  10.7 5.1 %collective-permute-start.6 = (f32[128,128]{1,0:T(8,128)S(1)}, f32[128,128]{1,0:T(8,128)S(1)}, u32[]{:S(2)}, u32[]{:S(2)}) collective-permute-start(f32[128,128]{1,0:T(8,128)S(1)} %get-tuple-element.30), channel_id=1, source_target_pairs={{0,24},{4,28},{8,16},{12,20},{16,8},{20,12},{24,0},{28,4},{1,25},{... | collective-permute-start | bytes 196616 | tf_op jit(solution)/shard_map/ppermute | solution.py:370
  11.2 4.6 %collective-permute-start.7 = (f32[128,128]{1,0:T(8,128)S(1)}, f32[128,128]{1,0:T(8,128)S(1)}, u32[]{:S(2)}, u32[]{:S(2)}) collective-permute-start(f32[128,128]{1,0:T(8,128)S(1)} %get-tuple-element.31), channel_id=1, source_target_pairs={{0,4},{4,0},{8,12},{12,8},{16,20},{20,16},{24,28},{28,24},{1,5},{5... | collective-permute-start | bytes 196616 | tf_op jit(solution)/shard_map/ppermute | solution.py:370
  11.7 4.1 %collective-permute-start.5 = (f32[32,128]{1,0:T(8,128)S(1)}, f32[32,128]{1,0:T(8,128)S(1)}, u32[]{:S(2)}, u32[]{:S(2)}) collective-permute-start(f32[32,128]{1,0:T(8,128)S(1)} %get-tuple-element.29), channel_id=1, source_target_pairs={{0,28},{4,24},{8,20},{12,16},{16,12},{20,8},{24,4},{28,0},{1,29},{... | collective-permute-start | bytes 49160 | tf_op jit(solution)/shard_map/ppermute | solution.py:370
  13.6 2.3 %collective-permute-start.9 = (f32[96,128]{1,0:T(8,128)S(1)}, f32[96,128]{1,0:T(8,128)S(1)}, u32[]{:S(2)}, u32[]{:S(2)}) collective-permute-start(f32[96,128]{1,0:T(8,128)S(1)} %get-tuple-element.32), channel_id=1, source_target_pairs={{0,8},{4,12},{8,0},{12,4},{16,24},{20,28},{24,16},{28,20},{1,9},{5... | collective-permute-start | bytes 147464 | tf_op jit(solution)/shard_map/ppermute | solution.py:370
  15.8 1.2 %collective-permute-start.8 = (f32[32,128]{1,0:T(8,128)S(1)}, f32[32,128]{1,0:T(8,128)S(1)}, u32[]{:S(2)}, u32[]{:S(2)}) collective-permute-start(f32[32,128]{1,0:T(8,128)S(1)} %slice_add_fusion.2.refs_0_), channel_id=1, source_target_pairs={{0,8},{4,12},{8,0},{12,4},{16,24},{20,28},{24,16},{28,20},{1,9},{5... | collective-permute-start | bytes 49160 | tf_op jit(solution)/shard_map/ppermute | solution.py:370
  18.0 4.1 %collective-permute-start.11 = (f32[128,128]{1,0:T(8,128)S(1)}, f32[128,128]{1,0:T(8,128)S(1)}, u32[]{:S(2)}, u32[]{:S(2)}) collective-permute-start(f32[128,128]{1,0:T(8,128)S(1)} %get-tuple-element.35), channel_id=1, source_target_pairs={{0,24},{4,28},{8,16},{12,20},{16,8},{20,12},{24,0},{28,4},{1,25},{... | collective-permute-start | bytes 196616 | tf_op jit(solution)/shard_map/ppermute | solution.py:370
  19.2 4.3 %collective-permute-start.12 = (f32[128,128]{1,0:T(8,128)S(1)}, f32[128,128]{1,0:T(8,128)S(1)}, u32[]{:S(2)}, u32[]{:S(2)}) collective-permute-start(f32[128,128]{1,0:T(8,128)S(1)} %get-tuple-element.36), channel_id=1, source_target_pairs={{0,4},{4,0},{8,12},{12,8},{16,20},{20,16},{24,28},{28,24},{1,5},{5... | collective-permute-start | bytes 196616 | tf_op jit(solution)/shard_map/ppermute | solution.py:370
  20.9 1.2 %collective-permute-start.10 = (f32[96,128]{1,0:T(8,128)S(1)}, f32[96,128]{1,0:T(8,128)S(1)}, u32[]{:S(2)}, u32[]{:S(2)}) collective-permute-start(f32[96,128]{1,0:T(8,128)S(1)} %get-tuple-element.34), channel_id=1, source_target_pairs={{0,8},{4,12},{8,0},{12,4},{16,24},{20,28},{24,16},{28,20},{1,9},{5... | collective-permute-start | bytes 147464 | tf_op jit(solution)/shard_map/ppermute | solution.py:370
  21.0 4.1 %collective-permute-start.13 = (f32[32,128]{1,0:T(8,128)S(1)}, f32[32,128]{1,0:T(8,128)S(1)}, u32[]{:S(2)}, u32[]{:S(2)}) collective-permute-start(f32[32,128]{1,0:T(8,128)S(1)} %get-tuple-element.38), channel_id=1, source_target_pairs={{0,28},{4,24},{8,20},{12,16},{16,12},{20,8},{24,4},{28,0},{1,29},{... | collective-permute-start | bytes 49160 | tf_op jit(solution)/shard_map/ppermute | solution.py:370
  24.0 9.2 %collective-permute-start.15 = (f32[128,384]{1,0:T(8,128)S(1)}, f32[128,384]{1,0:T(8,128)S(1)}, u32[]{:S(2)}, u32[]{:S(2)}) collective-permute-start(f32[128,384]{1,0:T(8,128)S(1)} %local_3.1.refs_4_), channel_id=1, source_target_pairs={{0,2},{1,3},{2,0},{3,1},{4,6},{5,7},{6,4},{7,5},{8,10},{9,11},{10,... | collective-permute-start | bytes 589832 | tf_op jit(solution)/shard_map/ppermute | solution.py:375
  25.0 1.3 %collective-permute-start.14 = (f32[32,128]{1,0:T(8,128)S(1)}, f32[32,128]{1,0:T(8,128)S(1)}, u32[]{:S(2)}, u32[]{:S(2)}) collective-permute-start(f32[32,128]{1,0:T(8,128)S(1)} %slice_add_fusion), channel_id=1, source_target_pairs={{0,8},{4,12},{8,0},{12,4},{16,24},{20,28},{24,16},{28,20},{1,9},{5... | collective-permute-start | bytes 49160 | tf_op jit(solution)/shard_map/ppermute | solution.py:370
  26.3 6.9 %collective-permute-start.16 = (f32[32,128]{1,0:T(8,128)S(1)}, f32[32,128]{1,0:T(8,128)S(1)}, u32[]{:S(2)}, u32[]{:S(2)}) collective-permute-start(f32[32,128]{1,0:T(8,128)S(1)} %add.42.refs_5_), channel_id=1, source_target_pairs={{0,2},{1,3},{2,0},{3,1},{4,6},{5,7},{6,4},{7,5},{8,10},{9,11},{10,... | collective-permute-start | bytes 49160 | tf_op jit(solution)/shard_map/ppermute | solution.py:375
  33.9 9.7 %collective-permute-start.17 = (f32[128,384]{1,0:T(8,128)S(1)}, f32[128,384]{1,0:T(8,128)S(1)}, u32[]{:S(2)}, u32[]{:S(2)}) collective-permute-start(f32[128,384]{1,0:T(8,128)S(1)} %filtered.1), channel_id=1, source_target_pairs={{0,1},{1,0},{2,3},{3,2},{4,5},{5,4},{6,7},{7,6},{8,9},{9,8},{10,11... | collective-permute-start | bytes 589832 | tf_op jit(solution)/shard_map/ppermute | solution.py:375

commit v6 on v5

--- a/solution.py
+++ b/solution.py
@@ -484,7 +484,7 @@
                 orbitals_here = [(rest, *tables)]
                 if paired:
                     total = functools.reduce(jnp.add, tables)
-                    orbitals_here = [(rest, total), (orb_swap(rest, 2), orb_swap(total, 2))]
+                    orbitals_here = [(rest, total), (orb_swap(rest, 1), orb_swap(total, 1))]
                 args = (cheb, energy, pv, row_of, hot, *sum(orbitals_here, ()))
                 return pl.pallas_call(
                     functools.partial(
@@ -513,7 +513,7 @@
         density = density + one_orbital(orbitals[at].reshape(sz.cells, nz))
     scale = 1.0 / (count_orb * size_orb)
     if paired:
-        density = density + orb_swap(density, 1)
+        density = density + orb_swap(density, 3)
     else:
         density = lax.psum(density, "orb")
     return (density * scale).reshape(ex, ey, nz)

time: 45.1 us -> 43 us (0.953); the launches traced: 44.3 us -> 42.7 us
  starting transfers between devices: 18.2 us -> 14 us
  waiting for transfers between devices: 19.7 us -> 22.4 us
    ppermute x3, starting transfers between devices: 6.93 us -> 3.1 us  [orb_swap(): return lax.ppermute(vals, 'orb', [(i, i ^ bit) for i in range(size)])]
    ppermute x3, waiting for transfers between devices: 10 us -> 12.9 us  [orb_swap(): return lax.ppermute(vals, 'orb', [(i, i ^ bit) for i in range(size)])]
  transfers between devices with their start and end apart: 18 -> 18, of which waited for: 10 -> 9; matrix products, arithmetic and copies ran while one was open for 0% -> 0% of each run, Pallas kernels for 3% -> 3%
where the time goes in v6:
time: 43 us; the launch traced here: 42.7 us
  waiting for transfers between devices  22.4 us (52%)
  starting transfers between devices  14 us (33%)
  Pallas kernels  5.52 us (13%)
  other arithmetic  0.73 us (2%)
    ppermute x3, waiting for transfers between devices, orb_swap(): return lax.ppermute(vals, 'orb', [(i, i ^ bit) for i in range(size)])  12.9 us
    ppermute x15, starting transfers between devices, swap(): return lax.ppermute(arr, ('gx', 'gy'), pairs)  10.9 us
    ppermute x15, waiting for transfers between devices, swap(): return lax.ppermute(arr, ('gx', 'gy'), pairs)  9.44 us
    ppermute x3, starting transfers between devices, orb_swap(): return lax.ppermute(vals, 'orb', [(i, i ^ bit) for i in range(size)])  3.1 us
    pallas_call x2, Pallas kernels, one_orbital(): pl.pallas_call(functools.partial(nonlocal_kernel, sz, degree, len(tables)...  1.87 us
    pallas_call x1, Pallas kernels, one_orbital(): pl.pallas_call(functools.partial(first_kernel, sz), out_shape=message_sha...  1.8 us
    pallas_call x3, Pallas kernels, one_orbital(): pl.pallas_call(functools.partial(local_kernel, sz, degree, len(from_y)),...  1.12 us
  transfers between devices with their start and end apart: 18, of which 9 were waited for; matrix products, arithmetic and copies ran while one was open for 0% of the time, Pallas kernels for 3%

profile of v6, /device:TPU:16, one launch (start us, length us, event | category | flops | bytes accessed | tf_op | source)
XLA Modules:
  0.0 42.7 jit_solution(5084432057217274026)
XLA Ops:
  0.0 1.8 %project_first.1 = (f32[96,128]{1,0:T(8,128)S(1)}, f32[128,128]{1,0:T(8,128)S(1)}, f32[128,128]{1,0:T(8,128)S(1)}, f32[32,128]{1,0:T(8,128)S(1)}, f32[12,128]{1,...) custom-call(s32[1]{0:T(128)} %bitcast.flag_ref, f32[128,384]{1,0:T(8,128)} %bitcast.13, ...), custom_call_target="tpu_custom_call" | custom-call | tf_op jit(solution)/shard_map/project_first/pallas_call | solution.py:448
  1.8 1.0 %collective-permute-start.1 = (f32[128,128]{1,0:T(8,128)S(1)}, f32[128,128]{1,0:T(8,128)S(1)}, u32[]{:S(2)}, u32[]{:S(2)}) collective-permute-start(f32[128,128]{1,0:T(8,128)S(1)} %get-tuple-element.26), channel_id=1, source_target_pairs={{0,24},{4,28},{8,16},{12,20},{16,8},{20,12},{24,0},{28,4},{1,25},{... | collective-permute-start | bytes 196616 | tf_op jit(solution)/shard_map/ppermute | solution.py:370
  2.8 1.5 %collective-permute-start.2 = (f32[128,128]{1,0:T(8,128)S(1)}, f32[128,128]{1,0:T(8,128)S(1)}, u32[]{:S(2)}, u32[]{:S(2)}) collective-permute-start(f32[128,128]{1,0:T(8,128)S(1)} %get-tuple-element.27), channel_id=1, source_target_pairs={{0,4},{4,0},{8,12},{12,8},{16,20},{20,16},{24,28},{28,24},{1,5},{5... | collective-permute-start | bytes 196616 | tf_op jit(solution)/shard_map/ppermute | solution.py:370
  4.3 0.5 %collective-permute-start = (f32[32,128]{1,0:T(8,128)S(1)}, f32[32,128]{1,0:T(8,128)S(1)}, u32[]{:S(2)}, u32[]{:S(2)}) collective-permute-start(f32[32,128]{1,0:T(8,128)S(1)} %get-tuple-element.25), channel_id=1, source_target_pairs={{0,28},{4,24},{8,20},{12,16},{16,12},{20,8},{24,4},{28,0},{1,29},{... | collective-permute-start | bytes 49160 | tf_op jit(solution)/shard_map/ppermute | solution.py:370
  4.8 0.2 collective-permute-start.4
  5.0 3.4 %collective-permute-done = f32[32,128]{1,0:T(8,128)S(1)} collective-permute-done((f32[32,128]{1,0:T(8,128)S(1)}, f32[32,128]{1,0:T(8,128)S(1)}, u32[]{:S(2)}, u32[]{:S(2)}) %collective-permute-start) | collective-permute-done | bytes 16416 | tf_op jit(solution)/shard_map/ppermute | solution.py:370
  8.4 0.0 collective-permute-done.1.refs_1_
  8.4 0.0 collective-permute-done.2.refs_2_
  8.4 0.0 copy-start
  8.4 0.5 %collective-permute-start.3 = (f32[32,128]{1,0:T(8,128)S(1)}, f32[32,128]{1,0:T(8,128)S(1)}, u32[]{:S(2)}, u32[]{:S(2)}) collective-permute-start(f32[32,128]{1,0:T(8,128)S(1)} %slice_add_fusion.4.refs_0_), channel_id=1, source_target_pairs={{0,8},{4,12},{8,0},{12,4},{16,24},{20,28},{24,16},{28,20},{1,9},{5... | collective-permute-start | bytes 49160 | tf_op jit(solution)/shard_map/ppermute | solution.py:370
  8.9 0.0 collective-permute-done.4.refs_0_
  8.9 0.0 copy-done.1
  8.9 0.0 copy-done.2
  8.9 0.0 copy-start.3
  8.9 0.3 local_1.1.refs_3_
  9.3 0.5 %collective-permute-done.3.refs_1_ = f32[32,128]{1,0:T(8,128)S(1)} collective-permute-done((f32[32,128]{1,0:T(8,128)S(1)}, f32[32,128]{1,0:T(8,128)S(1)}, u32[]{:S(2)}, u32[]{:S(2)}) %collective-permute-start.3) | collective-permute-done | bytes 16416 | tf_op jit(solution)/shard_map/ppermute | solution.py:370
  9.8 0.9 %nonlocal_1.1 = (f32[128,384]{1,0:T(8,128)S(1)}, f32[96,128]{1,0:T(8,128)S(1)}, f32[128,128]{1,0:T(8,128)S(1)}, f32[128,128]{1,0:T(8,128)S(1)}, f32[32,128]{1,0:T(8,128)S(1)}) custom-call(s32[1]{0:T(128)} %bitcast.flag_ref, f32[32,128]{1,0:T(8,128)S(1)} %slice_add_fusion.4.refs_0_, f32[32,128]{1,0:T(8,128)S(1)} %collective-permute-done.3.refs_1_, ...), custom_call_target="tpu_custom_call" | custom-call | tf_op jit(solution)/shard_map/nonlocal_1/pallas_call | solution.py:500
  10.7 0.5 %collective-permute-start.6 = (f32[128,128]{1,0:T(8,128)S(1)}, f32[128,128]{1,0:T(8,128)S(1)}, u32[]{:S(2)}, u32[]{:S(2)}) collective-permute-start(f32[128,128]{1,0:T(8,128)S(1)} %get-tuple-element.30), channel_id=1, source_target_pairs={{0,24},{4,28},{8,16},{12,20},{16,8},{20,12},{24,0},{28,4},{1,25},{... | collective-permute-start | bytes 196616 | tf_op jit(solution)/shard_map/ppermute | solution.py:370
  11.2 0.5 %collective-permute-start.7 = (f32[128,128]{1,0:T(8,128)S(1)}, f32[128,128]{1,0:T(8,128)S(1)}, u32[]{:S(2)}, u32[]{:S(2)}) collective-permute-start(f32[128,128]{1,0:T(8,128)S(1)} %get-tuple-element.31), channel_id=1, source_target_pairs={{0,4},{4,0},{8,12},{12,8},{16,20},{20,16},{24,28},{28,24},{1,5},{5... | collective-permute-start | bytes 196616 | tf_op jit(solution)/shard_map/ppermute | solution.py:370
  11.7 1.9 %collective-permute-start.5 = (f32[32,128]{1,0:T(8,128)S(1)}, f32[32,128]{1,0:T(8,128)S(1)}, u32[]{:S(2)}, u32[]{:S(2)}) collective-permute-start(f32[32,128]{1,0:T(8,128)S(1)} %get-tuple-element.29), channel_id=1, source_target_pairs={{0,28},{4,24},{8,20},{12,16},{16,12},{20,8},{24,4},{28,0},{1,29},{... | collective-permute-start | bytes 49160 | tf_op jit(solution)/shard_map/ppermute | solution.py:370
  13.6 0.6 %collective-permute-start.9 = (f32[96,128]{1,0:T(8,128)S(1)}, f32[96,128]{1,0:T(8,128)S(1)}, u32[]{:S(2)}, u32[]{:S(2)}) collective-permute-start(f32[96,128]{1,0:T(8,128)S(1)} %get-tuple-element.32), channel_id=1, source_target_pairs={{0,8},{4,12},{8,0},{12,4},{16,24},{20,28},{24,16},{28,20},{1,9},{5... | collective-permute-start | bytes 147464 | tf_op jit(solution)/shard_map/ppermute | solution.py:370
  14.3 1.5 %collective-permute-done.5 = f32[32,128]{1,0:T(8,128)S(1)} collective-permute-done((f32[32,128]{1,0:T(8,128)S(1)}, f32[32,128]{1,0:T(8,128)S(1)}, u32[]{:S(2)}, u32[]{:S(2)}) %collective-permute-start.5) | collective-permute-done | bytes 16416 | tf_op jit(solution)/shard_map/ppermute | solution.py:370
  15.8 0.0 collective-permute-done.6.refs_1_
  15.8 0.0 collective-permute-done.7.refs_2_
  15.8 0.2 collective-permute-start.8
  16.0 0.0 collective-permute-done.9.refs_0_
  16.0 0.4 local_2.1.refs_3_
  16.3 0.7 %collective-permute-done.8.refs_1_ = f32[32,128]{1,0:T(8,128)S(1)} collective-permute-done((f32[32,128]{1,0:T(8,128)S(1)}, f32[32,128]{1,0:T(8,128)S(1)}, u32[]{:S(2)}, u32[]{:S(2)}) %collective-permute-start.8) | collective-permute-done | bytes 16416 | tf_op jit(solution)/shard_map/ppermute | solution.py:370
  17.0 0.9 %nonlocal_2.1 = (f32[128,384]{1,0:T(8,128)S(1)}, f32[96,128]{1,0:T(8,128)S(1)}, f32[128,128]{1,0:T(8,128)S(1)}, f32[128,128]{1,0:T(8,128)S(1)}, f32[32,128]{1,0:T(8,128)S(1)}) custom-call(s32[1]{0:T(128)} %bitcast.flag_ref, f32[32,128]{1,0:T(8,128)S(1)} %slice_add_fusion.2.refs_0_, f32[32,128]{1,0:T(8,128)S(1)} %collective-permute-done.8.refs_1_, ...), custom_call_target="tpu_custom_call" | custom-call | tf_op jit(solution)/shard_map/nonlocal_2/pallas_call | solution.py:500
  18.0 1.3 %collective-permute-start.11 = (f32[128,128]{1,0:T(8,128)S(1)}, f32[128,128]{1,0:T(8,128)S(1)}, u32[]{:S(2)}, u32[]{:S(2)}) collective-permute-start(f32[128,128]{1,0:T(8,128)S(1)} %get-tuple-element.35), channel_id=1, source_target_pairs={{0,24},{4,28},{8,16},{12,20},{16,8},{20,12},{24,0},{28,4},{1,25},{... | collective-permute-start | bytes 196616 | tf_op jit(solution)/shard_map/ppermute | solution.py:370
  19.2 1.6 %collective-permute-start.12 = (f32[128,128]{1,0:T(8,128)S(1)}, f32[128,128]{1,0:T(8,128)S(1)}, u32[]{:S(2)}, u32[]{:S(2)}) collective-permute-start(f32[128,128]{1,0:T(8,128)S(1)} %get-tuple-element.36), channel_id=1, source_target_pairs={{0,4},{4,0},{8,12},{12,8},{16,20},{20,16},{24,28},{28,24},{1,5},{5... | collective-permute-start | bytes 196616 | tf_op jit(solution)/shard_map/ppermute | solution.py:370
  20.9 0.1 collective-permute-start.10
  21.0 0.4 collective-permute-start.13
  21.4 0.8 %collective-permute-done.10.refs_1_ = f32[96,128]{1,0:T(8,128)S(1)} collective-permute-done((f32[96,128]{1,0:T(8,128)S(1)}, f32[96,128]{1,0:T(8,128)S(1)}, u32[]{:S(2)}, u32[]{:S(2)}) %collective-permute-start.10) | collective-permute-done | bytes 49184 | tf_op jit(solution)/shard_map/ppermute | solution.py:370
  22.1 0.0 collective-permute-done.11.refs_2_
  22.1 1.5 %collective-permute-done.12.refs_3_ = f32[128,128]{1,0:T(8,128)S(1)} collective-permute-done((f32[128,128]{1,0:T(8,128)S(1)}, f32[128,128]{1,0:T(8,128)S(1)}, u32[]{:S(2)}, u32[]{:S(2)}) %collective-permute-start.12) | collective-permute-done | bytes 65568 | tf_op jit(solution)/shard_map/ppermute | solution.py:370
  23.6 0.4 local_3.1.refs_4_
  24.0 1.6 %collective-permute-start.15 = (f32[128,384]{1,0:T(8,128)S(1)}, f32[128,384]{1,0:T(8,128)S(1)}, u32[]{:S(2)}, u32[]{:S(2)}) collective-permute-start(f32[128,384]{1,0:T(8,128)S(1)} %local_3.1.refs_4_), channel_id=1, source_target_pairs={{0,1},{1,0},{2,3},{3,2},{4,5},{5,4},{6,7},{7,6},{8,9},{9,8},{10,11... | collective-permute-start | bytes 589832 | tf_op jit(solution)/shard_map/ppermute | solution.py:375
  25.7 0.0 collective-permute-done.13
  25.7 0.1 collective-permute-start.14
  25.7 1.2 %collective-permute-done.14 = f32[32,128]{1,0:T(8,128)S(1)} collective-permute-done((f32[32,128]{1,0:T(8,128)S(1)}, f32[32,128]{1,0:T(8,128)S(1)}, u32[]{:S(2)}, u32[]{:S(2)}) %collective-permute-start.14) | collective-permute-done | bytes 16416 | tf_op jit(solution)/shard_map/ppermute | solution.py:370
  26.9 0.9 %collective-permute-start.16 = (f32[32,128]{1,0:T(8,128)S(1)}, f32[32,128]{1,0:T(8,128)S(1)}, u32[]{:S(2)}, u32[]{:S(2)}) collective-permute-start(f32[32,128]{1,0:T(8,128)S(1)} %add.42.refs_5_), channel_id=1, source_target_pairs={{0,1},{1,0},{2,3},{3,2},{4,5},{5,4},{6,7},{7,6},{8,9},{9,8},{10,11... | collective-permute-start | bytes 49160 | tf_op jit(solution)/shard_map/ppermute | solution.py:375
  27.9 2.9 %collective-permute-done.16.refs_7_ = f32[32,128]{1,0:T(8,128)S(1)} collective-permute-done((f32[32,128]{1,0:T(8,128)S(1)}, f32[32,128]{1,0:T(8,128)S(1)}, u32[]{:S(2)}, u32[]{:S(2)}) %collective-permute-start.16) | collective-permute-done | bytes 16416 | tf_op jit(solution)/shard_map/ppermute | solution.py:375
  30.8 0.0 collective-permute-done.15.refs_6_
  30.8 0.7 %filtered.1 = f32[128,384]{1,0:T(8,128)S(1)} custom-call(f32[8,128]{1,0:T(8,128)S(1)} %get-tuple-element.22.refs_0_.cheb_ref, f32[32,128]{1,0:T(8,128)S(1)} %bitcast.22, bf16[512,384]{1,0:T(8,128)(2,1)S(1)} %bitcast.12, f32[12,128]{1,0:T(8,128)S(1)} %get-tuple-element.23.refs_5_.refs_2_, bf16[128,1536]{1,0:T(8,128)(2,1)S(1)} %get-tuple-element.24.refs_6_.refs_3_, ...), custom_call_target="tpu_custom_call" | custom-call | tf_op jit(solution)/shard_map/filtered/pallas_call | solution.py:489
  31.5 0.5 %collective-permute-start.17 = (f32[128,384]{1,0:T(8,128)S(1)}, f32[128,384]{1,0:T(8,128)S(1)}, u32[]{:S(2)}, u32[]{:S(2)}) collective-permute-start(f32[128,384]{1,0:T(8,128)S(1)} %filtered.1), channel_id=1, source_target_pairs={{0,3},{1,2},{2,1},{3,0},{4,7},{5,6},{6,5},{7,4},{8,11},{9,10},{10,... | collective-permute-start | bytes 589832 | tf_op jit(solution)/shard_map/ppermute | solution.py:375
  32.0 10.0 %collective-permute-done.17 = f32[128,384]{1,0:T(8,128)S(1)} collective-permute-done((f32[128,384]{1,0:T(8,128)S(1)}, f32[128,384]{1,0:T(8,128)S(1)}, u32[]{:S(2)}, u32[]{:S(2)}) %collective-permute-start.17) | collective-permute-done | bytes 196640 | tf_op jit(solution)/shard_map/ppermute | solution.py:375
  42.0 0.7 %add_multiply_fusion = f32[128,384]{1,0:T(8,128)} fusion(f32[128,384]{1,0:T(8,128)S(1)} %filtered.1, f32[128,384]{1,0:T(8,128)S(1)} %collective-permute-done.17), kind=kLoop, calls=%fused_computation | loop fusion | flops 98304 | bytes 589824 | tf_op jit(solution)/shard_map/mul | solution.py:519
  (8 shorter events, 0.0 us)
Async XLA Ops:
  0.0 8.9 %copy-start.1 = (f32[1,8,16,384]{3,2,1,0:T(8,128)S(1)}, f32[1,8,16,384]{3,2,1,0:T(8,128)}, u32[]{:S(2)}) copy-start(f32[1,8,16,384]{3,2,1,0:T(8,128)} %param.6) | copy-start | bytes 589828
  0.0 8.9 %copy-start.2 = (f32[8,16,384]{2,1,0:T(8,128)S(1)}, f32[8,16,384]{2,1,0:T(8,128)}, u32[]{:S(2)}) copy-start(f32[8,16,384]{2,1,0:T(8,128)} %param.7) | copy-start | bytes 589828
  1.8 6.6 %collective-permute-start.1 = (f32[128,128]{1,0:T(8,128)S(1)}, f32[128,128]{1,0:T(8,128)S(1)}, u32[]{:S(2)}, u32[]{:S(2)}) collective-permute-start(f32[128,128]{1,0:T(8,128)S(1)} %get-tuple-element.26), channel_id=1, source_target_pairs={{0,24},{4,28},{8,16},{12,20},{16,8},{20,12},{24,0},{28,4},{1,25},{... | collective-permute-start | bytes 196616 | tf_op jit(solution)/shard_map/ppermute | solution.py:370
  2.8 5.6 %collective-permute-start.2 = (f32[128,128]{1,0:T(8,128)S(1)}, f32[128,128]{1,0:T(8,128)S(1)}, u32[]{:S(2)}, u32[]{:S(2)}) collective-permute-start(f32[128,128]{1,0:T(8,128)S(1)} %get-tuple-element.27), channel_id=1, source_target_pairs={{0,4},{4,0},{8,12},{12,8},{16,20},{20,16},{24,28},{28,24},{1,5},{5... | collective-permute-start | bytes 196616 | tf_op jit(solution)/shard_map/ppermute | solution.py:370
  4.3 4.1 %collective-permute-start = (f32[32,128]{1,0:T(8,128)S(1)}, f32[32,128]{1,0:T(8,128)S(1)}, u32[]{:S(2)}, u32[]{:S(2)}) collective-permute-start(f32[32,128]{1,0:T(8,128)S(1)} %get-tuple-element.25), channel_id=1, source_target_pairs={{0,28},{4,24},{8,20},{12,16},{16,12},{20,8},{24,4},{28,0},{1,29},{... | collective-permute-start | bytes 49160 | tf_op jit(solution)/shard_map/ppermute | solution.py:370
  4.8 4.1 %collective-permute-start.4 = (f32[96,128]{1,0:T(8,128)S(1)}, f32[96,128]{1,0:T(8,128)S(1)}, u32[]{:S(2)}, u32[]{:S(2)}) collective-permute-start(f32[96,128]{1,0:T(8,128)S(1)} %get-tuple-element.28), channel_id=1, source_target_pairs={{0,8},{4,12},{8,0},{12,4},{16,24},{20,28},{24,16},{28,20},{1,9},{5... | collective-permute-start | bytes 147464 | tf_op jit(solution)/shard_map/ppermute | solution.py:370
  8.4 1.3 %copy-start = (bf16[4,8,16,384]{3,2,1,0:T(8,128)(2,1)S(1)}, bf16[4,8,16,384]{3,2,1,0:T(8,128)(2,1)}, u32[]{:S(2)}) copy-start(bf16[4,8,16,384]{3,2,1,0:T(8,128)(2,1)} %param.8) | copy-start | bytes 1179652
  8.4 1.3 %collective-permute-start.3 = (f32[32,128]{1,0:T(8,128)S(1)}, f32[32,128]{1,0:T(8,128)S(1)}, u32[]{:S(2)}, u32[]{:S(2)}) collective-permute-start(f32[32,128]{1,0:T(8,128)S(1)} %slice_add_fusion.4.refs_0_), channel_id=1, source_target_pairs={{0,8},{4,12},{8,0},{12,4},{16,24},{20,28},{24,16},{28,20},{1,9},{5... | collective-permute-start | bytes 49160 | tf_op jit(solution)/shard_map/ppermute | solution.py:370
  8.9 0.8 %copy-start.3 = (f32[4096]{0:T(1024)S(1)}, f32[4096]{0:T(1024)}, u32[]{:S(2)}) copy-start(f32[4096]{0:T(1024)} %param.10) | copy-start | bytes 49156
  10.7 5.1 %collective-permute-start.6 = (f32[128,128]{1,0:T(8,128)S(1)}, f32[128,128]{1,0:T(8,128)S(1)}, u32[]{:S(2)}, u32[]{:S(2)}) collective-permute-start(f32[128,128]{1,0:T(8,128)S(1)} %get-tuple-element.30), channel_id=1, source_target_pairs={{0,24},{4,28},{8,16},{12,20},{16,8},{20,12},{24,0},{28,4},{1,25},{... | collective-permute-start | bytes 196616 | tf_op jit(solution)/shard_map/ppermute | solution.py:370
  11.2 4.6 %collective-permute-start.7 = (f32[128,128]{1,0:T(8,128)S(1)}, f32[128,128]{1,0:T(8,128)S(1)}, u32[]{:S(2)}, u32[]{:S(2)}) collective-permute-start(f32[128,128]{1,0:T(8,128)S(1)} %get-tuple-element.31), channel_id=1, source_target_pairs={{0,4},{4,0},{8,12},{12,8},{16,20},{20,16},{24,28},{28,24},{1,5},{5... | collective-permute-start | bytes 196616 | tf_op jit(solution)/shard_map/ppermute | solution.py:370
  11.7 4.1 %collective-permute-start.5 = (f32[32,128]{1,0:T(8,128)S(1)}, f32[32,128]{1,0:T(8,128)S(1)}, u32[]{:S(2)}, u32[]{:S(2)}) collective-permute-start(f32[32,128]{1,0:T(8,128)S(1)} %get-tuple-element.29), channel_id=1, source_target_pairs={{0,28},{4,24},{8,20},{12,16},{16,12},{20,8},{24,4},{28,0},{1,29},{... | collective-permute-start | bytes 49160 | tf_op jit(solution)/shard_map/ppermute | solution.py:370
  13.6 2.3 %collective-permute-start.9 = (f32[96,128]{1,0:T(8,128)S(1)}, f32[96,128]{1,0:T(8,128)S(1)}, u32[]{:S(2)}, u32[]{:S(2)}) collective-permute-start(f32[96,128]{1,0:T(8,128)S(1)} %get-tuple-element.32), channel_id=1, source_target_pairs={{0,8},{4,12},{8,0},{12,4},{16,24},{20,28},{24,16},{28,20},{1,9},{5... | collective-permute-start | bytes 147464 | tf_op jit(solution)/shard_map/ppermute | solution.py:370
  15.8 1.2 %collective-permute-start.8 = (f32[32,128]{1,0:T(8,128)S(1)}, f32[32,128]{1,0:T(8,128)S(1)}, u32[]{:S(2)}, u32[]{:S(2)}) collective-permute-start(f32[32,128]{1,0:T(8,128)S(1)} %slice_add_fusion.2.refs_0_), channel_id=1, source_target_pairs={{0,8},{4,12},{8,0},{12,4},{16,24},{20,28},{24,16},{28,20},{1,9},{5... | collective-permute-start | bytes 49160 | tf_op jit(solution)/shard_map/ppermute | solution.py:370
  18.0 4.1 %collective-permute-start.11 = (f32[128,128]{1,0:T(8,128)S(1)}, f32[128,128]{1,0:T(8,128)S(1)}, u32[]{:S(2)}, u32[]{:S(2)}) collective-permute-start(f32[128,128]{1,0:T(8,128)S(1)} %get-tuple-element.35), channel_id=1, source_target_pairs={{0,24},{4,28},{8,16},{12,20},{16,8},{20,12},{24,0},{28,4},{1,25},{... | collective-permute-start | bytes 196616 | tf_op jit(solution)/shard_map/ppermute | solution.py:370
  19.2 4.3 %collective-permute-start.12 = (f32[128,128]{1,0:T(8,128)S(1)}, f32[128,128]{1,0:T(8,128)S(1)}, u32[]{:S(2)}, u32[]{:S(2)}) collective-permute-start(f32[128,128]{1,0:T(8,128)S(1)} %get-tuple-element.36), channel_id=1, source_target_pairs={{0,4},{4,0},{8,12},{12,8},{16,20},{20,16},{24,28},{28,24},{1,5},{5... | collective-permute-start | bytes 196616 | tf_op jit(solution)/shard_map/ppermute | solution.py:370
  20.9 1.2 %collective-permute-start.10 = (f32[96,128]{1,0:T(8,128)S(1)}, f32[96,128]{1,0:T(8,128)S(1)}, u32[]{:S(2)}, u32[]{:S(2)}) collective-permute-start(f32[96,128]{1,0:T(8,128)S(1)} %get-tuple-element.34), channel_id=1, source_target_pairs={{0,8},{4,12},{8,0},{12,4},{16,24},{20,28},{24,16},{28,20},{1,9},{5... | collective-permute-start | bytes 147464 | tf_op jit(solution)/shard_map/ppermute | solution.py:370
  21.0 4.7 %collective-permute-start.13 = (f32[32,128]{1,0:T(8,128)S(1)}, f32[32,128]{1,0:T(8,128)S(1)}, u32[]{:S(2)}, u32[]{:S(2)}) collective-permute-start(f32[32,128]{1,0:T(8,128)S(1)} %get-tuple-element.38), channel_id=1, source_target_pairs={{0,28},{4,24},{8,20},{12,16},{16,12},{20,8},{24,4},{28,0},{1,29},{... | collective-permute-start | bytes 49160 | tf_op jit(solution)/shard_map/ppermute | solution.py:370
  24.0 6.8 %collective-permute-start.15 = (f32[128,384]{1,0:T(8,128)S(1)}, f32[128,384]{1,0:T(8,128)S(1)}, u32[]{:S(2)}, u32[]{:S(2)}) collective-permute-start(f32[128,384]{1,0:T(8,128)S(1)} %local_3.1.refs_4_), channel_id=1, source_target_pairs={{0,1},{1,0},{2,3},{3,2},{4,5},{5,4},{6,7},{7,6},{8,9},{9,8},{10,11... | collective-permute-start | bytes 589832 | tf_op jit(solution)/shard_map/ppermute | solution.py:375
  25.7 1.2 %collective-permute-start.14 = (f32[32,128]{1,0:T(8,128)S(1)}, f32[32,128]{1,0:T(8,128)S(1)}, u32[]{:S(2)}, u32[]{:S(2)}) collective-permute-start(f32[32,128]{1,0:T(8,128)S(1)} %slice_add_fusion), channel_id=1, source_target_pairs={{0,8},{4,12},{8,0},{12,4},{16,24},{20,28},{24,16},{28,20},{1,9},{5... | collective-permute-start | bytes 49160 | tf_op jit(solution)/shard_map/ppermute | solution.py:370
  26.9 3.9 %collective-permute-start.16 = (f32[32,128]{1,0:T(8,128)S(1)}, f32[32,128]{1,0:T(8,128)S(1)}, u32[]{:S(2)}, u32[]{:S(2)}) collective-permute-start(f32[32,128]{1,0:T(8,128)S(1)} %add.42.refs_5_), channel_id=1, source_target_pairs={{0,1},{1,0},{2,3},{3,2},{4,5},{5,4},{6,7},{7,6},{8,9},{9,8},{10,11... | collective-permute-start | bytes 49160 | tf_op jit(solution)/shard_map/ppermute | solution.py:375
  31.5 10.5 %collective-permute-start.17 = (f32[128,384]{1,0:T(8,128)S(1)}, f32[128,384]{1,0:T(8,128)S(1)}, u32[]{:S(2)}, u32[]{:S(2)}) collective-permute-start(f32[128,384]{1,0:T(8,128)S(1)} %filtered.1), channel_id=1, source_target_pairs={{0,3},{1,2},{2,1},{3,0},{4,7},{5,6},{6,5},{7,4},{8,11},{9,10},{10,... | collective-permute-start | bytes 589832 | tf_op jit(solution)/shard_map/ppermute | solution.py:375

commit v7 on v6

--- a/solution.py
+++ b/solution.py
@@ -74,11 +74,10 @@
     return [(zb, slot) for zb in range(sz.zb) for slot in range(sz.slots)]
 
 
-def partial_table(sz, vals, pv_ref, row_of, hot_ref):
+def slot_sums(sz, vals, pv_ref):
     eye = iota((sz.cells, LANES), 0) == iota((sz.cells, LANES), 1)
     eye_all = jnp.concatenate([eye] * sz.slots, axis=0)
-    spread_first, spread_second = [], []
-    table_iota = iota((sz.rows, LANES), 0).astype(F32)
+    sums = {}
     for zb in range(sz.zb):
         first, second = pieces(vals[:, zb * LANES : (zb + 1) * LANES])
         weights = pv_ref[:, zb * LANES : (zb + 1) * LANES]
@@ -89,18 +88,43 @@
         )
         cross = jnp.where(eye_all, cross, 0.0)
         for slot in range(sz.slots):
-            sums = jnp.sum(
-                cross[slot * sz.cells : (slot + 1) * sz.cells], axis=0, keepdims=True
-            )
-            spread = jnp.where(chunk(sz, row_of, zb, slot) == table_iota, sums, 0.0)
-            a, b = pieces(spread)
-            spread_first.append(a)
-            spread_second.append(b)
+            part = cross[slot * sz.cells : (slot + 1) * sz.cells]
+            sums[zb, slot] = jnp.sum(part, axis=0, keepdims=True)
+    return sums
+
+
+def partial_table(sz, sums, row_of, hot_ref):
+    spread_first, spread_second = [], []
+    table_iota = iota((sz.rows, LANES), 0).astype(F32)
+    for zb, slot in chunks(sz):
+        hit = chunk(sz, row_of, zb, slot) == table_iota
+        a, b = pieces(sums[zb, slot])
+        spread_first.append(jnp.where(hit, a.astype(F32), 0.0).astype(BF16))
+        spread_second.append(jnp.where(hit, b.astype(F32), 0.0).astype(BF16))
     lhs = jnp.concatenate(
         [jnp.concatenate(spread_first, axis=1), jnp.concatenate(spread_second, axis=1)], axis=0
     )
     both = dot(lhs, hot_ref[...], NT)
     return both[: sz.rows] + both[sz.rows :]
+
+
+def overlap_row(sz, slot, other, zb):
+    return (slot * sz.slots + other) * sz.zb + zb
+
+
+def overlap_kernel(sz, after_ref, pv_ref, overlap_ref):
+    eye = iota((sz.cells, LANES), 0) == iota((sz.cells, LANES), 1)
+    for zb in range(sz.zb):
+        weights = pv_ref[:, zb * LANES : (zb + 1) * LANES]
+        cross = dot(weights, weights, NT)
+        for slot in range(sz.slots):
+            rows = cross[slot * sz.cells : (slot + 1) * sz.cells]
+            for other in range(slot, sz.slots):
+                block = rows[:, other * sz.cells : (other + 1) * sz.cells]
+                row = jnp.sum(jnp.where(eye, block, 0.0), axis=0, keepdims=True)
+                for at in {(slot, other), (other, slot)}:
+                    at = overlap_row(sz, *at, zb)
+                    overlap_ref[at : at + 1, :] = row
 
 
 def projected(sz, tables, pv_ref, row_of, hot_ref):
@@ -115,6 +139,7 @@
     table_iota = iota((sz.rows, LANES), 0).astype(F32)
     eye = iota((sz.cells, LANES), 0) == iota((sz.cells, LANES), 1)
     result = [[] for _ in tables]
+    weights = [{} for _ in tables]
     for zb in range(sz.zb):
         diag = [[] for _ in range(2 * count)]
         for slot in range(sz.slots):
@@ -124,6 +149,7 @@
                 weight = jnp.sum(
                     jnp.where(hit, found[n][:, at : at + LANES], 0.0), axis=0, keepdims=True
                 )
+                weights[n][zb, slot] = weight
                 a, b = pieces(jnp.where(eye, weight, 0.0))
                 diag[2 * n].append(a)
                 diag[2 * n + 1].append(b)
@@ -132,7 +158,7 @@
         for n in range(count):
             at = 2 * n * sz.cells
             result[n].append(both[at : at + sz.cells] + both[at + sz.cells : at + 2 * sz.cells])
-    return [jnp.concatenate(parts, axis=1) for parts in result]
+    return [jnp.concatenate(parts, axis=1) for parts in result], weights
 
 
 def from_message(sz, msg_ref, rows):
@@ -195,8 +221,7 @@
     return result + 16.0 * near - far
 
 
-def emit(sz, vals, flag_ref, pv_ref, row_of, hot_ref, ab_ref, bb_ref, yb_ref, table_ref):
-    table = partial_table(sz, vals, pv_ref, row_of, hot_ref)
+def emit(sz, vals, table, flag_ref, ab_ref, bb_ref, yb_ref, table_ref):
     table_ref[...] = table
     flag = flag_ref[0]
     top = vals[sz.cells - sz.xedge :]
@@ -247,9 +272,9 @@
         ).astype(BF16)
     get_vals.wait()
     get_pv.wait()
-    emit(
-        sz, vals_ref[...], flag_ref, pv_ref, row_of, hot_ref, ab_ref, bb_ref, yb_ref, table_ref
-    )
+    vals = vals_ref[...]
+    table = partial_table(sz, slot_sums(sz, vals, pv_ref), row_of, hot_ref)
+    emit(sz, vals, table, flag_ref, ab_ref, bb_ref, yb_ref, table_ref)
     get_cheb.wait()
     for n in range(STEPS + 1):
         cheb_out[n : n + 1, :] = jnp.full((1, LANES), cheb_ref[n], F32)
@@ -266,6 +291,8 @@
     a_ref, b_ref = refs.pop(0), refs.pop(0)
     y_refs = [refs.pop(0) for _ in range(n_y)]
     pot_ref = refs.pop(0)
+    if degree < STEPS:
+        pv_ref, sums_ref = refs.pop(0), refs.pop()
     *history, out_ref = refs
     vals = history[-1][...]
 
@@ -287,6 +314,10 @@
         for n in range(STEPS):
             result = result + coefficient(sz, cheb_ref, n) * history[n][...]
     out_ref[...] = result
+    if degree < STEPS:
+        for (zb, slot), row in slot_sums(sz, result, pv_ref).items():
+            at = slot * sz.zb + zb
+            sums_ref[at : at + 1, :] = row
 
 
 def added(table_refs):
@@ -300,12 +331,22 @@
     refs = list(refs)
     table_refs = [refs.pop(0) for _ in range(n_tables)]
     energy_ref, rest_ref, pv_ref, rows_ref, hot_ref = (refs.pop(0) for _ in range(5))
+    sums_ref, overlap_ref = refs.pop(0), refs.pop(0)
     row_of = rows_ref[...]
     double = 1.0 if degree == 1 else 2.0
     table = added(table_refs) * (energy_ref[...] * (double / E_HALF))
-    result = rest_ref[...] + projected(sz, [table], pv_ref, row_of, hot_ref)[0]
+    (part,), (weights,) = projected(sz, [table], pv_ref, row_of, hot_ref)
+    sums = {}
+    for zb, slot in chunks(sz):
+        total = chunk(sz, sums_ref, zb, slot)
+        for other in range(sz.slots):
+            at = overlap_row(sz, slot, other, zb)
+            total = total + overlap_ref[at : at + 1, :] * weights[zb, other]
+        sums[zb, slot] = total
+    table = partial_table(sz, sums, row_of, hot_ref)
+    result = rest_ref[...] + part
     refs[0][...] = result
-    emit(sz, result, flag_ref, pv_ref, row_of, hot_ref, *refs[1:])
+    emit(sz, result, table, flag_ref, *refs[1:])
 
 
 def last_kernel(sz, n_orbitals, n_tables, cheb_ref, *refs):
@@ -317,7 +358,8 @@
         rests.append(refs.pop(0))
         tables.append(added([refs.pop(0) for _ in range(n_tables)]) * scale)
     total = None
-    for rest_ref, part in zip(rests, projected(sz, tables, pv_ref, rows_ref[...], hot_ref)):
+    parts, _ = projected(sz, tables, pv_ref, rows_ref[...], hot_ref)
+    for rest_ref, part in zip(rests, parts):
         filtered = rest_ref[...] + part
         squared = filtered * filtered
         total = squared if total is None else total + squared
@@ -419,15 +461,17 @@
     field = jax.ShapeDtypeStruct((sz.cells, nz), F32)
     params = pltpu.CompilerParams(vmem_limit_bytes=48 << 20)
 
-    def exchange(to_a, to_b, to_y, table):
+    def exchange(to_a, to_b, to_y, table, aside):
         if whole:
             from_b = swap(to_b, lambda i, j: (size_first - 1 - i, j))
             from_y = swap(to_y, lambda i, j: (i, 1 - j))
             from_d = swap(table, lambda i, j: (size_first - 1 - i, 1 - j))
             from_a = swap(to_a, lambda i, j: (i ^ 1, j))
+            if aside is not None:
+                from_d, aside = lax.optimization_barrier((from_d, aside))
             table = table + from_d + from_b[sz.edge_rows :] + from_y[sz.yedge_rows :]
             other = swap(table, lambda i, j: (i ^ 1, j))
-            return [table, other], from_a, from_b, [from_y]
+            return [table, other], from_a, from_b, [from_y], aside
         edges_b = to_b[: sz.edge_rows]
         edges_y = to_y[: sz.yedge_rows]
         below = shift(edges_y, "gy", 1)
@@ -442,7 +486,7 @@
                     moved, windows[0], windows[1], size_first, size_second, dim, delta
                 )
             table = total
-        return [table], from_a, from_b, [below, above]
+        return [table], from_a, from_b, [below, above], aside
 
     def one_orbital(start):
         *messages, row_of, hot, cheb = pl.pallas_call(
@@ -465,18 +509,31 @@
             compiler_params=params,
             name="project_first",
         )(flag, *(in_place(arr) for arr in (start, pv, ids, cheb_coef)))
+        overlap = pl.pallas_call(
+            functools.partial(overlap_kernel, sz),
+            out_shape=jax.ShapeDtypeStruct((slots * slots * sz.zb, LANES), F32),
+            in_specs=vmem(2),
+            out_specs=vmem(1)[0],
+            compiler_params=params,
+            name="overlap",
+        )(row_of, pv)
         history = [start]
         for degree in range(1, STEPS + 1):
-            tables, from_a, from_b, from_y = exchange(*messages)
+            tables, from_a, from_b, from_y, aside = exchange(
+                *messages, overlap if degree == 1 else None
+            )
+            overlap = overlap if aside is None else aside
             last = degree == STEPS
-            args = (from_a, from_b, *from_y, pot, *history)
+            sums_shape = jax.ShapeDtypeStruct((slots * sz.zb, LANES), F32)
             if last:
-                args = (cheb, *args)
-            rest = pl.pallas_call(
+                args = (cheb, from_a, from_b, *from_y, pot, *history)
+            else:
+                args = (from_a, from_b, *from_y, pot, pv, *history)
+            rest, *sums = pl.pallas_call(
                 functools.partial(local_kernel, sz, degree, len(from_y)),
-                out_shape=field,
+                out_shape=(field,) if last else (field, sums_shape),
                 in_specs=smem(1) + vmem(len(args)),
-                out_specs=vmem(1)[0],
+                out_specs=tuple(vmem(1 if last else 2)),
                 compiler_params=params,
                 name=f"local_{degree}",
             )(flag, *args)
@@ -496,7 +553,7 @@
                     compiler_params=params,
                     name="filtered",
                 )(*args)
-            args = (*tables, energy, rest, pv, row_of, hot)
+            args = (*tables, energy, rest, pv, row_of, hot, *sums, overlap)
             out = pl.pallas_call(
                 functools.partial(nonlocal_kernel, sz, degree, len(tables)),
                 out_shape=(field,) + message_shapes,

time: 43 us -> 42.5 us (0.988)
  waiting for transfers between devices: 22.4 us -> 21.1 us
  Pallas kernels: 5.52 us -> 6.06 us
    ppermute x15, waiting for transfers between devices: 9.44 us -> 8.27 us  [swap(): return lax.ppermute(arr, ('gx', 'gy'), pairs)]
    pallas_call x2, Pallas kernels: 1.87 us -> 1.26 us  [one_orbital(): pl.pallas_call(functools.partial(nonlocal_kernel, sz, degree, len(tables)...]
    pallas_call x0 -> x1, Pallas kernels: none -> 0.58 us  [one_orbital(): pl.pallas_call(functools.partial(overlap_kernel, sz), out_shape=jax.Shape...]
    pallas_call x3, Pallas kernels: 1.12 us -> 1.7 us  [one_orbital(): pl.pallas_call(functools.partial(local_kernel, sz, degree, len(from_y)),...]
  transfers between devices with their start and end apart: 18 -> 18, of which waited for: 9 -> 9; matrix products, arithmetic and copies ran while one was open for 0% -> 0% of each run, Pallas kernels for 3% -> 5%
where the time goes in v7:
time: 42.5 us; the launch traced here: 42.2 us
  waiting for transfers between devices  21.1 us (50%)
  starting transfers between devices  14.1 us (33%)
  Pallas kernels  6.06 us (14%)
  other arithmetic  0.73 us (2%)
    ppermute x3, waiting for transfers between devices, orb_swap(): return lax.ppermute(vals, 'orb', [(i, i ^ bit) for i in range(size)])  12.9 us
    ppermute x15, starting transfers between devices, swap(): return lax.ppermute(arr, ('gx', 'gy'), pairs)  11 us
    ppermute x15, waiting for transfers between devices, swap(): return lax.ppermute(arr, ('gx', 'gy'), pairs)  8.27 us
    ppermute x3, starting transfers between devices, orb_swap(): return lax.ppermute(vals, 'orb', [(i, i ^ bit) for i in range(size)])  3.13 us
    pallas_call x1, Pallas kernels, one_orbital(): pl.pallas_call(functools.partial(first_kernel, sz), out_shape=message_sha...  1.8 us
    pallas_call x3, Pallas kernels, one_orbital(): pl.pallas_call(functools.partial(local_kernel, sz, degree, len(from_y)),...  1.7 us
    pallas_call x2, Pallas kernels, one_orbital(): pl.pallas_call(functools.partial(nonlocal_kernel, sz, degree, len(tables)...  1.26 us
  transfers between devices with their start and end apart: 18, of which 9 were waited for; matrix products, arithmetic and copies ran while one was open for 0% of the time, Pallas kernels for 5%

profile of v7, /device:TPU:16, one launch (start us, length us, event | category | flops | bytes accessed | tf_op | source)
XLA Modules:
  0.0 42.2 jit_solution(7754927121006974089)
XLA Ops:
  0.0 1.8 %project_first.1 = (f32[96,128]{1,0:T(8,128)S(1)}, f32[128,128]{1,0:T(8,128)S(1)}, f32[128,128]{1,0:T(8,128)S(1)}, f32[32,128]{1,0:T(8,128)S(1)}, f32[12,128]{1,...) custom-call(s32[1]{0:T(128)} %bitcast.flag_ref, f32[128,384]{1,0:T(8,128)} %bitcast.16, ...), custom_call_target="tpu_custom_call" | custom-call | tf_op jit(solution)/shard_map/project_first/pallas_call | solution.py:492
  1.8 1.0 %collective-permute-start.1 = (f32[128,128]{1,0:T(8,128)S(1)}, f32[128,128]{1,0:T(8,128)S(1)}, u32[]{:S(2)}, u32[]{:S(2)}) collective-permute-start(f32[128,128]{1,0:T(8,128)S(1)} %get-tuple-element.33), channel_id=1, source_target_pairs={{0,24},{4,28},{8,16},{12,20},{16,8},{20,12},{24,0},{28,4},{1,25},{... | collective-permute-start | bytes 196616 | tf_op jit(solution)/shard_map/ppermute | solution.py:412
  2.8 1.5 %collective-permute-start.2 = (f32[128,128]{1,0:T(8,128)S(1)}, f32[128,128]{1,0:T(8,128)S(1)}, u32[]{:S(2)}, u32[]{:S(2)}) collective-permute-start(f32[128,128]{1,0:T(8,128)S(1)} %get-tuple-element.34), channel_id=1, source_target_pairs={{0,4},{4,0},{8,12},{12,8},{16,20},{20,16},{24,28},{28,24},{1,5},{5... | collective-permute-start | bytes 196616 | tf_op jit(solution)/shard_map/ppermute | solution.py:412
  4.3 0.5 %collective-permute-start = (f32[32,128]{1,0:T(8,128)S(1)}, f32[32,128]{1,0:T(8,128)S(1)}, u32[]{:S(2)}, u32[]{:S(2)}) collective-permute-start(f32[32,128]{1,0:T(8,128)S(1)} %get-tuple-element.31), channel_id=1, source_target_pairs={{0,28},{4,24},{8,20},{12,16},{16,12},{20,8},{24,4},{28,0},{1,29},{... | collective-permute-start | bytes 49160 | tf_op jit(solution)/shard_map/ppermute | solution.py:412
  4.8 0.2 collective-permute-start.4
  5.0 0.0 copy-done
  5.0 0.6 %overlap.1.refs_8_ = f32[48,128]{1,0:T(8,128)S(1)} custom-call(f32[12,128]{1,0:T(8,128)S(1)} %get-tuple-element.29.after_ref.refs_5_.refs_2_, bf16[512,384]{1,0:T(8,128)(2,1)S(1)} %bitcast.10), custom_call_target="tpu_custom_call" | custom-call | tf_op jit(solution)/shard_map/overlap/pallas_call | solution.py:512
  5.6 2.8 %collective-permute-done = f32[32,128]{1,0:T(8,128)S(1)} collective-permute-done((f32[32,128]{1,0:T(8,128)S(1)}, f32[32,128]{1,0:T(8,128)S(1)}, u32[]{:S(2)}, u32[]{:S(2)}) %collective-permute-start) | collective-permute-done | bytes 16416 | tf_op jit(solution)/shard_map/ppermute | solution.py:412
  8.4 0.0 collective-permute-done.1.refs_1_
  8.4 0.0 collective-permute-done.2.refs_2_
  8.4 0.5 %collective-permute-start.3 = (f32[32,128]{1,0:T(8,128)S(1)}, f32[32,128]{1,0:T(8,128)S(1)}, u32[]{:S(2)}, u32[]{:S(2)}) collective-permute-start(f32[32,128]{1,0:T(8,128)S(1)} %slice_add_fusion.4.refs_0_), channel_id=1, source_target_pairs={{0,8},{4,12},{8,0},{12,4},{16,24},{20,28},{24,16},{28,20},{1,9},{5... | collective-permute-start | bytes 49160 | tf_op jit(solution)/shard_map/ppermute | solution.py:412
  8.9 0.0 collective-permute-done.4.refs_0_
  8.9 0.0 copy-done.1
  8.9 0.0 copy-start.3
  8.9 0.6 %local_1.1 = (f32[128,384]{1,0:T(8,128)S(1)}, f32[12,128]{1,0:T(8,128)S(1)}) custom-call(s32[1]{0:T(128)} %bitcast.flag_ref, f32[96,128]{1,0:T(8,128)S(1)} %collective-permute-done.4.refs_0_, f32[128,128]{1,0:T(8,128)S(1)} %collective-permute-done.1.refs_1_, f32[128,128]{1,0:T(8,128)S(1)} %collective-permute-done.2.refs_2_, f32[128,384]{1,0:T(8,128)S(1)} %bitcast.20, ...), custom_call_target="tpu_custom_call" | custom-call | tf_op jit(solution)/shard_map/local_1/pallas_call | solution.py:532
  9.6 0.2 collective-permute-done.3.refs_1_
  9.7 0.6 %nonlocal_1.1 = (f32[128,384]{1,0:T(8,128)S(1)}, f32[96,128]{1,0:T(8,128)S(1)}, f32[128,128]{1,0:T(8,128)S(1)}, f32[128,128]{1,0:T(8,128)S(1)}, f32[32,128]{1,0:T(8,128)S(1)}) custom-call(s32[1]{0:T(128)} %bitcast.flag_ref, f32[32,128]{1,0:T(8,128)S(1)} %slice_add_fusion.4.refs_0_, f32[32,128]{1,0:T(8,128)S(1)} %collective-permute-done.3.refs_1_, ...), custom_call_target="tpu_custom_call" | custom-call | tf_op jit(solution)/shard_map/nonlocal_1/pallas_call | solution.py:557
  10.4 0.5 %collective-permute-start.6 = (f32[128,128]{1,0:T(8,128)S(1)}, f32[128,128]{1,0:T(8,128)S(1)}, u32[]{:S(2)}, u32[]{:S(2)}) collective-permute-start(f32[128,128]{1,0:T(8,128)S(1)} %get-tuple-element.40), channel_id=1, source_target_pairs={{0,24},{4,28},{8,16},{12,20},{16,8},{20,12},{24,0},{28,4},{1,25},{... | collective-permute-start | bytes 196616 | tf_op jit(solution)/shard_map/ppermute | solution.py:412
  10.9 0.5 %collective-permute-start.7 = (f32[128,128]{1,0:T(8,128)S(1)}, f32[128,128]{1,0:T(8,128)S(1)}, u32[]{:S(2)}, u32[]{:S(2)}) collective-permute-start(f32[128,128]{1,0:T(8,128)S(1)} %get-tuple-element.41), channel_id=1, source_target_pairs={{0,4},{4,0},{8,12},{12,8},{16,20},{20,16},{24,28},{28,24},{1,5},{5... | collective-permute-start | bytes 196616 | tf_op jit(solution)/shard_map/ppermute | solution.py:412
  11.4 2.0 %collective-permute-start.5 = (f32[32,128]{1,0:T(8,128)S(1)}, f32[32,128]{1,0:T(8,128)S(1)}, u32[]{:S(2)}, u32[]{:S(2)}) collective-permute-start(f32[32,128]{1,0:T(8,128)S(1)} %get-tuple-element.39), channel_id=1, source_target_pairs={{0,28},{4,24},{8,20},{12,16},{16,12},{20,8},{24,4},{28,0},{1,29},{... | collective-permute-start | bytes 49160 | tf_op jit(solution)/shard_map/ppermute | solution.py:412
  13.4 0.6 %collective-permute-start.9 = (f32[96,128]{1,0:T(8,128)S(1)}, f32[96,128]{1,0:T(8,128)S(1)}, u32[]{:S(2)}, u32[]{:S(2)}) collective-permute-start(f32[96,128]{1,0:T(8,128)S(1)} %get-tuple-element.42), channel_id=1, source_target_pairs={{0,8},{4,12},{8,0},{12,4},{16,24},{20,28},{24,16},{28,20},{1,9},{5... | collective-permute-start | bytes 147464 | tf_op jit(solution)/shard_map/ppermute | solution.py:412
  14.0 1.5 %collective-permute-done.5 = f32[32,128]{1,0:T(8,128)S(1)} collective-permute-done((f32[32,128]{1,0:T(8,128)S(1)}, f32[32,128]{1,0:T(8,128)S(1)}, u32[]{:S(2)}, u32[]{:S(2)}) %collective-permute-start.5) | collective-permute-done | bytes 16416 | tf_op jit(solution)/shard_map/ppermute | solution.py:412
  15.5 0.0 collective-permute-done.6.refs_1_
  15.5 0.0 collective-permute-done.7.refs_2_
  15.5 0.2 collective-permute-start.8
  15.7 0.0 collective-permute-done.9.refs_0_
  15.7 0.7 %local_2.1 = (f32[128,384]{1,0:T(8,128)S(1)}, f32[12,128]{1,0:T(8,128)S(1)}) custom-call(s32[1]{0:T(128)} %bitcast.flag_ref, f32[96,128]{1,0:T(8,128)S(1)} %collective-permute-done.9.refs_0_, f32[128,128]{1,0:T(8,128)S(1)} %collective-permute-done.6.refs_1_, f32[128,128]{1,0:T(8,128)S(1)} %collective-permute-done.7.refs_2_, f32[128,384]{1,0:T(8,128)S(1)} %bitcast.21, ...), custom_call_target="tpu_custom_call" | custom-call | tf_op jit(solution)/shard_map/local_2/pallas_call | solution.py:532
  16.3 0.4 collective-permute-done.8.refs_1_
  16.8 0.6 %nonlocal_2.1 = (f32[128,384]{1,0:T(8,128)S(1)}, f32[96,128]{1,0:T(8,128)S(1)}, f32[128,128]{1,0:T(8,128)S(1)}, f32[128,128]{1,0:T(8,128)S(1)}, f32[32,128]{1,0:T(8,128)S(1)}) custom-call(s32[1]{0:T(128)} %bitcast.flag_ref, f32[32,128]{1,0:T(8,128)S(1)} %slice_add_fusion.2.refs_0_, f32[32,128]{1,0:T(8,128)S(1)} %collective-permute-done.8.refs_1_, ...), custom_call_target="tpu_custom_call" | custom-call | tf_op jit(solution)/shard_map/nonlocal_2/pallas_call | solution.py:557
  17.4 1.3 %collective-permute-start.11 = (f32[128,128]{1,0:T(8,128)S(1)}, f32[128,128]{1,0:T(8,128)S(1)}, u32[]{:S(2)}, u32[]{:S(2)}) collective-permute-start(f32[128,128]{1,0:T(8,128)S(1)} %get-tuple-element.47), channel_id=1, source_target_pairs={{0,24},{4,28},{8,16},{12,20},{16,8},{20,12},{24,0},{28,4},{1,25},{... | collective-permute-start | bytes 196616 | tf_op jit(solution)/shard_map/ppermute | solution.py:412
  18.7 1.6 %collective-permute-start.12 = (f32[128,128]{1,0:T(8,128)S(1)}, f32[128,128]{1,0:T(8,128)S(1)}, u32[]{:S(2)}, u32[]{:S(2)}) collective-permute-start(f32[128,128]{1,0:T(8,128)S(1)} %get-tuple-element.48), channel_id=1, source_target_pairs={{0,4},{4,0},{8,12},{12,8},{16,20},{20,16},{24,28},{28,24},{1,5},{5... | collective-permute-start | bytes 196616 | tf_op jit(solution)/shard_map/ppermute | solution.py:412
  20.4 0.1 collective-permute-start.10
  20.4 0.4 collective-permute-start.13
  20.8 0.8 %collective-permute-done.10.refs_1_ = f32[96,128]{1,0:T(8,128)S(1)} collective-permute-done((f32[96,128]{1,0:T(8,128)S(1)}, f32[96,128]{1,0:T(8,128)S(1)}, u32[]{:S(2)}, u32[]{:S(2)}) %collective-permute-start.10) | collective-permute-done | bytes 49184 | tf_op jit(solution)/shard_map/ppermute | solution.py:412
  21.6 0.0 collective-permute-done.11.refs_2_
  21.6 1.5 %collective-permute-done.12.refs_3_ = f32[128,128]{1,0:T(8,128)S(1)} collective-permute-done((f32[128,128]{1,0:T(8,128)S(1)}, f32[128,128]{1,0:T(8,128)S(1)}, u32[]{:S(2)}, u32[]{:S(2)}) %collective-permute-start.12) | collective-permute-done | bytes 65568 | tf_op jit(solution)/shard_map/ppermute | solution.py:412
  23.1 0.4 local_3.1.refs_4_
  23.5 1.6 %collective-permute-start.15 = (f32[128,384]{1,0:T(8,128)S(1)}, f32[128,384]{1,0:T(8,128)S(1)}, u32[]{:S(2)}, u32[]{:S(2)}) collective-permute-start(f32[128,384]{1,0:T(8,128)S(1)} %local_3.1.refs_4_), channel_id=1, source_target_pairs={{0,1},{1,0},{2,3},{3,2},{4,5},{5,4},{6,7},{7,6},{8,9},{9,8},{10,11... | collective-permute-start | bytes 589832 | tf_op jit(solution)/shard_map/ppermute | solution.py:417
  25.1 0.0 collective-permute-done.13
  25.1 0.1 collective-permute-start.14
  25.2 1.2 %collective-permute-done.14 = f32[32,128]{1,0:T(8,128)S(1)} collective-permute-done((f32[32,128]{1,0:T(8,128)S(1)}, f32[32,128]{1,0:T(8,128)S(1)}, u32[]{:S(2)}, u32[]{:S(2)}) %collective-permute-start.14) | collective-permute-done | bytes 16416 | tf_op jit(solution)/shard_map/ppermute | solution.py:412
  26.4 1.0 %collective-permute-start.16 = (f32[32,128]{1,0:T(8,128)S(1)}, f32[32,128]{1,0:T(8,128)S(1)}, u32[]{:S(2)}, u32[]{:S(2)}) collective-permute-start(f32[32,128]{1,0:T(8,128)S(1)} %add.42.refs_5_), channel_id=1, source_target_pairs={{0,1},{1,0},{2,3},{3,2},{4,5},{5,4},{6,7},{7,6},{8,9},{9,8},{10,11... | collective-permute-start | bytes 49160 | tf_op jit(solution)/shard_map/ppermute | solution.py:417
  27.4 2.9 %collective-permute-done.16.refs_7_ = f32[32,128]{1,0:T(8,128)S(1)} collective-permute-done((f32[32,128]{1,0:T(8,128)S(1)}, f32[32,128]{1,0:T(8,128)S(1)}, u32[]{:S(2)}, u32[]{:S(2)}) %collective-permute-start.16) | collective-permute-done | bytes 16416 | tf_op jit(solution)/shard_map/ppermute | solution.py:417
  30.2 0.0 collective-permute-done.15.refs_6_
  30.3 0.7 %filtered.1 = f32[128,384]{1,0:T(8,128)S(1)} custom-call(f32[8,128]{1,0:T(8,128)S(1)} %get-tuple-element.28.refs_0_.cheb_ref, f32[32,128]{1,0:T(8,128)S(1)} %bitcast.25, bf16[512,384]{1,0:T(8,128)(2,1)S(1)} %bitcast.15, f32[12,128]{1,0:T(8,128)S(1)} %get-tuple-element.29.after_ref.refs_5_.refs_2_, bf16[128,1536]{1,0:T(8,128)(2,1)S(1)} %get-tuple-element.30.refs_6_.refs_3_, ...), custom_call_target="tpu_custom_call" | custom-call | tf_op jit(solution)/shard_map/filtered/pallas_call | solution.py:546
  31.0 0.5 %collective-permute-start.17 = (f32[128,384]{1,0:T(8,128)S(1)}, f32[128,384]{1,0:T(8,128)S(1)}, u32[]{:S(2)}, u32[]{:S(2)}) collective-permute-start(f32[128,384]{1,0:T(8,128)S(1)} %filtered.1), channel_id=1, source_target_pairs={{0,3},{1,2},{2,1},{3,0},{4,7},{5,6},{6,5},{7,4},{8,11},{9,10},{10,... | collective-permute-start | bytes 589832 | tf_op jit(solution)/shard_map/ppermute | solution.py:417
  31.5 10.0 %collective-permute-done.17 = f32[128,384]{1,0:T(8,128)S(1)} collective-permute-done((f32[128,384]{1,0:T(8,128)S(1)}, f32[128,384]{1,0:T(8,128)S(1)}, u32[]{:S(2)}, u32[]{:S(2)}) %collective-permute-start.17) | collective-permute-done | bytes 196640 | tf_op jit(solution)/shard_map/ppermute | solution.py:417
  41.5 0.7 %add_multiply_fusion = f32[128,384]{1,0:T(8,128)} fusion(f32[128,384]{1,0:T(8,128)S(1)} %filtered.1, f32[128,384]{1,0:T(8,128)S(1)} %collective-permute-done.17), kind=kLoop, calls=%fused_computation | loop fusion | flops 98304 | bytes 589824 | tf_op jit(solution)/shard_map/mul | solution.py:576
  (9 shorter events, 0.0 us)
Async XLA Ops:
  0.0 5.0 %copy-start = (bf16[4,8,16,384]{3,2,1,0:T(8,128)(2,1)S(1)}, bf16[4,8,16,384]{3,2,1,0:T(8,128)(2,1)}, u32[]{:S(2)}) copy-start(bf16[4,8,16,384]{3,2,1,0:T(8,128)(2,1)} %param.8) | copy-start | bytes 1179652
  1.8 6.6 %collective-permute-start.1 = (f32[128,128]{1,0:T(8,128)S(1)}, f32[128,128]{1,0:T(8,128)S(1)}, u32[]{:S(2)}, u32[]{:S(2)}) collective-permute-start(f32[128,128]{1,0:T(8,128)S(1)} %get-tuple-element.33), channel_id=1, source_target_pairs={{0,24},{4,28},{8,16},{12,20},{16,8},{20,12},{24,0},{28,4},{1,25},{... | collective-permute-start | bytes 196616 | tf_op jit(solution)/shard_map/ppermute | solution.py:412
  2.8 5.6 %collective-permute-start.2 = (f32[128,128]{1,0:T(8,128)S(1)}, f32[128,128]{1,0:T(8,128)S(1)}, u32[]{:S(2)}, u32[]{:S(2)}) collective-permute-start(f32[128,128]{1,0:T(8,128)S(1)} %get-tuple-element.34), channel_id=1, source_target_pairs={{0,4},{4,0},{8,12},{12,8},{16,20},{20,16},{24,28},{28,24},{1,5},{5... | collective-permute-start | bytes 196616 | tf_op jit(solution)/shard_map/ppermute | solution.py:412
  4.3 4.1 %collective-permute-start = (f32[32,128]{1,0:T(8,128)S(1)}, f32[32,128]{1,0:T(8,128)S(1)}, u32[]{:S(2)}, u32[]{:S(2)}) collective-permute-start(f32[32,128]{1,0:T(8,128)S(1)} %get-tuple-element.31), channel_id=1, source_target_pairs={{0,28},{4,24},{8,20},{12,16},{16,12},{20,8},{24,4},{28,0},{1,29},{... | collective-permute-start | bytes 49160 | tf_op jit(solution)/shard_map/ppermute | solution.py:412
  4.8 4.1 %collective-permute-start.4 = (f32[96,128]{1,0:T(8,128)S(1)}, f32[96,128]{1,0:T(8,128)S(1)}, u32[]{:S(2)}, u32[]{:S(2)}) collective-permute-start(f32[96,128]{1,0:T(8,128)S(1)} %get-tuple-element.35), channel_id=1, source_target_pairs={{0,8},{4,12},{8,0},{12,4},{16,24},{20,28},{24,16},{28,20},{1,9},{5... | collective-permute-start | bytes 147464 | tf_op jit(solution)/shard_map/ppermute | solution.py:412
  5.0 3.9 %copy-start.1 = (f32[1,8,16,384]{3,2,1,0:T(8,128)S(1)}, f32[1,8,16,384]{3,2,1,0:T(8,128)}, u32[]{:S(2)}) copy-start(f32[1,8,16,384]{3,2,1,0:T(8,128)} %param.6) | copy-start | bytes 589828
  5.0 3.9 %copy-start.2 = (f32[8,16,384]{2,1,0:T(8,128)S(1)}, f32[8,16,384]{2,1,0:T(8,128)}, u32[]{:S(2)}) copy-start(f32[8,16,384]{2,1,0:T(8,128)} %param.7) | copy-start | bytes 589828
  8.4 1.3 %collective-permute-start.3 = (f32[32,128]{1,0:T(8,128)S(1)}, f32[32,128]{1,0:T(8,128)S(1)}, u32[]{:S(2)}, u32[]{:S(2)}) collective-permute-start(f32[32,128]{1,0:T(8,128)S(1)} %slice_add_fusion.4.refs_0_), channel_id=1, source_target_pairs={{0,8},{4,12},{8,0},{12,4},{16,24},{20,28},{24,16},{28,20},{1,9},{5... | collective-permute-start | bytes 49160 | tf_op jit(solution)/shard_map/ppermute | solution.py:412
  8.9 0.8 %copy-start.3 = (f32[4096]{0:T(1024)S(1)}, f32[4096]{0:T(1024)}, u32[]{:S(2)}) copy-start(f32[4096]{0:T(1024)} %param.10) | copy-start | bytes 49156
  10.4 5.1 %collective-permute-start.6 = (f32[128,128]{1,0:T(8,128)S(1)}, f32[128,128]{1,0:T(8,128)S(1)}, u32[]{:S(2)}, u32[]{:S(2)}) collective-permute-start(f32[128,128]{1,0:T(8,128)S(1)} %get-tuple-element.40), channel_id=1, source_target_pairs={{0,24},{4,28},{8,16},{12,20},{16,8},{20,12},{24,0},{28,4},{1,25},{... | collective-permute-start | bytes 196616 | tf_op jit(solution)/shard_map/ppermute | solution.py:412
  10.9 4.6 %collective-permute-start.7 = (f32[128,128]{1,0:T(8,128)S(1)}, f32[128,128]{1,0:T(8,128)S(1)}, u32[]{:S(2)}, u32[]{:S(2)}) collective-permute-start(f32[128,128]{1,0:T(8,128)S(1)} %get-tuple-element.41), channel_id=1, source_target_pairs={{0,4},{4,0},{8,12},{12,8},{16,20},{20,16},{24,28},{28,24},{1,5},{5... | collective-permute-start | bytes 196616 | tf_op jit(solution)/shard_map/ppermute | solution.py:412
  11.4 4.1 %collective-permute-start.5 = (f32[32,128]{1,0:T(8,128)S(1)}, f32[32,128]{1,0:T(8,128)S(1)}, u32[]{:S(2)}, u32[]{:S(2)}) collective-permute-start(f32[32,128]{1,0:T(8,128)S(1)} %get-tuple-element.39), channel_id=1, source_target_pairs={{0,28},{4,24},{8,20},{12,16},{16,12},{20,8},{24,4},{28,0},{1,29},{... | collective-permute-start | bytes 49160 | tf_op jit(solution)/shard_map/ppermute | solution.py:412
  13.4 2.3 %collective-permute-start.9 = (f32[96,128]{1,0:T(8,128)S(1)}, f32[96,128]{1,0:T(8,128)S(1)}, u32[]{:S(2)}, u32[]{:S(2)}) collective-permute-start(f32[96,128]{1,0:T(8,128)S(1)} %get-tuple-element.42), channel_id=1, source_target_pairs={{0,8},{4,12},{8,0},{12,4},{16,24},{20,28},{24,16},{28,20},{1,9},{5... | collective-permute-start | bytes 147464 | tf_op jit(solution)/shard_map/ppermute | solution.py:412
  15.5 1.2 %collective-permute-start.8 = (f32[32,128]{1,0:T(8,128)S(1)}, f32[32,128]{1,0:T(8,128)S(1)}, u32[]{:S(2)}, u32[]{:S(2)}) collective-permute-start(f32[32,128]{1,0:T(8,128)S(1)} %slice_add_fusion.2.refs_0_), channel_id=1, source_target_pairs={{0,8},{4,12},{8,0},{12,4},{16,24},{20,28},{24,16},{28,20},{1,9},{5... | collective-permute-start | bytes 49160 | tf_op jit(solution)/shard_map/ppermute | solution.py:412
  17.4 4.2 %collective-permute-start.11 = (f32[128,128]{1,0:T(8,128)S(1)}, f32[128,128]{1,0:T(8,128)S(1)}, u32[]{:S(2)}, u32[]{:S(2)}) collective-permute-start(f32[128,128]{1,0:T(8,128)S(1)} %get-tuple-element.47), channel_id=1, source_target_pairs={{0,24},{4,28},{8,16},{12,20},{16,8},{20,12},{24,0},{28,4},{1,25},{... | collective-permute-start | bytes 196616 | tf_op jit(solution)/shard_map/ppermute | solution.py:412
  18.7 4.3 %collective-permute-start.12 = (f32[128,128]{1,0:T(8,128)S(1)}, f32[128,128]{1,0:T(8,128)S(1)}, u32[]{:S(2)}, u32[]{:S(2)}) collective-permute-start(f32[128,128]{1,0:T(8,128)S(1)} %get-tuple-element.48), channel_id=1, source_target_pairs={{0,4},{4,0},{8,12},{12,8},{16,20},{20,16},{24,28},{28,24},{1,5},{5... | collective-permute-start | bytes 196616 | tf_op jit(solution)/shard_map/ppermute | solution.py:412
  20.4 1.2 %collective-permute-start.10 = (f32[96,128]{1,0:T(8,128)S(1)}, f32[96,128]{1,0:T(8,128)S(1)}, u32[]{:S(2)}, u32[]{:S(2)}) collective-permute-start(f32[96,128]{1,0:T(8,128)S(1)} %get-tuple-element.46), channel_id=1, source_target_pairs={{0,8},{4,12},{8,0},{12,4},{16,24},{20,28},{24,16},{28,20},{1,9},{5... | collective-permute-start | bytes 147464 | tf_op jit(solution)/shard_map/ppermute | solution.py:412
  20.4 4.7 %collective-permute-start.13 = (f32[32,128]{1,0:T(8,128)S(1)}, f32[32,128]{1,0:T(8,128)S(1)}, u32[]{:S(2)}, u32[]{:S(2)}) collective-permute-start(f32[32,128]{1,0:T(8,128)S(1)} %get-tuple-element.50), channel_id=1, source_target_pairs={{0,28},{4,24},{8,20},{12,16},{16,12},{20,8},{24,4},{28,0},{1,29},{... | collective-permute-start | bytes 49160 | tf_op jit(solution)/shard_map/ppermute | solution.py:412
  23.5 6.8 %collective-permute-start.15 = (f32[128,384]{1,0:T(8,128)S(1)}, f32[128,384]{1,0:T(8,128)S(1)}, u32[]{:S(2)}, u32[]{:S(2)}) collective-permute-start(f32[128,384]{1,0:T(8,128)S(1)} %local_3.1.refs_4_), channel_id=1, source_target_pairs={{0,1},{1,0},{2,3},{3,2},{4,5},{5,4},{6,7},{7,6},{8,9},{9,8},{10,11... | collective-permute-start | bytes 589832 | tf_op jit(solution)/shard_map/ppermute | solution.py:417
  25.1 1.2 %collective-permute-start.14 = (f32[32,128]{1,0:T(8,128)S(1)}, f32[32,128]{1,0:T(8,128)S(1)}, u32[]{:S(2)}, u32[]{:S(2)}) collective-permute-start(f32[32,128]{1,0:T(8,128)S(1)} %slice_add_fusion), channel_id=1, source_target_pairs={{0,8},{4,12},{8,0},{12,4},{16,24},{20,28},{24,16},{28,20},{1,9},{5... | collective-permute-start | bytes 49160 | tf_op jit(solution)/shard_map/ppermute | solution.py:412
  26.4 3.9 %collective-permute-start.16 = (f32[32,128]{1,0:T(8,128)S(1)}, f32[32,128]{1,0:T(8,128)S(1)}, u32[]{:S(2)}, u32[]{:S(2)}) collective-permute-start(f32[32,128]{1,0:T(8,128)S(1)} %add.42.refs_5_), channel_id=1, source_target_pairs={{0,1},{1,0},{2,3},{3,2},{4,5},{5,4},{6,7},{7,6},{8,9},{9,8},{10,11... | collective-permute-start | bytes 49160 | tf_op jit(solution)/shard_map/ppermute | solution.py:417
  31.0 10.5 %collective-permute-start.17 = (f32[128,384]{1,0:T(8,128)S(1)}, f32[128,384]{1,0:T(8,128)S(1)}, u32[]{:S(2)}, u32[]{:S(2)}) collective-permute-start(f32[128,384]{1,0:T(8,128)S(1)} %filtered.1), channel_id=1, source_target_pairs={{0,3},{1,2},{2,1},{3,0},{4,7},{5,6},{6,5},{7,4},{8,11},{9,10},{10,... | collective-permute-start | bytes 589832 | tf_op jit(solution)/shard_map/ppermute | solution.py:417

commit v8 on v7

--- a/solution.py
+++ b/solution.py
@@ -349,20 +349,16 @@
     emit(sz, result, table, flag_ref, *refs[1:])
 
 
-def last_kernel(sz, n_orbitals, n_tables, cheb_ref, *refs):
+def last_kernel(sz, n_tables, n_before, cheb_ref, *refs):
     refs = list(refs)
-    energy_ref, pv_ref, rows_ref, hot_ref = (refs.pop(0) for _ in range(4))
-    scale = energy_ref[...] * (2.0 / E_HALF * cheb_ref[STEPS : STEPS + 1, :])
-    rests, tables = [], []
-    for _ in range(n_orbitals):
-        rests.append(refs.pop(0))
-        tables.append(added([refs.pop(0) for _ in range(n_tables)]) * scale)
-    total = None
-    parts, _ = projected(sz, tables, pv_ref, rows_ref[...], hot_ref)
-    for rest_ref, part in zip(rests, parts):
-        filtered = rest_ref[...] + part
-        squared = filtered * filtered
-        total = squared if total is None else total + squared
+    energy_ref, pv_ref, rows_ref, hot_ref, rest_ref = (refs.pop(0) for _ in range(5))
+    table = added([refs.pop(0) for _ in range(n_tables)])
+    table = table * (energy_ref[...] * (2.0 / E_HALF * cheb_ref[STEPS : STEPS + 1, :]))
+    (part,), _ = projected(sz, [table], pv_ref, rows_ref[...], hot_ref)
+    filtered = rest_ref[...] + part
+    total = filtered * filtered
+    for _ in range(n_before):
+        total = total + refs.pop(0)[...]
     refs[0][...] = total
 
 
@@ -487,6 +483,17 @@
                 )
             table = total
         return [table], from_a, from_b, [below, above], aside
+
+    def square(cheb, row_of, hot, rest, tables, *before):
+        args = (cheb, energy, pv, row_of, hot, rest, *tables, *before)
+        return pl.pallas_call(
+            functools.partial(last_kernel, sz, len(tables), len(before)),
+            out_shape=field,
+            in_specs=vmem(len(args)),
+            out_specs=vmem(1)[0],
+            compiler_params=params,
+            name="square_more" if before else "square",
+        )(*args)
 
     def one_orbital(start):
         *messages, row_of, hot, cheb = pl.pallas_call(
@@ -538,21 +545,12 @@
                 name=f"local_{degree}",
             )(flag, *args)
             if last:
-                orbitals_here = [(rest, *tables)]
-                if paired:
-                    total = functools.reduce(jnp.add, tables)
-                    orbitals_here = [(rest, total), (orb_swap(rest, 1), orb_swap(total, 1))]
-                args = (cheb, energy, pv, row_of, hot, *sum(orbitals_here, ()))
-                return pl.pallas_call(
-                    functools.partial(
-                        last_kernel, sz, len(orbitals_here), len(orbitals_here[0]) - 1
-                    ),
-                    out_shape=field,
-                    in_specs=vmem(len(args)),
-                    out_specs=vmem(1)[0],
-                    compiler_params=params,
-                    name="filtered",
-                )(*args)
+                if not paired:
+                    return square(cheb, row_of, hot, rest, tables)
+                total = functools.reduce(jnp.add, tables)
+                other, other_total = orb_swap(rest, 1), orb_swap(total, 1)
+                own = square(cheb, row_of, hot, rest, [total])
+                return square(cheb, row_of, hot, other, [other_total], own)
             args = (*tables, energy, rest, pv, row_of, hot, *sums, overlap)
             out = pl.pallas_call(
                 functools.partial(nonlocal_kernel, sz, degree, len(tables)),

time: 42.5 us -> 42.3 us (level)
  waiting for transfers between devices: 21.1 us -> 20.6 us
    ppermute x3, waiting for transfers between devices: 12.9 us -> 12.3 us  [orb_swap(): return lax.ppermute(vals, 'orb', [(i, i ^ bit) for i in range(size)])]
    pallas_call x1 -> x2, Pallas kernels: 0.73 us -> 1.06 us  [square(): pl.pallas_call(functools.partial(last_kernel, sz, len(tables), len(before...]
  transfers between devices with their start and end apart: 18 -> 18, of which waited for: 9 -> 9; matrix products, arithmetic and copies ran while one was open for 0% -> 0% of each run, Pallas kernels for 5% -> 7%
where the time goes in v8:
time: 42.3 us; the launch traced here: 42 us
  waiting for transfers between devices  20.6 us (49%)
  starting transfers between devices  14.1 us (33%)
  Pallas kernels  6.4 us (15%)
  other arithmetic  0.73 us (2%)
    ppermute x3, waiting for transfers between devices, orb_swap(): return lax.ppermute(vals, 'orb', [(i, i ^ bit) for i in range(size)])  12.3 us
    ppermute x15, starting transfers between devices, swap(): return lax.ppermute(arr, ('gx', 'gy'), pairs)  11 us
    ppermute x15, waiting for transfers between devices, swap(): return lax.ppermute(arr, ('gx', 'gy'), pairs)  8.26 us
    ppermute x3, starting transfers between devices, orb_swap(): return lax.ppermute(vals, 'orb', [(i, i ^ bit) for i in range(size)])  3.12 us
    pallas_call x1, Pallas kernels, one_orbital(): pl.pallas_call(functools.partial(first_kernel, sz), out_shape=message_sha...  1.8 us
    pallas_call x3, Pallas kernels, one_orbital(): pl.pallas_call(functools.partial(local_kernel, sz, degree, len(from_y)),...  1.7 us
    pallas_call x2, Pallas kernels, one_orbital(): pl.pallas_call(functools.partial(nonlocal_kernel, sz, degree, len(tables)...  1.26 us
    pallas_call x2, Pallas kernels, square(): pl.pallas_call(functools.partial(last_kernel, sz, len(tables), len(before...  1.06 us
  transfers between devices with their start and end apart: 18, of which 9 were waited for; matrix products, arithmetic and copies ran while one was open for 0% of the time, Pallas kernels for 7%

profile of v8, /device:TPU:16, one launch (start us, length us, event | category | flops | bytes accessed | tf_op | source)
XLA Modules:
  0.0 42.0 jit_solution(6258398000136034748)
XLA Ops:
  0.0 1.8 %project_first.1 = (f32[96,128]{1,0:T(8,128)S(1)}, f32[128,128]{1,0:T(8,128)S(1)}, f32[128,128]{1,0:T(8,128)S(1)}, f32[32,128]{1,0:T(8,128)S(1)}, f32[12,128]{1,...) custom-call(s32[1]{0:T(128)} %bitcast.flag_ref, f32[128,384]{1,0:T(8,128)} %bitcast.17, ...), custom_call_target="tpu_custom_call" | custom-call | tf_op jit(solution)/shard_map/project_first/pallas_call | solution.py:499
  1.8 1.0 %collective-permute-start.1 = (f32[128,128]{1,0:T(8,128)S(1)}, f32[128,128]{1,0:T(8,128)S(1)}, u32[]{:S(2)}, u32[]{:S(2)}) collective-permute-start(f32[128,128]{1,0:T(8,128)S(1)} %get-tuple-element.33), channel_id=1, source_target_pairs={{0,24},{4,28},{8,16},{12,20},{16,8},{20,12},{24,0},{28,4},{1,25},{... | collective-permute-start | bytes 196616 | tf_op jit(solution)/shard_map/ppermute | solution.py:408
  2.8 1.5 %collective-permute-start.2 = (f32[128,128]{1,0:T(8,128)S(1)}, f32[128,128]{1,0:T(8,128)S(1)}, u32[]{:S(2)}, u32[]{:S(2)}) collective-permute-start(f32[128,128]{1,0:T(8,128)S(1)} %get-tuple-element.34), channel_id=1, source_target_pairs={{0,4},{4,0},{8,12},{12,8},{16,20},{20,16},{24,28},{28,24},{1,5},{5... | collective-permute-start | bytes 196616 | tf_op jit(solution)/shard_map/ppermute | solution.py:408
  4.3 0.5 %collective-permute-start = (f32[32,128]{1,0:T(8,128)S(1)}, f32[32,128]{1,0:T(8,128)S(1)}, u32[]{:S(2)}, u32[]{:S(2)}) collective-permute-start(f32[32,128]{1,0:T(8,128)S(1)} %get-tuple-element.31), channel_id=1, source_target_pairs={{0,28},{4,24},{8,20},{12,16},{16,12},{20,8},{24,4},{28,0},{1,29},{... | collective-permute-start | bytes 49160 | tf_op jit(solution)/shard_map/ppermute | solution.py:408
  4.8 0.2 collective-permute-start.4
  5.0 0.0 copy-done
  5.0 0.6 %overlap.1.refs_8_ = f32[48,128]{1,0:T(8,128)S(1)} custom-call(f32[12,128]{1,0:T(8,128)S(1)} %get-tuple-element.29.after_ref.refs_5_.refs_2_, bf16[512,384]{1,0:T(8,128)(2,1)S(1)} %bitcast.10), custom_call_target="tpu_custom_call" | custom-call | tf_op jit(solution)/shard_map/overlap/pallas_call | solution.py:519
  5.6 2.8 %collective-permute-done = f32[32,128]{1,0:T(8,128)S(1)} collective-permute-done((f32[32,128]{1,0:T(8,128)S(1)}, f32[32,128]{1,0:T(8,128)S(1)}, u32[]{:S(2)}, u32[]{:S(2)}) %collective-permute-start) | collective-permute-done | bytes 16416 | tf_op jit(solution)/shard_map/ppermute | solution.py:408
  8.4 0.0 collective-permute-done.1.refs_1_
  8.4 0.0 collective-permute-done.2.refs_2_
  8.4 0.5 %collective-permute-start.3 = (f32[32,128]{1,0:T(8,128)S(1)}, f32[32,128]{1,0:T(8,128)S(1)}, u32[]{:S(2)}, u32[]{:S(2)}) collective-permute-start(f32[32,128]{1,0:T(8,128)S(1)} %slice_add_fusion.4.refs_0_), channel_id=1, source_target_pairs={{0,8},{4,12},{8,0},{12,4},{16,24},{20,28},{24,16},{28,20},{1,9},{5... | collective-permute-start | bytes 49160 | tf_op jit(solution)/shard_map/ppermute | solution.py:408
  8.9 0.0 collective-permute-done.4.refs_0_
  8.9 0.0 copy-start.3
  8.9 0.6 %local_1.1 = (f32[128,384]{1,0:T(8,128)S(1)}, f32[12,128]{1,0:T(8,128)S(1)}) custom-call(s32[1]{0:T(128)} %bitcast.flag_ref, f32[96,128]{1,0:T(8,128)S(1)} %collective-permute-done.4.refs_0_, f32[128,128]{1,0:T(8,128)S(1)} %collective-permute-done.1.refs_1_, f32[128,128]{1,0:T(8,128)S(1)} %collective-permute-done.2.refs_2_, f32[128,384]{1,0:T(8,128)S(1)} %bitcast.21, ...), custom_call_target="tpu_custom_call" | custom-call | tf_op jit(solution)/shard_map/local_1/pallas_call | solution.py:539
  9.6 0.2 collective-permute-done.3.refs_1_
  9.7 0.6 %nonlocal_1.1 = (f32[128,384]{1,0:T(8,128)S(1)}, f32[96,128]{1,0:T(8,128)S(1)}, f32[128,128]{1,0:T(8,128)S(1)}, f32[128,128]{1,0:T(8,128)S(1)}, f32[32,128]{1,0:T(8,128)S(1)}) custom-call(s32[1]{0:T(128)} %bitcast.flag_ref, f32[32,128]{1,0:T(8,128)S(1)} %slice_add_fusion.4.refs_0_, f32[32,128]{1,0:T(8,128)S(1)} %collective-permute-done.3.refs_1_, ...), custom_call_target="tpu_custom_call" | custom-call | tf_op jit(solution)/shard_map/nonlocal_1/pallas_call | solution.py:555
  10.4 0.5 %collective-permute-start.6 = (f32[128,128]{1,0:T(8,128)S(1)}, f32[128,128]{1,0:T(8,128)S(1)}, u32[]{:S(2)}, u32[]{:S(2)}) collective-permute-start(f32[128,128]{1,0:T(8,128)S(1)} %get-tuple-element.40), channel_id=1, source_target_pairs={{0,24},{4,28},{8,16},{12,20},{16,8},{20,12},{24,0},{28,4},{1,25},{... | collective-permute-start | bytes 196616 | tf_op jit(solution)/shard_map/ppermute | solution.py:408
  10.9 0.5 %collective-permute-start.7 = (f32[128,128]{1,0:T(8,128)S(1)}, f32[128,128]{1,0:T(8,128)S(1)}, u32[]{:S(2)}, u32[]{:S(2)}) collective-permute-start(f32[128,128]{1,0:T(8,128)S(1)} %get-tuple-element.41), channel_id=1, source_target_pairs={{0,4},{4,0},{8,12},{12,8},{16,20},{20,16},{24,28},{28,24},{1,5},{5... | collective-permute-start | bytes 196616 | tf_op jit(solution)/shard_map/ppermute | solution.py:408
  11.4 2.0 %collective-permute-start.5 = (f32[32,128]{1,0:T(8,128)S(1)}, f32[32,128]{1,0:T(8,128)S(1)}, u32[]{:S(2)}, u32[]{:S(2)}) collective-permute-start(f32[32,128]{1,0:T(8,128)S(1)} %get-tuple-element.39), channel_id=1, source_target_pairs={{0,28},{4,24},{8,20},{12,16},{16,12},{20,8},{24,4},{28,0},{1,29},{... | collective-permute-start | bytes 49160 | tf_op jit(solution)/shard_map/ppermute | solution.py:408
  13.4 0.6 %collective-permute-start.9 = (f32[96,128]{1,0:T(8,128)S(1)}, f32[96,128]{1,0:T(8,128)S(1)}, u32[]{:S(2)}, u32[]{:S(2)}) collective-permute-start(f32[96,128]{1,0:T(8,128)S(1)} %get-tuple-element.42), channel_id=1, source_target_pairs={{0,8},{4,12},{8,0},{12,4},{16,24},{20,28},{24,16},{28,20},{1,9},{5... | collective-permute-start | bytes 147464 | tf_op jit(solution)/shard_map/ppermute | solution.py:408
  14.0 1.5 %collective-permute-done.5 = f32[32,128]{1,0:T(8,128)S(1)} collective-permute-done((f32[32,128]{1,0:T(8,128)S(1)}, f32[32,128]{1,0:T(8,128)S(1)}, u32[]{:S(2)}, u32[]{:S(2)}) %collective-permute-start.5) | collective-permute-done | bytes 16416 | tf_op jit(solution)/shard_map/ppermute | solution.py:408
  15.5 0.0 collective-permute-done.6.refs_1_
  15.5 0.0 collective-permute-done.7.refs_2_
  15.5 0.2 collective-permute-start.8
  15.7 0.0 collective-permute-done.9.refs_0_
  15.7 0.7 %local_2.1 = (f32[128,384]{1,0:T(8,128)S(1)}, f32[12,128]{1,0:T(8,128)S(1)}) custom-call(s32[1]{0:T(128)} %bitcast.flag_ref, f32[96,128]{1,0:T(8,128)S(1)} %collective-permute-done.9.refs_0_, f32[128,128]{1,0:T(8,128)S(1)} %collective-permute-done.6.refs_1_, f32[128,128]{1,0:T(8,128)S(1)} %collective-permute-done.7.refs_2_, f32[128,384]{1,0:T(8,128)S(1)} %bitcast.22, ...), custom_call_target="tpu_custom_call" | custom-call | tf_op jit(solution)/shard_map/local_2/pallas_call | solution.py:539
  16.4 0.4 collective-permute-done.8.refs_1_
  16.8 0.6 %nonlocal_2.1 = (f32[128,384]{1,0:T(8,128)S(1)}, f32[96,128]{1,0:T(8,128)S(1)}, f32[128,128]{1,0:T(8,128)S(1)}, f32[128,128]{1,0:T(8,128)S(1)}, f32[32,128]{1,0:T(8,128)S(1)}) custom-call(s32[1]{0:T(128)} %bitcast.flag_ref, f32[32,128]{1,0:T(8,128)S(1)} %slice_add_fusion.2.refs_0_, f32[32,128]{1,0:T(8,128)S(1)} %collective-permute-done.8.refs_1_, ...), custom_call_target="tpu_custom_call" | custom-call | tf_op jit(solution)/shard_map/nonlocal_2/pallas_call | solution.py:555
  17.4 1.3 %collective-permute-start.11 = (f32[128,128]{1,0:T(8,128)S(1)}, f32[128,128]{1,0:T(8,128)S(1)}, u32[]{:S(2)}, u32[]{:S(2)}) collective-permute-start(f32[128,128]{1,0:T(8,128)S(1)} %get-tuple-element.47), channel_id=1, source_target_pairs={{0,24},{4,28},{8,16},{12,20},{16,8},{20,12},{24,0},{28,4},{1,25},{... | collective-permute-start | bytes 196616 | tf_op jit(solution)/shard_map/ppermute | solution.py:408
  18.7 1.6 %collective-permute-start.12 = (f32[128,128]{1,0:T(8,128)S(1)}, f32[128,128]{1,0:T(8,128)S(1)}, u32[]{:S(2)}, u32[]{:S(2)}) collective-permute-start(f32[128,128]{1,0:T(8,128)S(1)} %get-tuple-element.48), channel_id=1, source_target_pairs={{0,4},{4,0},{8,12},{12,8},{16,20},{20,16},{24,28},{28,24},{1,5},{5... | collective-permute-start | bytes 196616 | tf_op jit(solution)/shard_map/ppermute | solution.py:408
  20.3 0.1 collective-permute-start.10
  20.4 0.4 %collective-permute-start.14 = (f32[32,128]{1,0:T(8,128)S(1)}, f32[32,128]{1,0:T(8,128)S(1)}, u32[]{:S(2)}, u32[]{:S(2)}) collective-permute-start(f32[32,128]{1,0:T(8,128)S(1)} %get-tuple-element.50), channel_id=1, source_target_pairs={{0,28},{4,24},{8,20},{12,16},{16,12},{20,8},{24,4},{28,0},{1,29},{... | collective-permute-start | bytes 49160 | tf_op jit(solution)/shard_map/ppermute | solution.py:408
  20.8 0.7 %collective-permute-done.10.refs_1_ = f32[96,128]{1,0:T(8,128)S(1)} collective-permute-done((f32[96,128]{1,0:T(8,128)S(1)}, f32[96,128]{1,0:T(8,128)S(1)}, u32[]{:S(2)}, u32[]{:S(2)}) %collective-permute-start.10) | collective-permute-done | bytes 49184 | tf_op jit(solution)/shard_map/ppermute | solution.py:408
  21.6 0.0 collective-permute-done.11.refs_2_
  21.6 1.5 %collective-permute-done.12.refs_3_ = f32[128,128]{1,0:T(8,128)S(1)} collective-permute-done((f32[128,128]{1,0:T(8,128)S(1)}, f32[128,128]{1,0:T(8,128)S(1)}, u32[]{:S(2)}, u32[]{:S(2)}) %collective-permute-start.12) | collective-permute-done | bytes 65568 | tf_op jit(solution)/shard_map/ppermute | solution.py:408
  23.1 0.4 local_3.1.refs_4_
  23.5 1.6 %collective-permute-start.13 = (f32[128,384]{1,0:T(8,128)S(1)}, f32[128,384]{1,0:T(8,128)S(1)}, u32[]{:S(2)}, u32[]{:S(2)}) collective-permute-start(f32[128,384]{1,0:T(8,128)S(1)} %local_3.1.refs_4_), channel_id=1, source_target_pairs={{0,1},{1,0},{2,3},{3,2},{4,5},{5,4},{6,7},{7,6},{8,9},{9,8},{10,11... | collective-permute-start | bytes 589832 | tf_op jit(solution)/shard_map/ppermute | solution.py:413
  25.1 0.0 collective-permute-done.14
  25.1 0.1 collective-permute-start.15
  25.2 1.2 %collective-permute-done.15 = f32[32,128]{1,0:T(8,128)S(1)} collective-permute-done((f32[32,128]{1,0:T(8,128)S(1)}, f32[32,128]{1,0:T(8,128)S(1)}, u32[]{:S(2)}, u32[]{:S(2)}) %collective-permute-start.15) | collective-permute-done | bytes 16416 | tf_op jit(solution)/shard_map/ppermute | solution.py:408
  26.4 1.0 %collective-permute-start.16 = (f32[32,128]{1,0:T(8,128)S(1)}, f32[32,128]{1,0:T(8,128)S(1)}, u32[]{:S(2)}, u32[]{:S(2)}) collective-permute-start(f32[32,128]{1,0:T(8,128)S(1)} %add.42.refs_5_), channel_id=1, source_target_pairs={{0,1},{1,0},{2,3},{3,2},{4,5},{5,4},{6,7},{7,6},{8,9},{9,8},{10,11... | collective-permute-start | bytes 49160 | tf_op jit(solution)/shard_map/ppermute | solution.py:413
  27.4 0.5 %square.1.refs_6_ = f32[128,384]{1,0:T(8,128)S(1)} custom-call(f32[8,128]{1,0:T(8,128)S(1)} %get-tuple-element.28.refs_0_.cheb_ref, f32[32,128]{1,0:T(8,128)S(1)} %bitcast.26, bf16[512,384]{1,0:T(8,128)(2,1)S(1)} %bitcast.15, f32[12,128]{1,0:T(8,128)S(1)} %get-tuple-element.29.after_ref.refs_5_.refs_2_, ...), custom_call_target="tpu_custom_call" | custom-call | tf_op jit(solution)/shard_map/square/pallas_call | solution.py:489
  27.9 2.4 %collective-permute-done.16.refs_5_ = f32[32,128]{1,0:T(8,128)S(1)} collective-permute-done((f32[32,128]{1,0:T(8,128)S(1)}, f32[32,128]{1,0:T(8,128)S(1)}, u32[]{:S(2)}, u32[]{:S(2)}) %collective-permute-start.16) | collective-permute-done | bytes 16416 | tf_op jit(solution)/shard_map/ppermute | solution.py:413
  30.2 0.0 collective-permute-done.13.refs_4_
  30.3 0.5 %square_more.1 = f32[128,384]{1,0:T(8,128)S(1)} custom-call(f32[8,128]{1,0:T(8,128)S(1)} %get-tuple-element.28.refs_0_.cheb_ref, f32[32,128]{1,0:T(8,128)S(1)} %bitcast.27, bf16[512,384]{1,0:T(8,128)(2,1)S(1)} %bitcast.16, f32[12,128]{1,0:T(8,128)S(1)} %get-tuple-element.29.after_ref.refs_5_.refs_2_, ...), custom_call_target="tpu_custom_call" | custom-call | tf_op jit(solution)/shard_map/square_more/pallas_call | solution.py:489
  30.8 0.5 %collective-permute-start.17 = (f32[128,384]{1,0:T(8,128)S(1)}, f32[128,384]{1,0:T(8,128)S(1)}, u32[]{:S(2)}, u32[]{:S(2)}) collective-permute-start(f32[128,384]{1,0:T(8,128)S(1)} %square_more.1), channel_id=1, source_target_pairs={{0,3},{1,2},{2,1},{3,0},{4,7},{5,6},{6,5},{7,4},{8,11},{9,10},{10,... | collective-permute-start | bytes 589832 | tf_op jit(solution)/shard_map/ppermute | solution.py:413
  31.3 10.0 %collective-permute-done.17 = f32[128,384]{1,0:T(8,128)S(1)} collective-permute-done((f32[128,384]{1,0:T(8,128)S(1)}, f32[128,384]{1,0:T(8,128)S(1)}, u32[]{:S(2)}, u32[]{:S(2)}) %collective-permute-start.17) | collective-permute-done | bytes 196640 | tf_op jit(solution)/shard_map/ppermute | solution.py:413
  41.3 0.7 %add_multiply_fusion = f32[128,384]{1,0:T(8,128)} fusion(f32[128,384]{1,0:T(8,128)S(1)} %square_more.1, f32[128,384]{1,0:T(8,128)S(1)} %collective-permute-done.17), kind=kLoop, calls=%fused_computation | loop fusion | flops 98304 | bytes 589824 | tf_op jit(solution)/shard_map/mul | solution.py:574
  (10 shorter events, 0.0 us)
Async XLA Ops:
  0.0 5.0 %copy-start = (bf16[4,8,16,384]{3,2,1,0:T(8,128)(2,1)S(1)}, bf16[4,8,16,384]{3,2,1,0:T(8,128)(2,1)}, u32[]{:S(2)}) copy-start(bf16[4,8,16,384]{3,2,1,0:T(8,128)(2,1)} %param.8) | copy-start | bytes 1179652
  1.8 6.6 %collective-permute-start.1 = (f32[128,128]{1,0:T(8,128)S(1)}, f32[128,128]{1,0:T(8,128)S(1)}, u32[]{:S(2)}, u32[]{:S(2)}) collective-permute-start(f32[128,128]{1,0:T(8,128)S(1)} %get-tuple-element.33), channel_id=1, source_target_pairs={{0,24},{4,28},{8,16},{12,20},{16,8},{20,12},{24,0},{28,4},{1,25},{... | collective-permute-start | bytes 196616 | tf_op jit(solution)/shard_map/ppermute | solution.py:408
  2.8 5.6 %collective-permute-start.2 = (f32[128,128]{1,0:T(8,128)S(1)}, f32[128,128]{1,0:T(8,128)S(1)}, u32[]{:S(2)}, u32[]{:S(2)}) collective-permute-start(f32[128,128]{1,0:T(8,128)S(1)} %get-tuple-element.34), channel_id=1, source_target_pairs={{0,4},{4,0},{8,12},{12,8},{16,20},{20,16},{24,28},{28,24},{1,5},{5... | collective-permute-start | bytes 196616 | tf_op jit(solution)/shard_map/ppermute | solution.py:408
  4.3 4.1 %collective-permute-start = (f32[32,128]{1,0:T(8,128)S(1)}, f32[32,128]{1,0:T(8,128)S(1)}, u32[]{:S(2)}, u32[]{:S(2)}) collective-permute-start(f32[32,128]{1,0:T(8,128)S(1)} %get-tuple-element.31), channel_id=1, source_target_pairs={{0,28},{4,24},{8,20},{12,16},{16,12},{20,8},{24,4},{28,0},{1,29},{... | collective-permute-start | bytes 49160 | tf_op jit(solution)/shard_map/ppermute | solution.py:408
  4.8 4.1 %collective-permute-start.4 = (f32[96,128]{1,0:T(8,128)S(1)}, f32[96,128]{1,0:T(8,128)S(1)}, u32[]{:S(2)}, u32[]{:S(2)}) collective-permute-start(f32[96,128]{1,0:T(8,128)S(1)} %get-tuple-element.35), channel_id=1, source_target_pairs={{0,8},{4,12},{8,0},{12,4},{16,24},{20,28},{24,16},{28,20},{1,9},{5... | collective-permute-start | bytes 147464 | tf_op jit(solution)/shard_map/ppermute | solution.py:408
  5.0 3.9 %copy-start.1 = (f32[1,8,16,384]{3,2,1,0:T(8,128)S(1)}, f32[1,8,16,384]{3,2,1,0:T(8,128)}, u32[]{:S(2)}) copy-start(f32[1,8,16,384]{3,2,1,0:T(8,128)} %param.6) | copy-start | bytes 589828
  5.0 3.9 %copy-start.2 = (f32[8,16,384]{2,1,0:T(8,128)S(1)}, f32[8,16,384]{2,1,0:T(8,128)}, u32[]{:S(2)}) copy-start(f32[8,16,384]{2,1,0:T(8,128)} %param.7) | copy-start | bytes 589828
  8.4 1.3 %collective-permute-start.3 = (f32[32,128]{1,0:T(8,128)S(1)}, f32[32,128]{1,0:T(8,128)S(1)}, u32[]{:S(2)}, u32[]{:S(2)}) collective-permute-start(f32[32,128]{1,0:T(8,128)S(1)} %slice_add_fusion.4.refs_0_), channel_id=1, source_target_pairs={{0,8},{4,12},{8,0},{12,4},{16,24},{20,28},{24,16},{28,20},{1,9},{5... | collective-permute-start | bytes 49160 | tf_op jit(solution)/shard_map/ppermute | solution.py:408
  8.9 0.8 %copy-start.3 = (f32[4096]{0:T(1024)S(1)}, f32[4096]{0:T(1024)}, u32[]{:S(2)}) copy-start(f32[4096]{0:T(1024)} %param.10) | copy-start | bytes 49156
  10.4 5.1 %collective-permute-start.6 = (f32[128,128]{1,0:T(8,128)S(1)}, f32[128,128]{1,0:T(8,128)S(1)}, u32[]{:S(2)}, u32[]{:S(2)}) collective-permute-start(f32[128,128]{1,0:T(8,128)S(1)} %get-tuple-element.40), channel_id=1, source_target_pairs={{0,24},{4,28},{8,16},{12,20},{16,8},{20,12},{24,0},{28,4},{1,25},{... | collective-permute-start | bytes 196616 | tf_op jit(solution)/shard_map/ppermute | solution.py:408
  10.9 4.6 %collective-permute-start.7 = (f32[128,128]{1,0:T(8,128)S(1)}, f32[128,128]{1,0:T(8,128)S(1)}, u32[]{:S(2)}, u32[]{:S(2)}) collective-permute-start(f32[128,128]{1,0:T(8,128)S(1)} %get-tuple-element.41), channel_id=1, source_target_pairs={{0,4},{4,0},{8,12},{12,8},{16,20},{20,16},{24,28},{28,24},{1,5},{5... | collective-permute-start | bytes 196616 | tf_op jit(solution)/shard_map/ppermute | solution.py:408
  11.4 4.1 %collective-permute-start.5 = (f32[32,128]{1,0:T(8,128)S(1)}, f32[32,128]{1,0:T(8,128)S(1)}, u32[]{:S(2)}, u32[]{:S(2)}) collective-permute-start(f32[32,128]{1,0:T(8,128)S(1)} %get-tuple-element.39), channel_id=1, source_target_pairs={{0,28},{4,24},{8,20},{12,16},{16,12},{20,8},{24,4},{28,0},{1,29},{... | collective-permute-start | bytes 49160 | tf_op jit(solution)/shard_map/ppermute | solution.py:408
  13.4 2.3 %collective-permute-start.9 = (f32[96,128]{1,0:T(8,128)S(1)}, f32[96,128]{1,0:T(8,128)S(1)}, u32[]{:S(2)}, u32[]{:S(2)}) collective-permute-start(f32[96,128]{1,0:T(8,128)S(1)} %get-tuple-element.42), channel_id=1, source_target_pairs={{0,8},{4,12},{8,0},{12,4},{16,24},{20,28},{24,16},{28,20},{1,9},{5... | collective-permute-start | bytes 147464 | tf_op jit(solution)/shard_map/ppermute | solution.py:408
  15.5 1.2 %collective-permute-start.8 = (f32[32,128]{1,0:T(8,128)S(1)}, f32[32,128]{1,0:T(8,128)S(1)}, u32[]{:S(2)}, u32[]{:S(2)}) collective-permute-start(f32[32,128]{1,0:T(8,128)S(1)} %slice_add_fusion.2.refs_0_), channel_id=1, source_target_pairs={{0,8},{4,12},{8,0},{12,4},{16,24},{20,28},{24,16},{28,20},{1,9},{5... | collective-permute-start | bytes 49160 | tf_op jit(solution)/shard_map/ppermute | solution.py:408
  17.4 4.2 %collective-permute-start.11 = (f32[128,128]{1,0:T(8,128)S(1)}, f32[128,128]{1,0:T(8,128)S(1)}, u32[]{:S(2)}, u32[]{:S(2)}) collective-permute-start(f32[128,128]{1,0:T(8,128)S(1)} %get-tuple-element.47), channel_id=1, source_target_pairs={{0,24},{4,28},{8,16},{12,20},{16,8},{20,12},{24,0},{28,4},{1,25},{... | collective-permute-start | bytes 196616 | tf_op jit(solution)/shard_map/ppermute | solution.py:408
  18.7 4.3 %collective-permute-start.12 = (f32[128,128]{1,0:T(8,128)S(1)}, f32[128,128]{1,0:T(8,128)S(1)}, u32[]{:S(2)}, u32[]{:S(2)}) collective-permute-start(f32[128,128]{1,0:T(8,128)S(1)} %get-tuple-element.48), channel_id=1, source_target_pairs={{0,4},{4,0},{8,12},{12,8},{16,20},{20,16},{24,28},{28,24},{1,5},{5... | collective-permute-start | bytes 196616 | tf_op jit(solution)/shard_map/ppermute | solution.py:408
  20.3 1.2 %collective-permute-start.10 = (f32[96,128]{1,0:T(8,128)S(1)}, f32[96,128]{1,0:T(8,128)S(1)}, u32[]{:S(2)}, u32[]{:S(2)}) collective-permute-start(f32[96,128]{1,0:T(8,128)S(1)} %get-tuple-element.46), channel_id=1, source_target_pairs={{0,8},{4,12},{8,0},{12,4},{16,24},{20,28},{24,16},{28,20},{1,9},{5... | collective-permute-start | bytes 147464 | tf_op jit(solution)/shard_map/ppermute | solution.py:408
  20.4 4.7 %collective-permute-start.14 = (f32[32,128]{1,0:T(8,128)S(1)}, f32[32,128]{1,0:T(8,128)S(1)}, u32[]{:S(2)}, u32[]{:S(2)}) collective-permute-start(f32[32,128]{1,0:T(8,128)S(1)} %get-tuple-element.50), channel_id=1, source_target_pairs={{0,28},{4,24},{8,20},{12,16},{16,12},{20,8},{24,4},{28,0},{1,29},{... | collective-permute-start | bytes 49160 | tf_op jit(solution)/shard_map/ppermute | solution.py:408
  23.5 6.8 %collective-permute-start.13 = (f32[128,384]{1,0:T(8,128)S(1)}, f32[128,384]{1,0:T(8,128)S(1)}, u32[]{:S(2)}, u32[]{:S(2)}) collective-permute-start(f32[128,384]{1,0:T(8,128)S(1)} %local_3.1.refs_4_), channel_id=1, source_target_pairs={{0,1},{1,0},{2,3},{3,2},{4,5},{5,4},{6,7},{7,6},{8,9},{9,8},{10,11... | collective-permute-start | bytes 589832 | tf_op jit(solution)/shard_map/ppermute | solution.py:413
  25.1 1.2 %collective-permute-start.15 = (f32[32,128]{1,0:T(8,128)S(1)}, f32[32,128]{1,0:T(8,128)S(1)}, u32[]{:S(2)}, u32[]{:S(2)}) collective-permute-start(f32[32,128]{1,0:T(8,128)S(1)} %slice_add_fusion), channel_id=1, source_target_pairs={{0,8},{4,12},{8,0},{12,4},{16,24},{20,28},{24,16},{28,20},{1,9},{5... | collective-permute-start | bytes 49160 | tf_op jit(solution)/shard_map/ppermute | solution.py:408
  26.4 3.9 %collective-permute-start.16 = (f32[32,128]{1,0:T(8,128)S(1)}, f32[32,128]{1,0:T(8,128)S(1)}, u32[]{:S(2)}, u32[]{:S(2)}) collective-permute-start(f32[32,128]{1,0:T(8,128)S(1)} %add.42.refs_5_), channel_id=1, source_target_pairs={{0,1},{1,0},{2,3},{3,2},{4,5},{5,4},{6,7},{7,6},{8,9},{9,8},{10,11... | collective-permute-start | bytes 49160 | tf_op jit(solution)/shard_map/ppermute | solution.py:413
  30.8 10.5 %collective-permute-start.17 = (f32[128,384]{1,0:T(8,128)S(1)}, f32[128,384]{1,0:T(8,128)S(1)}, u32[]{:S(2)}, u32[]{:S(2)}) collective-permute-start(f32[128,384]{1,0:T(8,128)S(1)} %square_more.1), channel_id=1, source_target_pairs={{0,3},{1,2},{2,1},{3,0},{4,7},{5,6},{6,5},{7,4},{8,11},{9,10},{10,... | collective-permute-start | bytes 589832 | tf_op jit(solution)/shard_map/ppermute | solution.py:413

commit v9 on v8

--- a/solution.py
+++ b/solution.py
@@ -228,6 +228,7 @@
     bottom = vals[: sz.xedge]
     is_high = flag == 0
     to_message(sz, ab_ref, jnp.where(is_high, top, bottom))
+    ab_ref[sz.edge_rows :, :] = table
     to_message(sz, bb_ref, jnp.where(is_high, bottom, top))
     bb_ref[sz.edge_rows :, :] = table
     to_message(sz, yb_ref, second_edges(sz, vals))
@@ -449,7 +450,7 @@
     pv = proj_vals.reshape(slots * sz.cells, nz)
     pot = local_pot.reshape(sz.cells, nz)
     message_shapes = (
-        jax.ShapeDtypeStruct((sz.edge_rows, LANES), F32),
+        jax.ShapeDtypeStruct((sz.edge_rows + rows, LANES), F32),
         jax.ShapeDtypeStruct((sz.edge_rows + rows, LANES), F32),
         jax.ShapeDtypeStruct((sz.yedge_rows + rows, LANES), F32),
         jax.ShapeDtypeStruct((rows, LANES), F32),
@@ -457,17 +458,33 @@
     field = jax.ShapeDtypeStruct((sz.cells, nz), F32)
     params = pltpu.CompilerParams(vmem_limit_bytes=48 << 20)
 
-    def exchange(to_a, to_b, to_y, table, aside):
-        if whole:
+    def exchange(to_a, to_b, to_y, table, aside, pair_last):
+        if whole and pair_last:
             from_b = swap(to_b, lambda i, j: (size_first - 1 - i, j))
             from_y = swap(to_y, lambda i, j: (i, 1 - j))
             from_d = swap(table, lambda i, j: (size_first - 1 - i, 1 - j))
-            from_a = swap(to_a, lambda i, j: (i ^ 1, j))
+            from_a = swap(to_a[: sz.edge_rows], lambda i, j: (i ^ 1, j))
             if aside is not None:
                 from_d, aside = lax.optimization_barrier((from_d, aside))
-            table = table + from_d + from_b[sz.edge_rows :] + from_y[sz.yedge_rows :]
+            table = table + from_d + from_y[sz.yedge_rows :] + from_b[sz.edge_rows :]
             other = swap(table, lambda i, j: (i ^ 1, j))
             return [table, other], from_a, from_b, [from_y], aside
+        if whole:
+            from_a = swap(to_a, lambda i, j: (i ^ 1, j))
+            from_b = swap(to_b, lambda i, j: (size_first - 1 - i, j))
+            from_y = swap(to_y, lambda i, j: (i, 1 - j))
+            chip = table + from_a[sz.edge_rows :]
+            if aside is not None:
+                aside = aside(chip, pv)
+            from_d = swap(chip, lambda i, j: (size_first - 1 - i, 1 - j))
+            if aside is not None:
+                from_y, aside = lax.optimization_barrier((from_y, aside))
+            beside = from_y[sz.yedge_rows :] + from_b[sz.edge_rows :]
+            other = swap(beside, lambda i, j: (i ^ 1, j))
+            return [chip, beside, other, from_d], from_a, from_b, [from_y], aside
+        to_a = to_a[: sz.edge_rows]
+        if aside is not None:
+            aside = aside(table, pv)
         edges_b = to_b[: sz.edge_rows]
         edges_y = to_y[: sz.yedge_rows]
         below = shift(edges_y, "gy", 1)
@@ -516,18 +533,19 @@
             compiler_params=params,
             name="project_first",
         )(flag, *(in_place(arr) for arr in (start, pv, ids, cheb_coef)))
-        overlap = pl.pallas_call(
+        overlap_after = pl.pallas_call(
             functools.partial(overlap_kernel, sz),
             out_shape=jax.ShapeDtypeStruct((slots * slots * sz.zb, LANES), F32),
             in_specs=vmem(2),
             out_specs=vmem(1)[0],
             compiler_params=params,
             name="overlap",
-        )(row_of, pv)
+        )
+        overlap = None
         history = [start]
         for degree in range(1, STEPS + 1):
             tables, from_a, from_b, from_y, aside = exchange(
-                *messages, overlap if degree == 1 else None
+                *messages, overlap_after if degree == 1 else None, degree == STEPS
             )
             overlap = overlap if aside is None else aside
             last = degree == STEPS

time: 42.3 us -> 41.2 us (0.974)
  waiting for transfers between devices: 20.6 us -> 19.8 us
    ppermute x15, waiting for transfers between devices: 8.26 us -> 7.23 us  [swap(): return lax.ppermute(arr, ('gx', 'gy'), pairs)]
  transfers between devices with their start and end apart: 18 -> 18, of which waited for: 9 -> 11; matrix products, arithmetic and copies ran while one was open for 0% -> 0% of each run, Pallas kernels for 7% -> 7%
where the time goes in v9:
time: 41.2 us; the launch traced here: 41 us
  waiting for transfers between devices  19.8 us (48%)
  starting transfers between devices  14 us (34%)
  Pallas kernels  6.39 us (16%)
  other arithmetic  0.73 us (2%)
    ppermute x3, waiting for transfers between devices, orb_swap(): return lax.ppermute(vals, 'orb', [(i, i ^ bit) for i in range(size)])  12.6 us
    ppermute x15, starting transfers between devices, swap(): return lax.ppermute(arr, ('gx', 'gy'), pairs)  11.1 us
    ppermute x15, waiting for transfers between devices, swap(): return lax.ppermute(arr, ('gx', 'gy'), pairs)  7.23 us
    ppermute x3, starting transfers between devices, orb_swap(): return lax.ppermute(vals, 'orb', [(i, i ^ bit) for i in range(size)])  2.9 us
    pallas_call x1, Pallas kernels, one_orbital(): pl.pallas_call(functools.partial(first_kernel, sz), out_shape=message_sha...  1.8 us
    pallas_call x3, Pallas kernels, one_orbital(): pl.pallas_call(functools.partial(local_kernel, sz, degree, len(from_y)),...  1.7 us
    pallas_call x2, Pallas kernels, one_orbital(): pl.pallas_call(functools.partial(nonlocal_kernel, sz, degree, len(tables)...  1.27 us
    pallas_call x2, Pallas kernels, square(): pl.pallas_call(functools.partial(last_kernel, sz, len(tables), len(before...  1.05 us
  transfers between devices with their start and end apart: 18, of which 11 were waited for; matrix products, arithmetic and copies ran while one was open for 0% of the time, Pallas kernels for 7%

profile of v9, /device:TPU:16, one launch (start us, length us, event | category | flops | bytes accessed | tf_op | source)
XLA Modules:
  0.0 41.0 jit_solution(6992307212573227416)
XLA Ops:
  0.0 1.8 %project_first.1 = (f32[128,128]{1,0:T(8,128)S(1)}, f32[128,128]{1,0:T(8,128)S(1)}, f32[128,128]{1,0:T(8,128)S(1)}, f32[32,128]{1,0:T(8,128)S(1)}, f32[12,128]{1...) custom-call(s32[1]{0:T(128)} %bitcast.flag_ref, f32[128,384]{1,0:T(8,128)} %bitcast.17, ...), custom_call_target="tpu_custom_call" | custom-call | tf_op jit(solution)/shard_map/project_first/pallas_call | solution.py:516
  1.8 0.1 collective-permute-start
  1.9 1.6 %collective-permute-start.1 = (f32[128,128]{1,0:T(8,128)S(1)}, f32[128,128]{1,0:T(8,128)S(1)}, u32[]{:S(2)}, u32[]{:S(2)}) collective-permute-start(f32[128,128]{1,0:T(8,128)S(1)} %get-tuple-element.33), channel_id=1, source_target_pairs={{0,4},{4,0},{8,12},{12,8},{16,20},{20,16},{24,28},{28,24},{1,5},{5... | collective-permute-start | bytes 196616 | tf_op jit(solution)/shard_map/ppermute | solution.py:409
  3.5 1.3 %collective-permute-start.2 = (f32[128,128]{1,0:T(8,128)S(1)}, f32[128,128]{1,0:T(8,128)S(1)}, u32[]{:S(2)}, u32[]{:S(2)}) collective-permute-start(f32[128,128]{1,0:T(8,128)S(1)} %get-tuple-element.35), channel_id=1, source_target_pairs={{0,24},{4,28},{8,16},{12,20},{16,8},{20,12},{24,0},{28,4},{1,25},{... | collective-permute-start | bytes 196616 | tf_op jit(solution)/shard_map/ppermute | solution.py:409
  4.7 0.0 collective-permute-done.refs_0_
  4.8 0.0 copy-start.1
  4.8 0.0 copy-start.2
  4.8 0.6 %overlap.1.refs_10_ = f32[48,128]{1,0:T(8,128)S(1)} custom-call(f32[32,128]{1,0:T(8,128)S(1)} %slice_add_fusion.5.after_ref.refs_0_, bf16[512,384]{1,0:T(8,128)(2,1)S(1)} %bitcast.10), custom_call_target="tpu_custom_call" | custom-call | tf_op jit(solution)/shard_map/overlap/pallas_call | solution.py:478
  5.4 0.7 %collective-permute-start.4 = (f32[32,128]{1,0:T(8,128)S(1)}, f32[32,128]{1,0:T(8,128)S(1)}, u32[]{:S(2)}, u32[]{:S(2)}) collective-permute-start(f32[32,128]{1,0:T(8,128)S(1)} %slice_add_fusion.5.after_ref.refs_0_), channel_id=1, source_target_pairs={{0,28},{4,24},{8,20},{12,16},{16,12},{20,8},{24,4},{28,0},{1,29},{... | collective-permute-start | bytes 49160 | tf_op jit(solution)/shard_map/ppermute | solution.py:409
  6.0 0.4 collective-permute-done.1.refs_2_
  6.4 1.1 %collective-permute-done.2.refs_1_ = f32[128,128]{1,0:T(8,128)S(1)} collective-permute-done((f32[128,128]{1,0:T(8,128)S(1)}, f32[128,128]{1,0:T(8,128)S(1)}, u32[]{:S(2)}, u32[]{:S(2)}) %collective-permute-start.2) | collective-permute-done | bytes 65568 | tf_op jit(solution)/shard_map/ppermute | solution.py:409
  7.5 0.2 collective-permute-start.3
  7.7 0.6 %local_1.1 = (f32[128,384]{1,0:T(8,128)S(1)}, f32[12,128]{1,0:T(8,128)S(1)}) custom-call(s32[1]{0:T(128)} %bitcast.flag_ref, f32[128,128]{1,0:T(8,128)S(1)} %collective-permute-done.refs_0_, f32[128,128]{1,0:T(8,128)S(1)} %collective-permute-done.2.refs_1_, f32[128,128]{1,0:T(8,128)S(1)} %collective-permute-done.1.refs_2_, f32[128,384]{1,0:T(8,128)S(1)} %bitcast.21, ...), custom_call_target="tpu_custom_call" | custom-call | tf_op jit(solution)/shard_map/local_1/pallas_call | solution.py:557
  8.3 1.1 %collective-permute-done.4.refs_3_ = f32[32,128]{1,0:T(8,128)S(1)} collective-permute-done((f32[32,128]{1,0:T(8,128)S(1)}, f32[32,128]{1,0:T(8,128)S(1)}, u32[]{:S(2)}, u32[]{:S(2)}) %collective-permute-start.4) | collective-permute-done | bytes 16416 | tf_op jit(solution)/shard_map/ppermute | solution.py:409
  9.5 0.0 collective-permute-done.3.refs_2_
  9.5 0.6 %nonlocal_1.1 = (f32[128,384]{1,0:T(8,128)S(1)}, f32[128,128]{1,0:T(8,128)S(1)}, f32[128,128]{1,0:T(8,128)S(1)}, f32[128,128]{1,0:T(8,128)S(1)}, f32[32,128]{1,0:T(8,128)S(1)}) custom-call(s32[1]{0:T(128)} %bitcast.flag_ref, f32[32,128]{1,0:T(8,128)S(1)} %slice_add_fusion.5.after_ref.refs_0_, f32[32,128]{1,0:T(8,128)S(1)} %slice_add_fusion.4.refs_1_, ...), custom_call_target="tpu_custom_call" | custom-call | tf_op jit(solution)/shard_map/nonlocal_1/pallas_call | solution.py:573
  10.1 0.4 %collective-permute-start.5 = (f32[128,128]{1,0:T(8,128)S(1)}, f32[128,128]{1,0:T(8,128)S(1)}, u32[]{:S(2)}, u32[]{:S(2)}) collective-permute-start(f32[128,128]{1,0:T(8,128)S(1)} %get-tuple-element.40), channel_id=1, source_target_pairs={{0,8},{4,12},{8,0},{12,4},{16,24},{20,28},{24,16},{28,20},{1,9},{5... | collective-permute-start | bytes 196616 | tf_op jit(solution)/shard_map/ppermute | solution.py:409
  10.6 0.5 %collective-permute-start.6 = (f32[128,128]{1,0:T(8,128)S(1)}, f32[128,128]{1,0:T(8,128)S(1)}, u32[]{:S(2)}, u32[]{:S(2)}) collective-permute-start(f32[128,128]{1,0:T(8,128)S(1)} %get-tuple-element.41), channel_id=1, source_target_pairs={{0,4},{4,0},{8,12},{12,8},{16,20},{20,16},{24,28},{28,24},{1,5},{5... | collective-permute-start | bytes 196616 | tf_op jit(solution)/shard_map/ppermute | solution.py:409
  11.0 0.5 %collective-permute-start.7 = (f32[128,128]{1,0:T(8,128)S(1)}, f32[128,128]{1,0:T(8,128)S(1)}, u32[]{:S(2)}, u32[]{:S(2)}) collective-permute-start(f32[128,128]{1,0:T(8,128)S(1)} %get-tuple-element.42), channel_id=1, source_target_pairs={{0,24},{4,28},{8,16},{12,20},{16,8},{20,12},{24,0},{28,4},{1,25},{... | collective-permute-start | bytes 196616 | tf_op jit(solution)/shard_map/ppermute | solution.py:409
  11.6 0.0 collective-permute-done.5.refs_0_
  11.6 2.2 %collective-permute-start.9 = (f32[32,128]{1,0:T(8,128)S(1)}, f32[32,128]{1,0:T(8,128)S(1)}, u32[]{:S(2)}, u32[]{:S(2)}) collective-permute-start(f32[32,128]{1,0:T(8,128)S(1)} %slice_add_fusion.3.refs_0_), channel_id=1, source_target_pairs={{0,28},{4,24},{8,20},{12,16},{16,12},{20,8},{24,4},{28,0},{1,29},{... | collective-permute-start | bytes 49160 | tf_op jit(solution)/shard_map/ppermute | solution.py:409
  13.8 1.0 %collective-permute-done.6.refs_2_ = f32[128,128]{1,0:T(8,128)S(1)} collective-permute-done((f32[128,128]{1,0:T(8,128)S(1)}, f32[128,128]{1,0:T(8,128)S(1)}, u32[]{:S(2)}, u32[]{:S(2)}) %collective-permute-start.6) | collective-permute-done | bytes 65568 | tf_op jit(solution)/shard_map/ppermute | solution.py:409
  14.8 0.5 %collective-permute-done.7.refs_1_ = f32[128,128]{1,0:T(8,128)S(1)} collective-permute-done((f32[128,128]{1,0:T(8,128)S(1)}, f32[128,128]{1,0:T(8,128)S(1)}, u32[]{:S(2)}, u32[]{:S(2)}) %collective-permute-start.7) | collective-permute-done | bytes 65568 | tf_op jit(solution)/shard_map/ppermute | solution.py:409
  15.4 0.1 collective-permute-start.8
  15.5 0.7 %local_2.1 = (f32[128,384]{1,0:T(8,128)S(1)}, f32[12,128]{1,0:T(8,128)S(1)}) custom-call(s32[1]{0:T(128)} %bitcast.flag_ref, f32[128,128]{1,0:T(8,128)S(1)} %collective-permute-done.5.refs_0_, f32[128,128]{1,0:T(8,128)S(1)} %collective-permute-done.7.refs_1_, f32[128,128]{1,0:T(8,128)S(1)} %collective-permute-done.6.refs_2_, f32[128,384]{1,0:T(8,128)S(1)} %bitcast.22, ...), custom_call_target="tpu_custom_call" | custom-call | tf_op jit(solution)/shard_map/local_2/pallas_call | solution.py:557
  16.1 0.6 %collective-permute-done.9.refs_3_ = f32[32,128]{1,0:T(8,128)S(1)} collective-permute-done((f32[32,128]{1,0:T(8,128)S(1)}, f32[32,128]{1,0:T(8,128)S(1)}, u32[]{:S(2)}, u32[]{:S(2)}) %collective-permute-start.9) | collective-permute-done | bytes 16416 | tf_op jit(solution)/shard_map/ppermute | solution.py:409
  16.7 0.0 collective-permute-done.8.refs_2_
  16.7 0.6 %nonlocal_2.1 = (f32[128,384]{1,0:T(8,128)S(1)}, f32[128,128]{1,0:T(8,128)S(1)}, f32[128,128]{1,0:T(8,128)S(1)}, f32[128,128]{1,0:T(8,128)S(1)}, f32[32,128]{1,0:T(8,128)S(1)}) custom-call(s32[1]{0:T(128)} %bitcast.flag_ref, f32[32,128]{1,0:T(8,128)S(1)} %slice_add_fusion.3.refs_0_, f32[32,128]{1,0:T(8,128)S(1)} %slice_add_fusion.2.refs_1_, ...), custom_call_target="tpu_custom_call" | custom-call | tf_op jit(solution)/shard_map/nonlocal_2/pallas_call | solution.py:573
  17.3 0.3 collective-permute-start.11
  17.7 1.5 %collective-permute-start.12 = (f32[128,128]{1,0:T(8,128)S(1)}, f32[128,128]{1,0:T(8,128)S(1)}, u32[]{:S(2)}, u32[]{:S(2)}) collective-permute-start(f32[128,128]{1,0:T(8,128)S(1)} %get-tuple-element.48), channel_id=1, source_target_pairs={{0,4},{4,0},{8,12},{12,8},{16,20},{20,16},{24,28},{28,24},{1,5},{5... | collective-permute-start | bytes 196616 | tf_op jit(solution)/shard_map/ppermute | solution.py:409
  19.2 0.1 collective-permute-start.10
  19.2 1.5 %collective-permute-start.14 = (f32[32,128]{1,0:T(8,128)S(1)}, f32[32,128]{1,0:T(8,128)S(1)}, u32[]{:S(2)}, u32[]{:S(2)}) collective-permute-start(f32[32,128]{1,0:T(8,128)S(1)} %get-tuple-element.50), channel_id=1, source_target_pairs={{0,28},{4,24},{8,20},{12,16},{16,12},{20,8},{24,4},{28,0},{1,29},{... | collective-permute-start | bytes 49160 | tf_op jit(solution)/shard_map/ppermute | solution.py:409
  20.8 0.0 collective-permute-done.10.refs_1_
  20.8 0.7 %collective-permute-done.11.refs_2_ = f32[128,128]{1,0:T(8,128)S(1)} collective-permute-done((f32[128,128]{1,0:T(8,128)S(1)}, f32[128,128]{1,0:T(8,128)S(1)}, u32[]{:S(2)}, u32[]{:S(2)}) %collective-permute-start.11) | collective-permute-done | bytes 65568 | tf_op jit(solution)/shard_map/ppermute | solution.py:409
  21.5 0.6 %collective-permute-done.12.refs_3_ = f32[128,128]{1,0:T(8,128)S(1)} collective-permute-done((f32[128,128]{1,0:T(8,128)S(1)}, f32[128,128]{1,0:T(8,128)S(1)}, u32[]{:S(2)}, u32[]{:S(2)}) %collective-permute-start.12) | collective-permute-done | bytes 65568 | tf_op jit(solution)/shard_map/ppermute | solution.py:409
  22.1 0.4 local_3.1.refs_4_
  22.5 1.6 %collective-permute-start.13 = (f32[128,384]{1,0:T(8,128)S(1)}, f32[128,384]{1,0:T(8,128)S(1)}, u32[]{:S(2)}, u32[]{:S(2)}) collective-permute-start(f32[128,384]{1,0:T(8,128)S(1)} %local_3.1.refs_4_), channel_id=1, source_target_pairs={{0,1},{1,0},{2,3},{3,2},{4,5},{5,4},{6,7},{7,6},{8,9},{9,8},{10,11... | collective-permute-start | bytes 589832 | tf_op jit(solution)/shard_map/ppermute | solution.py:414
  24.2 0.0 collective-permute-done.14
  24.2 0.1 collective-permute-start.15
  24.2 1.2 %collective-permute-done.15 = f32[32,128]{1,0:T(8,128)S(1)} collective-permute-done((f32[32,128]{1,0:T(8,128)S(1)}, f32[32,128]{1,0:T(8,128)S(1)}, u32[]{:S(2)}, u32[]{:S(2)}) %collective-permute-start.15) | collective-permute-done | bytes 16416 | tf_op jit(solution)/shard_map/ppermute | solution.py:409
  25.4 0.8 %collective-permute-start.16 = (f32[32,128]{1,0:T(8,128)S(1)}, f32[32,128]{1,0:T(8,128)S(1)}, u32[]{:S(2)}, u32[]{:S(2)}) collective-permute-start(f32[32,128]{1,0:T(8,128)S(1)} %add.34.refs_5_), channel_id=1, source_target_pairs={{0,1},{1,0},{2,3},{3,2},{4,5},{5,4},{6,7},{7,6},{8,9},{9,8},{10,11... | collective-permute-start | bytes 49160 | tf_op jit(solution)/shard_map/ppermute | solution.py:414
  26.2 0.5 %square.1.refs_6_ = f32[128,384]{1,0:T(8,128)S(1)} custom-call(f32[8,128]{1,0:T(8,128)S(1)} %get-tuple-element.28.refs_0_.cheb_ref, f32[32,128]{1,0:T(8,128)S(1)} %bitcast.26, bf16[512,384]{1,0:T(8,128)(2,1)S(1)} %bitcast.15, f32[12,128]{1,0:T(8,128)S(1)} %get-tuple-element.29.refs_7_.refs_2_, bf16[128,1536]{1,0:T(8,128)(2,1)S(1)} %get-tuple-element.30.refs_8_.refs_3_, ...), custom_call_target="tpu_custom_call" | custom-call | tf_op jit(solution)/shard_map/square/pallas_call | solution.py:506
  26.7 2.9 %collective-permute-done.16.refs_5_ = f32[32,128]{1,0:T(8,128)S(1)} collective-permute-done((f32[32,128]{1,0:T(8,128)S(1)}, f32[32,128]{1,0:T(8,128)S(1)}, u32[]{:S(2)}, u32[]{:S(2)}) %collective-permute-start.16) | collective-permute-done | bytes 16416 | tf_op jit(solution)/shard_map/ppermute | solution.py:414
  29.6 0.0 collective-permute-done.13.refs_4_
  29.6 0.5 %square_more.1 = f32[128,384]{1,0:T(8,128)S(1)} custom-call(f32[8,128]{1,0:T(8,128)S(1)} %get-tuple-element.28.refs_0_.cheb_ref, f32[32,128]{1,0:T(8,128)S(1)} %bitcast.27, bf16[512,384]{1,0:T(8,128)(2,1)S(1)} %bitcast.16, f32[12,128]{1,0:T(8,128)S(1)} %get-tuple-element.29.refs_7_.refs_2_, bf16[128,1536]{1,0:T(8,128)(2,1)S(1)} %get-tuple-element.30.refs_8_.refs_3_, ...), custom_call_target="tpu_custom_call" | custom-call | tf_op jit(solution)/shard_map/square_more/pallas_call | solution.py:506
  30.1 0.5 %collective-permute-start.17 = (f32[128,384]{1,0:T(8,128)S(1)}, f32[128,384]{1,0:T(8,128)S(1)}, u32[]{:S(2)}, u32[]{:S(2)}) collective-permute-start(f32[128,384]{1,0:T(8,128)S(1)} %square_more.1), channel_id=1, source_target_pairs={{0,3},{1,2},{2,1},{3,0},{4,7},{5,6},{6,5},{7,4},{8,11},{9,10},{10,... | collective-permute-start | bytes 589832 | tf_op jit(solution)/shard_map/ppermute | solution.py:414
  30.6 9.7 %collective-permute-done.17 = f32[128,384]{1,0:T(8,128)S(1)} collective-permute-done((f32[128,384]{1,0:T(8,128)S(1)}, f32[128,384]{1,0:T(8,128)S(1)}, u32[]{:S(2)}, u32[]{:S(2)}) %collective-permute-start.17) | collective-permute-done | bytes 196640 | tf_op jit(solution)/shard_map/ppermute | solution.py:414
  40.3 0.7 %add_multiply_fusion = f32[128,384]{1,0:T(8,128)} fusion(f32[128,384]{1,0:T(8,128)S(1)} %square_more.1, f32[128,384]{1,0:T(8,128)S(1)} %collective-permute-done.17), kind=kLoop, calls=%fused_computation | loop fusion | flops 98304 | bytes 589824 | tf_op jit(solution)/shard_map/mul | solution.py:592
  (13 shorter events, 0.0 us)
Async XLA Ops:
  0.0 4.8 %copy-start = (bf16[4,8,16,384]{3,2,1,0:T(8,128)(2,1)S(1)}, bf16[4,8,16,384]{3,2,1,0:T(8,128)(2,1)}, u32[]{:S(2)}) copy-start(bf16[4,8,16,384]{3,2,1,0:T(8,128)(2,1)} %param.8) | copy-start | bytes 1179652
  1.8 2.9 %collective-permute-start = (f32[128,128]{1,0:T(8,128)S(1)}, f32[128,128]{1,0:T(8,128)S(1)}, u32[]{:S(2)}, u32[]{:S(2)}) collective-permute-start(f32[128,128]{1,0:T(8,128)S(1)} %get-tuple-element.32), channel_id=1, source_target_pairs={{0,8},{4,12},{8,0},{12,4},{16,24},{20,28},{24,16},{28,20},{1,9},{5... | collective-permute-start | bytes 196616 | tf_op jit(solution)/shard_map/ppermute | solution.py:409
  1.9 4.5 %collective-permute-start.1 = (f32[128,128]{1,0:T(8,128)S(1)}, f32[128,128]{1,0:T(8,128)S(1)}, u32[]{:S(2)}, u32[]{:S(2)}) collective-permute-start(f32[128,128]{1,0:T(8,128)S(1)} %get-tuple-element.33), channel_id=1, source_target_pairs={{0,4},{4,0},{8,12},{12,8},{16,20},{20,16},{24,28},{28,24},{1,5},{5... | collective-permute-start | bytes 196616 | tf_op jit(solution)/shard_map/ppermute | solution.py:409
  3.5 4.0 %collective-permute-start.2 = (f32[128,128]{1,0:T(8,128)S(1)}, f32[128,128]{1,0:T(8,128)S(1)}, u32[]{:S(2)}, u32[]{:S(2)}) collective-permute-start(f32[128,128]{1,0:T(8,128)S(1)} %get-tuple-element.35), channel_id=1, source_target_pairs={{0,24},{4,28},{8,16},{12,20},{16,8},{20,12},{24,0},{28,4},{1,25},{... | collective-permute-start | bytes 196616 | tf_op jit(solution)/shard_map/ppermute | solution.py:409
  4.8 2.9 %copy-start.1 = (f32[1,8,16,384]{3,2,1,0:T(8,128)S(1)}, f32[1,8,16,384]{3,2,1,0:T(8,128)}, u32[]{:S(2)}) copy-start(f32[1,8,16,384]{3,2,1,0:T(8,128)} %param.6) | copy-start | bytes 589828
  4.8 2.9 %copy-start.2 = (f32[8,16,384]{2,1,0:T(8,128)S(1)}, f32[8,16,384]{2,1,0:T(8,128)}, u32[]{:S(2)}) copy-start(f32[8,16,384]{2,1,0:T(8,128)} %param.7) | copy-start | bytes 589828
  5.4 4.1 %collective-permute-start.4 = (f32[32,128]{1,0:T(8,128)S(1)}, f32[32,128]{1,0:T(8,128)S(1)}, u32[]{:S(2)}, u32[]{:S(2)}) collective-permute-start(f32[32,128]{1,0:T(8,128)S(1)} %slice_add_fusion.5.after_ref.refs_0_), channel_id=1, source_target_pairs={{0,28},{4,24},{8,20},{12,16},{16,12},{20,8},{24,4},{28,0},{1,29},{... | collective-permute-start | bytes 49160 | tf_op jit(solution)/shard_map/ppermute | solution.py:409
  7.5 2.0 %collective-permute-start.3 = (f32[32,128]{1,0:T(8,128)S(1)}, f32[32,128]{1,0:T(8,128)S(1)}, u32[]{:S(2)}, u32[]{:S(2)}) collective-permute-start(f32[32,128]{1,0:T(8,128)S(1)} %slice_add_fusion.4.refs_1_), channel_id=1, source_target_pairs={{0,8},{4,12},{8,0},{12,4},{16,24},{20,28},{24,16},{28,20},{1,9},{5... | collective-permute-start | bytes 49160 | tf_op jit(solution)/shard_map/ppermute | solution.py:409
  7.7 1.8 %copy-start.3 = (f32[4096]{0:T(1024)S(1)}, f32[4096]{0:T(1024)}, u32[]{:S(2)}) copy-start(f32[4096]{0:T(1024)} %param.10) | copy-start | bytes 49156
  10.1 1.5 %collective-permute-start.5 = (f32[128,128]{1,0:T(8,128)S(1)}, f32[128,128]{1,0:T(8,128)S(1)}, u32[]{:S(2)}, u32[]{:S(2)}) collective-permute-start(f32[128,128]{1,0:T(8,128)S(1)} %get-tuple-element.40), channel_id=1, source_target_pairs={{0,8},{4,12},{8,0},{12,4},{16,24},{20,28},{24,16},{28,20},{1,9},{5... | collective-permute-start | bytes 196616 | tf_op jit(solution)/shard_map/ppermute | solution.py:409
  10.6 4.3 %collective-permute-start.6 = (f32[128,128]{1,0:T(8,128)S(1)}, f32[128,128]{1,0:T(8,128)S(1)}, u32[]{:S(2)}, u32[]{:S(2)}) collective-permute-start(f32[128,128]{1,0:T(8,128)S(1)} %get-tuple-element.41), channel_id=1, source_target_pairs={{0,4},{4,0},{8,12},{12,8},{16,20},{20,16},{24,28},{28,24},{1,5},{5... | collective-permute-start | bytes 196616 | tf_op jit(solution)/shard_map/ppermute | solution.py:409
  11.0 4.3 %collective-permute-start.7 = (f32[128,128]{1,0:T(8,128)S(1)}, f32[128,128]{1,0:T(8,128)S(1)}, u32[]{:S(2)}, u32[]{:S(2)}) collective-permute-start(f32[128,128]{1,0:T(8,128)S(1)} %get-tuple-element.42), channel_id=1, source_target_pairs={{0,24},{4,28},{8,16},{12,20},{16,8},{20,12},{24,0},{28,4},{1,25},{... | collective-permute-start | bytes 196616 | tf_op jit(solution)/shard_map/ppermute | solution.py:409
  11.6 5.1 %collective-permute-start.9 = (f32[32,128]{1,0:T(8,128)S(1)}, f32[32,128]{1,0:T(8,128)S(1)}, u32[]{:S(2)}, u32[]{:S(2)}) collective-permute-start(f32[32,128]{1,0:T(8,128)S(1)} %slice_add_fusion.3.refs_0_), channel_id=1, source_target_pairs={{0,28},{4,24},{8,20},{12,16},{16,12},{20,8},{24,4},{28,0},{1,29},{... | collective-permute-start | bytes 49160 | tf_op jit(solution)/shard_map/ppermute | solution.py:409
  15.4 1.3 %collective-permute-start.8 = (f32[32,128]{1,0:T(8,128)S(1)}, f32[32,128]{1,0:T(8,128)S(1)}, u32[]{:S(2)}, u32[]{:S(2)}) collective-permute-start(f32[32,128]{1,0:T(8,128)S(1)} %slice_add_fusion.2.refs_1_), channel_id=1, source_target_pairs={{0,8},{4,12},{8,0},{12,4},{16,24},{20,28},{24,16},{28,20},{1,9},{5... | collective-permute-start | bytes 49160 | tf_op jit(solution)/shard_map/ppermute | solution.py:409
  17.3 4.2 %collective-permute-start.11 = (f32[128,128]{1,0:T(8,128)S(1)}, f32[128,128]{1,0:T(8,128)S(1)}, u32[]{:S(2)}, u32[]{:S(2)}) collective-permute-start(f32[128,128]{1,0:T(8,128)S(1)} %get-tuple-element.47), channel_id=1, source_target_pairs={{0,24},{4,28},{8,16},{12,20},{16,8},{20,12},{24,0},{28,4},{1,25},{... | collective-permute-start | bytes 196616 | tf_op jit(solution)/shard_map/ppermute | solution.py:409
  17.7 4.4 %collective-permute-start.12 = (f32[128,128]{1,0:T(8,128)S(1)}, f32[128,128]{1,0:T(8,128)S(1)}, u32[]{:S(2)}, u32[]{:S(2)}) collective-permute-start(f32[128,128]{1,0:T(8,128)S(1)} %get-tuple-element.48), channel_id=1, source_target_pairs={{0,4},{4,0},{8,12},{12,8},{16,20},{20,16},{24,28},{28,24},{1,5},{5... | collective-permute-start | bytes 196616 | tf_op jit(solution)/shard_map/ppermute | solution.py:409
  19.2 1.6 %collective-permute-start.10 = (f32[96,128]{1,0:T(8,128)S(1)}, f32[96,128]{1,0:T(8,128)S(1)}, u32[]{:S(2)}, u32[]{:S(2)}) collective-permute-start(f32[96,128]{1,0:T(8,128)S(1)} %slice.33), channel_id=1, source_target_pairs={{0,8},{4,12},{8,0},{12,4},{16,24},{20,28},{24,16},{28,20},{1,9},{5... | collective-permute-start | bytes 147464 | tf_op jit(solution)/shard_map/ppermute | solution.py:409
  19.2 4.9 %collective-permute-start.14 = (f32[32,128]{1,0:T(8,128)S(1)}, f32[32,128]{1,0:T(8,128)S(1)}, u32[]{:S(2)}, u32[]{:S(2)}) collective-permute-start(f32[32,128]{1,0:T(8,128)S(1)} %get-tuple-element.50), channel_id=1, source_target_pairs={{0,28},{4,24},{8,20},{12,16},{16,12},{20,8},{24,4},{28,0},{1,29},{... | collective-permute-start | bytes 49160 | tf_op jit(solution)/shard_map/ppermute | solution.py:409
  22.5 7.1 %collective-permute-start.13 = (f32[128,384]{1,0:T(8,128)S(1)}, f32[128,384]{1,0:T(8,128)S(1)}, u32[]{:S(2)}, u32[]{:S(2)}) collective-permute-start(f32[128,384]{1,0:T(8,128)S(1)} %local_3.1.refs_4_), channel_id=1, source_target_pairs={{0,1},{1,0},{2,3},{3,2},{4,5},{5,4},{6,7},{7,6},{8,9},{9,8},{10,11... | collective-permute-start | bytes 589832 | tf_op jit(solution)/shard_map/ppermute | solution.py:414
  24.2 1.2 %collective-permute-start.15 = (f32[32,128]{1,0:T(8,128)S(1)}, f32[32,128]{1,0:T(8,128)S(1)}, u32[]{:S(2)}, u32[]{:S(2)}) collective-permute-start(f32[32,128]{1,0:T(8,128)S(1)} %slice_add_fusion), channel_id=1, source_target_pairs={{0,8},{4,12},{8,0},{12,4},{16,24},{20,28},{24,16},{28,20},{1,9},{5... | collective-permute-start | bytes 49160 | tf_op jit(solution)/shard_map/ppermute | solution.py:409
  25.4 4.1 %collective-permute-start.16 = (f32[32,128]{1,0:T(8,128)S(1)}, f32[32,128]{1,0:T(8,128)S(1)}, u32[]{:S(2)}, u32[]{:S(2)}) collective-permute-start(f32[32,128]{1,0:T(8,128)S(1)} %add.34.refs_5_), channel_id=1, source_target_pairs={{0,1},{1,0},{2,3},{3,2},{4,5},{5,4},{6,7},{7,6},{8,9},{9,8},{10,11... | collective-permute-start | bytes 49160 | tf_op jit(solution)/shard_map/ppermute | solution.py:414
  30.1 10.2 %collective-permute-start.17 = (f32[128,384]{1,0:T(8,128)S(1)}, f32[128,384]{1,0:T(8,128)S(1)}, u32[]{:S(2)}, u32[]{:S(2)}) collective-permute-start(f32[128,384]{1,0:T(8,128)S(1)} %square_more.1), channel_id=1, source_target_pairs={{0,3},{1,2},{2,1},{3,0},{4,7},{5,6},{6,5},{7,4},{8,11},{9,10},{10,... | collective-permute-start | bytes 589832 | tf_op jit(solution)/shard_map/ppermute | solution.py:414

commit v10 on v9

--- a/solution.py
+++ b/solution.py
@@ -466,7 +466,7 @@
             from_a = swap(to_a[: sz.edge_rows], lambda i, j: (i ^ 1, j))
             if aside is not None:
                 from_d, aside = lax.optimization_barrier((from_d, aside))
-            table = table + from_d + from_y[sz.yedge_rows :] + from_b[sz.edge_rows :]
+            table = table + from_d + from_b[sz.edge_rows :] + from_y[sz.yedge_rows :]
             other = swap(table, lambda i, j: (i ^ 1, j))
             return [table, other], from_a, from_b, [from_y], aside
         if whole:
@@ -474,8 +474,6 @@
             from_b = swap(to_b, lambda i, j: (size_first - 1 - i, j))
             from_y = swap(to_y, lambda i, j: (i, 1 - j))
             chip = table + from_a[sz.edge_rows :]
-            if aside is not None:
-                aside = aside(chip, pv)
             from_d = swap(chip, lambda i, j: (size_first - 1 - i, 1 - j))
             if aside is not None:
                 from_y, aside = lax.optimization_barrier((from_y, aside))
@@ -483,8 +481,6 @@
             other = swap(beside, lambda i, j: (i ^ 1, j))
             return [chip, beside, other, from_d], from_a, from_b, [from_y], aside
         to_a = to_a[: sz.edge_rows]
-        if aside is not None:
-            aside = aside(table, pv)
         edges_b = to_b[: sz.edge_rows]
         edges_y = to_y[: sz.yedge_rows]
         below = shift(edges_y, "gy", 1)
@@ -533,19 +529,18 @@
             compiler_params=params,
             name="project_first",
         )(flag, *(in_place(arr) for arr in (start, pv, ids, cheb_coef)))
-        overlap_after = pl.pallas_call(
+        overlap = pl.pallas_call(
             functools.partial(overlap_kernel, sz),
             out_shape=jax.ShapeDtypeStruct((slots * slots * sz.zb, LANES), F32),
             in_specs=vmem(2),
             out_specs=vmem(1)[0],
             compiler_params=params,
             name="overlap",
-        )
-        overlap = None
+        )(row_of, pv)
         history = [start]
         for degree in range(1, STEPS + 1):
             tables, from_a, from_b, from_y, aside = exchange(
-                *messages, overlap_after if degree == 1 else None, degree == STEPS
+                *messages, overlap if degree == 1 else None, degree != 2
             )
             overlap = overlap if aside is None else aside
             last = degree == STEPS

time: 41.2 us -> 41.5 us (level)
  no operation moved by 1% of the time
where the time goes in v10:
time: 41.5 us; the launch traced here: 41.3 us
  waiting for transfers between devices  20.1 us (48%)
  starting transfers between devices  13.9 us (33%)
  Pallas kernels  6.4 us (15%)
  other arithmetic  0.73 us (2%)
    ppermute x3, waiting for transfers between devices, orb_swap(): return lax.ppermute(vals, 'orb', [(i, i ^ bit) for i in range(size)])  12.6 us
    ppermute x15, starting transfers between devices, swap(): return lax.ppermute(arr, ('gx', 'gy'), pairs)  10.8 us
    ppermute x15, waiting for transfers between devices, swap(): return lax.ppermute(arr, ('gx', 'gy'), pairs)  7.51 us
    ppermute x3, starting transfers between devices, orb_swap(): return lax.ppermute(vals, 'orb', [(i, i ^ bit) for i in range(size)])  3.06 us
    pallas_call x1, Pallas kernels, one_orbital(): pl.pallas_call(functools.partial(first_kernel, sz), out_shape=message_sha...  1.8 us
    pallas_call x3, Pallas kernels, one_orbital(): pl.pallas_call(functools.partial(local_kernel, sz, degree, len(from_y)),...  1.7 us
    pallas_call x2, Pallas kernels, one_orbital(): pl.pallas_call(functools.partial(nonlocal_kernel, sz, degree, len(tables)...  1.27 us
    pallas_call x2, Pallas kernels, square(): pl.pallas_call(functools.partial(last_kernel, sz, len(tables), len(before...  1.06 us
  transfers between devices with their start and end apart: 18, of which 11 were waited for; matrix products, arithmetic and copies ran while one was open for 0% of the time, Pallas kernels for 7%

profile of v10, /device:TPU:16, one launch (start us, length us, event | category | flops | bytes accessed | tf_op | source)
XLA Modules:
  0.0 41.3 jit_solution(9534241750868837758)
XLA Ops:
  0.0 1.8 %project_first.1 = (f32[128,128]{1,0:T(8,128)S(1)}, f32[128,128]{1,0:T(8,128)S(1)}, f32[128,128]{1,0:T(8,128)S(1)}, f32[32,128]{1,0:T(8,128)S(1)}, f32[12,128]{1...) custom-call(s32[1]{0:T(128)} %bitcast.flag_ref, f32[128,384]{1,0:T(8,128)} %bitcast.17, ...), custom_call_target="tpu_custom_call" | custom-call | tf_op jit(solution)/shard_map/project_first/pallas_call | solution.py:512
  1.8 1.0 %collective-permute-start.1 = (f32[128,128]{1,0:T(8,128)S(1)}, f32[128,128]{1,0:T(8,128)S(1)}, u32[]{:S(2)}, u32[]{:S(2)}) collective-permute-start(f32[128,128]{1,0:T(8,128)S(1)} %get-tuple-element.33), channel_id=1, source_target_pairs={{0,24},{4,28},{8,16},{12,20},{16,8},{20,12},{24,0},{28,4},{1,25},{... | collective-permute-start | bytes 196616 | tf_op jit(solution)/shard_map/ppermute | solution.py:409
  2.8 1.5 %collective-permute-start.2 = (f32[128,128]{1,0:T(8,128)S(1)}, f32[128,128]{1,0:T(8,128)S(1)}, u32[]{:S(2)}, u32[]{:S(2)}) collective-permute-start(f32[128,128]{1,0:T(8,128)S(1)} %get-tuple-element.34), channel_id=1, source_target_pairs={{0,4},{4,0},{8,12},{12,8},{16,20},{20,16},{24,28},{28,24},{1,5},{5... | collective-permute-start | bytes 196616 | tf_op jit(solution)/shard_map/ppermute | solution.py:409
  4.3 0.5 %collective-permute-start = (f32[32,128]{1,0:T(8,128)S(1)}, f32[32,128]{1,0:T(8,128)S(1)}, u32[]{:S(2)}, u32[]{:S(2)}) collective-permute-start(f32[32,128]{1,0:T(8,128)S(1)} %get-tuple-element.31), channel_id=1, source_target_pairs={{0,28},{4,24},{8,20},{12,16},{16,12},{20,8},{24,4},{28,0},{1,29},{... | collective-permute-start | bytes 49160 | tf_op jit(solution)/shard_map/ppermute | solution.py:409
  4.8 0.2 collective-permute-start.4
  5.0 0.0 copy-done
  5.0 0.6 %overlap.1.refs_8_.refs_10_ = f32[48,128]{1,0:T(8,128)S(1)} custom-call(f32[12,128]{1,0:T(8,128)S(1)} %get-tuple-element.29.after_ref.refs_5_.refs_7_.refs_2_, bf16[512,384]{1,0:T(8,128)(2,1)S(1)} %bitcast.10), custom_call_target="tpu_custom_call" | custom-call | tf_op jit(solution)/shard_map/overlap/pallas_call | solution.py:532
  5.6 2.8 %collective-permute-done = f32[32,128]{1,0:T(8,128)S(1)} collective-permute-done((f32[32,128]{1,0:T(8,128)S(1)}, f32[32,128]{1,0:T(8,128)S(1)}, u32[]{:S(2)}, u32[]{:S(2)}) %collective-permute-start) | collective-permute-done | bytes 16416 | tf_op jit(solution)/shard_map/ppermute | solution.py:409
  8.4 0.0 collective-permute-done.1.refs_1_
  8.4 0.0 collective-permute-done.2.refs_2_
  8.4 0.5 %collective-permute-start.3 = (f32[32,128]{1,0:T(8,128)S(1)}, f32[32,128]{1,0:T(8,128)S(1)}, u32[]{:S(2)}, u32[]{:S(2)}) collective-permute-start(f32[32,128]{1,0:T(8,128)S(1)} %slice_add_fusion.4.refs_0_), channel_id=1, source_target_pairs={{0,8},{4,12},{8,0},{12,4},{16,24},{20,28},{24,16},{28,20},{1,9},{5... | collective-permute-start | bytes 49160 | tf_op jit(solution)/shard_map/ppermute | solution.py:409
  8.9 0.0 collective-permute-done.4.refs_0_
  8.9 0.0 copy-start.3
  8.9 0.6 %local_1.1 = (f32[128,384]{1,0:T(8,128)S(1)}, f32[12,128]{1,0:T(8,128)S(1)}) custom-call(s32[1]{0:T(128)} %bitcast.flag_ref, f32[96,128]{1,0:T(8,128)S(1)} %collective-permute-done.4.refs_0_, f32[128,128]{1,0:T(8,128)S(1)} %collective-permute-done.1.refs_1_, f32[128,128]{1,0:T(8,128)S(1)} %collective-permute-done.2.refs_2_, f32[128,384]{1,0:T(8,128)S(1)} %bitcast.21, ...), custom_call_target="tpu_custom_call" | custom-call | tf_op jit(solution)/shard_map/local_1/pallas_call | solution.py:552
  9.6 0.2 collective-permute-done.3.refs_1_
  9.7 0.6 %nonlocal_1.1 = (f32[128,384]{1,0:T(8,128)S(1)}, f32[128,128]{1,0:T(8,128)S(1)}, f32[128,128]{1,0:T(8,128)S(1)}, f32[128,128]{1,0:T(8,128)S(1)}, f32[32,128]{1,0:T(8,128)S(1)}) custom-call(s32[1]{0:T(128)} %bitcast.flag_ref, f32[32,128]{1,0:T(8,128)S(1)} %slice_add_fusion.4.refs_0_, f32[32,128]{1,0:T(8,128)S(1)} %collective-permute-done.3.refs_1_, ...), custom_call_target="tpu_custom_call" | custom-call | tf_op jit(solution)/shard_map/nonlocal_1/pallas_call | solution.py:568
  10.4 0.4 collective-permute-start.5
  10.8 0.5 %collective-permute-start.6 = (f32[128,128]{1,0:T(8,128)S(1)}, f32[128,128]{1,0:T(8,128)S(1)}, u32[]{:S(2)}, u32[]{:S(2)}) collective-permute-start(f32[128,128]{1,0:T(8,128)S(1)} %get-tuple-element.41), channel_id=1, source_target_pairs={{0,4},{4,0},{8,12},{12,8},{16,20},{20,16},{24,28},{28,24},{1,5},{5... | collective-permute-start | bytes 196616 | tf_op jit(solution)/shard_map/ppermute | solution.py:409
  11.3 0.2 collective-permute-start.7
  11.5 0.2 collective-permute-done.5.refs_0_
  11.7 2.4 %collective-permute-start.9 = (f32[32,128]{1,0:T(8,128)S(1)}, f32[32,128]{1,0:T(8,128)S(1)}, u32[]{:S(2)}, u32[]{:S(2)}) collective-permute-start(f32[32,128]{1,0:T(8,128)S(1)} %slice_add_fusion.3.refs_0_), channel_id=1, source_target_pairs={{0,28},{4,24},{8,20},{12,16},{16,12},{20,8},{24,4},{28,0},{1,29},{... | collective-permute-start | bytes 49160 | tf_op jit(solution)/shard_map/ppermute | solution.py:409
  14.1 1.0 %collective-permute-done.6.refs_2_ = f32[128,128]{1,0:T(8,128)S(1)} collective-permute-done((f32[128,128]{1,0:T(8,128)S(1)}, f32[128,128]{1,0:T(8,128)S(1)}, u32[]{:S(2)}, u32[]{:S(2)}) %collective-permute-start.6) | collective-permute-done | bytes 65568 | tf_op jit(solution)/shard_map/ppermute | solution.py:409
  15.1 0.4 %collective-permute-done.7.refs_1_ = f32[128,128]{1,0:T(8,128)S(1)} collective-permute-done((f32[128,128]{1,0:T(8,128)S(1)}, f32[128,128]{1,0:T(8,128)S(1)}, u32[]{:S(2)}, u32[]{:S(2)}) %collective-permute-start.7) | collective-permute-done | bytes 65568 | tf_op jit(solution)/shard_map/ppermute | solution.py:409
  15.5 0.2 collective-permute-start.8
  15.7 0.6 %local_2.1 = (f32[128,384]{1,0:T(8,128)S(1)}, f32[12,128]{1,0:T(8,128)S(1)}) custom-call(s32[1]{0:T(128)} %bitcast.flag_ref, f32[128,128]{1,0:T(8,128)S(1)} %collective-permute-done.5.refs_0_, f32[128,128]{1,0:T(8,128)S(1)} %collective-permute-done.7.refs_1_, f32[128,128]{1,0:T(8,128)S(1)} %collective-permute-done.6.refs_2_, f32[128,384]{1,0:T(8,128)S(1)} %bitcast.22, ...), custom_call_target="tpu_custom_call" | custom-call | tf_op jit(solution)/shard_map/local_2/pallas_call | solution.py:552
  16.3 0.6 %collective-permute-done.9.refs_3_ = f32[32,128]{1,0:T(8,128)S(1)} collective-permute-done((f32[32,128]{1,0:T(8,128)S(1)}, f32[32,128]{1,0:T(8,128)S(1)}, u32[]{:S(2)}, u32[]{:S(2)}) %collective-permute-start.9) | collective-permute-done | bytes 16416 | tf_op jit(solution)/shard_map/ppermute | solution.py:409
  16.9 0.0 collective-permute-done.8.refs_2_
  16.9 0.6 %nonlocal_2.1 = (f32[128,384]{1,0:T(8,128)S(1)}, f32[128,128]{1,0:T(8,128)S(1)}, f32[128,128]{1,0:T(8,128)S(1)}, f32[128,128]{1,0:T(8,128)S(1)}, f32[32,128]{1,0:T(8,128)S(1)}) custom-call(s32[1]{0:T(128)} %bitcast.flag_ref, f32[32,128]{1,0:T(8,128)S(1)} %slice_add_fusion.3.refs_0_, f32[32,128]{1,0:T(8,128)S(1)} %slice_add_fusion.2.refs_1_, ...), custom_call_target="tpu_custom_call" | custom-call | tf_op jit(solution)/shard_map/nonlocal_2/pallas_call | solution.py:568
  17.6 0.3 collective-permute-start.11
  17.9 1.5 %collective-permute-start.12 = (f32[128,128]{1,0:T(8,128)S(1)}, f32[128,128]{1,0:T(8,128)S(1)}, u32[]{:S(2)}, u32[]{:S(2)}) collective-permute-start(f32[128,128]{1,0:T(8,128)S(1)} %get-tuple-element.48), channel_id=1, source_target_pairs={{0,4},{4,0},{8,12},{12,8},{16,20},{20,16},{24,28},{28,24},{1,5},{5... | collective-permute-start | bytes 196616 | tf_op jit(solution)/shard_map/ppermute | solution.py:409
  19.4 0.0 collective-permute-start.10
  19.4 1.6 %collective-permute-start.14 = (f32[32,128]{1,0:T(8,128)S(1)}, f32[32,128]{1,0:T(8,128)S(1)}, u32[]{:S(2)}, u32[]{:S(2)}) collective-permute-start(f32[32,128]{1,0:T(8,128)S(1)} %get-tuple-element.50), channel_id=1, source_target_pairs={{0,28},{4,24},{8,20},{12,16},{16,12},{20,8},{24,4},{28,0},{1,29},{... | collective-permute-start | bytes 49160 | tf_op jit(solution)/shard_map/ppermute | solution.py:409
  21.0 0.0 collective-permute-done.10.refs_1_
  21.0 0.8 %collective-permute-done.11.refs_2_ = f32[128,128]{1,0:T(8,128)S(1)} collective-permute-done((f32[128,128]{1,0:T(8,128)S(1)}, f32[128,128]{1,0:T(8,128)S(1)}, u32[]{:S(2)}, u32[]{:S(2)}) %collective-permute-start.11) | collective-permute-done | bytes 65568 | tf_op jit(solution)/shard_map/ppermute | solution.py:409
  21.7 0.4 collective-permute-done.12.refs_3_
  22.1 0.4 local_3.1.refs_4_
  22.6 1.6 %collective-permute-start.13 = (f32[128,384]{1,0:T(8,128)S(1)}, f32[128,384]{1,0:T(8,128)S(1)}, u32[]{:S(2)}, u32[]{:S(2)}) collective-permute-start(f32[128,384]{1,0:T(8,128)S(1)} %local_3.1.refs_4_), channel_id=1, source_target_pairs={{0,1},{1,0},{2,3},{3,2},{4,5},{5,4},{6,7},{7,6},{8,9},{9,8},{10,11... | collective-permute-start | bytes 589832 | tf_op jit(solution)/shard_map/ppermute | solution.py:414
  24.2 0.0 collective-permute-done.14
  24.2 0.1 collective-permute-start.15
  24.3 1.2 %collective-permute-done.15 = f32[32,128]{1,0:T(8,128)S(1)} collective-permute-done((f32[32,128]{1,0:T(8,128)S(1)}, f32[32,128]{1,0:T(8,128)S(1)}, u32[]{:S(2)}, u32[]{:S(2)}) %collective-permute-start.15) | collective-permute-done | bytes 16416 | tf_op jit(solution)/shard_map/ppermute | solution.py:409
  25.5 0.9 %collective-permute-start.16 = (f32[32,128]{1,0:T(8,128)S(1)}, f32[32,128]{1,0:T(8,128)S(1)}, u32[]{:S(2)}, u32[]{:S(2)}) collective-permute-start(f32[32,128]{1,0:T(8,128)S(1)} %add.38.refs_5_), channel_id=1, source_target_pairs={{0,1},{1,0},{2,3},{3,2},{4,5},{5,4},{6,7},{7,6},{8,9},{9,8},{10,11... | collective-permute-start | bytes 49160 | tf_op jit(solution)/shard_map/ppermute | solution.py:414
  26.4 0.5 %square.1.refs_6_ = f32[128,384]{1,0:T(8,128)S(1)} custom-call(f32[8,128]{1,0:T(8,128)S(1)} %get-tuple-element.28.refs_0_.cheb_ref, f32[32,128]{1,0:T(8,128)S(1)} %bitcast.26, bf16[512,384]{1,0:T(8,128)(2,1)S(1)} %bitcast.15, f32[12,128]{1,0:T(8,128)S(1)} %get-tuple-element.29.after_ref.refs_5_.refs_7_.refs_2_, ...), custom_call_target="tpu_custom_call" | custom-call | tf_op jit(solution)/shard_map/square/pallas_call | solution.py:502
  26.9 2.8 %collective-permute-done.16.refs_5_ = f32[32,128]{1,0:T(8,128)S(1)} collective-permute-done((f32[32,128]{1,0:T(8,128)S(1)}, f32[32,128]{1,0:T(8,128)S(1)}, u32[]{:S(2)}, u32[]{:S(2)}) %collective-permute-start.16) | collective-permute-done | bytes 16416 | tf_op jit(solution)/shard_map/ppermute | solution.py:414
  29.8 0.0 collective-permute-done.13.refs_4_
  29.8 0.5 %square_more.1 = f32[128,384]{1,0:T(8,128)S(1)} custom-call(f32[8,128]{1,0:T(8,128)S(1)} %get-tuple-element.28.refs_0_.cheb_ref, f32[32,128]{1,0:T(8,128)S(1)} %bitcast.27, bf16[512,384]{1,0:T(8,128)(2,1)S(1)} %bitcast.16, f32[12,128]{1,0:T(8,128)S(1)} %get-tuple-element.29.after_ref.refs_5_.refs_7_.refs_2_, ...), custom_call_target="tpu_custom_call" | custom-call | tf_op jit(solution)/shard_map/square_more/pallas_call | solution.py:502
  30.3 0.5 %collective-permute-start.17 = (f32[128,384]{1,0:T(8,128)S(1)}, f32[128,384]{1,0:T(8,128)S(1)}, u32[]{:S(2)}, u32[]{:S(2)}) collective-permute-start(f32[128,384]{1,0:T(8,128)S(1)} %square_more.1), channel_id=1, source_target_pairs={{0,3},{1,2},{2,1},{3,0},{4,7},{5,6},{6,5},{7,4},{8,11},{9,10},{10,... | collective-permute-start | bytes 589832 | tf_op jit(solution)/shard_map/ppermute | solution.py:414
  30.8 9.8 %collective-permute-done.17 = f32[128,384]{1,0:T(8,128)S(1)} collective-permute-done((f32[128,384]{1,0:T(8,128)S(1)}, f32[128,384]{1,0:T(8,128)S(1)}, u32[]{:S(2)}, u32[]{:S(2)}) %collective-permute-start.17) | collective-permute-done | bytes 196640 | tf_op jit(solution)/shard_map/ppermute | solution.py:414
  40.6 0.7 %add_multiply_fusion = f32[128,384]{1,0:T(8,128)} fusion(f32[128,384]{1,0:T(8,128)S(1)} %square_more.1, f32[128,384]{1,0:T(8,128)S(1)} %collective-permute-done.17), kind=kLoop, calls=%fused_computation | loop fusion | flops 98304 | bytes 589824 | tf_op jit(solution)/shard_map/mul | solution.py:587
  (13 shorter events, 0.0 us)
Async XLA Ops:
  0.0 5.0 %copy-start = (bf16[4,8,16,384]{3,2,1,0:T(8,128)(2,1)S(1)}, bf16[4,8,16,384]{3,2,1,0:T(8,128)(2,1)}, u32[]{:S(2)}) copy-start(bf16[4,8,16,384]{3,2,1,0:T(8,128)(2,1)} %param.8) | copy-start | bytes 1179652
  1.8 6.6 %collective-permute-start.1 = (f32[128,128]{1,0:T(8,128)S(1)}, f32[128,128]{1,0:T(8,128)S(1)}, u32[]{:S(2)}, u32[]{:S(2)}) collective-permute-start(f32[128,128]{1,0:T(8,128)S(1)} %get-tuple-element.33), channel_id=1, source_target_pairs={{0,24},{4,28},{8,16},{12,20},{16,8},{20,12},{24,0},{28,4},{1,25},{... | collective-permute-start | bytes 196616 | tf_op jit(solution)/shard_map/ppermute | solution.py:409
  2.8 5.6 %collective-permute-start.2 = (f32[128,128]{1,0:T(8,128)S(1)}, f32[128,128]{1,0:T(8,128)S(1)}, u32[]{:S(2)}, u32[]{:S(2)}) collective-permute-start(f32[128,128]{1,0:T(8,128)S(1)} %get-tuple-element.34), channel_id=1, source_target_pairs={{0,4},{4,0},{8,12},{12,8},{16,20},{20,16},{24,28},{28,24},{1,5},{5... | collective-permute-start | bytes 196616 | tf_op jit(solution)/shard_map/ppermute | solution.py:409
  4.3 4.1 %collective-permute-start = (f32[32,128]{1,0:T(8,128)S(1)}, f32[32,128]{1,0:T(8,128)S(1)}, u32[]{:S(2)}, u32[]{:S(2)}) collective-permute-start(f32[32,128]{1,0:T(8,128)S(1)} %get-tuple-element.31), channel_id=1, source_target_pairs={{0,28},{4,24},{8,20},{12,16},{16,12},{20,8},{24,4},{28,0},{1,29},{... | collective-permute-start | bytes 49160 | tf_op jit(solution)/shard_map/ppermute | solution.py:409
  4.8 4.1 %collective-permute-start.4 = (f32[96,128]{1,0:T(8,128)S(1)}, f32[96,128]{1,0:T(8,128)S(1)}, u32[]{:S(2)}, u32[]{:S(2)}) collective-permute-start(f32[96,128]{1,0:T(8,128)S(1)} %slice.29), channel_id=1, source_target_pairs={{0,8},{4,12},{8,0},{12,4},{16,24},{20,28},{24,16},{28,20},{1,9},{5... | collective-permute-start | bytes 147464 | tf_op jit(solution)/shard_map/ppermute | solution.py:409
  5.0 3.9 %copy-start.1 = (f32[1,8,16,384]{3,2,1,0:T(8,128)S(1)}, f32[1,8,16,384]{3,2,1,0:T(8,128)}, u32[]{:S(2)}) copy-start(f32[1,8,16,384]{3,2,1,0:T(8,128)} %param.6) | copy-start | bytes 589828
  5.0 3.9 %copy-start.2 = (f32[8,16,384]{2,1,0:T(8,128)S(1)}, f32[8,16,384]{2,1,0:T(8,128)}, u32[]{:S(2)}) copy-start(f32[8,16,384]{2,1,0:T(8,128)} %param.7) | copy-start | bytes 589828
  8.4 1.3 %collective-permute-start.3 = (f32[32,128]{1,0:T(8,128)S(1)}, f32[32,128]{1,0:T(8,128)S(1)}, u32[]{:S(2)}, u32[]{:S(2)}) collective-permute-start(f32[32,128]{1,0:T(8,128)S(1)} %slice_add_fusion.4.refs_0_), channel_id=1, source_target_pairs={{0,8},{4,12},{8,0},{12,4},{16,24},{20,28},{24,16},{28,20},{1,9},{5... | collective-permute-start | bytes 49160 | tf_op jit(solution)/shard_map/ppermute | solution.py:409
  8.9 0.8 %copy-start.3 = (f32[4096]{0:T(1024)S(1)}, f32[4096]{0:T(1024)}, u32[]{:S(2)}) copy-start(f32[4096]{0:T(1024)} %param.10) | copy-start | bytes 49156
  10.4 1.3 %collective-permute-start.5 = (f32[128,128]{1,0:T(8,128)S(1)}, f32[128,128]{1,0:T(8,128)S(1)}, u32[]{:S(2)}, u32[]{:S(2)}) collective-permute-start(f32[128,128]{1,0:T(8,128)S(1)} %get-tuple-element.40), channel_id=1, source_target_pairs={{0,8},{4,12},{8,0},{12,4},{16,24},{20,28},{24,16},{28,20},{1,9},{5... | collective-permute-start | bytes 196616 | tf_op jit(solution)/shard_map/ppermute | solution.py:409
  10.8 4.3 %collective-permute-start.6 = (f32[128,128]{1,0:T(8,128)S(1)}, f32[128,128]{1,0:T(8,128)S(1)}, u32[]{:S(2)}, u32[]{:S(2)}) collective-permute-start(f32[128,128]{1,0:T(8,128)S(1)} %get-tuple-element.41), channel_id=1, source_target_pairs={{0,4},{4,0},{8,12},{12,8},{16,20},{20,16},{24,28},{28,24},{1,5},{5... | collective-permute-start | bytes 196616 | tf_op jit(solution)/shard_map/ppermute | solution.py:409
  11.3 4.2 %collective-permute-start.7 = (f32[128,128]{1,0:T(8,128)S(1)}, f32[128,128]{1,0:T(8,128)S(1)}, u32[]{:S(2)}, u32[]{:S(2)}) collective-permute-start(f32[128,128]{1,0:T(8,128)S(1)} %get-tuple-element.42), channel_id=1, source_target_pairs={{0,24},{4,28},{8,16},{12,20},{16,8},{20,12},{24,0},{28,4},{1,25},{... | collective-permute-start | bytes 196616 | tf_op jit(solution)/shard_map/ppermute | solution.py:409
  11.7 5.2 %collective-permute-start.9 = (f32[32,128]{1,0:T(8,128)S(1)}, f32[32,128]{1,0:T(8,128)S(1)}, u32[]{:S(2)}, u32[]{:S(2)}) collective-permute-start(f32[32,128]{1,0:T(8,128)S(1)} %slice_add_fusion.3.refs_0_), channel_id=1, source_target_pairs={{0,28},{4,24},{8,20},{12,16},{16,12},{20,8},{24,4},{28,0},{1,29},{... | collective-permute-start | bytes 49160 | tf_op jit(solution)/shard_map/ppermute | solution.py:409
  15.5 1.4 %collective-permute-start.8 = (f32[32,128]{1,0:T(8,128)S(1)}, f32[32,128]{1,0:T(8,128)S(1)}, u32[]{:S(2)}, u32[]{:S(2)}) collective-permute-start(f32[32,128]{1,0:T(8,128)S(1)} %slice_add_fusion.2.refs_1_), channel_id=1, source_target_pairs={{0,8},{4,12},{8,0},{12,4},{16,24},{20,28},{24,16},{28,20},{1,9},{5... | collective-permute-start | bytes 49160 | tf_op jit(solution)/shard_map/ppermute | solution.py:409
  17.6 4.2 %collective-permute-start.11 = (f32[128,128]{1,0:T(8,128)S(1)}, f32[128,128]{1,0:T(8,128)S(1)}, u32[]{:S(2)}, u32[]{:S(2)}) collective-permute-start(f32[128,128]{1,0:T(8,128)S(1)} %get-tuple-element.47), channel_id=1, source_target_pairs={{0,24},{4,28},{8,16},{12,20},{16,8},{20,12},{24,0},{28,4},{1,25},{... | collective-permute-start | bytes 196616 | tf_op jit(solution)/shard_map/ppermute | solution.py:409
  17.9 4.3 %collective-permute-start.12 = (f32[128,128]{1,0:T(8,128)S(1)}, f32[128,128]{1,0:T(8,128)S(1)}, u32[]{:S(2)}, u32[]{:S(2)}) collective-permute-start(f32[128,128]{1,0:T(8,128)S(1)} %get-tuple-element.48), channel_id=1, source_target_pairs={{0,4},{4,0},{8,12},{12,8},{16,20},{20,16},{24,28},{28,24},{1,5},{5... | collective-permute-start | bytes 196616 | tf_op jit(solution)/shard_map/ppermute | solution.py:409
  19.4 1.6 %collective-permute-start.10 = (f32[96,128]{1,0:T(8,128)S(1)}, f32[96,128]{1,0:T(8,128)S(1)}, u32[]{:S(2)}, u32[]{:S(2)}) collective-permute-start(f32[96,128]{1,0:T(8,128)S(1)} %slice.33), channel_id=1, source_target_pairs={{0,8},{4,12},{8,0},{12,4},{16,24},{20,28},{24,16},{28,20},{1,9},{5... | collective-permute-start | bytes 147464 | tf_op jit(solution)/shard_map/ppermute | solution.py:409
  19.4 4.8 %collective-permute-start.14 = (f32[32,128]{1,0:T(8,128)S(1)}, f32[32,128]{1,0:T(8,128)S(1)}, u32[]{:S(2)}, u32[]{:S(2)}) collective-permute-start(f32[32,128]{1,0:T(8,128)S(1)} %get-tuple-element.50), channel_id=1, source_target_pairs={{0,28},{4,24},{8,20},{12,16},{16,12},{20,8},{24,4},{28,0},{1,29},{... | collective-permute-start | bytes 49160 | tf_op jit(solution)/shard_map/ppermute | solution.py:409
  22.6 7.2 %collective-permute-start.13 = (f32[128,384]{1,0:T(8,128)S(1)}, f32[128,384]{1,0:T(8,128)S(1)}, u32[]{:S(2)}, u32[]{:S(2)}) collective-permute-start(f32[128,384]{1,0:T(8,128)S(1)} %local_3.1.refs_4_), channel_id=1, source_target_pairs={{0,1},{1,0},{2,3},{3,2},{4,5},{5,4},{6,7},{7,6},{8,9},{9,8},{10,11... | collective-permute-start | bytes 589832 | tf_op jit(solution)/shard_map/ppermute | solution.py:414
  24.2 1.2 %collective-permute-start.15 = (f32[32,128]{1,0:T(8,128)S(1)}, f32[32,128]{1,0:T(8,128)S(1)}, u32[]{:S(2)}, u32[]{:S(2)}) collective-permute-start(f32[32,128]{1,0:T(8,128)S(1)} %slice_add_fusion), channel_id=1, source_target_pairs={{0,8},{4,12},{8,0},{12,4},{16,24},{20,28},{24,16},{28,20},{1,9},{5... | collective-permute-start | bytes 49160 | tf_op jit(solution)/shard_map/ppermute | solution.py:409
  25.5 4.3 %collective-permute-start.16 = (f32[32,128]{1,0:T(8,128)S(1)}, f32[32,128]{1,0:T(8,128)S(1)}, u32[]{:S(2)}, u32[]{:S(2)}) collective-permute-start(f32[32,128]{1,0:T(8,128)S(1)} %add.38.refs_5_), channel_id=1, source_target_pairs={{0,1},{1,0},{2,3},{3,2},{4,5},{5,4},{6,7},{7,6},{8,9},{9,8},{10,11... | collective-permute-start | bytes 49160 | tf_op jit(solution)/shard_map/ppermute | solution.py:414
  30.3 10.2 %collective-permute-start.17 = (f32[128,384]{1,0:T(8,128)S(1)}, f32[128,384]{1,0:T(8,128)S(1)}, u32[]{:S(2)}, u32[]{:S(2)}) collective-permute-start(f32[128,384]{1,0:T(8,128)S(1)} %square_more.1), channel_id=1, source_target_pairs={{0,3},{1,2},{2,1},{3,0},{4,7},{5,6},{6,5},{7,4},{8,11},{9,10},{10,... | collective-permute-start | bytes 589832 | tf_op jit(solution)/shard_map/ppermute | solution.py:414

commit v11 on v9

--- a/solution.py
+++ b/solution.py
@@ -474,11 +474,10 @@
             from_b = swap(to_b, lambda i, j: (size_first - 1 - i, j))
             from_y = swap(to_y, lambda i, j: (i, 1 - j))
             chip = table + from_a[sz.edge_rows :]
-            if aside is not None:
-                aside = aside(chip, pv)
             from_d = swap(chip, lambda i, j: (size_first - 1 - i, 1 - j))
             if aside is not None:
-                from_y, aside = lax.optimization_barrier((from_y, aside))
+                aside = aside(from_y, pv)
+                from_b, aside = lax.optimization_barrier((from_b, aside))
             beside = from_y[sz.yedge_rows :] + from_b[sz.edge_rows :]
             other = swap(beside, lambda i, j: (i ^ 1, j))
             return [chip, beside, other, from_d], from_a, from_b, [from_y], aside

time: 41.2 us -> 41.5 us (level)
  no operation moved by 1% of the time
where the time goes in v11:
time: 41.5 us; the launch traced here: 41.4 us
  waiting for transfers between devices  19.8 us (48%)
  starting transfers between devices  14.4 us (35%)
  Pallas kernels  6.4 us (15%)
  other arithmetic  0.73 us (2%)
    ppermute x3, waiting for transfers between devices, orb_swap(): return lax.ppermute(vals, 'orb', [(i, i ^ bit) for i in range(size)])  12.5 us
    ppermute x15, starting transfers between devices, swap(): return lax.ppermute(arr, ('gx', 'gy'), pairs)  11.4 us
    ppermute x15, waiting for transfers between devices, swap(): return lax.ppermute(arr, ('gx', 'gy'), pairs)  7.26 us
    ppermute x3, starting transfers between devices, orb_swap(): return lax.ppermute(vals, 'orb', [(i, i ^ bit) for i in range(size)])  2.95 us
    pallas_call x1, Pallas kernels, one_orbital(): pl.pallas_call(functools.partial(first_kernel, sz), out_shape=message_sha...  1.8 us
    pallas_call x3, Pallas kernels, one_orbital(): pl.pallas_call(functools.partial(local_kernel, sz, degree, len(from_y)),...  1.7 us
    pallas_call x2, Pallas kernels, one_orbital(): pl.pallas_call(functools.partial(nonlocal_kernel, sz, degree, len(tables)...  1.27 us
    pallas_call x2, Pallas kernels, square(): pl.pallas_call(functools.partial(last_kernel, sz, len(tables), len(before...  1.05 us
  transfers between devices with their start and end apart: 18, of which 11 were waited for; matrix products, arithmetic and copies ran while one was open for 0% of the time, Pallas kernels for 7%

profile of v11, /device:TPU:16, one launch (start us, length us, event | category | flops | bytes accessed | tf_op | source)
XLA Modules:
  0.0 41.4 jit_solution(3701607607932354330)
XLA Ops:
  0.0 1.8 %project_first.1 = (f32[128,128]{1,0:T(8,128)S(1)}, f32[128,128]{1,0:T(8,128)S(1)}, f32[128,128]{1,0:T(8,128)S(1)}, f32[32,128]{1,0:T(8,128)S(1)}, f32[12,128]{1...) custom-call(s32[1]{0:T(128)} %bitcast.flag_ref, f32[128,384]{1,0:T(8,128)} %bitcast.17, ...), custom_call_target="tpu_custom_call" | custom-call | tf_op jit(solution)/shard_map/project_first/pallas_call | solution.py:515
  1.8 0.1 collective-permute-start
  1.9 1.6 %collective-permute-start.1 = (f32[128,128]{1,0:T(8,128)S(1)}, f32[128,128]{1,0:T(8,128)S(1)}, u32[]{:S(2)}, u32[]{:S(2)}) collective-permute-start(f32[128,128]{1,0:T(8,128)S(1)} %get-tuple-element.33), channel_id=1, source_target_pairs={{0,4},{4,0},{8,12},{12,8},{16,20},{20,16},{24,28},{28,24},{1,5},{5... | collective-permute-start | bytes 196616 | tf_op jit(solution)/shard_map/ppermute | solution.py:409
  3.5 1.3 %collective-permute-start.2 = (f32[128,128]{1,0:T(8,128)S(1)}, f32[128,128]{1,0:T(8,128)S(1)}, u32[]{:S(2)}, u32[]{:S(2)}) collective-permute-start(f32[128,128]{1,0:T(8,128)S(1)} %get-tuple-element.34), channel_id=1, source_target_pairs={{0,24},{4,28},{8,16},{12,20},{16,8},{20,12},{24,0},{28,4},{1,25},{... | collective-permute-start | bytes 196616 | tf_op jit(solution)/shard_map/ppermute | solution.py:409
  4.7 0.0 collective-permute-done.refs_0_
  4.8 0.0 copy-start.2
  4.8 0.7 %collective-permute-start.4 = (f32[32,128]{1,0:T(8,128)S(1)}, f32[32,128]{1,0:T(8,128)S(1)}, u32[]{:S(2)}, u32[]{:S(2)}) collective-permute-start(f32[32,128]{1,0:T(8,128)S(1)} %slice_add_fusion.5.refs_0_), channel_id=1, source_target_pairs={{0,28},{4,24},{8,20},{12,16},{16,12},{20,8},{24,4},{28,0},{1,29},{... | collective-permute-start | bytes 49160 | tf_op jit(solution)/shard_map/ppermute | solution.py:409
  5.4 1.0 %collective-permute-done.1.after_ref.refs_2_ = f32[128,128]{1,0:T(8,128)S(1)} collective-permute-done((f32[128,128]{1,0:T(8,128)S(1)}, f32[128,128]{1,0:T(8,128)S(1)}, u32[]{:S(2)}, u32[]{:S(2)}) %collective-permute-start.1) | collective-permute-done | bytes 65568 | tf_op jit(solution)/shard_map/ppermute | solution.py:409
  6.4 0.6 %overlap.1.refs_10_ = f32[48,128]{1,0:T(8,128)S(1)} custom-call(f32[128,128]{1,0:T(8,128)S(1)} %collective-permute-done.1.after_ref.refs_2_, bf16[512,384]{1,0:T(8,128)(2,1)S(1)} %bitcast.10), custom_call_target="tpu_custom_call" | custom-call | tf_op jit(solution)/shard_map/overlap/pallas_call | solution.py:479
  7.0 0.5 %collective-permute-done.2.refs_1_ = f32[128,128]{1,0:T(8,128)S(1)} collective-permute-done((f32[128,128]{1,0:T(8,128)S(1)}, f32[128,128]{1,0:T(8,128)S(1)}, u32[]{:S(2)}, u32[]{:S(2)}) %collective-permute-start.2) | collective-permute-done | bytes 65568 | tf_op jit(solution)/shard_map/ppermute | solution.py:409
  7.5 0.3 collective-permute-start.3
  7.8 0.6 %local_1.1 = (f32[128,384]{1,0:T(8,128)S(1)}, f32[12,128]{1,0:T(8,128)S(1)}) custom-call(s32[1]{0:T(128)} %bitcast.flag_ref, f32[128,128]{1,0:T(8,128)S(1)} %collective-permute-done.refs_0_, f32[128,128]{1,0:T(8,128)S(1)} %collective-permute-done.2.refs_1_, f32[128,128]{1,0:T(8,128)S(1)} %collective-permute-done.1.after_ref.refs_2_, ...), custom_call_target="tpu_custom_call" | custom-call | tf_op jit(solution)/shard_map/local_1/pallas_call | solution.py:556
  8.5 0.4 %collective-permute-done.4.refs_3_ = f32[32,128]{1,0:T(8,128)S(1)} collective-permute-done((f32[32,128]{1,0:T(8,128)S(1)}, f32[32,128]{1,0:T(8,128)S(1)}, u32[]{:S(2)}, u32[]{:S(2)}) %collective-permute-start.4) | collective-permute-done | bytes 16416 | tf_op jit(solution)/shard_map/ppermute | solution.py:409
  8.9 0.0 collective-permute-done.3.refs_2_
  8.9 0.0 copy-done.3
  8.9 0.6 %nonlocal_1.1 = (f32[128,384]{1,0:T(8,128)S(1)}, f32[128,128]{1,0:T(8,128)S(1)}, f32[128,128]{1,0:T(8,128)S(1)}, f32[128,128]{1,0:T(8,128)S(1)}, f32[32,128]{1,0:T(8,128)S(1)}) custom-call(s32[1]{0:T(128)} %bitcast.flag_ref, f32[32,128]{1,0:T(8,128)S(1)} %slice_add_fusion.5.refs_0_, f32[32,128]{1,0:T(8,128)S(1)} %slice_add_fusion.4.refs_1_, ...), custom_call_target="tpu_custom_call" | custom-call | tf_op jit(solution)/shard_map/nonlocal_1/pallas_call | solution.py:572
  9.5 0.4 %collective-permute-start.5 = (f32[128,128]{1,0:T(8,128)S(1)}, f32[128,128]{1,0:T(8,128)S(1)}, u32[]{:S(2)}, u32[]{:S(2)}) collective-permute-start(f32[128,128]{1,0:T(8,128)S(1)} %get-tuple-element.40), channel_id=1, source_target_pairs={{0,8},{4,12},{8,0},{12,4},{16,24},{20,28},{24,16},{28,20},{1,9},{5... | collective-permute-start | bytes 196616 | tf_op jit(solution)/shard_map/ppermute | solution.py:409
  10.0 0.7 %collective-permute-start.6 = (f32[128,128]{1,0:T(8,128)S(1)}, f32[128,128]{1,0:T(8,128)S(1)}, u32[]{:S(2)}, u32[]{:S(2)}) collective-permute-start(f32[128,128]{1,0:T(8,128)S(1)} %get-tuple-element.41), channel_id=1, source_target_pairs={{0,4},{4,0},{8,12},{12,8},{16,20},{20,16},{24,28},{28,24},{1,5},{5... | collective-permute-start | bytes 196616 | tf_op jit(solution)/shard_map/ppermute | solution.py:409
  10.6 1.2 %collective-permute-start.7 = (f32[128,128]{1,0:T(8,128)S(1)}, f32[128,128]{1,0:T(8,128)S(1)}, u32[]{:S(2)}, u32[]{:S(2)}) collective-permute-start(f32[128,128]{1,0:T(8,128)S(1)} %get-tuple-element.42), channel_id=1, source_target_pairs={{0,24},{4,28},{8,16},{12,20},{16,8},{20,12},{24,0},{28,4},{1,25},{... | collective-permute-start | bytes 196616 | tf_op jit(solution)/shard_map/ppermute | solution.py:409
  11.8 0.0 collective-permute-done.5.refs_0_
  11.8 1.4 %collective-permute-start.9 = (f32[32,128]{1,0:T(8,128)S(1)}, f32[32,128]{1,0:T(8,128)S(1)}, u32[]{:S(2)}, u32[]{:S(2)}) collective-permute-start(f32[32,128]{1,0:T(8,128)S(1)} %slice_add_fusion.3.refs_0_), channel_id=1, source_target_pairs={{0,28},{4,24},{8,20},{12,16},{16,12},{20,8},{24,4},{28,0},{1,29},{... | collective-permute-start | bytes 49160 | tf_op jit(solution)/shard_map/ppermute | solution.py:409
  13.2 1.0 %collective-permute-done.6.refs_2_ = f32[128,128]{1,0:T(8,128)S(1)} collective-permute-done((f32[128,128]{1,0:T(8,128)S(1)}, f32[128,128]{1,0:T(8,128)S(1)}, u32[]{:S(2)}, u32[]{:S(2)}) %collective-permute-start.6) | collective-permute-done | bytes 65568 | tf_op jit(solution)/shard_map/ppermute | solution.py:409
  14.2 0.6 %collective-permute-done.7.refs_1_ = f32[128,128]{1,0:T(8,128)S(1)} collective-permute-done((f32[128,128]{1,0:T(8,128)S(1)}, f32[128,128]{1,0:T(8,128)S(1)}, u32[]{:S(2)}, u32[]{:S(2)}) %collective-permute-start.7) | collective-permute-done | bytes 65568 | tf_op jit(solution)/shard_map/ppermute | solution.py:409
  14.8 0.1 collective-permute-start.8
  14.9 0.7 %local_2.1 = (f32[128,384]{1,0:T(8,128)S(1)}, f32[12,128]{1,0:T(8,128)S(1)}) custom-call(s32[1]{0:T(128)} %bitcast.flag_ref, f32[128,128]{1,0:T(8,128)S(1)} %collective-permute-done.5.refs_0_, f32[128,128]{1,0:T(8,128)S(1)} %collective-permute-done.7.refs_1_, f32[128,128]{1,0:T(8,128)S(1)} %collective-permute-done.6.refs_2_, f32[128,384]{1,0:T(8,128)S(1)} %bitcast.22, ...), custom_call_target="tpu_custom_call" | custom-call | tf_op jit(solution)/shard_map/local_2/pallas_call | solution.py:556
  15.6 0.4 %collective-permute-done.9.refs_3_ = f32[32,128]{1,0:T(8,128)S(1)} collective-permute-done((f32[32,128]{1,0:T(8,128)S(1)}, f32[32,128]{1,0:T(8,128)S(1)}, u32[]{:S(2)}, u32[]{:S(2)}) %collective-permute-start.9) | collective-permute-done | bytes 16416 | tf_op jit(solution)/shard_map/ppermute | solution.py:409
  16.0 0.0 collective-permute-done.8.refs_2_
  16.0 0.6 %nonlocal_2.1 = (f32[128,384]{1,0:T(8,128)S(1)}, f32[128,128]{1,0:T(8,128)S(1)}, f32[128,128]{1,0:T(8,128)S(1)}, f32[128,128]{1,0:T(8,128)S(1)}, f32[32,128]{1,0:T(8,128)S(1)}) custom-call(s32[1]{0:T(128)} %bitcast.flag_ref, f32[32,128]{1,0:T(8,128)S(1)} %slice_add_fusion.3.refs_0_, f32[32,128]{1,0:T(8,128)S(1)} %slice_add_fusion.2.refs_1_, ...), custom_call_target="tpu_custom_call" | custom-call | tf_op jit(solution)/shard_map/nonlocal_2/pallas_call | solution.py:572
  16.6 1.4 %collective-permute-start.11 = (f32[128,128]{1,0:T(8,128)S(1)}, f32[128,128]{1,0:T(8,128)S(1)}, u32[]{:S(2)}, u32[]{:S(2)}) collective-permute-start(f32[128,128]{1,0:T(8,128)S(1)} %get-tuple-element.47), channel_id=1, source_target_pairs={{0,24},{4,28},{8,16},{12,20},{16,8},{20,12},{24,0},{28,4},{1,25},{... | collective-permute-start | bytes 196616 | tf_op jit(solution)/shard_map/ppermute | solution.py:409
  18.1 1.5 %collective-permute-start.12 = (f32[128,128]{1,0:T(8,128)S(1)}, f32[128,128]{1,0:T(8,128)S(1)}, u32[]{:S(2)}, u32[]{:S(2)}) collective-permute-start(f32[128,128]{1,0:T(8,128)S(1)} %get-tuple-element.48), channel_id=1, source_target_pairs={{0,4},{4,0},{8,12},{12,8},{16,20},{20,16},{24,28},{28,24},{1,5},{5... | collective-permute-start | bytes 196616 | tf_op jit(solution)/shard_map/ppermute | solution.py:409
  19.6 0.0 collective-permute-start.10
  19.6 0.7 %collective-permute-start.14 = (f32[32,128]{1,0:T(8,128)S(1)}, f32[32,128]{1,0:T(8,128)S(1)}, u32[]{:S(2)}, u32[]{:S(2)}) collective-permute-start(f32[32,128]{1,0:T(8,128)S(1)} %get-tuple-element.50), channel_id=1, source_target_pairs={{0,28},{4,24},{8,20},{12,16},{16,12},{20,8},{24,4},{28,0},{1,29},{... | collective-permute-start | bytes 49160 | tf_op jit(solution)/shard_map/ppermute | solution.py:409
  20.3 0.5 %collective-permute-done.10.refs_1_ = f32[96,128]{1,0:T(8,128)S(1)} collective-permute-done((f32[96,128]{1,0:T(8,128)S(1)}, f32[96,128]{1,0:T(8,128)S(1)}, u32[]{:S(2)}, u32[]{:S(2)}) %collective-permute-start.10) | collective-permute-done | bytes 49184 | tf_op jit(solution)/shard_map/ppermute | solution.py:409
  20.8 0.0 collective-permute-done.11.refs_2_
  20.8 1.7 %collective-permute-done.12.refs_3_ = f32[128,128]{1,0:T(8,128)S(1)} collective-permute-done((f32[128,128]{1,0:T(8,128)S(1)}, f32[128,128]{1,0:T(8,128)S(1)}, u32[]{:S(2)}, u32[]{:S(2)}) %collective-permute-start.12) | collective-permute-done | bytes 65568 | tf_op jit(solution)/shard_map/ppermute | solution.py:409
  22.5 0.4 local_3.1.refs_4_
  22.9 1.6 %collective-permute-start.13 = (f32[128,384]{1,0:T(8,128)S(1)}, f32[128,384]{1,0:T(8,128)S(1)}, u32[]{:S(2)}, u32[]{:S(2)}) collective-permute-start(f32[128,384]{1,0:T(8,128)S(1)} %local_3.1.refs_4_), channel_id=1, source_target_pairs={{0,1},{1,0},{2,3},{3,2},{4,5},{5,4},{6,7},{7,6},{8,9},{9,8},{10,11... | collective-permute-start | bytes 589832 | tf_op jit(solution)/shard_map/ppermute | solution.py:414
  24.5 0.0 collective-permute-done.14
  24.5 0.1 collective-permute-start.15
  24.6 1.2 %collective-permute-done.15 = f32[32,128]{1,0:T(8,128)S(1)} collective-permute-done((f32[32,128]{1,0:T(8,128)S(1)}, f32[32,128]{1,0:T(8,128)S(1)}, u32[]{:S(2)}, u32[]{:S(2)}) %collective-permute-start.15) | collective-permute-done | bytes 16416 | tf_op jit(solution)/shard_map/ppermute | solution.py:409
  25.8 0.8 %collective-permute-start.16 = (f32[32,128]{1,0:T(8,128)S(1)}, f32[32,128]{1,0:T(8,128)S(1)}, u32[]{:S(2)}, u32[]{:S(2)}) collective-permute-start(f32[32,128]{1,0:T(8,128)S(1)} %add.34.refs_5_), channel_id=1, source_target_pairs={{0,1},{1,0},{2,3},{3,2},{4,5},{5,4},{6,7},{7,6},{8,9},{9,8},{10,11... | collective-permute-start | bytes 49160 | tf_op jit(solution)/shard_map/ppermute | solution.py:414
  26.6 0.5 %square.1.refs_6_ = f32[128,384]{1,0:T(8,128)S(1)} custom-call(f32[8,128]{1,0:T(8,128)S(1)} %get-tuple-element.28.refs_0_.cheb_ref, f32[32,128]{1,0:T(8,128)S(1)} %bitcast.26, bf16[512,384]{1,0:T(8,128)(2,1)S(1)} %bitcast.15, f32[12,128]{1,0:T(8,128)S(1)} %get-tuple-element.29.refs_7_.refs_2_, bf16[128,1536]{1,0:T(8,128)(2,1)S(1)} %get-tuple-element.30.refs_8_.refs_3_, ...), custom_call_target="tpu_custom_call" | custom-call | tf_op jit(solution)/shard_map/square/pallas_call | solution.py:505
  27.1 2.6 %collective-permute-done.16.refs_5_ = f32[32,128]{1,0:T(8,128)S(1)} collective-permute-done((f32[32,128]{1,0:T(8,128)S(1)}, f32[32,128]{1,0:T(8,128)S(1)}, u32[]{:S(2)}, u32[]{:S(2)}) %collective-permute-start.16) | collective-permute-done | bytes 16416 | tf_op jit(solution)/shard_map/ppermute | solution.py:414
  29.8 0.0 collective-permute-done.13.refs_4_
  29.8 0.5 %square_more.1 = f32[128,384]{1,0:T(8,128)S(1)} custom-call(f32[8,128]{1,0:T(8,128)S(1)} %get-tuple-element.28.refs_0_.cheb_ref, f32[32,128]{1,0:T(8,128)S(1)} %bitcast.27, bf16[512,384]{1,0:T(8,128)(2,1)S(1)} %bitcast.16, f32[12,128]{1,0:T(8,128)S(1)} %get-tuple-element.29.refs_7_.refs_2_, bf16[128,1536]{1,0:T(8,128)(2,1)S(1)} %get-tuple-element.30.refs_8_.refs_3_, ...), custom_call_target="tpu_custom_call" | custom-call | tf_op jit(solution)/shard_map/square_more/pallas_call | solution.py:505
  30.3 0.5 %collective-permute-start.17 = (f32[128,384]{1,0:T(8,128)S(1)}, f32[128,384]{1,0:T(8,128)S(1)}, u32[]{:S(2)}, u32[]{:S(2)}) collective-permute-start(f32[128,384]{1,0:T(8,128)S(1)} %square_more.1), channel_id=1, source_target_pairs={{0,3},{1,2},{2,1},{3,0},{4,7},{5,6},{6,5},{7,4},{8,11},{9,10},{10,... | collective-permute-start | bytes 589832 | tf_op jit(solution)/shard_map/ppermute | solution.py:414
  30.8 9.9 %collective-permute-done.17 = f32[128,384]{1,0:T(8,128)S(1)} collective-permute-done((f32[128,384]{1,0:T(8,128)S(1)}, f32[128,384]{1,0:T(8,128)S(1)}, u32[]{:S(2)}, u32[]{:S(2)}) %collective-permute-start.17) | collective-permute-done | bytes 196640 | tf_op jit(solution)/shard_map/ppermute | solution.py:414
  40.7 0.7 %add_multiply_fusion = f32[128,384]{1,0:T(8,128)} fusion(f32[128,384]{1,0:T(8,128)S(1)} %square_more.1, f32[128,384]{1,0:T(8,128)S(1)} %collective-permute-done.17), kind=kLoop, calls=%fused_computation | loop fusion | flops 98304 | bytes 589824 | tf_op jit(solution)/shard_map/mul | solution.py:591
  (13 shorter events, 0.0 us)
Async XLA Ops:
  0.0 6.4 %copy-start = (bf16[4,8,16,384]{3,2,1,0:T(8,128)(2,1)S(1)}, bf16[4,8,16,384]{3,2,1,0:T(8,128)(2,1)}, u32[]{:S(2)}) copy-start(bf16[4,8,16,384]{3,2,1,0:T(8,128)(2,1)} %param.8) | copy-start | bytes 1179652
  1.8 2.9 %collective-permute-start = (f32[128,128]{1,0:T(8,128)S(1)}, f32[128,128]{1,0:T(8,128)S(1)}, u32[]{:S(2)}, u32[]{:S(2)}) collective-permute-start(f32[128,128]{1,0:T(8,128)S(1)} %get-tuple-element.32), channel_id=1, source_target_pairs={{0,8},{4,12},{8,0},{12,4},{16,24},{20,28},{24,16},{28,20},{1,9},{5... | collective-permute-start | bytes 196616 | tf_op jit(solution)/shard_map/ppermute | solution.py:409
  1.9 4.5 %collective-permute-start.1 = (f32[128,128]{1,0:T(8,128)S(1)}, f32[128,128]{1,0:T(8,128)S(1)}, u32[]{:S(2)}, u32[]{:S(2)}) collective-permute-start(f32[128,128]{1,0:T(8,128)S(1)} %get-tuple-element.33), channel_id=1, source_target_pairs={{0,4},{4,0},{8,12},{12,8},{16,20},{20,16},{24,28},{28,24},{1,5},{5... | collective-permute-start | bytes 196616 | tf_op jit(solution)/shard_map/ppermute | solution.py:409
  3.5 4.0 %collective-permute-start.2 = (f32[128,128]{1,0:T(8,128)S(1)}, f32[128,128]{1,0:T(8,128)S(1)}, u32[]{:S(2)}, u32[]{:S(2)}) collective-permute-start(f32[128,128]{1,0:T(8,128)S(1)} %get-tuple-element.34), channel_id=1, source_target_pairs={{0,24},{4,28},{8,16},{12,20},{16,8},{20,12},{24,0},{28,4},{1,25},{... | collective-permute-start | bytes 196616 | tf_op jit(solution)/shard_map/ppermute | solution.py:409
  4.8 3.1 %copy-start.1 = (f32[1,8,16,384]{3,2,1,0:T(8,128)S(1)}, f32[1,8,16,384]{3,2,1,0:T(8,128)}, u32[]{:S(2)}) copy-start(f32[1,8,16,384]{3,2,1,0:T(8,128)} %param.6) | copy-start | bytes 589828
  4.8 3.1 %copy-start.2 = (f32[8,16,384]{2,1,0:T(8,128)S(1)}, f32[8,16,384]{2,1,0:T(8,128)}, u32[]{:S(2)}) copy-start(f32[8,16,384]{2,1,0:T(8,128)} %param.7) | copy-start | bytes 589828
  4.8 4.1 %collective-permute-start.4 = (f32[32,128]{1,0:T(8,128)S(1)}, f32[32,128]{1,0:T(8,128)S(1)}, u32[]{:S(2)}, u32[]{:S(2)}) collective-permute-start(f32[32,128]{1,0:T(8,128)S(1)} %slice_add_fusion.5.refs_0_), channel_id=1, source_target_pairs={{0,28},{4,24},{8,20},{12,16},{16,12},{20,8},{24,4},{28,0},{1,29},{... | collective-permute-start | bytes 49160 | tf_op jit(solution)/shard_map/ppermute | solution.py:409
  7.5 1.4 %collective-permute-start.3 = (f32[32,128]{1,0:T(8,128)S(1)}, f32[32,128]{1,0:T(8,128)S(1)}, u32[]{:S(2)}, u32[]{:S(2)}) collective-permute-start(f32[32,128]{1,0:T(8,128)S(1)} %slice_add_fusion.4.refs_1_), channel_id=1, source_target_pairs={{0,8},{4,12},{8,0},{12,4},{16,24},{20,28},{24,16},{28,20},{1,9},{5... | collective-permute-start | bytes 49160 | tf_op jit(solution)/shard_map/ppermute | solution.py:409
  7.8 1.1 %copy-start.3 = (f32[4096]{0:T(1024)S(1)}, f32[4096]{0:T(1024)}, u32[]{:S(2)}) copy-start(f32[4096]{0:T(1024)} %param.10) | copy-start | bytes 49156
  9.5 2.3 %collective-permute-start.5 = (f32[128,128]{1,0:T(8,128)S(1)}, f32[128,128]{1,0:T(8,128)S(1)}, u32[]{:S(2)}, u32[]{:S(2)}) collective-permute-start(f32[128,128]{1,0:T(8,128)S(1)} %get-tuple-element.40), channel_id=1, source_target_pairs={{0,8},{4,12},{8,0},{12,4},{16,24},{20,28},{24,16},{28,20},{1,9},{5... | collective-permute-start | bytes 196616 | tf_op jit(solution)/shard_map/ppermute | solution.py:409
  10.0 4.3 %collective-permute-start.6 = (f32[128,128]{1,0:T(8,128)S(1)}, f32[128,128]{1,0:T(8,128)S(1)}, u32[]{:S(2)}, u32[]{:S(2)}) collective-permute-start(f32[128,128]{1,0:T(8,128)S(1)} %get-tuple-element.41), channel_id=1, source_target_pairs={{0,4},{4,0},{8,12},{12,8},{16,20},{20,16},{24,28},{28,24},{1,5},{5... | collective-permute-start | bytes 196616 | tf_op jit(solution)/shard_map/ppermute | solution.py:409
  10.6 4.1 %collective-permute-start.7 = (f32[128,128]{1,0:T(8,128)S(1)}, f32[128,128]{1,0:T(8,128)S(1)}, u32[]{:S(2)}, u32[]{:S(2)}) collective-permute-start(f32[128,128]{1,0:T(8,128)S(1)} %get-tuple-element.42), channel_id=1, source_target_pairs={{0,24},{4,28},{8,16},{12,20},{16,8},{20,12},{24,0},{28,4},{1,25},{... | collective-permute-start | bytes 196616 | tf_op jit(solution)/shard_map/ppermute | solution.py:409
  11.8 4.2 %collective-permute-start.9 = (f32[32,128]{1,0:T(8,128)S(1)}, f32[32,128]{1,0:T(8,128)S(1)}, u32[]{:S(2)}, u32[]{:S(2)}) collective-permute-start(f32[32,128]{1,0:T(8,128)S(1)} %slice_add_fusion.3.refs_0_), channel_id=1, source_target_pairs={{0,28},{4,24},{8,20},{12,16},{16,12},{20,8},{24,4},{28,0},{1,29},{... | collective-permute-start | bytes 49160 | tf_op jit(solution)/shard_map/ppermute | solution.py:409
  14.8 1.2 %collective-permute-start.8 = (f32[32,128]{1,0:T(8,128)S(1)}, f32[32,128]{1,0:T(8,128)S(1)}, u32[]{:S(2)}, u32[]{:S(2)}) collective-permute-start(f32[32,128]{1,0:T(8,128)S(1)} %slice_add_fusion.2.refs_1_), channel_id=1, source_target_pairs={{0,8},{4,12},{8,0},{12,4},{16,24},{20,28},{24,16},{28,20},{1,9},{5... | collective-permute-start | bytes 49160 | tf_op jit(solution)/shard_map/ppermute | solution.py:409
  16.6 4.2 %collective-permute-start.11 = (f32[128,128]{1,0:T(8,128)S(1)}, f32[128,128]{1,0:T(8,128)S(1)}, u32[]{:S(2)}, u32[]{:S(2)}) collective-permute-start(f32[128,128]{1,0:T(8,128)S(1)} %get-tuple-element.47), channel_id=1, source_target_pairs={{0,24},{4,28},{8,16},{12,20},{16,8},{20,12},{24,0},{28,4},{1,25},{... | collective-permute-start | bytes 196616 | tf_op jit(solution)/shard_map/ppermute | solution.py:409
  18.1 4.4 %collective-permute-start.12 = (f32[128,128]{1,0:T(8,128)S(1)}, f32[128,128]{1,0:T(8,128)S(1)}, u32[]{:S(2)}, u32[]{:S(2)}) collective-permute-start(f32[128,128]{1,0:T(8,128)S(1)} %get-tuple-element.48), channel_id=1, source_target_pairs={{0,4},{4,0},{8,12},{12,8},{16,20},{20,16},{24,28},{28,24},{1,5},{5... | collective-permute-start | bytes 196616 | tf_op jit(solution)/shard_map/ppermute | solution.py:409
  19.6 1.2 %collective-permute-start.10 = (f32[96,128]{1,0:T(8,128)S(1)}, f32[96,128]{1,0:T(8,128)S(1)}, u32[]{:S(2)}, u32[]{:S(2)}) collective-permute-start(f32[96,128]{1,0:T(8,128)S(1)} %slice.33), channel_id=1, source_target_pairs={{0,8},{4,12},{8,0},{12,4},{16,24},{20,28},{24,16},{28,20},{1,9},{5... | collective-permute-start | bytes 147464 | tf_op jit(solution)/shard_map/ppermute | solution.py:409
  19.6 4.9 %collective-permute-start.14 = (f32[32,128]{1,0:T(8,128)S(1)}, f32[32,128]{1,0:T(8,128)S(1)}, u32[]{:S(2)}, u32[]{:S(2)}) collective-permute-start(f32[32,128]{1,0:T(8,128)S(1)} %get-tuple-element.50), channel_id=1, source_target_pairs={{0,28},{4,24},{8,20},{12,16},{16,12},{20,8},{24,4},{28,0},{1,29},{... | collective-permute-start | bytes 49160 | tf_op jit(solution)/shard_map/ppermute | solution.py:409
  22.9 6.9 %collective-permute-start.13 = (f32[128,384]{1,0:T(8,128)S(1)}, f32[128,384]{1,0:T(8,128)S(1)}, u32[]{:S(2)}, u32[]{:S(2)}) collective-permute-start(f32[128,384]{1,0:T(8,128)S(1)} %local_3.1.refs_4_), channel_id=1, source_target_pairs={{0,1},{1,0},{2,3},{3,2},{4,5},{5,4},{6,7},{7,6},{8,9},{9,8},{10,11... | collective-permute-start | bytes 589832 | tf_op jit(solution)/shard_map/ppermute | solution.py:414
  24.5 1.2 %collective-permute-start.15 = (f32[32,128]{1,0:T(8,128)S(1)}, f32[32,128]{1,0:T(8,128)S(1)}, u32[]{:S(2)}, u32[]{:S(2)}) collective-permute-start(f32[32,128]{1,0:T(8,128)S(1)} %slice_add_fusion), channel_id=1, source_target_pairs={{0,8},{4,12},{8,0},{12,4},{16,24},{20,28},{24,16},{28,20},{1,9},{5... | collective-permute-start | bytes 49160 | tf_op jit(solution)/shard_map/ppermute | solution.py:409
  25.8 4.0 %collective-permute-start.16 = (f32[32,128]{1,0:T(8,128)S(1)}, f32[32,128]{1,0:T(8,128)S(1)}, u32[]{:S(2)}, u32[]{:S(2)}) collective-permute-start(f32[32,128]{1,0:T(8,128)S(1)} %add.34.refs_5_), channel_id=1, source_target_pairs={{0,1},{1,0},{2,3},{3,2},{4,5},{5,4},{6,7},{7,6},{8,9},{9,8},{10,11... | collective-permute-start | bytes 49160 | tf_op jit(solution)/shard_map/ppermute | solution.py:414
  30.3 10.4 %collective-permute-start.17 = (f32[128,384]{1,0:T(8,128)S(1)}, f32[128,384]{1,0:T(8,128)S(1)}, u32[]{:S(2)}, u32[]{:S(2)}) collective-permute-start(f32[128,384]{1,0:T(8,128)S(1)} %square_more.1), channel_id=1, source_target_pairs={{0,3},{1,2},{2,1},{3,0},{4,7},{5,6},{6,5},{7,4},{8,11},{9,10},{10,... | collective-permute-start | bytes 589832 | tf_op jit(solution)/shard_map/ppermute | solution.py:414
